TPU v7x, 32 devices: a whole 2x2x4 slice. The times are simulated.
32 devices in a mesh: dp: 8 (over y, x, core), ctx: 4 (over z).
Axes of the slice: x: 2, y: 2, z: 4, core: 2. Of those that a mesh axis runs over, the one named last changes fastest.
Arguments:
- layer_in: bfloat16 [8, 2, 1, 1024, 896], P('dp', None, None, 'ctx'), may hold values from -6 to 6
- doc_ids: int32 [8, 2, 1, 1024], P('dp'), may hold values from 0 to 7, never falling along the last dimension, each value on 1 to 512 neighbouring positions
- cotangent: bfloat16 [8, 2, 1, 1024, 896], P('dp', None, None, 'ctx'), may hold values from -6 to 6
- first_gain: bfloat16 [896], P(('dp', 'ctx')), may hold values from 0.099609375 to 1.8984375
- query_weight: bfloat16 [896, 896], P(('dp', 'ctx')), may hold values from -0.1875 to 0.1875
- query_bias: bfloat16 [896], P(('dp', 'ctx')), may hold values from -3 to 3
- key_weight: bfloat16 [896, 128], P(('dp', 'ctx')), may hold values from -0.1875 to 0.1875
- key_bias: bfloat16 [128], P(('dp', 'ctx')), may hold values from -3 to 3
- value_weight: bfloat16 [896, 128], P(('dp', 'ctx')), may hold values from -0.1875 to 0.1875
- value_bias: bfloat16 [128], P(('dp', 'ctx')), may hold values from -3 to 3
- out_weight: bfloat16 [896, 896], P(('dp', 'ctx')), may hold values from -1 to 1
- second_gain: bfloat16 [896], P(('dp', 'ctx')), may hold values from 0.099609375 to 1.8984375
- gate_weight: bfloat16 [896, 4864], P('dp', 'ctx'), may hold values from -0.1875 to 0.1875
- up_weight: bfloat16 [896, 4864], P('dp', 'ctx'), may hold values from -0.1875 to 0.1875
- down_weight: bfloat16 [4864, 896], P('ctx', 'dp'), may hold values from -0.078125 to 0.078125
Outputs:
- layer_out: bfloat16 [8, 2, 1, 1024, 896], P('dp', None, None, 'ctx')
- input_grad: float32 [8, 2, 1, 1024, 896], P('dp', None, None, 'ctx')
- first_gain_grad: float32 [896], P(('dp', 'ctx'))
- query_weight_grad: float32 [896, 896], P(('dp', 'ctx'))
- query_bias_grad: float32 [896], P(('dp', 'ctx'))
- key_weight_grad: float32 [896, 128], P(('dp', 'ctx'))
- key_bias_grad: float32 [128], P(('dp', 'ctx'))
- value_weight_grad: float32 [896, 128], P(('dp', 'ctx'))
- value_bias_grad: float32 [128], P(('dp', 'ctx'))
- out_weight_grad: float32 [896, 896], P(('dp', 'ctx'))
- second_gain_grad: float32 [896], P(('dp', 'ctx'))
- gate_weight_grad: float32 [896, 4864], P('dp', 'ctx')
- up_weight_grad: float32 [896, 4864], P('dp', 'ctx')
- down_weight_grad: float32 [4864, 896], P('ctx', 'dp')
Inputs may be any that keep to these rules, and one draw needn't show every extreme that they name: `doc_ids`: along each sequence the document numbers never fall, every number from 0 to 7 occurs, and no document holds more than 512 tokens; some document holds exactly that many.
All inputs are finite; a program needn't handle non-finite values.
Results may differ from a plain program's by a relative error of at most 0.017.
Values may be sent and summed in bfloat16 or wider, within the bound.
No kernel may reach another device: no remote copies, remote signals or barrier semaphores. Data moves between devices by JAX's collectives and lax.ppermute only.
A program may use at most 192 MiB of HBM per device.

v0:
```python
import jax
import jax.numpy as jnp
from jax import lax
from jax.sharding import PartitionSpec as P

D = 896
HEADS = 14
KV_HEADS = 2
HEAD = 64


epsilon = 1e-06
theta = 10000.0
masked = -1e30


def rotation(positions, head_size):
    exponent = jnp.arange(head_size // 2, dtype=jnp.float32) * (2.0 / head_size)
    frequency = jnp.power(jnp.float32(theta), -exponent)
    angle = positions.astype(jnp.float32)[:, None] * frequency[None, :]
    angle = jnp.concatenate([angle, angle], axis=-1)
    return (jnp.cos(angle)[:, None, :], jnp.sin(angle)[:, None, :])


def turned(values_in):
    half_width = values_in.shape[-1] // 2
    return jnp.concatenate([-values_in[..., half_width:], values_in[..., :half_width]], axis=-1)


def turned_back(values_in):
    half_width = values_in.shape[-1] // 2
    return jnp.concatenate([values_in[..., half_width:], -values_in[..., :half_width]], axis=-1)


def rotate(values_in, cosines, sines):
    return values_in * cosines + turned(values_in) * sines


def rotate_back(values_in, cosines, sines):
    return values_in * cosines + turned_back(values_in * sines)


def scaled(values_in):
    return lax.rsqrt(jnp.mean(values_in * values_in, axis=-1, keepdims=True) + epsilon)


def norm_back(grad_in, values_in, inverse, gain_full):
    weighted = grad_in * gain_full
    return inverse * weighted - values_in * (inverse * inverse * inverse) * jnp.mean(
        weighted * values_in, axis=-1, keepdims=True
    )


def raw_scores(queries, keys_in, allowed, score_scale):
    scores = (
        jnp.einsum("qkgd,skd->kgqs", queries, keys_in, preferred_element_type=jnp.float32)
        * score_scale
    )
    return jnp.where(allowed, scores, masked)


def attend(queries, keys_in, values_in, allowed, score_scale):
    scores = raw_scores(queries, keys_in, allowed, score_scale)
    largest = jnp.max(scores, axis=-1, keepdims=True)
    exponent = jnp.exp(scores - largest)
    totals = jnp.sum(exponent, axis=-1, keepdims=True)
    soft_low = (exponent / totals).astype(jnp.bfloat16)
    mixed_heads = jnp.einsum(
        "kgqs,skd->qkgd", soft_low, values_in, preferred_element_type=jnp.float32
    )
    return (mixed_heads, largest, totals)


def attend_back(queries, keys_in, values_in, allowed, largest, totals, grad_mixed, score_scale):
    scores = raw_scores(queries, keys_in, allowed, score_scale)
    soft_weights = jnp.exp(scores - largest) / totals
    soft_low = soft_weights.astype(jnp.bfloat16)
    grad_soft = jnp.einsum(
        "qkgd,skd->kgqs", grad_mixed, values_in, preferred_element_type=jnp.float32
    )
    row_delta = jnp.sum(soft_weights * grad_soft, axis=-1, keepdims=True)
    grad_scores = (soft_weights * (grad_soft - row_delta)).astype(jnp.bfloat16)
    grad_queries = (
        jnp.einsum("kgqs,skd->qkgd", grad_scores, keys_in, preferred_element_type=jnp.float32)
        * score_scale
    )
    grad_keys = (
        jnp.einsum("kgqs,qkgd->skd", grad_scores, queries, preferred_element_type=jnp.float32)
        * score_scale
    )
    grad_values = jnp.einsum(
        "kgqs,qkgd->skd", soft_low, grad_mixed, preferred_element_type=jnp.float32
    )
    return (grad_queries, grad_keys, grad_values)


def add_pairs(first_set, second_set):
    return tuple(
        (earlier_part + later_part for earlier_part, later_part in zip(first_set, second_set))
    )


def body(
    layer_in,
    doc_ids,
    cotangent,
    first_gain,
    query_weight,
    query_bias,
    key_weight,
    key_bias,
    value_weight,
    value_bias,
    out_weight,
    second_gain,
    gate_weight,
    up_weight,
    down_weight,
):
    device_rank = lax.axis_index("ctx")
    micro_count = layer_in.shape[1]
    sequence_count = layer_in.shape[2]
    shard_rows = layer_in.shape[3]
    model_width = layer_in.shape[4]
    key_count = doc_ids.shape[3]
    group_size = HEADS // KV_HEADS
    query_width = HEADS * HEAD
    pair_width = KV_HEADS * HEAD
    hidden_part = gate_weight.shape[1]
    score_scale = HEAD ** (-0.5)

    def fetch_all(after):
        held = lax.optimization_barrier(
            (
                (
                    first_gain,
                    query_weight,
                    query_bias,
                    key_weight,
                    key_bias,
                    value_weight,
                    value_bias,
                    out_weight,
                    second_gain,
                    gate_weight,
                    up_weight,
                    down_weight,
                ),
                after,
            )
        )[0]
        attention_set = (
            lax.all_gather(held[0], ("dp", "ctx"), axis=0, tiled=True),
            lax.all_gather(held[1], ("dp", "ctx"), axis=0, tiled=True),
            lax.all_gather(held[2], ("dp", "ctx"), axis=0, tiled=True),
            lax.all_gather(held[3], ("dp", "ctx"), axis=0, tiled=True),
            lax.all_gather(held[4], ("dp", "ctx"), axis=0, tiled=True),
            lax.all_gather(held[5], ("dp", "ctx"), axis=0, tiled=True),
            lax.all_gather(held[6], ("dp", "ctx"), axis=0, tiled=True),
            lax.all_gather(held[7], ("dp", "ctx"), axis=0, tiled=True),
            lax.all_gather(held[8], ("dp", "ctx"), axis=0, tiled=True),
        )
        feed_set = (
            lax.all_gather(held[9], "dp", axis=0, tiled=True),
            lax.all_gather(held[10], "dp", axis=0, tiled=True),
            lax.all_gather(held[11], "dp", axis=1, tiled=True),
        )
        return tuple(attention_set) + tuple(feed_set)

    attention_shapes = (
        (D,),
        (D, query_width),
        (query_width,),
        (D, pair_width),
        (pair_width,),
        (D, pair_width),
        (pair_width,),
        (query_width, D),
        (D,),
    )
    feed_shapes = ((D, hidden_part), (D, hidden_part), (hidden_part, D))
    attention_sums = tuple((jnp.zeros(shape_one, jnp.float32) for shape_one in attention_shapes))
    feed_sums = tuple((jnp.zeros(shape_one, jnp.float32) for shape_one in feed_shapes))
    attention_shards = None
    feed_shards = None
    out_list = []
    grad_list = []
    for micro_batch in range(micro_count):
        gathered = fetch_all(layer_in[0, micro_batch])
        (
            gain_one,
            w_query,
            b_query,
            w_key,
            b_key,
            w_value,
            b_value,
            w_out,
            gain_two,
            w_gate,
            w_up,
            w_down,
        ) = gathered
        tokens = layer_in[0, micro_batch].astype(jnp.float32).reshape(-1, model_width)
        docs_all = doc_ids[0, micro_batch]
        own_docs = lax.dynamic_slice_in_dim(docs_all, device_rank * shard_rows, shard_rows, 1)
        row_index = device_rank * shard_rows + jnp.arange(shard_rows, dtype=jnp.int32)
        earlier = jnp.sum((docs_all[:, None, :] < own_docs[:, :, None]).astype(jnp.int32), axis=2)
        positions = row_index[None, :] - earlier
        allowed = (own_docs[:, :, None] == docs_all[:, None, :]) & (
            jnp.arange(key_count, dtype=jnp.int32)[None, None, :] <= row_index[None, :, None]
        )
        cosines, sines = rotation(positions.reshape(-1), HEAD)
        inverse_one = scaled(tokens)
        normed_one = (tokens * inverse_one * gain_one.astype(jnp.float32)).astype(jnp.bfloat16)
        queries = jnp.dot(normed_one, w_query, preferred_element_type=jnp.float32) + b_query.astype(
            jnp.float32
        )
        keys_pre = jnp.dot(normed_one, w_key, preferred_element_type=jnp.float32) + b_key.astype(
            jnp.float32
        )
        values_pre = jnp.dot(
            normed_one, w_value, preferred_element_type=jnp.float32
        ) + b_value.astype(jnp.float32)
        rot_query = rotate(queries.reshape(-1, HEADS, HEAD), cosines, sines).astype(jnp.bfloat16)
        rot_keys = rotate(keys_pre.reshape(-1, KV_HEADS, HEAD), cosines, sines).astype(jnp.bfloat16)
        values_low = values_pre.astype(jnp.bfloat16)
        keys_all, values_all = (
            lax.all_gather(
                rot_keys.reshape(sequence_count, shard_rows, pair_width), "ctx", axis=1, tiled=True
            ),
            lax.all_gather(
                values_low.reshape(sequence_count, shard_rows, pair_width),
                "ctx",
                axis=1,
                tiled=True,
            ),
        )
        query_seq = rot_query.reshape(sequence_count, shard_rows, KV_HEADS, group_size, HEAD)
        keys_seq = keys_all.reshape(sequence_count, key_count, KV_HEADS, HEAD)
        values_seq = values_all.reshape(sequence_count, key_count, KV_HEADS, HEAD)
        mixed_heads, largest, totals = lax.map(
            lambda item_pack: attend(
                item_pack[0], item_pack[1], item_pack[2], item_pack[3], score_scale
            ),
            (query_seq, keys_seq, values_seq, allowed),
        )
        mixed_low = mixed_heads.reshape(-1, query_width).astype(jnp.bfloat16)
        middle = tokens + jnp.dot(mixed_low, w_out, preferred_element_type=jnp.float32)
        inverse_two = scaled(middle)
        normed_two = (middle * inverse_two * gain_two.astype(jnp.float32)).astype(jnp.bfloat16)
        rows_all = lax.all_gather(
            normed_two.reshape(sequence_count, shard_rows, model_width), "ctx", axis=1, tiled=True
        ).reshape(-1, model_width)
        gate_pre = jnp.dot(rows_all, w_gate, preferred_element_type=jnp.float32)
        up_pre = jnp.dot(rows_all, w_up, preferred_element_type=jnp.float32)
        sigmoid_gate = jax.nn.sigmoid(gate_pre)
        activated = (gate_pre * sigmoid_gate * up_pre).astype(jnp.bfloat16)
        partial_out = jnp.dot(activated, w_down, preferred_element_type=jnp.float32)
        feed_out = (
            lax.psum_scatter(
                partial_out.reshape(sequence_count, key_count, model_width).astype(jnp.bfloat16),
                "ctx",
                scatter_dimension=1,
                tiled=True,
            )
            .astype(jnp.float32)
            .reshape(-1, model_width)
        )
        result = middle + feed_out
        out_list.append(
            result.astype(jnp.bfloat16).reshape(sequence_count, shard_rows, model_width)
        )
        gathered = fetch_all(result)
        (
            gain_one,
            w_query,
            b_query,
            w_key,
            b_key,
            w_value,
            b_value,
            w_out,
            gain_two,
            w_gate,
            w_up,
            w_down,
        ) = gathered
        upstream = cotangent[0, micro_batch].astype(jnp.float32).reshape(-1, model_width)
        upstream_low = upstream.astype(jnp.bfloat16)
        upstream_all = lax.all_gather(
            upstream_low.reshape(sequence_count, shard_rows, model_width), "ctx", axis=1, tiled=True
        ).reshape(-1, model_width)
        grad_down = jnp.einsum(
            "nf,nd->fd", activated, upstream_all, preferred_element_type=jnp.float32
        )
        grad_act = jnp.einsum("nd,fd->nf", upstream_all, w_down, preferred_element_type=jnp.float32)
        grad_gate = (
            grad_act * up_pre * sigmoid_gate * (1.0 + gate_pre * (1.0 - sigmoid_gate))
        ).astype(jnp.bfloat16)
        grad_up = (grad_act * gate_pre * sigmoid_gate).astype(jnp.bfloat16)
        grad_gate_w = jnp.einsum(
            "nd,nf->df", rows_all, grad_gate, preferred_element_type=jnp.float32
        )
        grad_up_w = jnp.einsum("nd,nf->df", rows_all, grad_up, preferred_element_type=jnp.float32)
        normed_part = jnp.einsum(
            "nf,df->nd", grad_gate, w_gate, preferred_element_type=jnp.float32
        ) + jnp.einsum("nf,df->nd", grad_up, w_up, preferred_element_type=jnp.float32)
        grad_normed_two = lax.psum_scatter(
            normed_part.reshape(sequence_count, key_count, model_width),
            "ctx",
            scatter_dimension=1,
            tiled=True,
        ).reshape(-1, model_width)
        grad_gain_two = jnp.sum(grad_normed_two * (middle * inverse_two), axis=0)
        feed_local = (grad_gate_w, grad_up_w, grad_down)
        feed_sums = add_pairs(feed_sums, feed_local)
        grad_middle = upstream + norm_back(
            grad_normed_two, middle, inverse_two, gain_two.astype(jnp.float32)
        )
        branch_low = grad_middle.astype(jnp.bfloat16)
        grad_out_w = jnp.einsum(
            "nq,nd->qd", mixed_low, branch_low, preferred_element_type=jnp.float32
        )
        grad_mixed = jnp.einsum(
            "nd,qd->nq", branch_low, w_out, preferred_element_type=jnp.float32
        ).astype(jnp.bfloat16)
        grad_mixed_seq = grad_mixed.reshape(sequence_count, shard_rows, KV_HEADS, group_size, HEAD)
        grad_queries, grad_keys, grad_values = lax.map(
            lambda item_pack: attend_back(
                item_pack[0],
                item_pack[1],
                item_pack[2],
                item_pack[3],
                item_pack[4],
                item_pack[5],
                item_pack[6],
                score_scale,
            ),
            (query_seq, keys_seq, values_seq, allowed, largest, totals, grad_mixed_seq),
        )
        grad_keys_own, grad_values_own = (
            lax.psum_scatter(
                grad_keys.reshape(sequence_count, key_count, pair_width),
                "ctx",
                scatter_dimension=1,
                tiled=True,
            ),
            lax.psum_scatter(
                grad_values.reshape(sequence_count, key_count, pair_width),
                "ctx",
                scatter_dimension=1,
                tiled=True,
            ),
        )
        query_grad_low = rotate_back(grad_queries.reshape(-1, HEADS, HEAD), cosines, sines).astype(
            jnp.bfloat16
        )
        query_grad_low = query_grad_low.reshape(-1, query_width)
        key_grad_low = rotate_back(
            grad_keys_own.reshape(-1, KV_HEADS, HEAD), cosines, sines
        ).astype(jnp.bfloat16)
        key_grad_low = key_grad_low.reshape(-1, pair_width)
        value_grad_low = grad_values_own.reshape(-1, pair_width).astype(jnp.bfloat16)
        grad_query_w = jnp.einsum(
            "nd,nq->dq", normed_one, query_grad_low, preferred_element_type=jnp.float32
        )
        grad_key_w = jnp.einsum(
            "nd,nq->dq", normed_one, key_grad_low, preferred_element_type=jnp.float32
        )
        grad_value_w = jnp.einsum(
            "nd,nq->dq", normed_one, value_grad_low, preferred_element_type=jnp.float32
        )
        grad_normed_one = (
            jnp.einsum("nq,dq->nd", query_grad_low, w_query, preferred_element_type=jnp.float32)
            + jnp.einsum("nq,dq->nd", key_grad_low, w_key, preferred_element_type=jnp.float32)
            + jnp.einsum("nq,dq->nd", value_grad_low, w_value, preferred_element_type=jnp.float32)
        )
        grad_gain_one = jnp.sum(grad_normed_one * (tokens * inverse_one), axis=0)
        token_grad = grad_middle + norm_back(
            grad_normed_one, tokens, inverse_one, gain_one.astype(jnp.float32)
        )
        grad_list.append(token_grad.reshape(sequence_count, shard_rows, model_width))
        attention_local = (
            grad_gain_one,
            grad_query_w,
            jnp.sum(query_grad_low.astype(jnp.float32), axis=0),
            grad_key_w,
            jnp.sum(key_grad_low.astype(jnp.float32), axis=0),
            grad_value_w,
            jnp.sum(value_grad_low.astype(jnp.float32), axis=0),
            grad_out_w,
            grad_gain_two,
        )
        attention_sums = add_pairs(attention_sums, attention_local)
    feed_shards = tuple(
        (
            lax.psum_scatter(
                feed_sums[0].astype(jnp.bfloat16), "dp", scatter_dimension=0, tiled=True
            ).astype(jnp.float32),
            lax.psum_scatter(
                feed_sums[1].astype(jnp.bfloat16), "dp", scatter_dimension=0, tiled=True
            ).astype(jnp.float32),
            lax.psum_scatter(
                feed_sums[2].astype(jnp.bfloat16), "dp", scatter_dimension=1, tiled=True
            ).astype(jnp.float32),
        )
    )
    attention_shards = tuple(
        (
            lax.psum_scatter(attention_sums[0], ("dp", "ctx"), scatter_dimension=0, tiled=True),
            lax.psum_scatter(attention_sums[1], ("dp", "ctx"), scatter_dimension=0, tiled=True),
            lax.psum_scatter(attention_sums[2], ("dp", "ctx"), scatter_dimension=0, tiled=True),
            lax.psum_scatter(attention_sums[3], ("dp", "ctx"), scatter_dimension=0, tiled=True),
            lax.psum_scatter(attention_sums[4], ("dp", "ctx"), scatter_dimension=0, tiled=True),
            lax.psum_scatter(attention_sums[5], ("dp", "ctx"), scatter_dimension=0, tiled=True),
            lax.psum_scatter(attention_sums[6], ("dp", "ctx"), scatter_dimension=0, tiled=True),
            lax.psum_scatter(attention_sums[7], ("dp", "ctx"), scatter_dimension=0, tiled=True),
            lax.psum_scatter(attention_sums[8], ("dp", "ctx"), scatter_dimension=0, tiled=True),
        )
    )
    layer_out = jnp.stack(out_list)[None]
    input_grad = jnp.stack(grad_list)[None]
    return (
        layer_out,
        input_grad,
        attention_shards[0],
        attention_shards[1],
        attention_shards[2],
        attention_shards[3],
        attention_shards[4],
        attention_shards[5],
        attention_shards[6],
        attention_shards[7],
        attention_shards[8],
        feed_shards[0],
        feed_shards[1],
        feed_shards[2],
    )


def solution(mesh):
    return jax.shard_map(
        body,
        mesh=mesh,
        in_specs=(
            P("dp", None, None, "ctx", None),
            P("dp", None, None, None),
            P("dp", None, None, "ctx", None),
            P(("dp", "ctx")),
            P(("dp", "ctx"), None),
            P(("dp", "ctx")),
            P(("dp", "ctx"), None),
            P(("dp", "ctx")),
            P(("dp", "ctx"), None),
            P(("dp", "ctx")),
            P(("dp", "ctx"), None),
            P(("dp", "ctx")),
            P("dp", "ctx"),
            P("dp", "ctx"),
            P("ctx", "dp"),
        ),
        out_specs=(
            P("dp", None, None, "ctx", None),
            P("dp", None, None, "ctx", None),
            P(("dp", "ctx")),
            P(("dp", "ctx"), None),
            P(("dp", "ctx")),
            P(("dp", "ctx"), None),
            P(("dp", "ctx")),
            P(("dp", "ctx"), None),
            P(("dp", "ctx")),
            P(("dp", "ctx"), None),
            P(("dp", "ctx")),
            P("dp", "ctx"),
            P("dp", "ctx"),
            P("ctx", "dp"),
        ),
        check_vma=False,
    )
```

profile of v0, /device:TPU:0, one launch (start us, length us, event | category | flops | bytes accessed | tf_op | source)
XLA Modules:
  0.0 1764.6 jit_solution(16620072690701701629)
XLA Ops:
  13.7 42.2 %all-reduce.24 = (bf16[128]{0:T(256)(128)(2,1)S(1)}, bf16[896]{0:T(1024)(128)(2,1)S(1)}, bf16[128]{0:T(256)(128)(2,1)S(1)}, bf16[896]{0:T(1024)(128)(2,1)S(1)}, bf16[896]{0:T(1024)(128)(2,1)S(1)}) all-reduce(bf16[128]{0:T(256)(128)(2,1)S(1)} %dynamic-update-slice.1, ...), channel_id=1, replica_groups=mesh['dp'=8,'ctx'=4] {'dp','ctx'}, use_global_device_ids=true, to_apply=%add.1 | all-reduce | flops 2944 | bytes 11776
  57.4 69.0 %all-gather.8 = bf16[32,28,128]{2,1,0:T(8,128)(2,1)S(1)} all-gather(bf16[1,28,128]{2,1,0:T(8,128)(2,1)} %bitcast.560), channel_id=1, replica_groups=mesh['dp'=8,'ctx'=4] {'dp','ctx'}, dimensions={0}, use_global_device_ids=true | all-gather | bytes 236544 | tf_op jit(solution)/shard_map/all_gather | solution.py:158
  128.8 65.8 %all-gather.9 = bf16[32,28,128]{2,1,0:T(8,128)(2,1)S(1)} all-gather(bf16[1,28,128]{2,1,0:T(8,128)(2,1)S(1)} %bitcast.557), channel_id=1, replica_groups=mesh['dp'=8,'ctx'=4] {'dp','ctx'}, dimensions={0}, use_global_device_ids=true | all-gather | bytes 236544 | tf_op jit(solution)/shard_map/all_gather | solution.py:156
  197.5 14.1 all-gather
  212.4 13.8 all-gather.3
  227.2 15.2 all-gather.1
  242.5 15.0 all-gather.4
  269.5 10.8 fusion.162
  280.3 7.4 fusion.52
  296.3 10.9 fusion.163
  307.2 6.7 fusion.49
  318.2 38.6 %all-gather.58.cloned.1.call-done = bf16[1024,896]{1,0:T(8,128)(2,1)} async-done(((bf16[256,896]{1,0:T(8,128)(2,1)}), bf16[1024,896]{1,0:T(8,128)(2,1)}) %all-gather.58.cloned.1.call-update) | async-done | bytes 1835024 | tf_op jit(solution)/shard_map/all_gather | solution.py:252
  356.8 7.2 fusion.164
  364.0 22.2 %all-gather.42.cloned.1.call-done = bf16[896,1216]{1,0:T(8,128)(2,1)} async-done(((bf16[112,1216]{1,0:T(8,128)(2,1)}), bf16[896,1216]{1,0:T(8,128)(2,1)}) %all-gather.42.cloned.1.call-update) | async-done | bytes 2179088 | tf_op jit(solution)/shard_map/all_gather | solution.py:165
  386.2 10.2 multiply_convert_fusion.1
  396.4 20.3 %all-gather.44.cloned.1.call-done = bf16[1216,896]{0,1:T(8,128)(2,1)} async-done(((bf16[1216,112]{0,1:T(8,128)(2,1)}), bf16[1216,896]{0,1:T(8,128)(2,1)}) %all-gather.44.cloned.1.call-update) | async-done | bytes 2179088 | tf_op jit(solution)/shard_map/all_gather | solution.py:166
  416.7 6.6 convert_bitcast_fusion.1
  423.7 36.5 %all-gather.60.cloned.1.call-done = bf16[1024,896]{1,0:T(8,128)(2,1)} async-done(((bf16[256,896]{1,0:T(8,128)(2,1)}), bf16[1024,896]{1,0:T(8,128)(2,1)}) %all-gather.60.cloned.1.call-update) | async-done | bytes 1835024 | tf_op jit(solution)/shard_map/all_gather | solution.py:252
  460.2 5.2 fusion.165
  465.5 5.2 multiply_convert_fusion
  478.1 22.7 %reduce-scatter.20.cloned.1.call-done = bf16[1,256,896]{2,1,0:T(8,128)(2,1)} async-done(((bf16[1,1024,896]{2,1,0:T(8,128)(2,1)}), bf16[1,256,896]{2,1,0:T(8,128)(2,1)}) %reduce-scatter.20.cloned.1.call-update) | async-done | bytes 458768 | tf_op jit(solution)/shard_map/reduce_scatter | solution.py:261
  502.0 40.3 %reduce-scatter.22.cloned.1.call-done = bf16[1,256,896]{2,1,0:T(8,128)(2,1)} async-done(((bf16[1,1024,896]{2,1,0:T(8,128)(2,1)}), bf16[1,256,896]{2,1,0:T(8,128)(2,1)}) %reduce-scatter.22.cloned.1.call-update) | async-done | bytes 458768 | tf_op jit(solution)/shard_map/reduce_scatter | solution.py:261
  545.8 39.0 %all-gather.62.cloned.1.call-done = bf16[1,1,1,1024,896]{4,3,2,1,0:T(8,128)(2,1)} async-done(((bf16[1,1,1,256,896]{4,3,2,1,0:T(8,128)(2,1)}), bf16[1,1,1,1024,896]{4,3,2,1,0:T(8,128)(2,1)}) %all-gather.62.cloned.1.call-update) | async-done | bytes 1835024 | tf_op jit(solution)/shard_map/all_gather | solution.py:291
  584.9 6.9 fusion.41
  591.8 35.5 %all-gather.64.cloned.1.call-done = bf16[1,1,1,1024,896]{4,3,2,1,0:T(8,128)(2,1)} async-done(((bf16[1,1,1,256,896]{4,3,2,1,0:T(8,128)(2,1)}), bf16[1,1,1,1024,896]{4,3,2,1,0:T(8,128)(2,1)}) %all-gather.64.cloned.1.call-update) | async-done | bytes 1835024 | tf_op jit(solution)/shard_map/all_gather | solution.py:291
  627.3 7.6 add_convert_fusion
  638.0 18.7 %all-gather.46.cloned.1.call-done = bf16[1216,896]{0,1:T(8,128)(2,1)} async-done(((bf16[1216,112]{0,1:T(8,128)(2,1)}), bf16[1216,896]{0,1:T(8,128)(2,1)}) %all-gather.46.cloned.1.call-update) | async-done | bytes 2179088 | tf_op jit(solution)/shard_map/all_gather | solution.py:166
  656.7 11.1 fusion.29
  669.2 4.7 fusion.170
  673.9 13.5 all-gather.52.cloned.1.call-done
  687.4 11.1 fusion.24
  699.9 4.2 add_convert_fusion.2
  704.2 5.0 fusion.171
  717.9 7.2 fusion.166
  725.1 23.3 %all-gather.50.cloned.1.call-done = bf16[896,1216]{1,0:T(8,128)(2,1)} async-done(((bf16[112,1216]{1,0:T(8,128)(2,1)}), bf16[896,1216]{1,0:T(8,128)(2,1)}) %all-gather.50.cloned.1.call-update) | async-done | bytes 2179088 | tf_op jit(solution)/shard_map/all_gather | solution.py:165
  748.4 8.3 add_bitcast_fusion.1
  756.7 22.2 %all-gather.54.cloned.1.call-done = bf16[896,1216]{1,0:T(8,128)(2,1)} async-done(((bf16[112,1216]{1,0:T(8,128)(2,1)}), bf16[896,1216]{1,0:T(8,128)(2,1)}) %all-gather.54.cloned.1.call-update) | async-done | bytes 2179088 | tf_op jit(solution)/shard_map/all_gather | solution.py:164
  778.9 7.2 fusion.168
  786.0 23.4 %all-gather.56.cloned.1.call-done = bf16[896,1216]{1,0:T(8,128)(2,1)} async-done(((bf16[112,1216]{1,0:T(8,128)(2,1)}), bf16[896,1216]{1,0:T(8,128)(2,1)}) %all-gather.56.cloned.1.call-update) | async-done | bytes 2179088 | tf_op jit(solution)/shard_map/all_gather | solution.py:165
  809.4 8.2 add_bitcast_fusion
  817.7 37.1 %reduce-scatter.40.cloned.1.call-done = bf16[1216,112]{0,1:T(8,128)(2,1)} async-done(((bf16[1216,896]{0,1:T(8,128)(2,1)}), bf16[1216,112]{0,1:T(8,128)(2,1)}) %reduce-scatter.40.cloned.1.call-update) | async-done | bytes 272400 | tf_op jit(solution)/shard_map/reduce_scatter | solution.py:404
  856.6 69.3 %all-gather.14 = bf16[32,28,128]{2,1,0:T(8,128)(2,1)S(1)} all-gather(bf16[1,28,128]{2,1,0:T(8,128)(2,1)S(1)} %bitcast.558), channel_id=1, replica_groups=mesh['dp'=8,'ctx'=4] {'dp','ctx'}, dimensions={0}, use_global_device_ids=true | all-gather | bytes 236544 | tf_op jit(solution)/shard_map/all_gather | solution.py:156
  926.7 66.2 %all-gather.15 = bf16[32,28,128]{2,1,0:T(8,128)(2,1)S(1)} all-gather(bf16[1,28,128]{2,1,0:T(8,128)(2,1)S(1)} %bitcast.561), channel_id=1, replica_groups=mesh['dp'=8,'ctx'=4] {'dp','ctx'}, dimensions={0}, use_global_device_ids=true | all-gather | bytes 236544 | tf_op jit(solution)/shard_map/all_gather | solution.py:158
  994.5 40.1 %all-reduce.23 = (bf16[896]{0:T(1024)(128)(2,1)S(1)}, bf16[896]{0:T(1024)(128)(2,1)S(1)}, bf16[896]{0:T(1024)(128)(2,1)S(1)}, bf16[896]{0:T(1024)(128)(2,1)S(1)}) all-reduce(bf16[896]{0:T(1024)(128)(2,1)S(1)} %dynamic-update-slice.7, bf16[896]{0:T(1024)(128)(2,1)S(1)} %dynamic-update-slice.8, ...), channel_id=1, replica_groups=mesh['dp'=8,'ctx'=4] {'dp','ctx'}, use_global_device_ids=true, to_apply=%add.7 | all-reduce | flops 3584 | bytes 14336
  1035.8 68.1 %all-gather.18 = bf16[32,28,128]{2,1,0:T(8,128)(2,1)S(1)} all-gather(bf16[1,28,128]{2,1,0:T(8,128)(2,1)S(1)} %bitcast.559), channel_id=1, replica_groups=mesh['dp'=8,'ctx'=4] {'dp','ctx'}, dimensions={0}, use_global_device_ids=true | all-gather | bytes 236544 | tf_op jit(solution)/shard_map/all_gather | solution.py:156
  1104.7 66.0 %all-gather.19 = bf16[32,28,128]{2,1,0:T(8,128)(2,1)S(1)} all-gather(bf16[1,28,128]{2,1,0:T(8,128)(2,1)S(1)} %bitcast.562), channel_id=1, replica_groups=mesh['dp'=8,'ctx'=4] {'dp','ctx'}, dimensions={0}, use_global_device_ids=true | all-gather | bytes 236544 | tf_op jit(solution)/shard_map/all_gather | solution.py:158
  1190.4 59.5 %reduce-scatter.24.cloned.1.call-done = f32[1,256,896]{2,1,0:T(8,128)} async-done(((f32[1,1024,896]{2,1,0:T(8,128)}), f32[1,256,896]{2,1,0:T(8,128)}) %reduce-scatter.24.cloned.1.call-update) | async-done | bytes 917520 | tf_op jit(solution)/shard_map/reduce_scatter | solution.py:309
  1251.3 69.7 %reduce-scatter.30.cloned.1.call-done = f32[1,256,896]{2,1,0:T(8,128)} async-done(((f32[1,1024,896]{2,1,0:T(8,128)}), f32[1,256,896]{2,1,0:T(8,128)}) %reduce-scatter.30.cloned.1.call-update) | async-done | bytes 917520 | tf_op jit(solution)/shard_map/reduce_scatter | solution.py:309
  1328.3 13.1 fusion.9
  1342.9 6.8 fusion.11
  1360.5 13.5 fusion.6
  1375.1 6.8 fusion.8
  1391.3 4.8 convolution_add_fusion
  1399.3 8.5 fusion.34
  1408.2 8.5 fusion.30
  1428.6 15.2 reduce-scatter.28.cloned.1.call-done
  1446.3 19.6 %reduce-scatter.34.cloned.1.call-done = f32[1,256,128]{1,2,0:T(8,128)} async-done(((f32[1,1024,128]{1,2,0:T(8,128)}), f32[1,256,128]{1,2,0:T(8,128)}) %reduce-scatter.34.cloned.1.call-update) | async-done | bytes 131088 | tf_op jit(solution)/shard_map/reduce_scatter | solution.py:349
  1468.0 183.9 %fusion.155 = (f32[32,896]{1,0:T(8,128)}, f32[32,128]{1,0:T(8,128)S(1)}, f32[32,128]{1,0:T(8,128)S(1)}, f32[32,896]{1,0:T(8,128)S(1)}) fusion(f32[896,896]{1,0:T(8,128)} %convolution_add_fusion.1, f32[896,128]{1,0:T(8,128)} %convolution_add_fusion.11, f32[896,128]{1,0:T(8,128)} %convolution_add_fusion.10, f32[896,896]{1,0:T(8,128)} %convolution_add_fusion), kind=kCustom, calls=%all-reduce-scatter.4 | all-reduce-scatter fusion | flops 2097153 | bytes 7602176
  1670.4 4.6 collective-permute-start.11
  1675.4 38.1 %all-reduce.22 = (f32[896]{0:T(1024)S(1)}, f32[896]{0:T(1024)S(1)}, f32[128]{0:T(128)S(1)}, f32[128]{0:T(128)S(1)}, f32[896]{0:T(1024)S(1)}) all-reduce(f32[896]{0:T(1024)S(1)} %add.382, f32[896]{0:T(1024)S(1)} %copy-done.57, f32[128]{0:T(128)S(1)} %add.395, f32[128]{0:T(128)S(1)} %add.397, ...), channel_id=18, replica_groups=mesh['dp'=8,'ctx'=4] {'dp','ctx'}, use_global_device_ids=true, to_apply=%region_26.27.clone | all-reduce | flops 2944 | bytes 23552
  1716.5 4.5 collective-permute-start.9
  1733.5 4.4 collective-permute-start
  1738.6 4.7 collective-permute-start.14
  1746.4 4.7 collective-permute-start.13
  (448 shorter events, 187.8 us)
Async XLA Ops:
  7.2 121.6 %copy-start.48 = (bf16[28,128]{1,0:T(8,128)(2,1)S(1)}, bf16[28,128]{1,0:T(8,128)(2,1)}, u32[]{:S(2)}) copy-start(bf16[28,128]{1,0:T(8,128)(2,1)} %param.21) | copy-start | bytes 21508
  7.2 121.2 %copy-start.1 = (bf16[1,2,1,256,896]{4,3,2,1,0:T(8,128)(2,1)S(1)}, bf16[1,2,1,256,896]{4,3,2,1,0:T(8,128)(2,1)}, u32[]{:S(2)}) copy-start(bf16[1,2,1,256,896]{4,3,2,1,0:T(8,128)(2,1)} %param.15) | copy-start | bytes 2752516
  7.2 251.7 %all-gather.66.cloned.1.call-start = ((), (), s32[]{:S(2)}) async-start(), calls=%async_computation.35 | async-start | bytes 1892352 | tf_op jit(solution)/shard_map/all_gather | solution.py:154
  7.9 279.8 %all-gather.68.cloned.1.call-start = ((), (), s32[]{:S(2)}) async-start(), calls=%async_computation.36 | async-start | bytes 1892352 | tf_op jit(solution)/shard_map/all_gather | solution.py:160
  8.7 309.5 %all-gather.40.cloned.1.call-start = ((), (), s32[]{:S(2)}) async-start(), calls=%async_computation.11 | async-start | bytes 2580480 | tf_op jit(solution)/shard_map/all_gather | solution.py:164
  9.4 347.4 %all-gather.58.cloned.1.call-start = ((), (), s32[]{:S(2)}) async-start(), calls=%async_computation.31 | async-start | bytes 2293760 | tf_op jit(solution)/shard_map/all_gather | solution.py:252
  57.4 205.6 %copy-start.46 = (f32[896]{0:T(1024)}, f32[896]{0:T(1024)S(1)}, u32[]{:S(2)}) copy-start(f32[896]{0:T(1024)S(1)} %convert_element_type.398) | copy-start | bytes 10756
  126.4 69.0 %copy-start.64 = (s32[1,2,1,1024]{3,2,1,0:T(1,128)S(1)}, s32[1,2,1,1024]{3,2,1,0:T(1,128)}, u32[]{:S(2)}) copy-start(s32[1,2,1,1024]{3,2,1,0:T(1,128)} %param.16) | copy-start | bytes 24580
  127.0 134.3 %copy-start.51 = (f32[256]{0:T(256)}, f32[256]{0:T(256)S(1)}, u32[]{:S(2)}) copy-start(f32[256]{0:T(256)S(1)} %get-tuple-element.325) | copy-start | bytes 3076
  127.0 135.9 %copy-start.61 = (f32[256]{0:T(256)}, f32[256]{0:T(256)S(1)}, u32[]{:S(2)}) copy-start(f32[256]{0:T(256)S(1)} %get-tuple-element.355) | copy-start | bytes 3076
  196.8 97.0 %copy-start.14 = (f32[256,64]{0,1:T(8,128)}, f32[256,64]{0,1:T(8,128)S(1)}, u32[]{:S(2)}) copy-start(f32[256,64]{0,1:T(8,128)S(1)} %get-tuple-element.317) | copy-start | bytes 196612
  196.8 97.0 %copy-start.28 = (f32[256,64]{0,1:T(8,128)}, f32[256,64]{0,1:T(8,128)S(1)}, u32[]{:S(2)}) copy-start(f32[256,64]{0,1:T(8,128)S(1)} %get-tuple-element.316) | copy-start | bytes 196612
  197.5 71.0 %copy-start.16 = (f32[256,64]{0,1:T(8,128)}, f32[256,64]{0,1:T(8,128)S(1)}, u32[]{:S(2)}) copy-start(f32[256,64]{0,1:T(8,128)S(1)} %get-tuple-element.314) | copy-start | bytes 196612
  197.5 71.0 %copy-start.26 = (f32[256,64]{0,1:T(8,128)}, f32[256,64]{0,1:T(8,128)S(1)}, u32[]{:S(2)}) copy-start(f32[256,64]{0,1:T(8,128)S(1)} %get-tuple-element.313) | copy-start | bytes 196612
  316.0 70.2 %all-gather.42.cloned.1.call-start = ((), (), s32[]{:S(2)}) async-start(), calls=%async_computation.12 | async-start | bytes 2580480 | tf_op jit(solution)/shard_map/all_gather | solution.py:165
  316.6 100.1 %all-gather.44.cloned.1.call-start = ((), (), s32[]{:S(2)}) async-start(), calls=%async_computation.13 | async-start | bytes 2580480 | tf_op jit(solution)/shard_map/all_gather | solution.py:166
  317.1 143.1 %all-gather.60.cloned.1.call-start = ((), (), s32[]{:S(2)}) async-start(), calls=%async_computation.32 | async-start | bytes 2293760 | tf_op jit(solution)/shard_map/all_gather | solution.py:252
  317.9 183.0 %reduce-scatter.20.cloned.1.call-start = ((), (), s32[]{:S(2)}) async-start(), calls=%async_computation.14 | async-start | bytes 2293760 | tf_op jit(solution)/shard_map/reduce_scatter | solution.py:261
  423.3 119.0 %reduce-scatter.22.cloned.1.call-start = ((), (), s32[]{:S(2)}) async-start(), calls=%async_computation.15 | async-start | bytes 2293760 | tf_op jit(solution)/shard_map/reduce_scatter | solution.py:261
  476.2 108.6 %all-gather.62.cloned.1.call-start = ((), (), s32[]{:S(2)}) async-start(), calls=%async_computation.33 | async-start | bytes 2293760 | tf_op jit(solution)/shard_map/all_gather | solution.py:291
  477.3 150.0 %all-gather.64.cloned.1.call-start = ((), (), s32[]{:S(2)}) async-start(), calls=%async_computation.34 | async-start | bytes 2293760 | tf_op jit(solution)/shard_map/all_gather | solution.py:291
  478.1 178.6 %all-gather.46.cloned.1.call-start = ((), (), s32[]{:S(2)}) async-start(), calls=%async_computation.16 | async-start | bytes 2580480 | tf_op jit(solution)/shard_map/all_gather | solution.py:166
  502.0 185.4 %all-gather.52.cloned.1.call-start = ((), (), s32[]{:S(2)}) async-start(), calls=%async_computation.22 | async-start | bytes 2580480 | tf_op jit(solution)/shard_map/all_gather | solution.py:166
  543.5 174.4 %all-gather.48.cloned.1.call-start = ((), (), s32[]{:S(2)}) async-start(), calls=%async_computation.17 | async-start | bytes 2580480 | tf_op jit(solution)/shard_map/all_gather | solution.py:164
  544.0 204.3 %all-gather.50.cloned.1.call-start = ((), (), s32[]{:S(2)}) async-start(), calls=%async_computation.18 | async-start | bytes 2580480 | tf_op jit(solution)/shard_map/all_gather | solution.py:165
  544.6 234.3 %all-gather.54.cloned.1.call-start = ((), (), s32[]{:S(2)}) async-start(), calls=%async_computation.23 | async-start | bytes 2580480 | tf_op jit(solution)/shard_map/all_gather | solution.py:164
  545.2 264.2 %all-gather.56.cloned.1.call-start = ((), (), s32[]{:S(2)}) async-start(), calls=%async_computation.24 | async-start | bytes 2580480 | tf_op jit(solution)/shard_map/all_gather | solution.py:165
  545.8 309.1 %reduce-scatter.40.cloned.1.call-start = ((), (), s32[]{:S(2)}) async-start(), calls=%async_computation.30 | async-start | bytes 2580480 | tf_op jit(solution)/shard_map/reduce_scatter | solution.py:404
  634.9 537.5 %all-gather.70.cloned.1.call-start = ((), (), s32[]{:S(2)}) async-start(), calls=%async_computation.37 | async-start | bytes 1892352 | tf_op jit(solution)/shard_map/all_gather | solution.py:160
  635.7 540.3 %all-gather.72.cloned.1.call-start = ((), (), s32[]{:S(2)}) async-start(), calls=%async_computation.38 | async-start | bytes 1892352 | tf_op jit(solution)/shard_map/all_gather | solution.py:154
  636.3 543.3 %all-gather.74.cloned.1.call-start = ((), (), s32[]{:S(2)}) async-start(), calls=%async_computation.39 | async-start | bytes 1892352 | tf_op jit(solution)/shard_map/all_gather | solution.py:160
  637.0 546.1 %all-gather.76.cloned.1.call-start = ((), (), s32[]{:S(2)}) async-start(), calls=%async_computation.40 | async-start | bytes 1892352 | tf_op jit(solution)/shard_map/all_gather | solution.py:154
  637.8 548.9 %reduce-scatter.36.cloned.1.call-start = ((), (), s32[]{:S(2)}) async-start(), calls=%async_computation.28 | async-start | bytes 2580480 | tf_op jit(solution)/shard_map/reduce_scatter | solution.py:398
  704.1 484.5 %reduce-scatter.38.cloned.1.call-start = ((), (), s32[]{:S(2)}) async-start(), calls=%async_computation.29 | async-start | bytes 2580480 | tf_op jit(solution)/shard_map/reduce_scatter | solution.py:401
  713.3 536.6 %reduce-scatter.24.cloned.1.call-start = ((), (), s32[]{:S(2)}) async-start(), calls=%async_computation.19 | async-start | bytes 4587520 | tf_op jit(solution)/shard_map/reduce_scatter | solution.py:309
  756.7 564.3 %reduce-scatter.30.cloned.1.call-start = ((), (), s32[]{:S(2)}) async-start(), calls=%async_computation.25 | async-start | bytes 4587520 | tf_op jit(solution)/shard_map/reduce_scatter | solution.py:309
  817.6 109.1 %copy-start.50 = (bf16[28,128]{1,0:T(8,128)(2,1)S(1)}, bf16[28,128]{1,0:T(8,128)(2,1)}, u32[]{:S(2)}) copy-start(bf16[28,128]{1,0:T(8,128)(2,1)} %param.23) | copy-start | bytes 21508
  817.7 176.0 %copy-start.74 = (bf16[28]{0:T(256)(128)(2,1)S(1)}, bf16[28]{0:T(256)(128)(2,1)}, u32[]{:S(2)}) copy-start(bf16[28]{0:T(256)(128)(2,1)} %param.18) | copy-start | bytes 172
  817.7 176.2 %copy-start.75 = (bf16[28]{0:T(256)(128)(2,1)S(1)}, bf16[28]{0:T(256)(128)(2,1)}, u32[]{:S(2)}) copy-start(bf16[28]{0:T(256)(128)(2,1)} %param.26) | copy-start | bytes 172
  817.7 606.7 %reduce-scatter.26.cloned.1.call-start = ((), (), s32[]{:S(2)}) async-start(), calls=%async_computation.20 | async-start | bytes 655360 | tf_op jit(solution)/shard_map/reduce_scatter | solution.py:343
  1186.7 135.7 %copy-start.65 = (f32[256]{0:T(256)S(1)}, f32[256]{0:T(256)}, u32[]{:S(2)}) copy-start(f32[256]{0:T(256)} %get-tuple-element.328) | copy-start | bytes 3076
  1356.2 69.2 %reduce-scatter.32.cloned.1.call-start = ((), (), s32[]{:S(2)}) async-start(), calls=%async_computation.26 | async-start | bytes 655360 | tf_op jit(solution)/shard_map/reduce_scatter | solution.py:343
  1399.3 44.5 %reduce-scatter.28.cloned.1.call-start = ((), (), s32[]{:S(2)}) async-start(), calls=%async_computation.21 | async-start | bytes 655360 | tf_op jit(solution)/shard_map/reduce_scatter | solution.py:349
  1407.9 58.1 %reduce-scatter.34.cloned.1.call-start = ((), (), s32[]{:S(2)}) async-start(), calls=%async_computation.27 | async-start | bytes 655360 | tf_op jit(solution)/shard_map/reduce_scatter | solution.py:349
  1468.0 195.0 %copy-start.21 = (f32[1,256,128]{1,2,0:T(8,128)S(1)}, f32[1,256,128]{1,2,0:T(8,128)}, u32[]{:S(2)}) copy-start(f32[1,256,128]{1,2,0:T(8,128)} %reduce-scatter.26.cloned.1.call-done) | copy-start | bytes 393220
  1468.0 195.0 %copy-start.19 = (f32[256,896]{1,0:T(8,128)S(1)}, f32[256,896]{1,0:T(8,128)}, u32[]{:S(2)}) copy-start(f32[256,896]{1,0:T(8,128)} %fusion.167) | copy-start | bytes 2752516
  1468.0 196.4 %copy-start.22 = (f32[1,256,128]{1,2,0:T(8,128)S(1)}, f32[1,256,128]{1,2,0:T(8,128)}, u32[]{:S(2)}) copy-start(f32[1,256,128]{1,2,0:T(8,128)} %reduce-scatter.32.cloned.1.call-done) | copy-start | bytes 393220
  1651.9 64.6 %collective-permute-start.6 = (f32[32,128]{1,0:T(8,128)S(1)}, f32[32,128]{1,0:T(8,128)}, u32[]{:S(2)}, u32[]{:S(2)}) collective-permute-start(f32[32,128]{1,0:T(8,128)S(1)} %get-tuple-element.275), channel_id=1, source_target_pairs={{0,3},{1,4},{2,5},{3,6},{4,7},{5,8},{6,9},{7,10},{8,11},{9,12},{10... | collective-permute-start | bytes 49160
  1653.9 67.1 %collective-permute-start.5 = (f32[32,128]{1,0:T(8,128)S(1)}, f32[32,128]{1,0:T(8,128)}, u32[]{:S(2)}, u32[]{:S(2)}) collective-permute-start(f32[32,128]{1,0:T(8,128)S(1)} %get-tuple-element.275), channel_id=1, source_target_pairs={{0,2},{1,3},{2,4},{3,5},{4,6},{5,7},{6,8},{7,9},{8,10},{9,11},{10,... | collective-permute-start | bytes 49160
  1656.4 66.8 %collective-permute-start.4 = (f32[32,128]{1,0:T(8,128)S(1)}, f32[32,128]{1,0:T(8,128)}, u32[]{:S(2)}, u32[]{:S(2)}) collective-permute-start(f32[32,128]{1,0:T(8,128)S(1)} %get-tuple-element.275), channel_id=1, source_target_pairs={{0,1},{1,2},{2,3},{3,4},{4,5},{5,6},{6,7},{7,8},{8,9},{9,10},{10,1... | collective-permute-start | bytes 49160
  1658.9 74.6 %collective-permute-start.10 = (f32[32,128]{1,0:T(8,128)S(1)}, f32[32,128]{1,0:T(8,128)}, u32[]{:S(2)}, u32[]{:S(2)}) collective-permute-start(f32[32,128]{1,0:T(8,128)S(1)} %get-tuple-element.276), channel_id=1, source_target_pairs={{0,3},{1,4},{2,5},{3,6},{4,7},{5,8},{6,9},{7,10},{8,11},{9,12},{10... | collective-permute-start | bytes 49160
  1667.0 3.4 collective-permute-start.7
  1668.9 47.5 %copy-start.32 = (f32[32,896]{1,0:T(8,128)S(1)}, f32[32,896]{1,0:T(8,128)}, u32[]{:S(2)}) copy-start(f32[32,896]{1,0:T(8,128)} %get-tuple-element.274) | copy-start | bytes 344068
  1670.4 59.8 %collective-permute-start.11 = (f32[28,128]{1,0:T(8,128)}, f32[28,128]{1,0:T(8,128)S(1)}, u32[]{:S(2)}, u32[]{:S(2)}) collective-permute-start(f32[28,128]{1,0:T(8,128)} %slice.108), channel_id=1, source_target_pairs={{0,4},{1,5},{2,6},{3,7},{4,8},{5,9},{6,10},{7,11},{8,12},{9,13},{1... | collective-permute-start | bytes 43016
  1716.5 22.0 %collective-permute-start.9 = (f32[32,128]{1,0:T(8,128)S(1)}, f32[32,128]{1,0:T(8,128)S(1)}, u32[]{:S(2)}, u32[]{:S(2)}) collective-permute-start(f32[32,128]{1,0:T(8,128)S(1)} %get-tuple-element.276), channel_id=1, source_target_pairs={{0,2},{1,3},{2,4},{3,5},{4,6},{5,7},{6,8},{7,9},{8,10},{9,11},{10,... | collective-permute-start | bytes 49160
  1721.0 22.3 %collective-permute-start.8 = (f32[32,128]{1,0:T(8,128)S(1)}, f32[32,128]{1,0:T(8,128)S(1)}, u32[]{:S(2)}, u32[]{:S(2)}) collective-permute-start(f32[32,128]{1,0:T(8,128)S(1)} %get-tuple-element.276), channel_id=1, source_target_pairs={{0,1},{1,2},{2,3},{3,4},{4,5},{5,6},{6,7},{7,8},{8,9},{9,10},{10,1... | collective-permute-start | bytes 49160
  1723.2 27.9 %collective-permute-start.2 = (f32[32,896]{1,0:T(8,128)S(1)}, f32[32,896]{1,0:T(8,128)S(1)}, u32[]{:S(2)}, u32[]{:S(2)}) collective-permute-start(f32[32,896]{1,0:T(8,128)S(1)} %copy-done.32), channel_id=1, source_target_pairs={{0,3},{1,4},{2,5},{3,6},{4,7},{5,8},{6,9},{7,10},{8,11},{9,12},{10... | collective-permute-start | bytes 344072
  1730.3 22.7 %collective-permute-start.1 = (f32[32,896]{1,0:T(8,128)S(1)}, f32[32,896]{1,0:T(8,128)S(1)}, u32[]{:S(2)}, u32[]{:S(2)}) collective-permute-start(f32[32,896]{1,0:T(8,128)S(1)} %copy-done.32), channel_id=1, source_target_pairs={{0,2},{1,3},{2,4},{3,5},{4,6},{5,7},{6,8},{7,9},{8,10},{9,11},{10,... | collective-permute-start | bytes 344072
  1733.5 21.1 %collective-permute-start = (f32[32,896]{1,0:T(8,128)S(1)}, f32[32,896]{1,0:T(8,128)S(1)}, u32[]{:S(2)}, u32[]{:S(2)}) collective-permute-start(f32[32,896]{1,0:T(8,128)S(1)} %copy-done.32), channel_id=1, source_target_pairs={{0,1},{1,2},{2,3},{3,4},{4,5},{5,6},{6,7},{7,8},{8,9},{9,10},{10,1... | collective-permute-start | bytes 344072
  1738.6 17.5 collective-permute-start.14
  1743.3 3.1 collective-permute-start.3
  1746.4 9.6 collective-permute-start.13
  1751.1 5.0 collective-permute-start.12
  1753.0 3.0 collective-permute-start.15
  (74 other events, 499.4 us)
Sparse Core Ops, SparseCore 0:
  10.9 58.6 all-gather.65
  72.4 54.8 all-gather.67
  129.2 28.1 all-gather.39
  316.1 40.6 all-gather.57
  358.5 27.5 all-gather.41
  387.9 28.7 all-gather.43
  418.8 41.3 all-gather.59
  462.5 38.2 reduce-scatter.19
  503.7 38.5 reduce-scatter.21
  544.3 40.5 all-gather.61
  587.0 40.2 all-gather.63
  629.1 27.5 all-gather.45
  658.6 28.7 all-gather.51
  689.1 28.7 all-gather.47
  719.6 28.7 all-gather.49
  750.1 28.7 all-gather.53
  780.6 28.7 all-gather.55
  812.6 42.2 reduce-scatter.39
  858.1 55.8 all-gather.69
  917.1 54.9 all-gather.71
  975.3 54.8 all-gather.73
  1033.4 54.9 all-gather.75
  1092.1 41.3 reduce-scatter.35
  1136.7 42.2 reduce-scatter.37
  1181.4 68.3 reduce-scatter.23
  1252.1 68.7 reduce-scatter.29
  1356.3 22.0 reduce-scatter.25
  1399.4 22.0 reduce-scatter.31
  1423.8 19.9 reduce-scatter.27
  1446.0 19.8 reduce-scatter.33
where the time goes:
time: 1780 us; the launch traced here: 1760 us
  blocking collectives  767 us (43%)
  waiting for transfers between devices  571 us (32%)
  matrix products  250 us (14%)
  local copies, waits for them, and re-layouts  57 us (3%)
  other arithmetic  52 us (3%)
  starting transfers between devices  51.6 us (3%)
    unnamed x4, blocking collectives  304 us
    all_gather x3, blocking collectives, fetch_all(): lax.all_gather(held[3], ('dp', 'ctx'), axis=0, tiled=True)  203 us
    all_gather x3, blocking collectives, fetch_all(): lax.all_gather(held[5], ('dp', 'ctx'), axis=0, tiled=True)  201 us
    reduce_scatter x2, waiting for transfers between devices, body(): lax.psum_scatter(normed_part.reshape(sequence_count, key_count, model_wid...  129 us
    all_gather x2, waiting for transfers between devices, body(): lax.all_gather(normed_two.reshape(sequence_count, shard_rows, model_width...  75.1 us
    all_gather x2, waiting for transfers between devices, body(): lax.all_gather(upstream_low.reshape(sequence_count, shard_rows, model_wid...  74.6 us
    all_gather x3, waiting for transfers between devices, fetch_all(): lax.all_gather(held[10], 'dp', axis=0, tiled=True)  68.8 us
    reduce_scatter x2, waiting for transfers between devices, body(): lax.psum_scatter(partial_out.reshape(sequence_count, key_count, model_wid...  63.1 us
  transfers between devices with their start and end apart: 46, of which 20 were waited for; matrix products, arithmetic and copies ran while one was open for 18% of the time, Pallas kernels for 0%

commit v1 on v0

v1 whole, which is shorter than its diff:
```python
import jax
import jax.numpy as jnp
from jax import lax
from jax.sharding import PartitionSpec as P

D = 896
HEADS = 14
KV_HEADS = 2
HEAD = 64
LONGEST = 512
LANES = 128

epsilon = 1e-06
theta = 10000.0
masked = -1e30
bf16 = jnp.bfloat16
f32 = jnp.float32


def turned(values_in):
    half_width = values_in.shape[-1] // 2
    return jnp.concatenate([-values_in[..., half_width:], values_in[..., :half_width]], axis=-1)


def turned_back(values_in):
    half_width = values_in.shape[-1] // 2
    return jnp.concatenate([values_in[..., half_width:], -values_in[..., :half_width]], axis=-1)


def rotate(values_in, cosines, sines):
    return values_in * cosines + turned(values_in) * sines


def rotate_back(values_in, cosines, sines):
    return values_in * cosines + turned_back(values_in * sines)


def scaled(values_in):
    return lax.rsqrt(jnp.mean(values_in * values_in, axis=-1, keepdims=True) + epsilon)


def norm_back(grad_in, values_in, inverse, gain_full):
    weighted = grad_in * gain_full
    return inverse * weighted - values_in * (inverse * inverse * inverse) * jnp.mean(
        weighted * values_in, axis=-1, keepdims=True
    )


def dot(left, right, left_dim, right_dim):
    return lax.dot_general(
        left, right, (((left_dim,), (right_dim,)), ((), ())), preferred_element_type=f32
    )


def raw_scores(queries, keys_in, allowed):
    scores = jnp.einsum("qkgd,skd->kgqs", queries, keys_in, preferred_element_type=f32)
    return jnp.where(allowed, scores * HEAD**-0.5, masked)


def attend(queries, keys_in, values_in, allowed):
    scores = raw_scores(queries, keys_in, allowed)
    largest = jnp.max(scores, axis=-1, keepdims=True)
    exponent = jnp.exp(scores - largest)
    totals = jnp.sum(exponent, axis=-1, keepdims=True)
    soft_low = (exponent / totals).astype(bf16)
    mixed_heads = jnp.einsum("kgqs,skd->qkgd", soft_low, values_in, preferred_element_type=f32)
    return mixed_heads, largest, totals


def attend_back(queries, keys_in, values_in, allowed, largest, totals, grad_mixed):
    scores = raw_scores(queries, keys_in, allowed)
    soft_weights = jnp.exp(scores - largest) / totals
    soft_low = soft_weights.astype(bf16)
    grad_soft = jnp.einsum("qkgd,skd->kgqs", grad_mixed, values_in, preferred_element_type=f32)
    row_delta = jnp.sum(soft_weights * grad_soft, axis=-1, keepdims=True)
    grad_scores = (soft_weights * (grad_soft - row_delta)).astype(bf16)
    scale = HEAD**-0.5
    grad_queries = (
        jnp.einsum("kgqs,skd->qkgd", grad_scores, keys_in, preferred_element_type=f32) * scale
    )
    grad_keys = (
        jnp.einsum("kgqs,qkgd->skd", grad_scores, queries, preferred_element_type=f32) * scale
    )
    grad_values = jnp.einsum("kgqs,qkgd->skd", soft_low, grad_mixed, preferred_element_type=f32)
    return grad_queries, grad_keys, grad_values


def body(
    layer_in,
    doc_ids,
    cotangent,
    first_gain,
    query_weight,
    query_bias,
    key_weight,
    key_bias,
    value_weight,
    value_bias,
    out_weight,
    second_gain,
    gate_weight,
    up_weight,
    down_weight,
):
    parts = lax.axis_size("ctx")
    groups = lax.axis_size("dp")
    rank = lax.axis_index("ctx")
    micro_count = layer_in.shape[1]
    shard_rows = layer_in.shape[3]
    key_count = doc_ids.shape[3]
    group_size = HEADS // KV_HEADS
    query_width = HEADS * HEAD
    pair_width = KV_HEADS * HEAD
    hidden = gate_weight.shape[1]
    hidden_pad = -(-hidden // LANES) * LANES
    weight_rows = query_weight.shape[0]
    bias_rows = key_bias.shape[0]
    earlier_parts = min(parts - 1, -(-(LONGEST - 1) // shard_rows))

    def around(values_in, steps):
        return lax.ppermute(
            values_in, "ctx", [(s, (s + steps) % parts) for s in range(parts)]
        )

    def pieces_of(values_in):
        return [values_in] + [around(values_in, d) for d in range(1, parts)]

    def collected(values_in):
        pieces = pieces_of(values_in)
        ordered = [pieces[d] for d in range(parts - 1, -1, -1)]
        ordered = jnp.stack(ordered + ordered[:-1])
        taken = lax.dynamic_slice_in_dim(ordered, parts - 1 - rank, parts, 0)
        return taken.reshape((-1,) + values_in.shape[1:])

    def returned(pieces):
        total = pieces[0]
        for d in range(1, parts):
            total = total + around(pieces[d].astype(bf16), parts - d).astype(f32)
        return total

    def column(values_in):
        return jnp.pad(values_in, (0, weight_rows - values_in.shape[0]))[:, None]

    def wide(values_in):
        return jnp.pad(values_in, ((0, 0), (0, hidden_pad - hidden)))

    small = jnp.concatenate(
        [column(v) for v in (first_gain, second_gain, query_bias, key_bias, value_bias)], axis=1
    )
    small = jnp.pad(small, ((0, 0), (0, LANES - small.shape[1])))
    own_attention = jnp.concatenate(
        [query_weight, key_weight, value_weight, small, out_weight], axis=1
    )
    block_attention = collected(own_attention)
    first_width = query_width + 2 * pair_width + LANES
    first_set = lax.all_gather(block_attention[:, :first_width], "dp", axis=0, tiled=True)
    rest_block = jnp.concatenate(
        [wide(gate_weight), wide(up_weight), wide(down_weight.T), block_attention[:, first_width:]],
        axis=1,
    )
    rest_block = lax.optimization_barrier((rest_block, first_set[0, 0]))[0]
    rest_set = lax.all_gather(rest_block, "dp", axis=0, tiled=True)

    w_qkv = first_set[:, : query_width + 2 * pair_width]
    smalls = first_set[:, query_width + 2 * pair_width :]
    gain_one = smalls[:, 0].astype(f32)
    gain_two = smalls[:, 1].astype(f32)
    bias_all = jnp.concatenate(
        [smalls[:, 2]]
        + [smalls[:, k].reshape(-1, weight_rows)[:, :bias_rows].reshape(-1) for k in (3, 4)]
    ).astype(f32)
    w_gate = rest_set[:, :hidden_pad]
    w_up = rest_set[:, hidden_pad : 2 * hidden_pad]
    w_down = rest_set[:, 2 * hidden_pad : 3 * hidden_pad]
    w_out = rest_set[:, 3 * hidden_pad :]

    exponent = jnp.arange(HEAD // 2, dtype=f32) * (2.0 / HEAD)
    frequency = jnp.power(f32(theta), -exponent)

    upstreams = [cotangent[0, m, 0] for m in range(micro_count)]
    upstream_pieces = [pieces_of(u) for u in upstreams]

    kept = []
    for m in range(micro_count):
        tokens = layer_in[0, m, 0].astype(f32)
        docs_all = doc_ids[0, m, 0]
        own_docs = lax.dynamic_slice_in_dim(docs_all, rank * shard_rows, shard_rows, 0)
        row_index = rank * shard_rows + jnp.arange(shard_rows, dtype=jnp.int32)
        begins = jnp.sum((docs_all[None, :] < own_docs[:, None]).astype(jnp.int32), axis=1)
        positions = row_index - begins
        angle = positions.astype(f32)[:, None] * frequency[None, :]
        angle = jnp.concatenate([angle, angle], axis=-1)
        cosines, sines = jnp.cos(angle)[:, None, :], jnp.sin(angle)[:, None, :]
        key_index = (rank - earlier_parts) * shard_rows + jnp.arange(
            (earlier_parts + 1) * shard_rows, dtype=jnp.int32
        )
        allowed = (key_index[None, :] >= begins[:, None]) & (
            key_index[None, :] <= row_index[:, None]
        )
        inverse_one = scaled(tokens)
        normed_one = (tokens * inverse_one * gain_one).astype(bf16)
        qkv = dot(normed_one, w_qkv, 1, 0) + bias_all
        rot_query = rotate(
            qkv[:, :query_width].reshape(-1, HEADS, HEAD), cosines, sines
        ).astype(bf16)
        rot_keys = rotate(
            qkv[:, query_width : query_width + pair_width].reshape(-1, KV_HEADS, HEAD),
            cosines,
            sines,
        ).astype(bf16)
        own_pair = jnp.concatenate(
            [rot_keys.reshape(-1, pair_width), qkv[:, query_width + pair_width :].astype(bf16)],
            axis=1,
        )
        pair = [
            lax.ppermute(own_pair, "ctx", [(s, s + d) for s in range(parts - d)])
            for d in range(earlier_parts, 0, -1)
        ] + [own_pair]
        pair = jnp.concatenate(pair, axis=0)
        keys_in = pair[:, :pair_width].reshape(-1, KV_HEADS, HEAD)
        values_in = pair[:, pair_width:].reshape(-1, KV_HEADS, HEAD)
        queries = rot_query.reshape(-1, KV_HEADS, group_size, HEAD)
        mixed_heads, largest, totals = attend(queries, keys_in, values_in, allowed)
        mixed_low = mixed_heads.reshape(-1, query_width).astype(bf16)
        middle = tokens + dot(mixed_low, w_out, 1, 0)
        inverse_two = scaled(middle)
        normed_two = (middle * inverse_two * gain_two).astype(bf16)
        rows_all = jnp.concatenate(pieces_of(normed_two), axis=0)
        kept.append(
            dict(
                tokens=tokens, cosines=cosines, sines=sines, allowed=allowed,
                inverse_one=inverse_one, normed_one=normed_one, queries=queries,
                keys_in=keys_in, values_in=values_in, largest=largest, totals=totals,
                mixed_low=mixed_low, middle=middle, inverse_two=inverse_two, rows_all=rows_all,
            )
        )

    outs = []
    for m in range(micro_count):
        k = kept[m]
        rows_all = k["rows_all"]
        gate_pre = dot(rows_all, w_gate, 1, 0)
        up_pre = dot(rows_all, w_up, 1, 0)
        sigmoid_gate = jax.nn.sigmoid(gate_pre)
        activated = (gate_pre * sigmoid_gate * up_pre).astype(bf16)
        partial_out = dot(activated, w_down, 1, 1).reshape(parts, shard_rows, D)
        feed_out = returned([partial_out[d] for d in range(parts)])
        outs.append((k["middle"] + feed_out).astype(bf16))
        upstream_all = jnp.concatenate(upstream_pieces[m], axis=0)
        grad_act = dot(upstream_all, w_down, 1, 0)
        grad_gate = (
            grad_act * up_pre * sigmoid_gate * (1.0 + gate_pre * (1.0 - sigmoid_gate))
        ).astype(bf16)
        grad_up = (grad_act * gate_pre * sigmoid_gate).astype(bf16)
        normed_part = dot(grad_gate, w_gate, 1, 1) + dot(grad_up, w_up, 1, 1)
        normed_part = normed_part.reshape(parts, shard_rows, D)
        k["grad_normed_two"] = returned([normed_part[d] for d in range(parts)])
        k.update(
            activated=activated, grad_gate=grad_gate, grad_up=grad_up, upstream_all=upstream_all
        )

    def both(name):
        return jnp.concatenate([k[name] for k in kept], axis=0)

    rows_both = both("rows_all")
    feed_local = jnp.concatenate(
        [
            dot(rows_both, both("grad_gate"), 0, 0).astype(bf16),
            dot(rows_both, both("grad_up"), 0, 0).astype(bf16),
            dot(both("upstream_all"), both("activated"), 0, 0).astype(bf16),
        ],
        axis=1,
    )
    feed_sum = lax.psum_scatter(feed_local, "dp", scatter_dimension=0, tiled=True).astype(f32)

    inputs_grad = []
    gain_one_sum = gain_two_sum = 0.0
    for m in range(micro_count):
        k = kept[m]
        upstream = upstreams[m].astype(f32)
        grad_middle = upstream + norm_back(
            k["grad_normed_two"], k["middle"], k["inverse_two"], gain_two
        )
        gain_two_sum += jnp.sum(k["grad_normed_two"] * (k["middle"] * k["inverse_two"]), axis=0)
        branch_low = grad_middle.astype(bf16)
        grad_mixed = dot(branch_low, w_out, 1, 1).astype(bf16)
        grad_queries, grad_keys, grad_values = attend_back(
            k["queries"], k["keys_in"], k["values_in"], k["allowed"], k["largest"], k["totals"],
            grad_mixed.reshape(-1, KV_HEADS, group_size, HEAD),
        )
        grad_pair = jnp.concatenate(
            [grad_keys.reshape(-1, pair_width), grad_values.reshape(-1, pair_width)], axis=1
        ).reshape(earlier_parts + 1, shard_rows, 2 * pair_width)
        own_grad = grad_pair[earlier_parts]
        for d in range(1, earlier_parts + 1):
            own_grad = own_grad + lax.ppermute(
                grad_pair[earlier_parts - d].astype(bf16),
                "ctx",
                [(s, s - d) for s in range(d, parts)],
            ).astype(f32)
        query_grad = rotate_back(
            grad_queries.reshape(-1, HEADS, HEAD), k["cosines"], k["sines"]
        ).reshape(-1, query_width)
        key_grad = rotate_back(
            own_grad[:, :pair_width].reshape(-1, KV_HEADS, HEAD), k["cosines"], k["sines"]
        ).reshape(-1, pair_width)
        low = jnp.concatenate([query_grad, key_grad, own_grad[:, pair_width:]], axis=1).astype(bf16)
        grad_normed_one = dot(low, w_qkv, 1, 1)
        gain_one_sum += jnp.sum(grad_normed_one * (k["tokens"] * k["inverse_one"]), axis=0)
        inputs_grad.append(
            grad_middle + norm_back(grad_normed_one, k["tokens"], k["inverse_one"], gain_one)
        )
        k.update(low=low, branch_low=branch_low)

    low = both("low")
    bias_sum = jnp.sum(low.astype(f32), axis=0)

    def spread(values_in):
        values_in = values_in.reshape(-1, bias_rows)
        return jnp.pad(values_in, ((0, 0), (0, weight_rows - bias_rows))).reshape(-1)

    small_sums = jnp.stack(
        [
            gain_one_sum,
            gain_two_sum,
            bias_sum[:query_width],
            spread(bias_sum[query_width : query_width + pair_width]),
            spread(bias_sum[query_width + pair_width :]),
        ],
        axis=1,
    )
    small_sums = jnp.pad(small_sums, ((0, 0), (0, LANES - small_sums.shape[1])))
    attention_local = jnp.concatenate(
        [
            dot(both("normed_one"), low, 0, 0).astype(bf16),
            small_sums.astype(bf16),
            dot(both("mixed_low"), both("branch_low"), 0, 0).astype(bf16),
        ],
        axis=1,
    )
    attention_block = lax.psum_scatter(attention_local, "dp", scatter_dimension=0, tiled=True)
    attention_block = attention_block.reshape(parts, weight_rows, -1)

    def block_for(steps):
        return lax.dynamic_index_in_dim(
            attention_block, (rank + steps) % parts, 0, keepdims=False
        )

    attention_sum = block_for(0).astype(f32)
    for d in range(1, parts):
        attention_sum = attention_sum + around(block_for(d), d).astype(f32)

    edge = query_width + 2 * pair_width
    return (
        jnp.stack(outs)[None, :, None],
        jnp.stack(inputs_grad)[None, :, None],
        attention_sum[:, edge],
        attention_sum[:, :query_width],
        attention_sum[:, edge + 2],
        attention_sum[:, query_width : query_width + pair_width],
        attention_sum[:bias_rows, edge + 3],
        attention_sum[:, query_width + pair_width : edge],
        attention_sum[:bias_rows, edge + 4],
        attention_sum[:, edge + LANES :],
        attention_sum[:, edge + 1],
        feed_sum[:, :hidden],
        feed_sum[:, hidden_pad : hidden_pad + hidden],
        feed_sum[:, 2 * hidden_pad : 2 * hidden_pad + hidden].T,
    )


def solution(mesh):
    both = ("dp", "ctx")
    rows = P(both, None)
    line = P(both)
    tokens = P("dp", None, None, "ctx", None)
    return jax.shard_map(
        body,
        mesh=mesh,
        in_specs=(
            tokens, P("dp", None, None, None), tokens, line, rows, line, rows, line, rows, line,
            rows, line, P("dp", "ctx"), P("dp", "ctx"), P("ctx", "dp"),
        ),
        out_specs=(
            tokens, tokens, line, rows, line, rows, line, rows, line, rows, line,
            P("dp", "ctx"), P("dp", "ctx"), P("ctx", "dp"),
        ),
        check_vma=False,
    )
```

time: 1780 us -> 631 us (0.35)
  blocking collectives: 767 us -> 0 us
  waiting for transfers between devices: 571 us -> 172 us
  starting transfers between devices: 51.6 us -> 183 us
  matrix products: 250 us -> 164 us
    all_gather x10 -> x0, blocking collectives: 462 us -> none  [the longest x3 203 us: fetch_all(): lax.all_gather(held[3], ('dp', 'ctx'), axis=0, tiled=True)]
    unnamed x4 -> x0, blocking collectives: 304 us -> none
    all_gather x19 -> x2, waiting for transfers between devices: 297 us -> 20.4 us  [the longest x1 20.4 us: body(): lax.all_gather(block_attention[:, :first_width], 'dp', axis=0, tiled=True)]
    reduce_scatter x11 -> x2, waiting for transfers between devices: 264 us -> 62.4 us  [the longest x1 50.6 us: body(): lax.psum_scatter(feed_local, 'dp', scatter_dimension=0, tiled=True)]
    ppermute x0 -> x38, starting transfers between devices: none -> 183 us  [the longest x30 165 us: around(): lax.ppermute(values_in, 'ctx', [(s, (s + steps) % parts) for s in range(p...]
    ppermute x0 -> x38, waiting for transfers between devices: none -> 89.3 us  [the longest x30 75 us: around(): lax.ppermute(values_in, 'ctx', [(s, (s + steps) % parts) for s in range(p...]
    unnamed x16 -> x0, starting transfers between devices: 48.7 us -> none
    dot_general x42 -> x25, matrix products: 160 us -> 120 us  [dot(): lax.dot_general(left, right, (((left_dim,), (right_dim,)), ((), ())), pre...]
  transfers between devices with their start and end apart: 46 -> 42, of which waited for: 20 -> 18; matrix products, arithmetic and copies ran while one was open for 18% -> 29% of each run, Pallas kernels for 0% -> 0%
where the time goes in v1:
time: 631 us; the launch traced here: 624 us
  starting transfers between devices  183 us (29%)
  waiting for transfers between devices  172 us (27%)
  matrix products  164 us (26%)
  local copies, waits for them, and re-layouts  45 us (7%)
  other arithmetic  43.8 us (7%)
  between operations  16 us (3%)
    ppermute x30, starting transfers between devices, around(): lax.ppermute(values_in, 'ctx', [(s, (s + steps) % parts) for s in range(p...  165 us
    dot_general x25, matrix products, dot(): lax.dot_general(left, right, (((left_dim,), (right_dim,)), ((), ())), pre...  120 us
    ppermute x30, waiting for transfers between devices, around(): lax.ppermute(values_in, 'ctx', [(s, (s + steps) % parts) for s in range(p...  75 us
    reduce_scatter x1, waiting for transfers between devices, body(): lax.psum_scatter(feed_local, 'dp', scatter_dimension=0, tiled=True)  50.6 us
    all_gather x1, waiting for transfers between devices, body(): lax.all_gather(block_attention[:, :first_width], 'dp', axis=0, tiled=True)  20.4 us
    unnamed x235, local copies, waits for them, and re-layouts  17 us
    sub x2, matrix products, attend(): exponent = jnp.exp(scores - largest)  13.4 us
  transfers between devices with their start and end apart: 42, of which 18 were waited for; matrix products, arithmetic and copies ran while one was open for 29% of the time, Pallas kernels for 0%

profile of v1, /device:TPU:0, one launch (start us, length us, event | category | flops | bytes accessed | tf_op | source)
XLA Modules:
  0.0 624.2 jit_solution(12052565131552549550)
XLA Ops:
  11.9 5.0 collective-permute-start
  18.0 3.1 collective-permute-done
  21.1 7.7 %collective-permute-done.1 = bf16[28,2176]{1,0:T(8,128)(2,1)S(1)} collective-permute-done((bf16[28,2176]{1,0:T(8,128)(2,1)S(1)}, bf16[28,2176]{1,0:T(8,128)(2,1)S(1)}, u32[]{:S(2)}, u32[]{:S(2)}) %collective-permute-start.1) | collective-permute-done | bytes 121888 | tf_op jit(solution)/shard_map/ppermute | solution.py:121
  38.7 20.4 %all-gather.3.cloned.1.call-done = bf16[896,1280]{1,0:T(8,128)(2,1)} async-done(((bf16[112,1280]{1,0:T(8,128)(2,1)}), bf16[896,1280]{1,0:T(8,128)(2,1)}) %all-gather.3.cloned.1.call-update) | async-done | bytes 2293776 | tf_op jit(solution)/shard_map/all_gather | solution.py:156
  63.7 2.6 convolution_add_fusion.1
  73.6 5.0 collective-permute-start.3
  78.6 4.0 collective-permute-start.4
  82.7 2.6 convolution_add_fusion
  100.6 7.3 %fusion.231 = (f32[2,7,256]{2,1,0:T(8,128)S(1)}, f32[2,7,256,768]{2,3,1,0:T(8,128)}) fusion(pred[256,768]{0,1:T(8,128)(4,1)} %get-tuple-element.187, bf16[768,2,64,1]{0,2,3,1:T(8,128)(2,1)S(1)} %bitcast.289, bf16[256,2,7,64]{0,3,2,1:T(8,128)(2,1)S(1)} %fusion.159), kind=kOutput, calls=%fused_computation.403 | convolution fusion | flops 363332352 | bytes 11876352 | tf_op jit(solution)/shard_map/sub | solution.py:63
  107.9 6.1 fusion.234
  114.1 5.5 fusion.100
  122.8 2.3 multiply_reduce_fusion.5
  130.1 2.9 collective-permute-start.7
  133.0 2.4 multiply_reduce_fusion.4
  135.4 6.1 collective-permute-done.5
  141.5 19.6 %collective-permute-start.19 = (bf16[256,896]{1,0:T(8,128)(2,1)S(1)}, bf16[256,896]{1,0:T(8,128)(2,1)S(1)}, u32[]{:S(2)}, u32[]{:S(2)}) collective-permute-start(bf16[256,896]{1,0:T(8,128)(2,1)S(1)} %copy-done.36), channel_id=1, source_target_pairs={{0,1},{1,2},{2,3},{3,0},{4,5},{5,6},{6,7},{7,4},{8,9},{9,10},{10,1... | collective-permute-start | bytes 1376264 | tf_op jit(solution)/shard_map/ppermute | solution.py:121
  164.8 24.6 %collective-permute-start.21 = (bf16[256,896]{1,0:T(8,128)(2,1)S(1)}, bf16[256,896]{1,0:T(8,128)(2,1)S(1)}, u32[]{:S(2)}, u32[]{:S(2)}) collective-permute-start(bf16[256,896]{1,0:T(8,128)(2,1)S(1)} %copy-done.36), channel_id=1, source_target_pairs={{0,3},{1,0},{2,1},{3,2},{4,7},{5,4},{6,5},{7,6},{8,11},{9,8},{10,9... | collective-permute-start | bytes 1376264 | tf_op jit(solution)/shard_map/ppermute | solution.py:121
  191.2 6.1 fusion.80
  197.3 6.1 fusion.88
  205.5 3.2 collective-permute-done.21
  208.7 20.0 %collective-permute-start.15 = (bf16[256,896]{1,0:T(8,128)(2,1)S(1)}, bf16[256,896]{1,0:T(8,128)(2,1)S(1)}, u32[]{:S(2)}, u32[]{:S(2)}) collective-permute-start(bf16[256,896]{1,0:T(8,128)(2,1)S(1)} %get-tuple-element.107), channel_id=1, source_target_pairs={{0,3},{1,0},{2,1},{3,2},{4,7},{5,4},{6,5},{7,6},{8,11},{9,8},{10,9... | collective-permute-start | bytes 1376264 | tf_op jit(solution)/shard_map/ppermute | solution.py:121
  228.6 10.3 %multiply_convert_fusion.2 = (bf16[1024,1280]{1,0:T(8,128)(2,1)}, bf16[1024,1280]{1,0:T(8,128)(2,1)}, bf16[1024,1280]{1,0:T(8,128)(2,1)S(1)}) fusion(f32[1024,1280]{1,0:T(8,128)} %fusion.88, f32[1024,1280]{1,0:T(8,128)} %fusion.80, bf16[896,4736]{1,0:T(8,128)(2,1)S(1)} %copy-done.80, bf16[256,896]{1,0:T(8,128)(2,1)S(1)} %collective-permute-done.21, ...), kind=kOutput, calls=%fused_computation.45 | convolution fusion | flops 2377121792 | bytes 22478848 | tf_op jit(solution)/shard_map/dot_general | solution.py:50
  239.0 5.5 fusion.233
  244.6 4.7 fusion.84
  249.3 2.9 fusion.232
  256.6 6.1 fusion.78
  262.7 6.1 fusion.86
  269.0 2.4 collective-permute-start.22
  271.3 5.1 collective-permute-done.29
  276.4 10.2 %multiply_convert_fusion = (bf16[1024,1280]{1,0:T(8,128)(2,1)}, bf16[1024,1280]{1,0:T(8,128)(2,1)S(1)}, bf16[1024,1280]{1,0:T(8,128)(2,1)S(1)}) fusion(f32[1024,1280]{1,0:T(8,128)} %fusion.86, f32[1024,1280]{1,0:T(8,128)} %fusion.78, bf16[896,4736]{1,0:T(8,128)(2,1)} %all-gather.5.cloned.1.call-done, bf16[256,896]{1,0:T(8,128)(2,1)S(1)} %collective-permute-done.29, ...), kind=kOutput, calls=%fused_computation.43 | convolution fusion | flops 2377121792 | bytes 22478848 | tf_op jit(solution)/shard_map/dot_general | solution.py:50
  286.7 6.4 %fusion.82 = f32[1024,896]{1,0:T(8,128)S(1)} fusion(bf16[1024,1280]{1,0:T(8,128)(2,1)S(1)} %get-tuple-element.120, bf16[896,4736]{1,0:T(8,128)(2,1)} %all-gather.5.cloned.1.call-done), kind=kOutput, calls=%fused_computation.121 | convolution fusion | flops 2348810240 | bytes 8585216 | tf_op jit(solution)/shard_map/dot_general | solution.py:50
  293.1 4.6 fusion.235
  297.8 7.2 %collective-permute-start.24 = (bf16[256,896]{1,0:T(8,128)(2,1)S(1)}, bf16[256,896]{1,0:T(8,128)(2,1)S(1)}, u32[]{:S(2)}, u32[]{:S(2)}) collective-permute-start(bf16[256,896]{1,0:T(8,128)(2,1)S(1)} %get-tuple-element.123), channel_id=1, source_target_pairs={{0,1},{1,2},{2,3},{3,0},{4,5},{5,6},{6,7},{7,4},{8,9},{9,10},{10,1... | collective-permute-start | bytes 1376264 | tf_op jit(solution)/shard_map/ppermute | solution.py:121
  305.0 18.6 %collective-permute-done.9 = bf16[256,896]{1,0:T(8,128)(2,1)S(1)} collective-permute-done((bf16[256,896]{1,0:T(8,128)(2,1)S(1)}, bf16[256,896]{1,0:T(8,128)(2,1)S(1)}, u32[]{:S(2)}, u32[]{:S(2)}) %collective-permute-start.9) | collective-permute-done | bytes 458784 | tf_op jit(solution)/shard_map/ppermute | solution.py:121
  323.6 31.8 %collective-permute-start.32 = (bf16[256,896]{1,0:T(8,128)(2,1)S(1)}, bf16[256,896]{1,0:T(8,128)(2,1)S(1)}, u32[]{:S(2)}, u32[]{:S(2)}) collective-permute-start(bf16[256,896]{1,0:T(8,128)(2,1)S(1)} %get-tuple-element.126), channel_id=1, source_target_pairs={{0,1},{1,2},{2,3},{3,0},{4,5},{5,6},{6,7},{7,4},{8,9},{9,10},{10,1... | collective-permute-start | bytes 1376264 | tf_op jit(solution)/shard_map/ppermute | solution.py:121
  355.4 4.5 fusion.236
  360.1 4.5 collective-permute-done.23
  365.9 28.6 %collective-permute-start.18 = (bf16[256,896]{1,0:T(8,128)(2,1)S(1)}, bf16[256,896]{1,0:T(8,128)(2,1)S(1)}, u32[]{:S(2)}, u32[]{:S(2)}) collective-permute-start(bf16[256,896]{1,0:T(8,128)(2,1)S(1)} %get-tuple-element.132), channel_id=1, source_target_pairs={{0,1},{1,2},{2,3},{3,0},{4,5},{5,6},{6,7},{7,4},{8,9},{9,10},{10,1... | collective-permute-start | bytes 1376264 | tf_op jit(solution)/shard_map/ppermute | solution.py:121
  394.6 9.3 %collective-permute-done.31 = bf16[256,896]{1,0:T(8,128)(2,1)S(1)} collective-permute-done((bf16[256,896]{1,0:T(8,128)(2,1)S(1)}, bf16[256,896]{1,0:T(8,128)(2,1)S(1)}, u32[]{:S(2)}, u32[]{:S(2)}) %collective-permute-start.31) | collective-permute-done | bytes 458784 | tf_op jit(solution)/shard_map/ppermute | solution.py:121
  405.7 12.3 %collective-permute-done.17 = bf16[256,896]{1,0:T(8,128)(2,1)S(1)} collective-permute-done((bf16[256,896]{1,0:T(8,128)(2,1)S(1)}, bf16[256,896]{1,0:T(8,128)(2,1)S(1)}, u32[]{:S(2)}, u32[]{:S(2)}) %collective-permute-start.17) | collective-permute-done | bytes 458784 | tf_op jit(solution)/shard_map/ppermute | solution.py:121
  421.0 2.9 convolution_convert_fusion.3
  426.0 6.2 fusion.5
  432.8 2.6 fusion.45
  435.4 3.0 fusion.7
  440.5 2.5 fusion.106
  443.0 2.9 convolution_convert_fusion.2
  448.0 6.2 fusion.2
  456.6 2.6 fusion.4
  472.4 5.9 collective-permute-done.26
  478.5 5.8 collective-permute-done.34
  484.7 2.7 convolution_convert_fusion
  488.2 2.6 fusion.90
  490.9 2.7 fusion.133
  493.9 3.5 fusion.31
  504.3 7.6 %fusion.38 = bf16[896,1280]{1,0:T(8,128)(2,1)S(1)} fusion(bf16[2048,896]{1,0:T(8,128)(2,1)} %constant_dynamic-update-slice_fusion.5, bf16[1024,1280]{1,0:T(8,128)(2,1)S(1)} %copy-done.96, bf16[1024,1280]{1,0:T(8,128)(2,1)S(1)} %copy-done.94), kind=kOutput, calls=%fused_computation.55 | convolution fusion | flops 4709253120 | bytes 11206656 | tf_op jit(solution)/shard_map/dot_general | solution.py:50
  511.9 7.4 %fusion.35 = bf16[896,1280]{1,0:T(8,128)(2,1)S(1)} fusion(bf16[2048,896]{1,0:T(8,128)(2,1)} %constant_dynamic-update-slice_fusion.5, bf16[1024,1280]{1,0:T(8,128)(2,1)S(1)} %copy-done.92, bf16[1024,1280]{1,0:T(8,128)(2,1)S(1)} %copy-done.90), kind=kOutput, calls=%fused_computation.54 | convolution fusion | flops 4709253120 | bytes 11206656 | tf_op jit(solution)/shard_map/dot_general | solution.py:50
  519.3 5.4 fusion.32
  524.7 3.3 pad_maximum_fusion
  531.1 3.3 fusion.138
  534.4 11.8 %reduce-scatter.3.cloned.1.call-done = bf16[112,2176]{1,0:T(8,128)(2,1)} async-done(((bf16[896,2176]{1,0:T(8,128)(2,1)}), bf16[112,2176]{1,0:T(8,128)(2,1)}) %reduce-scatter.3.cloned.1.call-update) | async-done | bytes 487440 | tf_op jit(solution)/shard_map/reduce_scatter | solution.py:341
  548.9 2.4 collective-permute-start.36
  552.8 2.8 maximum_bitcast_fusion
  555.9 4.8 collective-permute-done.36
  563.6 50.6 %reduce-scatter.5.cloned.1.call-done = bf16[112,3840]{1,0:T(8,128)(2,1)} async-done(((bf16[896,3840]{1,0:T(8,128)(2,1)}), bf16[112,3840]{1,0:T(8,128)(2,1)}) %reduce-scatter.5.cloned.1.call-update) | async-done | bytes 860176 | tf_op jit(solution)/shard_map/reduce_scatter | solution.py:274
  (446 shorter events, 113.0 us)
Async XLA Ops:
  7.2 22.8 %copy-start.60 = (bf16[1216,112]{0,1:T(8,128)(2,1)S(1)}, bf16[1216,112]{0,1:T(8,128)(2,1)}, u32[]{:S(2)}) copy-start(bf16[1216,112]{0,1:T(8,128)(2,1)} %param.29) | copy-start | bytes 817156
  7.2 22.8 %copy-start.62 = (bf16[112,1216]{1,0:T(8,128)(2,1)S(1)}, bf16[112,1216]{1,0:T(8,128)(2,1)}, u32[]{:S(2)}) copy-start(bf16[112,1216]{1,0:T(8,128)(2,1)} %param.27) | copy-start | bytes 817156
  7.2 22.8 %copy-start.61 = (bf16[112,1216]{1,0:T(8,128)(2,1)S(1)}, bf16[112,1216]{1,0:T(8,128)(2,1)}, u32[]{:S(2)}) copy-start(bf16[112,1216]{1,0:T(8,128)(2,1)} %param.28) | copy-start | bytes 817156
  7.2 51.9 %all-gather.3.cloned.1.call-start = ((), (), s32[]{:S(2)}) async-start(), calls=%async_computation.2 | async-start | bytes 2580480 | tf_op jit(solution)/shard_map/all_gather | solution.py:156
  11.9 9.1 %collective-permute-start = (bf16[28,2176]{1,0:T(8,128)(2,1)S(1)}, bf16[28,2176]{1,0:T(8,128)(2,1)S(1)}, u32[]{:S(2)}, u32[]{:S(2)}) collective-permute-start(bf16[28,2176]{1,0:T(8,128)(2,1)S(1)} %constant_dynamic-update-slice_fusion), channel_id=1, source_target_pairs={{0,3},{1,0},{2,1},{3,2},{4,7},{5,4},{6,5},{7,6},{8,11},{9,8},{10,9... | collective-permute-start | bytes 365576 | tf_op jit(solution)/shard_map/ppermute | solution.py:121
  17.0 11.8 %collective-permute-start.1 = (bf16[28,2176]{1,0:T(8,128)(2,1)S(1)}, bf16[28,2176]{1,0:T(8,128)(2,1)S(1)}, u32[]{:S(2)}, u32[]{:S(2)}) collective-permute-start(bf16[28,2176]{1,0:T(8,128)(2,1)S(1)} %constant_dynamic-update-slice_fusion), channel_id=1, source_target_pairs={{0,2},{1,3},{2,0},{3,1},{4,6},{5,7},{6,4},{7,5},{8,10},{9,11},{10,... | collective-permute-start | bytes 365576 | tf_op jit(solution)/shard_map/ppermute | solution.py:121
  17.0 11.8 %collective-permute-start.2 = (bf16[28,2176]{1,0:T(8,128)(2,1)S(1)}, bf16[28,2176]{1,0:T(8,128)(2,1)S(1)}, u32[]{:S(2)}, u32[]{:S(2)}) collective-permute-start(bf16[28,2176]{1,0:T(8,128)(2,1)S(1)} %constant_dynamic-update-slice_fusion), channel_id=1, source_target_pairs={{0,1},{1,2},{2,3},{3,0},{4,5},{5,6},{6,7},{7,4},{8,9},{9,10},{10,1... | collective-permute-start | bytes 365576 | tf_op jit(solution)/shard_map/ppermute | solution.py:121
  29.9 92.9 %all-gather.5.cloned.1.call-start = ((), (), s32[]{:S(2)}) async-start(), calls=%async_computation.3 | async-start | bytes 9547776 | tf_op jit(solution)/shard_map/all_gather | solution.py:162
  31.1 515.1 %reduce-scatter.3.cloned.1.call-start = ((), (), s32[]{:S(2)}) async-start(), calls=%async_computation.4 | async-start | bytes 4386816 | tf_op jit(solution)/shard_map/reduce_scatter | solution.py:341
  32.1 236.7 %collective-permute-start.27 = (bf16[256,896]{1,0:T(8,128)(2,1)}, bf16[256,896]{1,0:T(8,128)(2,1)}, u32[]{:S(2)}, u32[]{:S(2)}) collective-permute-start(bf16[256,896]{1,0:T(8,128)(2,1)} %get-tuple-element.145), channel_id=1, source_target_pairs={{0,1},{1,2},{2,3},{3,0},{4,5},{5,6},{6,7},{7,4},{8,9},{9,10},{10,1... | collective-permute-start | bytes 1376264 | tf_op jit(solution)/shard_map/ppermute | solution.py:121
  32.9 236.1 %collective-permute-start.28 = (bf16[256,896]{1,0:T(8,128)(2,1)}, bf16[256,896]{1,0:T(8,128)(2,1)}, u32[]{:S(2)}, u32[]{:S(2)}) collective-permute-start(bf16[256,896]{1,0:T(8,128)(2,1)} %get-tuple-element.145), channel_id=1, source_target_pairs={{0,2},{1,3},{2,0},{3,1},{4,6},{5,7},{6,4},{7,5},{8,10},{9,11},{10,... | collective-permute-start | bytes 1376264 | tf_op jit(solution)/shard_map/ppermute | solution.py:121
  35.6 58.4 %copy-start.17 = (f32[256,64]{0,1:T(8,128)}, f32[256,64]{0,1:T(8,128)S(1)}, u32[]{:S(2)}) copy-start(f32[256,64]{0,1:T(8,128)S(1)} %get-tuple-element.181) | copy-start | bytes 196612
  35.6 58.4 %copy-start.21 = (f32[256,64]{0,1:T(8,128)}, f32[256,64]{0,1:T(8,128)S(1)}, u32[]{:S(2)}) copy-start(f32[256,64]{0,1:T(8,128)S(1)} %get-tuple-element.182) | copy-start | bytes 196612
  36.5 57.7 %copy-start.15 = (f32[256,64]{0,1:T(8,128)}, f32[256,64]{0,1:T(8,128)S(1)}, u32[]{:S(2)}) copy-start(f32[256,64]{0,1:T(8,128)S(1)} %get-tuple-element.183) | copy-start | bytes 196612
  36.5 57.7 %copy-start.19 = (f32[256,64]{0,1:T(8,128)}, f32[256,64]{0,1:T(8,128)S(1)}, u32[]{:S(2)}) copy-start(f32[256,64]{0,1:T(8,128)S(1)} %get-tuple-element.184) | copy-start | bytes 196612
  37.6 28.7 %copy-start.72 = (f32[256]{0:T(256)}, f32[256]{0:T(256)S(1)}, u32[]{:S(2)}) copy-start(f32[256]{0:T(256)S(1)} %get-tuple-element.197) | copy-start | bytes 3076
  37.6 28.7 %copy-start.74 = (f32[256]{0:T(256)}, f32[256]{0:T(256)S(1)}, u32[]{:S(2)}) copy-start(f32[256]{0:T(256)S(1)} %get-tuple-element.227) | copy-start | bytes 3076
  67.0 19.3 %copy-start.32 = (bf16[256,128]{1,0:T(8,128)(2,1)}, bf16[256,128]{1,0:T(8,128)(2,1)S(1)}, u32[]{:S(2)}) copy-start(bf16[256,128]{1,0:T(8,128)(2,1)S(1)} %slice.643) | copy-start | bytes 196612
  73.6 20.8 %collective-permute-start.3 = (bf16[256,256]{1,0:T(8,128)(2,1)}, bf16[256,256]{1,0:T(8,128)(2,1)}, u32[]{:S(2)}, u32[]{:S(2)}) collective-permute-start(bf16[256,256]{1,0:T(8,128)(2,1)} %pad_maximum_fusion.15), channel_id=1, source_target_pairs={{0,2},{1,3},{4,6},{5,7},{8,10},{9,11},{12,14},{13,15},{16,18},{17,... | collective-permute-start | bytes 393224 | tf_op jit(solution)/shard_map/ppermute | solution.py:216
  78.6 17.4 %collective-permute-start.4 = (bf16[256,256]{1,0:T(8,128)(2,1)}, bf16[256,256]{1,0:T(8,128)(2,1)}, u32[]{:S(2)}, u32[]{:S(2)}) collective-permute-start(bf16[256,256]{1,0:T(8,128)(2,1)} %pad_maximum_fusion.15), channel_id=1, source_target_pairs={{0,1},{1,2},{2,3},{4,5},{5,6},{6,7},{8,9},{9,10},{10,11},{12,13},{... | collective-permute-start | bytes 393224 | tf_op jit(solution)/shard_map/ppermute | solution.py:216
  91.9 5.5 collective-permute-start.11
  94.2 13.7 %copy-start.12 = (bf16[256,2,7,64]{0,3,2,1:T(8,128)(2,1)}, bf16[256,2,7,64]{0,3,2,1:T(8,128)(2,1)S(1)}, u32[]{:S(2)}) copy-start(bf16[256,2,7,64]{0,3,2,1:T(8,128)(2,1)S(1)} %fusion.159) | copy-start | bytes 1376260
  94.4 13.5 %copy-start.10 = (bf16[256,2,7,64]{0,3,2,1:T(8,128)(2,1)}, bf16[256,2,7,64]{0,3,2,1:T(8,128)(2,1)S(1)}, u32[]{:S(2)}) copy-start(bf16[256,2,7,64]{0,3,2,1:T(8,128)(2,1)S(1)} %fusion.161) | copy-start | bytes 1376260
  94.4 4.8 collective-permute-start.12
  97.4 16.7 %copy-start.63 = (bf16[768,128]{0,1:T(8,128)(2,1)}, bf16[768,128]{0,1:T(8,128)(2,1)S(1)}, u32[]{:S(2)}) copy-start(bf16[768,128]{0,1:T(8,128)(2,1)S(1)} %copy.170) | copy-start | bytes 589828
  100.6 19.0 %copy-start.64 = (bf16[768,128]{0,1:T(8,128)(2,1)}, bf16[768,128]{0,1:T(8,128)(2,1)S(1)}, u32[]{:S(2)}) copy-start(bf16[768,128]{0,1:T(8,128)(2,1)S(1)} %copy.178) | copy-start | bytes 589828
  125.1 16.4 %copy-start.36 = (bf16[256,896]{1,0:T(8,128)(2,1)S(1)}, bf16[256,896]{1,0:T(8,128)(2,1)}, u32[]{:S(2)}) copy-start(bf16[256,896]{1,0:T(8,128)(2,1)} %get-tuple-element.144) | copy-start | bytes 1376260
  126.1 15.4 %collective-permute-start.5 = (bf16[256,896]{1,0:T(8,128)(2,1)S(1)}, bf16[256,896]{1,0:T(8,128)(2,1)S(1)}, u32[]{:S(2)}, u32[]{:S(2)}) collective-permute-start(bf16[256,896]{1,0:T(8,128)(2,1)S(1)} %get-tuple-element.109), channel_id=1, source_target_pairs={{0,1},{1,2},{2,3},{3,0},{4,5},{5,6},{6,7},{7,4},{8,9},{9,10},{10,1... | collective-permute-start | bytes 1376264 | tf_op jit(solution)/shard_map/ppermute | solution.py:121
  128.4 33.6 %collective-permute-start.6 = (bf16[256,896]{1,0:T(8,128)(2,1)S(1)}, bf16[256,896]{1,0:T(8,128)(2,1)S(1)}, u32[]{:S(2)}, u32[]{:S(2)}) collective-permute-start(bf16[256,896]{1,0:T(8,128)(2,1)S(1)} %get-tuple-element.109), channel_id=1, source_target_pairs={{0,2},{1,3},{2,0},{3,1},{4,6},{5,7},{6,4},{7,5},{8,10},{9,11},{10,... | collective-permute-start | bytes 1376264 | tf_op jit(solution)/shard_map/ppermute | solution.py:121
  130.1 34.7 %collective-permute-start.7 = (bf16[256,896]{1,0:T(8,128)(2,1)S(1)}, bf16[256,896]{1,0:T(8,128)(2,1)S(1)}, u32[]{:S(2)}, u32[]{:S(2)}) collective-permute-start(bf16[256,896]{1,0:T(8,128)(2,1)S(1)} %get-tuple-element.109), channel_id=1, source_target_pairs={{0,3},{1,0},{2,1},{3,2},{4,7},{5,4},{6,5},{7,6},{8,11},{9,8},{10,9... | collective-permute-start | bytes 1376264 | tf_op jit(solution)/shard_map/ppermute | solution.py:121
  133.0 58.2 %copy-start.80 = (bf16[896,4736]{1,0:T(8,128)(2,1)S(1)}, bf16[896,4736]{1,0:T(8,128)(2,1)}, u32[]{:S(2)}) copy-start(bf16[896,4736]{1,0:T(8,128)(2,1)} %all-gather.5.cloned.1.call-done) | copy-start | bytes 25460740
  141.5 61.9 %collective-permute-start.19 = (bf16[256,896]{1,0:T(8,128)(2,1)S(1)}, bf16[256,896]{1,0:T(8,128)(2,1)S(1)}, u32[]{:S(2)}, u32[]{:S(2)}) collective-permute-start(bf16[256,896]{1,0:T(8,128)(2,1)S(1)} %copy-done.36), channel_id=1, source_target_pairs={{0,1},{1,2},{2,3},{3,0},{4,5},{5,6},{6,7},{7,4},{8,9},{9,10},{10,1... | collective-permute-start | bytes 1376264 | tf_op jit(solution)/shard_map/ppermute | solution.py:121
  162.0 42.0 %collective-permute-start.20 = (bf16[256,896]{1,0:T(8,128)(2,1)S(1)}, bf16[256,896]{1,0:T(8,128)(2,1)S(1)}, u32[]{:S(2)}, u32[]{:S(2)}) collective-permute-start(bf16[256,896]{1,0:T(8,128)(2,1)S(1)} %copy-done.36), channel_id=1, source_target_pairs={{0,2},{1,3},{2,0},{3,1},{4,6},{5,7},{6,4},{7,5},{8,10},{9,11},{10,... | collective-permute-start | bytes 1376264 | tf_op jit(solution)/shard_map/ppermute | solution.py:121
  164.8 43.8 %collective-permute-start.21 = (bf16[256,896]{1,0:T(8,128)(2,1)S(1)}, bf16[256,896]{1,0:T(8,128)(2,1)S(1)}, u32[]{:S(2)}, u32[]{:S(2)}) collective-permute-start(bf16[256,896]{1,0:T(8,128)(2,1)S(1)} %copy-done.36), channel_id=1, source_target_pairs={{0,3},{1,0},{2,1},{3,2},{4,7},{5,4},{6,5},{7,6},{8,11},{9,8},{10,9... | collective-permute-start | bytes 1376264 | tf_op jit(solution)/shard_map/ppermute | solution.py:121
  203.4 35.6 %copy-start.37 = (bf16[256,896]{1,0:T(8,128)(2,1)}, bf16[256,896]{1,0:T(8,128)(2,1)S(1)}, u32[]{:S(2)}) copy-start(bf16[256,896]{1,0:T(8,128)(2,1)S(1)} %collective-permute-done.19) | copy-start | bytes 1376260
  203.4 49.1 %collective-permute-start.13 = (bf16[256,896]{1,0:T(8,128)(2,1)S(1)}, bf16[256,896]{1,0:T(8,128)(2,1)S(1)}, u32[]{:S(2)}, u32[]{:S(2)}) collective-permute-start(bf16[256,896]{1,0:T(8,128)(2,1)S(1)} %get-tuple-element.107), channel_id=1, source_target_pairs={{0,1},{1,2},{2,3},{3,0},{4,5},{5,6},{6,7},{7,4},{8,9},{9,10},{10,1... | collective-permute-start | bytes 1376264 | tf_op jit(solution)/shard_map/ppermute | solution.py:121
  203.9 35.0 %copy-start.39 = (bf16[256,896]{1,0:T(8,128)(2,1)}, bf16[256,896]{1,0:T(8,128)(2,1)S(1)}, u32[]{:S(2)}) copy-start(bf16[256,896]{1,0:T(8,128)(2,1)S(1)} %collective-permute-done.20) | copy-start | bytes 1376260
  203.9 48.6 %collective-permute-start.14 = (bf16[256,896]{1,0:T(8,128)(2,1)S(1)}, bf16[256,896]{1,0:T(8,128)(2,1)S(1)}, u32[]{:S(2)}, u32[]{:S(2)}) collective-permute-start(bf16[256,896]{1,0:T(8,128)(2,1)S(1)} %get-tuple-element.107), channel_id=1, source_target_pairs={{0,2},{1,3},{2,0},{3,1},{4,6},{5,7},{6,4},{7,5},{8,10},{9,11},{10,... | collective-permute-start | bytes 1376264 | tf_op jit(solution)/shard_map/ppermute | solution.py:121
  208.7 30.3 %copy-start.41 = (bf16[256,896]{1,0:T(8,128)(2,1)}, bf16[256,896]{1,0:T(8,128)(2,1)S(1)}, u32[]{:S(2)}) copy-start(bf16[256,896]{1,0:T(8,128)(2,1)S(1)} %collective-permute-done.21) | copy-start | bytes 1376260
  208.7 45.9 %collective-permute-start.15 = (bf16[256,896]{1,0:T(8,128)(2,1)S(1)}, bf16[256,896]{1,0:T(8,128)(2,1)S(1)}, u32[]{:S(2)}, u32[]{:S(2)}) collective-permute-start(bf16[256,896]{1,0:T(8,128)(2,1)S(1)} %get-tuple-element.107), channel_id=1, source_target_pairs={{0,3},{1,0},{2,1},{3,2},{4,7},{5,4},{6,5},{7,6},{8,11},{9,8},{10,9... | collective-permute-start | bytes 1376264 | tf_op jit(solution)/shard_map/ppermute | solution.py:121
  252.5 23.9 %collective-permute-start.29 = (bf16[256,896]{1,0:T(8,128)(2,1)}, bf16[256,896]{1,0:T(8,128)(2,1)S(1)}, u32[]{:S(2)}, u32[]{:S(2)}) collective-permute-start(bf16[256,896]{1,0:T(8,128)(2,1)} %get-tuple-element.145), channel_id=1, source_target_pairs={{0,3},{1,0},{2,1},{3,2},{4,7},{5,4},{6,5},{7,6},{8,11},{9,8},{10,9... | collective-permute-start | bytes 1376264 | tf_op jit(solution)/shard_map/ppermute | solution.py:121
  252.6 45.2 %collective-permute-start.10 = (bf16[256,896]{1,0:T(8,128)(2,1)S(1)}, bf16[256,896]{1,0:T(8,128)(2,1)S(1)}, u32[]{:S(2)}, u32[]{:S(2)}) collective-permute-start(bf16[256,896]{1,0:T(8,128)(2,1)S(1)} %get-tuple-element.129), channel_id=1, source_target_pairs={{0,1},{1,2},{2,3},{3,0},{4,5},{5,6},{6,7},{7,4},{8,9},{9,10},{10,1... | collective-permute-start | bytes 1376264 | tf_op jit(solution)/shard_map/ppermute | solution.py:121
  254.6 50.4 %collective-permute-start.8 = (bf16[256,896]{1,0:T(8,128)(2,1)S(1)}, bf16[256,896]{1,0:T(8,128)(2,1)S(1)}, u32[]{:S(2)}, u32[]{:S(2)}) collective-permute-start(bf16[256,896]{1,0:T(8,128)(2,1)S(1)} %get-tuple-element.128), channel_id=1, source_target_pairs={{0,3},{1,0},{2,1},{3,2},{4,7},{5,4},{6,5},{7,6},{8,11},{9,8},{10,9... | collective-permute-start | bytes 1376264 | tf_op jit(solution)/shard_map/ppermute | solution.py:121
  268.8 54.8 %collective-permute-start.9 = (bf16[256,896]{1,0:T(8,128)(2,1)S(1)}, bf16[256,896]{1,0:T(8,128)(2,1)S(1)}, u32[]{:S(2)}, u32[]{:S(2)}) collective-permute-start(bf16[256,896]{1,0:T(8,128)(2,1)S(1)} %get-tuple-element.130), channel_id=1, source_target_pairs={{0,2},{1,3},{2,0},{3,1},{4,6},{5,7},{6,4},{7,5},{8,10},{9,11},{10,... | collective-permute-start | bytes 1376264 | tf_op jit(solution)/shard_map/ppermute | solution.py:121
  269.0 54.6 %collective-permute-start.22 = (bf16[256,896]{1,0:T(8,128)(2,1)S(1)}, bf16[256,896]{1,0:T(8,128)(2,1)S(1)}, u32[]{:S(2)}, u32[]{:S(2)}) collective-permute-start(bf16[256,896]{1,0:T(8,128)(2,1)S(1)} %get-tuple-element.122), channel_id=1, source_target_pairs={{0,3},{1,0},{2,1},{3,2},{4,7},{5,4},{6,5},{7,6},{8,11},{9,8},{10,9... | collective-permute-start | bytes 1376264 | tf_op jit(solution)/shard_map/ppermute | solution.py:121
  276.4 88.1 %collective-permute-start.23 = (bf16[256,896]{1,0:T(8,128)(2,1)S(1)}, bf16[256,896]{1,0:T(8,128)(2,1)S(1)}, u32[]{:S(2)}, u32[]{:S(2)}) collective-permute-start(bf16[256,896]{1,0:T(8,128)(2,1)S(1)} %get-tuple-element.124), channel_id=1, source_target_pairs={{0,2},{1,3},{2,0},{3,1},{4,6},{5,7},{6,4},{7,5},{8,10},{9,11},{10,... | collective-permute-start | bytes 1376264 | tf_op jit(solution)/shard_map/ppermute | solution.py:121
  286.6 68.7 %copy-start.87 = (bf16[1024,1280]{1,0:T(8,128)(2,1)}, bf16[1024,1280]{1,0:T(8,128)(2,1)S(1)}, u32[]{:S(2)}) copy-start(bf16[1024,1280]{1,0:T(8,128)(2,1)S(1)} %get-tuple-element.121) | copy-start | bytes 7864324
  297.8 66.8 %collective-permute-start.24 = (bf16[256,896]{1,0:T(8,128)(2,1)S(1)}, bf16[256,896]{1,0:T(8,128)(2,1)S(1)}, u32[]{:S(2)}, u32[]{:S(2)}) collective-permute-start(bf16[256,896]{1,0:T(8,128)(2,1)S(1)} %get-tuple-element.123), channel_id=1, source_target_pairs={{0,1},{1,2},{2,3},{3,0},{4,5},{5,6},{6,7},{7,4},{8,9},{9,10},{10,1... | collective-permute-start | bytes 1376264 | tf_op jit(solution)/shard_map/ppermute | solution.py:121
  305.0 60.9 %collective-permute-start.30 = (bf16[256,896]{1,0:T(8,128)(2,1)S(1)}, bf16[256,896]{1,0:T(8,128)(2,1)S(1)}, u32[]{:S(2)}, u32[]{:S(2)}) collective-permute-start(bf16[256,896]{1,0:T(8,128)(2,1)S(1)} %get-tuple-element.125), channel_id=1, source_target_pairs={{0,3},{1,0},{2,1},{3,2},{4,7},{5,4},{6,5},{7,6},{8,11},{9,8},{10,9... | collective-permute-start | bytes 1376264 | tf_op jit(solution)/shard_map/ppermute | solution.py:121
  323.6 80.2 %collective-permute-start.31 = (bf16[256,896]{1,0:T(8,128)(2,1)S(1)}, bf16[256,896]{1,0:T(8,128)(2,1)S(1)}, u32[]{:S(2)}, u32[]{:S(2)}) collective-permute-start(bf16[256,896]{1,0:T(8,128)(2,1)S(1)} %get-tuple-element.127), channel_id=1, source_target_pairs={{0,2},{1,3},{2,0},{3,1},{4,6},{5,7},{6,4},{7,5},{8,10},{9,11},{10,... | collective-permute-start | bytes 1376264 | tf_op jit(solution)/shard_map/ppermute | solution.py:121
  323.6 80.2 %collective-permute-start.32 = (bf16[256,896]{1,0:T(8,128)(2,1)S(1)}, bf16[256,896]{1,0:T(8,128)(2,1)S(1)}, u32[]{:S(2)}, u32[]{:S(2)}) collective-permute-start(bf16[256,896]{1,0:T(8,128)(2,1)S(1)} %get-tuple-element.126), channel_id=1, source_target_pairs={{0,1},{1,2},{2,3},{3,0},{4,5},{5,6},{6,7},{7,4},{8,9},{9,10},{10,1... | collective-permute-start | bytes 1376264 | tf_op jit(solution)/shard_map/ppermute | solution.py:121
  364.6 41.1 %collective-permute-start.16 = (bf16[256,896]{1,0:T(8,128)(2,1)S(1)}, bf16[256,896]{1,0:T(8,128)(2,1)S(1)}, u32[]{:S(2)}, u32[]{:S(2)}) collective-permute-start(bf16[256,896]{1,0:T(8,128)(2,1)S(1)} %get-tuple-element.131), channel_id=1, source_target_pairs={{0,3},{1,0},{2,1},{3,2},{4,7},{5,4},{6,5},{7,6},{8,11},{9,8},{10,9... | collective-permute-start | bytes 1376264 | tf_op jit(solution)/shard_map/ppermute | solution.py:121
  364.6 53.4 %collective-permute-start.17 = (bf16[256,896]{1,0:T(8,128)(2,1)S(1)}, bf16[256,896]{1,0:T(8,128)(2,1)S(1)}, u32[]{:S(2)}, u32[]{:S(2)}) collective-permute-start(bf16[256,896]{1,0:T(8,128)(2,1)S(1)} %get-tuple-element.133), channel_id=1, source_target_pairs={{0,2},{1,3},{2,0},{3,1},{4,6},{5,7},{6,4},{7,5},{8,10},{9,11},{10,... | collective-permute-start | bytes 1376264 | tf_op jit(solution)/shard_map/ppermute | solution.py:121
  365.9 52.0 %collective-permute-start.18 = (bf16[256,896]{1,0:T(8,128)(2,1)S(1)}, bf16[256,896]{1,0:T(8,128)(2,1)S(1)}, u32[]{:S(2)}, u32[]{:S(2)}) collective-permute-start(bf16[256,896]{1,0:T(8,128)(2,1)S(1)} %get-tuple-element.132), channel_id=1, source_target_pairs={{0,1},{1,2},{2,3},{3,0},{4,5},{5,6},{6,7},{7,4},{8,9},{9,10},{10,1... | collective-permute-start | bytes 1376264 | tf_op jit(solution)/shard_map/ppermute | solution.py:121
  418.0 14.2 %slice-start.3 = ((s8[11010048]{0:T(1024)(128)(4,1)}), s8[2621440]{0:T(1024)(128)(4,1)S(1)}, s32[]{:S(2)}) async-start(s8[11010048]{0:T(1024)(128)(4,1)} %bitcast.271), calls=%async_computation.9 | async-start | bytes 5242880
  440.5 13.7 %slice-start = ((s8[11010048]{0:T(1024)(128)(4,1)}), s8[2621440]{0:T(1024)(128)(4,1)S(1)}, s32[]{:S(2)}) async-start(s8[11010048]{0:T(1024)(128)(4,1)} %bitcast.269), calls=%async_computation.6 | async-start | bytes 5242880
  463.4 9.0 %collective-permute-start.25 = (bf16[256,256]{0,1:T(8,128)(2,1)S(1)}, bf16[256,256]{0,1:T(8,128)(2,1)S(1)}, u32[]{:S(2)}, u32[]{:S(2)}) collective-permute-start(bf16[256,256]{0,1:T(8,128)(2,1)S(1)} %get-tuple-element.157), channel_id=1, source_target_pairs={{1,0},{2,1},{3,2},{5,4},{6,5},{7,6},{9,8},{10,9},{11,10},{13,12},{... | collective-permute-start | bytes 393224 | tf_op jit(solution)/shard_map/ppermute | solution.py:296
  464.7 13.6 %collective-permute-start.26 = (bf16[256,256]{0,1:T(8,128)(2,1)S(1)}, bf16[256,256]{0,1:T(8,128)(2,1)S(1)}, u32[]{:S(2)}, u32[]{:S(2)}) collective-permute-start(bf16[256,256]{0,1:T(8,128)(2,1)S(1)} %get-tuple-element.158), channel_id=1, source_target_pairs={{2,0},{3,1},{6,4},{7,5},{10,8},{11,9},{14,12},{15,13},{18,16},{19,... | collective-permute-start | bytes 393224 | tf_op jit(solution)/shard_map/ppermute | solution.py:296
  466.6 11.9 %collective-permute-start.33 = (bf16[256,256]{0,1:T(8,128)(2,1)S(1)}, bf16[256,256]{0,1:T(8,128)(2,1)S(1)}, u32[]{:S(2)}, u32[]{:S(2)}) collective-permute-start(bf16[256,256]{0,1:T(8,128)(2,1)S(1)} %get-tuple-element.159), channel_id=1, source_target_pairs={{1,0},{2,1},{3,2},{5,4},{6,5},{7,6},{9,8},{10,9},{11,10},{13,12},{... | collective-permute-start | bytes 393224 | tf_op jit(solution)/shard_map/ppermute | solution.py:296
  468.0 16.2 %collective-permute-start.34 = (bf16[256,256]{0,1:T(8,128)(2,1)S(1)}, bf16[256,256]{0,1:T(8,128)(2,1)S(1)}, u32[]{:S(2)}, u32[]{:S(2)}) collective-permute-start(bf16[256,256]{0,1:T(8,128)(2,1)S(1)} %get-tuple-element.160), channel_id=1, source_target_pairs={{2,0},{3,1},{6,4},{7,5},{10,8},{11,9},{14,12},{15,13},{18,16},{19,... | collective-permute-start | bytes 393224 | tf_op jit(solution)/shard_map/ppermute | solution.py:296
  497.4 116.7 %reduce-scatter.5.cloned.1.call-start = ((), (), s32[]{:S(2)}) async-start(), calls=%async_computation.5 | async-start | bytes 7741440 | tf_op jit(solution)/shard_map/reduce_scatter | solution.py:274
  547.4 8.5 %collective-permute-start.35 = (bf16[28,2176]{1,0:T(8,128)(2,1)S(1)}, bf16[28,2176]{1,0:T(8,128)(2,1)S(1)}, u32[]{:S(2)}, u32[]{:S(2)}) collective-permute-start(bf16[28,2176]{1,0:T(8,128)(2,1)S(1)} %get-tuple-element.154), channel_id=1, source_target_pairs={{0,1},{1,2},{2,3},{3,0},{4,5},{5,6},{6,7},{7,4},{8,9},{9,10},{10,1... | collective-permute-start | bytes 365576 | tf_op jit(solution)/shard_map/ppermute | solution.py:121
  548.9 11.8 %collective-permute-start.36 = (bf16[28,2176]{1,0:T(8,128)(2,1)S(1)}, bf16[28,2176]{1,0:T(8,128)(2,1)S(1)}, u32[]{:S(2)}, u32[]{:S(2)}) collective-permute-start(bf16[28,2176]{1,0:T(8,128)(2,1)S(1)} %get-tuple-element.156), channel_id=1, source_target_pairs={{0,2},{1,3},{2,0},{3,1},{4,6},{5,7},{6,4},{7,5},{8,10},{9,11},{10,... | collective-permute-start | bytes 365576 | tf_op jit(solution)/shard_map/ppermute | solution.py:121
  551.3 9.4 %collective-permute-start.37 = (bf16[28,2176]{1,0:T(8,128)(2,1)S(1)}, bf16[28,2176]{1,0:T(8,128)(2,1)S(1)}, u32[]{:S(2)}, u32[]{:S(2)}) collective-permute-start(bf16[28,2176]{1,0:T(8,128)(2,1)S(1)} %get-tuple-element.155), channel_id=1, source_target_pairs={{0,3},{1,0},{2,1},{3,2},{4,7},{5,4},{6,5},{7,6},{8,11},{9,8},{10,9... | collective-permute-start | bytes 365576 | tf_op jit(solution)/shard_map/ppermute | solution.py:121
  (85 other events, 414.1 us)
Sparse Core Ops, SparseCore 0:
  30.0 29.0 all-gather.2
  61.0 54.7 all-gather.4
  497.5 48.6 reduce-scatter.2
  549.5 64.5 reduce-scatter.4

commit v2 on v1

v2 whole, which is shorter than its diff:
```python
import functools
import jax, jax.numpy as jnp
from jax import lax
from jax.sharding import PartitionSpec as P
from jax.experimental import pallas as pl
from jax.experimental.pallas import tpu as pltpu
D=896; HEADS=14; KV_HEADS=2; HEAD=64; LANES=128
QW=896; KW=128
epsilon=1e-6
bf16=jnp.bfloat16; f32=jnp.float32
LIMIT=56*1024*1024
COST=pl.CostEstimate(flops=1, bytes_accessed=1, transcendentals=0)

def dot(left, right, left_dim, right_dim):
    return lax.dot_general(left, right, (((left_dim,), (right_dim,)), ((), ())), preferred_element_type=f32)

def half_turn(v, back):
    lane = lax.broadcasted_iota(jnp.int32, v.shape, 1) & (HEAD-1)
    width=v.shape[1]
    up = pltpu.roll(v, width-HEAD//2, 1)
    down = pltpu.roll(v, HEAD//2, 1)
    return jnp.where(lane < HEAD//2, up, down)

def scaled(v):
    return lax.rsqrt(jnp.mean(v*v, axis=-1, keepdims=True)+epsilon)

def project_kernel(x_ref, wq_ref, wkv_ref, ws_ref, spread_ref, cos_ref, sin_ref, rq_ref, kv_ref, n1_ref, rows_ref, bias_ref):
    @pl.when(pl.program_id(0)==0)
    def _():
        table = ws_ref[...].astype(f32).T[:8]
        rows_ref[...] = table
        close = dot(table.astype(bf16), spread_ref[...],1,0)
        bias_ref[:, :QW] = table[2:3]
        bias_ref[:, QW:QW+KW] = close[3:4]
        bias_ref[:, QW+KW:] = close[4:5]
    x = x_ref[0].astype(f32)
    n1 = (x*scaled(x)*rows_ref[0:1]).astype(bf16)
    n1_ref[0] = n1
    cos = cos_ref[0]; sin = sin_ref[0]
    q = dot(n1, wq_ref[...],1,0) + bias_ref[:, :QW]
    for b in range(QW//LANES):
        v = q[:, b*LANES:(b+1)*LANES]
        r = (v*cos + half_turn(v,False)*sin).astype(bf16)
        rq_ref[0,:, b*LANES:(b+1)*LANES] = (r.astype(f32)*HEAD**-0.5).astype(bf16)
    kv = dot(n1, wkv_ref[...],1,0) + bias_ref[:, QW:]
    v = kv[:, :KW]
    kv_ref[0,:, :KW] = (v*cos + half_turn(v,False)*sin).astype(bf16)
    kv_ref[0,:, KW:] = kv[:, KW:].astype(bf16)

def project(x, first_set, spread, cos, sin):
    m, rows, _ = x.shape
    full=lambda shape,idx: pl.BlockSpec(shape, lambda i: idx)
    blk=lambda w: pl.BlockSpec((1,rows,w), lambda i:(i,0,0))
    return pl.pallas_call(
        project_kernel, grid=(m,),
        in_specs=[blk(D), full((D,QW),(0,1)), full((D,2*KW),(0,7)), full((D,LANES),(0,16)), full((D,LANES),(0,0)), blk(LANES), blk(LANES)],
        out_specs=[blk(QW), blk(2*KW), blk(D), full((8,D),(0,0))],
        out_shape=[jax.ShapeDtypeStruct((m,rows,QW),bf16), jax.ShapeDtypeStruct((m,rows,2*KW),bf16), jax.ShapeDtypeStruct((m,rows,D),bf16), jax.ShapeDtypeStruct((8,D),f32)],
        scratch_shapes=[pltpu.VMEM((1,QW+2*KW),f32)],
        compiler_params=pltpu.CompilerParams(vmem_limit_bytes=LIMIT), cost_estimate=COST,
        name="project",
    )(x, first_set, first_set, first_set, spread, cos, sin)

BLOCK=128
def units():
    group=HEADS//KV_HEADS
    out=[]
    for g in range(KV_HEADS):
        for parity in range(2):
            blocks=[h//2 for h in range(g*group,(g+1)*group) if h%2==parity]
            out.append((g,parity,blocks))
    return out

def padded(v, g, parity, lane):
    if g != parity:
        v = pltpu.roll(v.astype(f32), HEAD, 1).astype(bf16)
    keep = (lane >= HEAD) if parity else (lane < HEAD)
    return jnp.where(keep, v, jnp.zeros_like(v))

def mask_bias(begins, rank_base, q0, window, reach):
    key = lax.broadcasted_iota(jnp.int32,(window,BLOCK),0) + (rank_base + q0 - reach)
    query = lax.broadcasted_iota(jnp.int32,(window,BLOCK),1) + (rank_base + q0)
    ok = (key >= begins) & (key <= query)
    return jnp.where(ok, 0.0, -1e30).astype(f32)

def fill_padded(kv_refs, k_ref, v_ref):
    rows = kv_refs[0].shape[0]
    lane = lax.broadcasted_iota(jnp.int32,(rows,LANES),1)
    for p,ref in enumerate(kv_refs):
        kv=ref[...]
        for g,parity,_ in units():
            u=2*g+parity
            k_ref[u, p*rows:(p+1)*rows] = padded(kv[:, :KW], g, parity, lane)
            v_ref[u, p*rows:(p+1)*rows] = padded(kv[:, KW:], g, parity, lane)

def attend_kernel(base_ref, rq_ref, kv0_ref, kv1_ref, kv2_ref, begin_ref, wo_ref, x_ref, rows_ref, *refs):
    n2_ref, mixed_ref, middle_ref, lse_ref, k_ref, v_ref = refs[-6:]
    qb = pl.program_id(0)
    rows = kv0_ref.shape[0]
    reach=512; window=reach+BLOCK
    @pl.when(qb==0)
    def _():
        fill_padded((kv2_ref,kv1_ref,kv0_ref), k_ref, v_ref)
    q0 = qb*BLOCK
    bias = mask_bias(begin_ref[...], base_ref[0], q0, window, reach)
    parts=[None]*7
    start = pl.multiple_of(q0 + (2*rows - reach), BLOCK)
    for g,parity,blocks in units():
        u=2*g+parity
        qs = jnp.concatenate([rq_ref[:, b*LANES:(b+1)*LANES] for b in blocks], axis=0)
        keys = k_ref[u, pl.ds(start,window)]
        vals = v_ref[u, pl.ds(start,window)]
        s = dot(keys, qs, 1, 1) + jnp.concatenate([bias]*len(blocks),axis=1)
        top = jnp.max(s, axis=0, keepdims=True)
        e = jnp.exp(s-top)
        total = jnp.sum(e, axis=0, keepdims=True)
        p = (e*(1.0/total)).astype(bf16)
        o = dot(vals, p, 0, 0)
        lse = top+jnp.log(total)
        for i,b in enumerate(blocks):
            piece=o[:, i*BLOCK:(i+1)*BLOCK]
            parts[b] = piece if parts[b] is None else parts[b]+piece
            lse_ref[0, 2*b+parity:2*b+parity+1, :] = lse[:, i*BLOCK:(i+1)*BLOCK]
    for b in range(7):
        mixed_ref[:, b*LANES:(b+1)*LANES] = parts[b].T.astype(bf16)
    middle = x_ref[...].astype(f32) + dot(mixed_ref[...], wo_ref[...],1,0)
    middle_ref[...] = middle
    n2_ref[...] = (middle*scaled(middle)*rows_ref[1:2]).astype(bf16)

def attend(m, base, rq, kvs, begins, first_set, x, rows_table, before):
    micros, rows, _ = rq.shape; nq=rows//BLOCK
    full=lambda shape: pl.BlockSpec(shape, lambda i: (0,)*len(shape))
    blk=lambda w: pl.BlockSpec((None,BLOCK,w), lambda i:(m,i,0))
    sd=jax.ShapeDtypeStruct
    return pl.pallas_call(
        attend_kernel, grid=(nq,),
        in_specs=[pl.BlockSpec(memory_space=pltpu.SMEM), blk(QW)]+[pl.BlockSpec((None,rows,2*KW),lambda i:(m,0,0))]*3+[pl.BlockSpec((None,1,BLOCK),lambda i:(m,0,i)), full((D,QW)), blk(D), full((8,D))]+[pl.BlockSpec(memory_space=pl.ANY)]*len(before),
        out_specs=[pl.BlockSpec((BLOCK,D),lambda i:(i,0)), blk(QW), blk(D), pl.BlockSpec((None,1,16,BLOCK),lambda i:(m,i,0,0))],
        out_shape=[sd((rows,D),bf16), sd((micros,rows,QW),bf16), sd((micros,rows,D),f32), sd((micros,nq,16,BLOCK),f32)],
        scratch_shapes=[pltpu.VMEM((4,3*rows,LANES),bf16), pltpu.VMEM((4,3*rows,LANES),bf16)],
        input_output_aliases={9+k:1+k for k in range(len(before))},
        compiler_params=pltpu.CompilerParams(vmem_limit_bytes=LIMIT), cost_estimate=COST,
        name="attend",
    )(base, rq, *kvs, begins, first_set, x, rows_table, *before)

def attend_back_kernel(base_ref, rq_ref, kv0_ref, kv1_ref, kv2_ref, begin_ref, wo_ref, rows_ref, lse_ref, middle_ref, dy_ref, cos_ref, sin_ref, *refs, count):
    gs=refs[:count]
    far1_ref, far2_ref, dmid_ref, dmb_ref, dq_ref, own_ref, gain_ref, k_ref, v_ref, dk_ref, dv_ref = refs[-11:]
    qb = pl.program_id(0); nq=pl.num_programs(0)
    rows = kv0_ref.shape[0]
    reach=512; window=reach+BLOCK
    @pl.when(qb==0)
    def _():
        fill_padded((kv2_ref,kv1_ref,kv0_ref), k_ref, v_ref)
        dk_ref[...] = jnp.zeros_like(dk_ref)
        dv_ref[...] = jnp.zeros_like(dv_ref)
        gain_ref[...] = jnp.zeros_like(gain_ref)
    dn2 = gs[0][...].astype(f32)
    for g_ref in gs[1:]:
        dn2 = dn2+g_ref[...].astype(f32)
    middle = middle_ref[...]
    inv = scaled(middle)
    gain_ref[...] += jnp.broadcast_to(jnp.sum(dn2*(middle*inv),axis=0,keepdims=True), gain_ref.shape)
    w2 = dn2*rows_ref[1:2]
    dmid = dy_ref[...].astype(f32) + inv*w2 - middle*(inv*inv*inv)*jnp.mean(w2*middle,axis=-1,keepdims=True)
    dmid_ref[...] = dmid
    dmb = dmid.astype(bf16)
    dmb_ref[...] = dmb
    dmixed = dot(dmb, wo_ref[...],1,1).astype(bf16)
    q0 = qb*BLOCK
    bias = mask_bias(begin_ref[...], base_ref[0], q0, window, reach)
    start = pl.multiple_of(q0 + (2*rows - reach), BLOCK)
    parts=[None]*7
    for g,parity,blocks in units():
        u=2*g+parity
        n=len(blocks)
        qs = jnp.concatenate([rq_ref[:, b*LANES:(b+1)*LANES] for b in blocks], axis=0)
        ds_ = jnp.concatenate([dmixed[:, b*LANES:(b+1)*LANES] for b in blocks], axis=0)
        keys = k_ref[u, pl.ds(start,window)]
        vals = v_ref[u, pl.ds(start,window)]
        lse = jnp.concatenate([lse_ref[0, 2*b+parity:2*b+parity+1, :] for b in blocks],axis=1)
        p = jnp.exp(dot(keys,qs,1,1) + jnp.concatenate([bias]*n,axis=1) - lse)
        dp = dot(vals, ds_, 1, 1)
        t = p*dp
        ds = (t-p*jnp.sum(t,axis=0,keepdims=True)).astype(bf16)
        pb = p.astype(bf16)
        o = dot(keys, ds, 0, 0)
        for i,b in enumerate(blocks):
            piece=o[:, i*BLOCK:(i+1)*BLOCK]
            parts[b] = piece if parts[b] is None else parts[b]+piece
        dk = dot(ds, qs, 1, 0); dv = dot(pb, ds_, 1, 0)
        keep = lax.broadcasted_iota(jnp.int32,(window,LANES),1)
        keep = (keep>=HEAD) if parity else (keep<HEAD)
        dk = jnp.where(keep, dk, 0.0); dv=jnp.where(keep,dv,0.0)
        if g!=parity:
            dk = pltpu.roll(dk,HEAD,1); dv=pltpu.roll(dv,HEAD,1)
        dk_ref[pl.ds(start,window)] += dk
        dv_ref[pl.ds(start,window)] += dv
    cos=cos_ref[...]; sin=sin_ref[...]
    for b in range(7):
        gq = parts[b].T*HEAD**-0.5
        dq_ref[:, b*LANES:(b+1)*LANES] = (gq*cos + half_turn(gq*sin,True)).astype(bf16)
    @pl.when(qb==nq-1)
    def _():
        own_ref[:, :KW] = dk_ref[2*rows:]; own_ref[:, KW:] = dv_ref[2*rows:]
        far1_ref[:, :KW] = dk_ref[rows:2*rows].astype(bf16); far1_ref[:, KW:] = dv_ref[rows:2*rows].astype(bf16)
        far2_ref[:, :KW] = dk_ref[:rows].astype(bf16); far2_ref[:, KW:] = dv_ref[:rows].astype(bf16)

def attend_back(m, base, rq, kvs, begins, first_set, rows_table, lse, middle, dy, gs, cos, sin, before):
    micros, rows, _ = rq.shape; nq=rows//BLOCK
    full=lambda shape: pl.BlockSpec(shape, lambda i: (0,)*len(shape))
    blk=lambda w: pl.BlockSpec((None,BLOCK,w), lambda i:(m,i,0))
    one=lambda h,w: pl.BlockSpec((None,h,w), lambda i:(m,0,0))
    sd=jax.ShapeDtypeStruct
    at=12+len(gs)
    return pl.pallas_call(
        functools.partial(attend_back_kernel,count=len(gs)), grid=(nq,),
        in_specs=[pl.BlockSpec(memory_space=pltpu.SMEM), blk(QW)]+[one(rows,2*KW)]*3+[pl.BlockSpec((None,1,BLOCK),lambda i:(m,0,i)), full((D,QW)), full((8,D)),
            pl.BlockSpec((None,1,16,BLOCK),lambda i:(m,i,0,0)), blk(D), blk(D)]+[blk(LANES)]*2+[pl.BlockSpec((BLOCK,D),lambda i:(i,0))]*len(gs)+[pl.BlockSpec(memory_space=pl.ANY)]*len(before),
        out_specs=[full((rows,2*KW)), full((rows,2*KW)), blk(D), blk(D), blk(QW), one(rows,2*KW), one(8,D)],
        out_shape=[sd((rows,2*KW),bf16), sd((rows,2*KW),bf16), sd((micros,rows,D),f32), sd((micros,rows,D),bf16), sd((micros,rows,QW),bf16), sd((micros,rows,2*KW),f32), sd((micros,8,D),f32)],
        scratch_shapes=[pltpu.VMEM((4,3*rows,LANES),bf16)]*2+[pltpu.VMEM((3*rows,LANES),f32)]*2,
        input_output_aliases={at+1+k:2+k for k in range(len(before))},
        compiler_params=pltpu.CompilerParams(vmem_limit_bytes=LIMIT), cost_estimate=COST,
        name="attend_back",
    )(base, rq, *kvs, begins, first_set, rows_table, lse, middle, dy, cos, sin, *gs, *before)

CHUNK=256

class Tokens:
    def __init__(self, kind, arrays, micro=None):
        self.kind, self.arrays, self.micro = kind, tuple(arrays), micro
    def specs(self, rows):
        if self.kind=="whole":
            return [pl.BlockSpec((rows,D), lambda i: (i,0))]
        if self.micro is None:
            return [pl.BlockSpec((rows,D), lambda i: (0,0), pipeline_mode=pl.Buffered(1))]*len(self.arrays)
        return [pl.BlockSpec((None,rows,D), lambda i: (self.micro,0,0), pipeline_mode=pl.Buffered(1))]*len(self.arrays)
    def take(self, refs, i, rank, parts, into):
        if self.kind=="whole":
            into[...]=refs[0][...]
        elif self.kind=="around":
            for k in range(parts):
                @pl.when(lax.rem(rank-i+parts,parts)==k)
                def _(k=k): into[...]=refs[k][...]
        else:
            for k in range(-(parts-1),parts):
                ref = refs[0] if k==0 else refs[2*k-1] if k>0 else refs[-2*k]
                @pl.when(rank-i==k)
                def _(ref=ref): into[...]=ref[...]

def feed_kernel(rank_ref, *refs, parts, kept, toks, grads):
    n_t=len(toks.arrays); n_g=len(grads.arrays)
    ts=refs[:n_t]; gs=refs[n_t:n_t+n_g]; refs=refs[n_t+n_g:]
    wg_ref,wu_ref,wd_ref=refs[:3]
    refs=refs[3+kept:]
    backs=refs[:parts]; outs=refs[parts:2*parts]
    x_ref,y_ref,pair_ref,act_ref=refs[2*parts:]
    i=pl.program_id(0); rank=rank_ref[0]
    toks.take(ts,i,rank,parts,x_ref); grads.take(gs,i,rank,parts,y_ref)
    x=x_ref[...]; y=y_ref[...]
    width=wg_ref.shape[1]
    for j in range(width//CHUNK):
        c=slice(j*CHUNK,(j+1)*CHUNK); c2=slice(width+j*CHUNK,width+(j+1)*CHUNK)
        g=dot(x,wg_ref[:,c],1,0); u=dot(x,wu_ref[:,c],1,0); da=dot(y,wd_ref[:,c],1,0)
        s=jax.nn.sigmoid(g)
        gs_=g*s
        act_ref[:,c]=(gs_*u).astype(bf16)
        pair_ref[:,c]=(da*u*s*(1.0+g*(1.0-s))).astype(bf16)
        pair_ref[:,c2]=(da*gs_).astype(bf16)
    out=dot(act_ref[...],wd_ref[...],1,1)
    res=dot(pair_ref[:,:width],wg_ref[...],1,1)+dot(pair_ref[:,width:],wu_ref[...],1,1)
    for value,places in ((out,outs),(res,backs)):
        for k in range(parts):
            @pl.when(lax.rem(rank-i+parts,parts)==k)
            def _(k=k,value=value,places=places):
                places[k][...]=value.astype(places[k].dtype)

def feed(rank, toks, grads, rest_set, hidden_pad, micro, micros, parts, rows, before):
    full=lambda shape,idx=(0,0): pl.BlockSpec(shape, lambda i: idx)
    blk=lambda w,first=0: pl.BlockSpec((rows,w), lambda i:(first+i,0))
    sd=jax.ShapeDtypeStruct
    everything=rows*parts*micros
    kept=len(before)
    specs=[full((rows,D))]*parts+[pl.BlockSpec((None,rows,D),lambda i:(micro,0,0))]*parts
    shapes=[sd((rows,D),f32)]+[sd((rows,D),bf16)]*(parts-1)+[sd((micros,rows,D),f32)]+[sd((micros,rows,D),bf16)]*(parts-1)
    n_in=1+len(toks.arrays)+len(grads.arrays)+3
    out=pl.pallas_call(
        functools.partial(feed_kernel,parts=parts,kept=kept,toks=toks,grads=grads), grid=(parts,),
        in_specs=[pl.BlockSpec(memory_space=pltpu.SMEM)]+toks.specs(rows)+grads.specs(rows)+[pl.BlockSpec((D,hidden_pad),lambda i,k=k:(0,k),pipeline_mode=pl.Buffered(1)) for k in range(3)]+[pl.BlockSpec(memory_space=pl.ANY)]*kept,
        out_specs=specs+[blk(w,micro*parts) for w in (D,D,2*hidden_pad,hidden_pad)],
        out_shape=shapes+[sd((everything,w),bf16) for w in (D,D,2*hidden_pad,hidden_pad)],
        input_output_aliases={n_in+k:parts+k for k in range(kept)},
        compiler_params=pltpu.CompilerParams(vmem_limit_bytes=LIMIT), cost_estimate=COST,
        name="feed",
    )(rank,*toks.arrays,*grads.arrays,rest_set,rest_set,rest_set,*before)
    return out[:parts], out[parts:]

def finish_kernel(bit_ref, dq_ref, own_ref, cos_ref, sin_ref, wq_ref, wkv_ref, rows_ref, x_ref, n1_ref, dmid_ref, mixed_ref, dmb_ref, spread_ref, gain2_ref, *refs, near, block):
    far=refs[:-6]
    ig_ref, keep_ref, send_ref, acc_ref, small_ref, sum_ref = refs[-6:]
    i=pl.program_id(0)
    @pl.when(i==0)
    def _():
        acc_ref[...]=jnp.zeros_like(acc_ref)
        small_ref[...]=jnp.zeros_like(small_ref)
    for m in range(len(far)//near):
        @pl.when(i==m)
        def _(m=m):
            own=own_ref[...]
            for ref in far[m*near:(m+1)*near]:
                own=own+ref[...].astype(f32)
            sum_ref[...]=own
    own=sum_ref[...]
    k=own[:, :KW]
    cos=cos_ref[...]; sin=sin_ref[...]
    dk=(k*cos+half_turn(k*sin,True)).astype(bf16)
    dv=own[:, KW:].astype(bf16)
    dkv=jnp.concatenate([dk,dv],axis=1)
    dq=dq_ref[...]
    dn1=dot(dq,wq_ref[...],1,1)+dot(dkv,wkv_ref[...],1,1)
    x=x_ref[...].astype(f32); inv=scaled(x)
    small_ref[0:1]+=jnp.sum(dn1*(x*inv),axis=0,keepdims=True)
    small_ref[1:2]+=gain2_ref[0:1]
    small_ref[2:3]+=jnp.sum(dq.astype(f32),axis=0,keepdims=True)
    small_ref[3:4,:2*KW]+=jnp.sum(dkv.astype(f32),axis=0,keepdims=True)
    w1=dn1*rows_ref[0:1]
    ig_ref[...]=dmid_ref[...]+inv*w1-x*(inv*inv*inv)*jnp.mean(w1*x,axis=-1,keepdims=True)
    n1=n1_ref[...]
    acc_ref[:, :QW]+=dot(mixed_ref[...],dmb_ref[...],0,0)
    acc_ref[:, QW:2*QW]+=dot(n1,dq,0,0)
    acc_ref[:, 2*QW:2*QW+2*KW]+=dot(n1,dkv,0,0)
    @pl.when(i==pl.num_programs(0)-1)
    def _():
        pair=jnp.concatenate([small_ref[3:4,:KW],small_ref[3:4,KW:2*KW],jnp.zeros((6,KW),f32)],axis=0).astype(bf16)
        table=jnp.concatenate([small_ref[0:3],dot(pair,spread_ref[...],1,1)[0:2],jnp.zeros((LANES-5,D),f32)],axis=0)
        acc_ref[:, 2*QW+2*KW:]=table.T
        if block:
            for j in range(D//block//2):
                at=pl.multiple_of((2*j+bit_ref[0])*block,16)
                keep_ref[j*block:(j+1)*block]=acc_ref[pl.ds(at,block)].astype(bf16)
                at=pl.multiple_of((2*j+1-bit_ref[0])*block,16)
                send_ref[j*block:(j+1)*block]=acc_ref[pl.ds(at,block)].astype(bf16)
        else:
            keep_ref[...]=acc_ref[:D//2].astype(bf16)
            send_ref[...]=acc_ref[D//2:].astype(bf16)

def finish(bit,dq,own,far,cos,sin,first_set,rows_table,x,n1,dmid,mixed,dmb,spread,gain2,block):
    m,rows,_=x.shape
    full=lambda shape,idx=(0,0): pl.BlockSpec(shape, lambda i: idx)
    blk=lambda w,h=rows: pl.BlockSpec((None,h,w), lambda i:(i,0,0))
    sd=jax.ShapeDtypeStruct
    width=2*QW+2*KW+LANES
    near=len(far[0])
    far=[f for pieces in far for f in pieces]
    return pl.pallas_call(
        functools.partial(finish_kernel,near=near,block=block), grid=(m,),
        in_specs=[pl.BlockSpec(memory_space=pltpu.SMEM),blk(QW),blk(2*KW),blk(LANES),blk(LANES),full((D,QW),(0,1)),full((D,2*KW),(0,7)),full((8,D)),blk(D),blk(D),blk(D),blk(QW),blk(D),full((D,LANES)),blk(D,8)]+[full((rows,2*KW))]*len(far),
        out_specs=[blk(D),full((D//2,width)),full((D//2,width))],
        out_shape=[sd((m,rows,D),f32),sd((D//2,width),bf16),sd((D//2,width),bf16)],
        scratch_shapes=[pltpu.VMEM((D,width),f32),pltpu.VMEM((8,D),f32),pltpu.VMEM((rows,2*KW),f32)],
        compiler_params=pltpu.CompilerParams(vmem_limit_bytes=LIMIT), cost_estimate=COST,
        name="finish",
    )(bit,dq,own,cos,sin,first_set,first_set,rows_table,x,n1,dmid,mixed,dmb,spread,gain2,*far)

def weights_kernel(x_ref, y_ref, pair_ref, act_ref, out_ref, left_ref, *, split):
    j=pl.program_id(0)
    @pl.when(j==0)
    def _(): left_ref[...]=x_ref[...].T
    @pl.when(j==split)
    def _(): left_ref[...]=y_ref[...].T
    @pl.when(j<split)
    def _(): out_ref[...]=dot(left_ref[...],pair_ref[...],1,0).astype(bf16)
    @pl.when(j>=split)
    def _(): out_ref[...]=dot(left_ref[...],act_ref[...],1,0).astype(bf16)

def weights(x,y,pair,act,chunk=256):
    rows=x.shape[0]; width=pair.shape[1]+act.shape[1]; split=pair.shape[1]//chunk
    one=pl.BlockSpec((rows,D),lambda j:(0,0),pipeline_mode=pl.Buffered(1))
    return pl.pallas_call(
        functools.partial(weights_kernel,split=split), grid=(width//chunk,),
        in_specs=[one,one,pl.BlockSpec((rows,chunk),lambda j:(0,jnp.minimum(j,split-1))),pl.BlockSpec((rows,chunk),lambda j:(0,jnp.maximum(j-split,0)))],
        out_specs=pl.BlockSpec((D,chunk),lambda j:(0,j)), out_shape=jax.ShapeDtypeStruct((D,width),bf16),
        scratch_shapes=[pltpu.VMEM((D,rows),bf16)],
        compiler_params=pltpu.CompilerParams(vmem_limit_bytes=LIMIT), cost_estimate=COST,
        name="weights",
    )(x,y,pair,act)


LONGEST = 512


def after(values_in, *needed):
    return lax.optimization_barrier((values_in, needed))[0]


theta = 10000.0


def body(
    layer_in,
    doc_ids,
    cotangent,
    first_gain,
    query_weight,
    query_bias,
    key_weight,
    key_bias,
    value_weight,
    value_bias,
    out_weight,
    second_gain,
    gate_weight,
    up_weight,
    down_weight,
):
    parts = lax.axis_size("ctx")
    rank = lax.axis_index("ctx")
    micros = layer_in.shape[1]
    shard_rows = layer_in.shape[3]
    hidden = gate_weight.shape[1]
    hidden_pad = -(-hidden // (2 * LANES)) * 2 * LANES
    weight_rows = query_weight.shape[0]
    bias_rows = key_bias.shape[0]
    reach_parts = -(-LONGEST // shard_rows)

    def around(values_in, steps):
        return lax.ppermute(values_in, "ctx", [(s, (s + steps) % parts) for s in range(parts)])

    def pieces_of(values_in):
        return [values_in] + [around(values_in, d) for d in range(1, parts)]

    def collected(values_in):
        pieces = pieces_of(values_in)
        ordered = [pieces[d] for d in range(parts - 1, -1, -1)]
        ordered = jnp.stack(ordered + ordered[:-1])
        taken = lax.dynamic_slice_in_dim(ordered, parts - 1 - rank, parts, 0)
        return taken.reshape((-1,) + values_in.shape[1:])

    def ahead(values_in):
        return lax.ppermute(values_in, "ctx", [(s, s + 1) for s in range(parts - 1)])

    def behind(values_in):
        return lax.ppermute(values_in, "ctx", [(s + 1, s) for s in range(parts - 1)])

    def column(values_in):
        return jnp.pad(values_in, (0, weight_rows - values_in.shape[0]))[:, None]

    def wide(values_in):
        return jnp.pad(values_in, ((0, 0), (0, hidden_pad - hidden)))

    small = jnp.concatenate(
        [column(v) for v in (first_gain, second_gain, query_bias, key_bias, value_bias)], axis=1
    )
    small = jnp.pad(small, ((0, 0), (0, LANES - small.shape[1])))
    own_attention = jnp.concatenate(
        [out_weight, query_weight, key_weight, value_weight, small], axis=1
    )
    first_set = lax.all_gather(collected(own_attention), "dp", axis=0, tiled=True)
    rest_block = jnp.concatenate([wide(gate_weight), wide(up_weight), wide(down_weight.T)], axis=1)
    rest_block = lax.optimization_barrier((rest_block, first_set[0, 0]))[0]
    rest_set = lax.all_gather(rest_block, "dp", axis=0, tiled=True)

    row = jnp.arange(D, dtype=jnp.int32)[:, None]
    place = row // weight_rows * bias_rows + row % weight_rows
    spread = (
        (place == jnp.arange(LANES, dtype=jnp.int32)[None, :]) & (row % weight_rows < bias_rows)
    ).astype(bf16)

    docs = doc_ids[0, :, 0]
    own_docs = lax.dynamic_slice_in_dim(docs, rank * shard_rows, shard_rows, 1)
    begins = jnp.sum((docs[:, None, :] < own_docs[:, :, None]).astype(jnp.int32), axis=2)
    row_index = rank * shard_rows + jnp.arange(shard_rows, dtype=jnp.int32)
    positions = row_index[None, :] - begins
    frequency = jnp.power(f32(theta), -(jnp.arange(HEAD // 2, dtype=f32) * (2.0 / HEAD)))
    angle = positions.astype(f32)[:, :, None] * frequency
    cosines, sines = jnp.cos(angle), jnp.sin(angle)
    cosines = jnp.concatenate([cosines] * (2 * LANES // HEAD), axis=2)
    sines = jnp.concatenate([-sines, sines] * (LANES // HEAD), axis=2)
    base = (rank * shard_rows).reshape(1)

    tokens = layer_in[0, :, 0]
    upstream = cotangent[0, :, 0]
    chains = [[upstream[m]] for m in range(micros)]
    moving = [(upstream[m], upstream[m]) for m in range(micros)]

    def next_round(m):
        moving[m] = (ahead(moving[m][0]), behind(moving[m][1]))
        chains[m] += list(moving[m])

    for m in range(micros):
        next_round(m)
    next_round(0)
    first_set = after(first_set, moving)
    for m in range(1, micros):
        next_round(m)

    rot_query, pairs, normed_one, rows_table = project(tokens, first_set, spread, cosines, sines)
    pairs = after(pairs, moving)
    kvs = [pairs] + [
        lax.ppermute(pairs, "ctx", [(s, s + d) for s in range(parts - d)])
        for d in range(1, reach_parts + 1)
    ]
    moving = after(moving, kvs[1:])
    while len(chains[0]) < 2 * parts - 1:
        for m in range(micros):
            next_round(m)

    begins = begins[:, None, :]
    exchanged = []
    held = ()
    for m in range(micros):
        if m == 1:
            kvs = after(kvs, moving)
        normed_two, *held = attend(
            m, base, rot_query, kvs, begins, first_set, tokens, rows_table, held
        )
        exchanged.append(Tokens("around", pieces_of(normed_two)))
    mixed, middle, log_sums = held

    backs = []
    before = ()
    rank_one = rank.reshape(1)
    for m in range(micros):
        back, before = feed(
            rank_one, exchanged[m], Tokens("chain", chains[m]), rest_set, hidden_pad, m, micros,
            parts, shard_rows, before,
        )
        backs.append([back[0]] + [around(back[d], parts - d) for d in range(1, parts)])
    partials = before[:parts]

    feed_local = weights(*before[parts:])
    backs[0] = after(backs[0], feed_local)
    far = []
    ended = ()
    arrived = {}
    for m in range(micros):
        if m == micros - 1:
            backs[m], feed_local, ended, far = after((backs[m], feed_local, ended, far))
            arrived[1] = around(after(partials[1], backs[m]), parts - 1)
        far1, far2, *ended = attend_back(
            m, base, rot_query, kvs, begins, first_set, rows_table, log_sums, middle, upstream,
            backs[m], cosines, sines, ended,
        )
        if m == micros - 1:
            far1, far2, arrived[1] = after((far1, far2, arrived[1]))
        far.append(
            [
                lax.ppermute(part, "ctx", [(s, s - d) for s in range(d, parts)])
                for d, part in ((1, far1), (2, far2))
            ]
        )
    feed_sum = lax.psum_scatter(feed_local, "dp", scatter_dimension=0, tiled=True).astype(f32)

    group_rank = lax.axis_index("dp")
    groups = lax.axis_size("dp")
    bits = [1 << k for k in range(groups.bit_length() - 1)]
    block_rows = parts * weight_rows
    even = block_rows % 16 == 0
    grad_middle, branch_low, query_grad, own_pair, gain_sum = ended
    input_grad, keep, send = finish(
        (group_rank % 2).reshape(1), query_grad, own_pair, far, cosines, sines, first_set,
        rows_table, tokens, normed_one, grad_middle, mixed, branch_low, spread, gain_sum,
        block_rows if even else 0,
    )
    if not even:
        both = jnp.concatenate([keep, send]).reshape(groups // 2, 2, block_rows, -1)
        keep, send = (
            lax.dynamic_index_in_dim(both, v, 1, keepdims=False)
            for v in (group_rank % 2, 1 - group_rank % 2)
        )

    arrived[3] = around(after(partials[3], far), parts - 3)

    def swapped(values_in, bit):
        return lax.ppermute(values_in, "dp", [(s, s ^ bit) for s in range(groups)])

    def halved(blocks, order):
        for k, bit in enumerate(order):
            size = blocks.shape[0]
            at = sorted(order[k:]).index(bit)
            view = blocks.reshape((size >> (at + 1), 2, 1 << at) + blocks.shape[1:])
            own = (group_rank // bit) % 2
            kept = lax.dynamic_index_in_dim(view, own, 1, keepdims=False)
            sent = lax.dynamic_index_in_dim(view, 1 - own, 1, keepdims=False)
            got = swapped(sent.astype(bf16), bit)
            blocks = (kept.astype(f32) + got.astype(f32)).reshape((size // 2,) + blocks.shape[1:])
        return blocks

    blocks = keep.astype(f32) + swapped(send, 1).astype(f32)
    blocks, arrived[3] = after((blocks, arrived[3]))
    arrived[2] = around(after(partials[2], blocks), parts - 2)
    blocks = blocks.reshape(groups // 2, block_rows, -1)
    cut = QW + 2 * LANES
    attention_block = jnp.concatenate(
        [halved(blocks[:, :, :cut], bits[1:])[0], halved(blocks[:, :, cut:], bits[:0:-1])[0]], axis=1
    ).astype(bf16)
    attention_block, arrived[2] = after((attention_block, arrived[2]))
    attention_block = attention_block.reshape(parts, weight_rows, -1)

    def block_for(steps):
        return lax.dynamic_index_in_dim(
            attention_block, (rank + steps) % parts, 0, keepdims=False
        )

    sums = block_for(0).astype(f32)
    for d in range(1, parts):
        sums = sums + around(block_for(d), d).astype(f32)

    total = middle + partials[0]
    for d in range(1, parts):
        total = total + arrived[d].astype(f32)

    edge = 2 * QW + 2 * KW
    return (
        total.astype(bf16)[None, :, None],
        input_grad[None, :, None],
        sums[:, edge],
        sums[:, QW : 2 * QW],
        sums[:, edge + 2],
        sums[:, 2 * QW : 2 * QW + KW],
        sums[:bias_rows, edge + 3],
        sums[:, 2 * QW + KW : edge],
        sums[:bias_rows, edge + 4],
        sums[:, :QW],
        sums[:, edge + 1],
        feed_sum[:, :hidden],
        feed_sum[:, hidden_pad : hidden_pad + hidden],
        feed_sum[:, 2 * hidden_pad : 2 * hidden_pad + hidden].T,
    )


def solution(mesh):
    both = ("dp", "ctx")
    rows = P(both, None)
    line = P(both)
    tokens = P("dp", None, None, "ctx", None)
    return jax.shard_map(
        body,
        mesh=mesh,
        in_specs=(
            tokens, P("dp", None, None, None), tokens, line, rows, line, rows, line, rows, line,
            rows, line, P("dp", "ctx"), P("dp", "ctx"), P("ctx", "dp"),
        ),
        out_specs=(
            tokens, tokens, line, rows, line, rows, line, rows, line, rows, line,
            P("dp", "ctx"), P("dp", "ctx"), P("ctx", "dp"),
        ),
        check_vma=False,
    )
```

time: 631 us -> 461 us (0.73)
  matrix products: 164 us -> 0 us
  Pallas kernels: 0 us -> 140 us
  starting transfers between devices: 183 us -> 107 us
  other arithmetic: 43.8 us -> 15.5 us
  local copies, waits for them, and re-layouts: 45 us -> 20.6 us
  waiting for transfers between devices: 172 us -> 154 us
    dot_general x35 -> x0, matrix products: 151 us -> none  [the longest x25 120 us: dot(): lax.dot_general(left, right, (((left_dim,), (right_dim,)), ((), ())), pre...]
    pallas_call x0 -> x9, Pallas kernels: none -> 140 us  [the longest x2 52.1 us: feed(): pl.pallas_call(functools.partial(feed_kernel, parts=parts, kept=kept, tok...]
    ppermute x30 -> x21, starting transfers between devices: 165 us -> 54.5 us  [around(): lax.ppermute(values_in, 'ctx', [(s, (s + steps) % parts) for s in range(p...]
    reduce_scatter x1, waiting for transfers between devices: 50.6 us -> 0.01 us  [body(): lax.psum_scatter(feed_local, 'dp', scatter_dimension=0, tiled=True)]
    ppermute x8 -> x23, waiting for transfers between devices: 14.3 us -> 57.9 us  [the longest x6 18 us: behind(): lax.ppermute(values_in, 'ctx', [(s + 1, s) for s in range(parts - 1)])]
    ppermute x8 -> x23, starting transfers between devices: 17.9 us -> 52.7 us  [the longest x6 29.5 us: ahead(): lax.ppermute(values_in, 'ctx', [(s, s + 1) for s in range(parts - 1)])]
    ppermute x30 -> x21, waiting for transfers between devices: 75 us -> 96.3 us  [around(): lax.ppermute(values_in, 'ctx', [(s, (s + steps) % parts) for s in range(p...]
    all_gather x1, waiting for transfers between devices: 20.4 us -> 0.01 us  [body(): lax.all_gather(collected(own_attention), 'dp', axis=0, tiled=True)]
  transfers between devices with their start and end apart: 42 -> 47, of which waited for: 18 -> 27; matrix products, arithmetic and copies ran while one was open for 29% -> 5% of each run, Pallas kernels for 0% -> 31%
where the time goes in v2:
time: 461 us; the launch traced here: 452 us
  waiting for transfers between devices  154 us (33%)
  Pallas kernels  140 us (30%)
  starting transfers between devices  107 us (23%)
  local copies, waits for them, and re-layouts  20.6 us (4%)
  other arithmetic  15.5 us (3%)
  between operations  15 us (3%)
    ppermute x21, waiting for transfers between devices, around(): lax.ppermute(values_in, 'ctx', [(s, (s + steps) % parts) for s in range(p...  96.3 us
    ppermute x21, starting transfers between devices, around(): lax.ppermute(values_in, 'ctx', [(s, (s + steps) % parts) for s in range(p...  54.5 us
    pallas_call x2, Pallas kernels, feed(): pl.pallas_call(functools.partial(feed_kernel, parts=parts, kept=kept, tok...  52.1 us
    ppermute x6, starting transfers between devices, ahead(): lax.ppermute(values_in, 'ctx', [(s, s + 1) for s in range(parts - 1)])  29.5 us
    pallas_call x2, Pallas kernels, attend_back(): pl.pallas_call(functools.partial(attend_back_kernel, count=len(gs)), grid...  26.4 us
    pallas_call x1, Pallas kernels, weights(): pl.pallas_call(functools.partial(weights_kernel, split=split), grid=(widt...  25.6 us
    pallas_call x2, Pallas kernels, attend(): pl.pallas_call(attend_kernel, grid=(nq,), in_specs=[pl.BlockSpec(memory_s...  18.7 us
    ppermute x6, waiting for transfers between devices, behind(): lax.ppermute(values_in, 'ctx', [(s + 1, s) for s in range(parts - 1)])  18 us
  transfers between devices with their start and end apart: 47, of which 27 were waited for; matrix products, arithmetic and copies ran while one was open for 5% of the time, Pallas kernels for 31%

profile of v2, /device:TPU:0, one launch (start us, length us, event | category | flops | bytes accessed | tf_op | source)
XLA Modules:
  0.0 452.3 jit_solution(7078465598230577898)
XLA Ops:
  11.8 5.1 %collective-permute-start = (bf16[28,2176]{1,0:T(8,128)(2,1)S(1)}, bf16[28,2176]{1,0:T(8,128)(2,1)S(1)}, u32[]{:S(2)}, u32[]{:S(2)}) collective-permute-start(bf16[28,2176]{1,0:T(8,128)(2,1)S(1)} %constant_dynamic-update-slice_fusion), channel_id=1, source_target_pairs={{0,3},{1,0},{2,1},{3,2},{4,7},{5,4},{6,5},{7,6},{8,11},{9,8},{10,9... | collective-permute-start | bytes 365576 | tf_op jit(solution)/shard_map/ppermute | solution.py:428
  17.9 3.1 collective-permute-done
  21.0 7.7 %collective-permute-done.1 = bf16[28,2176]{1,0:T(8,128)(2,1)S(1)} collective-permute-done((bf16[28,2176]{1,0:T(8,128)(2,1)S(1)}, bf16[28,2176]{1,0:T(8,128)(2,1)S(1)}, u32[]{:S(2)}, u32[]{:S(2)}) %collective-permute-start.1) | collective-permute-done | bytes 121888 | tf_op jit(solution)/shard_map/ppermute | solution.py:428
  31.1 2.7 collective-permute-start.3
  33.9 1.3 collective-permute-start.5
  35.2 5.0 %collective-permute-start.7 = (bf16[256,896]{1,0:T(8,128)(2,1)S(1)}, bf16[256,896]{1,0:T(8,128)(2,1)S(1)}, u32[]{:S(2)}, u32[]{:S(2)}) collective-permute-start(bf16[256,896]{1,0:T(8,128)(2,1)S(1)} %get-tuple-element.251.refs_4_), channel_id=1, source_target_pairs={{0,1},{1,2},{2,3},{4,5},{5,6},{6,7},{8,9},{9,10},{10,11},{12,13},{... | collective-permute-start | bytes 1376264 | tf_op jit(solution)/shard_map/ppermute | solution.py:441
  40.2 1.3 collective-permute-start.8
  43.0 1.8 collective-permute-done.3.refs_5_
  44.8 4.4 collective-permute-start.4
  51.0 8.4 %collective-permute-done.8.refs_6_ = bf16[256,896]{1,0:T(8,128)(2,1)S(1)} collective-permute-done((bf16[256,896]{1,0:T(8,128)(2,1)S(1)}, bf16[256,896]{1,0:T(8,128)(2,1)S(1)}, u32[]{:S(2)}, u32[]{:S(2)}) %collective-permute-start.8) | collective-permute-done | bytes 458784 | tf_op jit(solution)/shard_map/ppermute | solution.py:444
  60.8 4.6 %collective-permute-start.9 = (bf16[256,896]{1,0:T(8,128)(2,1)S(1)}, bf16[256,896]{1,0:T(8,128)(2,1)S(1)}, u32[]{:S(2)}, u32[]{:S(2)}) collective-permute-start(bf16[256,896]{1,0:T(8,128)(2,1)S(1)} %collective-permute-done.7.refs_5_), channel_id=1, source_target_pairs={{0,1},{1,2},{2,3},{4,5},{5,6},{6,7},{8,9},{9,10},{10,11},{12,13},{... | collective-permute-start | bytes 1376264 | tf_op jit(solution)/shard_map/ppermute | solution.py:441
  69.4 5.6 %project.1 = (bf16[2,256,896]{2,1,0:T(8,128)(2,1)}, bf16[2,256,256]{2,1,0:T(8,128)(2,1)}, bf16[2,256,896]{2,1,0:T(8,128)(2,1)}, f32[8,896]{1,0:T(8,128)}) custom-call(bf16[2,256,896]{2,1,0:T(8,128)(2,1)} %bitcast.69, bf16[896,2176]{1,0:T(8,128)(2,1)} %all-gather.3.cloned.1.call-done.wq_ref.wkv_ref.ws_ref.wo_ref, ...), custom_call_target="tpu_custom_call" | custom-call | flops 1 | bytes 1 | tf_op jit(solution)/shard_map/project/pallas_call | solution.py:54
  75.0 2.3 collective-permute-done.10.refs_8_
  77.3 3.6 collective-permute-start.11
  81.0 1.6 collective-permute-start.12
  82.7 5.2 %collective-permute-done.11.kv1_ref = bf16[2,256,256]{2,1,0:T(8,128)(2,1)S(1)} collective-permute-done((bf16[2,256,256]{2,1,0:T(8,128)(2,1)}, bf16[2,256,256]{2,1,0:T(8,128)(2,1)S(1)}, u32[]{:S(2)}, u32[]{:S(2)}) %collective-permute-start.11) | collective-permute-done | bytes 262176 | tf_op jit(solution)/shard_map/ppermute | solution.py:501
  87.9 2.8 collective-permute-done.12.kv2_ref
  90.7 8.3 %collective-permute-start.13 = (bf16[256,896]{1,0:T(8,128)(2,1)S(1)}, bf16[256,896]{1,0:T(8,128)(2,1)S(1)}, u32[]{:S(2)}, u32[]{:S(2)}) collective-permute-start(bf16[256,896]{1,0:T(8,128)(2,1)S(1)} %copy-done.24), channel_id=1, source_target_pairs={{0,1},{1,2},{2,3},{4,5},{5,6},{6,7},{8,9},{9,10},{10,11},{12,13},{... | collective-permute-start | bytes 1376264 | tf_op jit(solution)/shard_map/ppermute | solution.py:441
  98.9 1.3 collective-permute-start.14
  100.2 4.6 %collective-permute-start.15 = (bf16[256,896]{1,0:T(8,128)(2,1)S(1)}, bf16[256,896]{1,0:T(8,128)(2,1)S(1)}, u32[]{:S(2)}, u32[]{:S(2)}) collective-permute-start(bf16[256,896]{1,0:T(8,128)(2,1)S(1)} %collective-permute-done.9.refs_7_), channel_id=1, source_target_pairs={{0,1},{1,2},{2,3},{4,5},{5,6},{6,7},{8,9},{9,10},{10,11},{12,13},{... | collective-permute-start | bytes 1376264 | tf_op jit(solution)/shard_map/ppermute | solution.py:441
  104.8 1.3 collective-permute-start.16
  106.7 9.3 %attend.2 = (bf16[256,896]{1,0:T(8,128)(2,1)}, bf16[2,256,896]{2,1,0:T(8,128)(2,1)}, f32[2,256,896]{2,1,0:T(8,128)}, f32[2,2,16,128]{3,2,1,0:T(8,128)}) custom-call(s32[1]{0:T(128)} %bitcast.base_ref, bf16[2,256,896]{2,1,0:T(8,128)(2,1)} %get-tuple-element.103.rq_ref, bf16[2,256,256]{2,1,0:T(8,128)(2,1)} %get-tuple-element.110.kv0_ref, ...), custom_call_target="tpu_custom_call" | custom-call | flops 1 | bytes 1 | tf_op jit(solution)/shard_map/attend/pallas_call | solution.py:135
  116.0 2.8 collective-permute-start.20
  118.7 3.2 collective-permute-start.21
  123.0 5.8 %collective-permute-done.16.refs_10_ = bf16[256,896]{1,0:T(8,128)(2,1)S(1)} collective-permute-done((bf16[256,896]{1,0:T(8,128)(2,1)S(1)}, bf16[256,896]{1,0:T(8,128)(2,1)S(1)}, u32[]{:S(2)}, u32[]{:S(2)}) %collective-permute-start.16) | collective-permute-done | bytes 458784 | tf_op jit(solution)/shard_map/ppermute | solution.py:444
  128.9 9.4 %attend.3 = (bf16[256,896]{1,0:T(8,128)(2,1)}, bf16[2,256,896]{2,1,0:T(8,128)(2,1)}, f32[2,256,896]{2,1,0:T(8,128)}, f32[2,2,16,128]{3,2,1,0:T(8,128)}) custom-call(s32[1]{0:T(128)} %bitcast.base_ref, bf16[2,256,896]{2,1,0:T(8,128)(2,1)} %get-tuple-element.103.rq_ref, ...), custom_call_target="tpu_custom_call", output_to_operand_aliasing={{1}: (9, {}), {2}: (10, {}), {3}: (11, {})} | custom-call | flops 1 | bytes 1 | tf_op jit(solution)/shard_map/attend/pallas_call | solution.py:135
  138.4 13.4 %collective-permute-start.17 = (bf16[256,896]{1,0:T(8,128)(2,1)}, bf16[256,896]{1,0:T(8,128)(2,1)S(1)}, u32[]{:S(2)}, u32[]{:S(2)}) collective-permute-start(bf16[256,896]{1,0:T(8,128)(2,1)} %get-tuple-element.118.refs_0_), channel_id=1, source_target_pairs={{0,1},{1,2},{2,3},{3,0},{4,5},{5,6},{6,7},{7,4},{8,9},{9,10},{10,1... | collective-permute-start | bytes 1376264 | tf_op jit(solution)/shard_map/ppermute | solution.py:428
  151.8 2.4 collective-permute-start.19
  154.2 17.1 %collective-permute-done.21.refs_2_ = bf16[256,896]{1,0:T(8,128)(2,1)} collective-permute-done((bf16[256,896]{1,0:T(8,128)(2,1)}, bf16[256,896]{1,0:T(8,128)(2,1)}, u32[]{:S(2)}, u32[]{:S(2)}) %collective-permute-start.21) | collective-permute-done | bytes 458784 | tf_op jit(solution)/shard_map/ppermute | solution.py:428
  171.3 26.1 %feed.2 = (f32[256,896]{1,0:T(8,128)}, bf16[256,896]{1,0:T(8,128)(2,1)}, bf16[256,896]{1,0:T(8,128)(2,1)}, bf16[256,896]{1,0:T(8,128)(2,1)}, f32[2,256,896]{2,1,...) custom-call(s32[1]{0:T(128)} %bitcast.13.rank_ref, ...), custom_call_target="tpu_custom_call" | custom-call | flops 1 | bytes 1 | tf_op jit(solution)/shard_map/feed/pallas_call | solution.py:288
  197.4 12.5 %collective-permute-start.26 = (bf16[256,896]{1,0:T(8,128)(2,1)}, bf16[256,896]{1,0:T(8,128)(2,1)S(1)}, u32[]{:S(2)}, u32[]{:S(2)}) collective-permute-start(bf16[256,896]{1,0:T(8,128)(2,1)} %get-tuple-element.139), channel_id=1, source_target_pairs={{0,3},{1,0},{2,1},{3,2},{4,7},{5,4},{6,5},{7,6},{8,11},{9,8},{10,9... | collective-permute-start | bytes 1376264 | tf_op jit(solution)/shard_map/ppermute | solution.py:428
  209.9 1.9 collective-permute-start.27
  212.9 26.1 %feed.3 = (f32[256,896]{1,0:T(8,128)}, bf16[256,896]{1,0:T(8,128)(2,1)}, bf16[256,896]{1,0:T(8,128)(2,1)}, bf16[256,896]{1,0:T(8,128)(2,1)}, f32[2,256,896]{2,1,...) custom-call(s32[1]{0:T(128)} %bitcast.13.rank_ref, ...), custom_call_target="tpu_custom_call", output_to_operand_aliasing={{4}: (15, {}), {5}: (16, {}), {6}: (17, {}), {7}: (18, {}),... | custom-call | flops 1 | bytes 1 | tf_op jit(solution)/shard_map/feed/pallas_call | solution.py:288
  239.0 3.7 collective-permute-start.23
  243.5 25.6 %weights.1 = bf16[896,3840]{1,0:T(8,128)(2,1)} custom-call(bf16[2048,896]{1,0:T(8,128)(2,1)} %get-tuple-element.134.x_ref, bf16[2048,896]{1,0:T(8,128)(2,1)} %get-tuple-element.135.y_ref, bf16[2048,2560]{1,0:T(8,128)(2,1)} %get-tuple-element.136.pair_ref, bf16[2048,1280]{1,0:T(8,128)(2,1)} %get-tuple-element.137.act_ref), custom_call_target="tpu_custom_call" | custom-call | flops 1 | bytes 1 | tf_op jit(solution)/shard_map/weights/pallas_call | solution.py:380
  269.1 1.5 collective-permute-done.27.refs_2_
  271.4 13.2 %attend_back.2 = (bf16[256,256]{1,0:T(8,128)(2,1)}, bf16[256,256]{1,0:T(8,128)(2,1)}, f32[2,256,896]{2,1,0:T(8,128)}, bf16[2,256,896]{2,1,0:T(8,128)(2,1)}, bf16...) custom-call(s32[1]{0:T(128)} %bitcast.base_ref, ...), custom_call_target="tpu_custom_call" | custom-call | flops 1 | bytes 1 | tf_op jit(solution)/shard_map/attend_back/pallas_call | solution.py:216
  284.6 1.3 collective-permute-start.29
  285.9 1.3 collective-permute-start.30
  287.2 2.8 collective-permute-done.24.refs_2_
  290.0 1.7 collective-permute-done.29.refs_0_
  291.7 4.9 %collective-permute-done.30.refs_1_ = bf16[256,256]{1,0:T(8,128)(2,1)S(1)} collective-permute-done((bf16[256,256]{1,0:T(8,128)(2,1)}, bf16[256,256]{1,0:T(8,128)(2,1)S(1)}, u32[]{:S(2)}, u32[]{:S(2)}) %collective-permute-start.30) | collective-permute-done | bytes 131104 | tf_op jit(solution)/shard_map/ppermute | solution.py:549
  298.5 13.2 %attend_back.3 = (bf16[256,256]{1,0:T(8,128)(2,1)}, bf16[256,256]{1,0:T(8,128)(2,1)}, f32[2,256,896]{2,1,0:T(8,128)}, bf16[2,256,896]{2,1,0:T(8,128)(2,1)}, bf16...) custom-call(s32[1]{0:T(128)} %bitcast.base_ref, ...), custom_call_target="tpu_custom_call", output_to_operand_aliasing={{2}: (17, {}), {3}: (18, {}), {4}: (19, {}), {5}: (20, {}),... | custom-call | flops 1 | bytes 1 | tf_op jit(solution)/shard_map/attend_back/pallas_call | solution.py:216
  311.7 4.7 %collective-permute-done.31 = bf16[2,256,896]{2,1,0:T(8,128)(2,1)} collective-permute-done((bf16[2,256,896]{2,1,0:T(8,128)(2,1)S(1)}, bf16[2,256,896]{2,1,0:T(8,128)(2,1)}, u32[]{:S(2)}, u32[]{:S(2)}) %collective-permute-start.31) | collective-permute-done | bytes 917536 | tf_op jit(solution)/shard_map/ppermute | solution.py:428
  319.0 5.2 %collective-permute-done.32.refs_2_ = bf16[256,256]{1,0:T(8,128)(2,1)S(1)} collective-permute-done((bf16[256,256]{1,0:T(8,128)(2,1)}, bf16[256,256]{1,0:T(8,128)(2,1)S(1)}, u32[]{:S(2)}, u32[]{:S(2)}) %collective-permute-start.32) | collective-permute-done | bytes 131104 | tf_op jit(solution)/shard_map/ppermute | solution.py:549
  324.3 2.9 collective-permute-done.33.refs_3_
  327.8 11.4 %finish.1 = (f32[2,256,896]{2,1,0:T(8,128)}, bf16[448,2176]{1,0:T(8,128)(2,1)}, bf16[448,2176]{1,0:T(8,128)(2,1)}) custom-call(s32[1]{0:T(128)} %bitcast.16.bit_ref, bf16[2,256,896]{2,1,0:T(8,128)(2,1)} %get-tuple-element.167.dq_ref, f32[2,256,256]{2,1,0:T(8,128)} %get-tuple-element.168.own_ref, f32[2,256,128]{2,1,0:T(8,128)} %get-tuple-element.267.cos_ref, ...), custom_call_target="tpu_custom_call" | custom-call | flops 1 | bytes 1 | tf_op jit(solution)/shard_map/finish/pallas_call | solution.py:356
  339.3 2.0 collective-permute-start.35
  341.2 2.1 collective-permute-done.34
  343.4 1.9 convert_add_fusion
  345.3 18.5 %collective-permute-done.35 = bf16[2,256,896]{2,1,0:T(8,128)(2,1)S(1)} collective-permute-done((bf16[2,256,896]{2,1,0:T(8,128)(2,1)S(1)}, bf16[2,256,896]{2,1,0:T(8,128)(2,1)S(1)}, u32[]{:S(2)}, u32[]{:S(2)}) %collective-permute-start.35) | collective-permute-done | bytes 917536 | tf_op jit(solution)/shard_map/ppermute | solution.py:428
  366.1 1.5 collective-permute-start.38
  367.6 1.7 slice.71
  369.4 1.5 collective-permute-start.36
  370.9 7.3 %collective-permute-done.38 = bf16[1,2,112,1024]{3,2,1,0:T(8,128)(2,1)S(1)} collective-permute-done((bf16[1,2,112,1024]{3,2,1,0:T(8,128)(2,1)S(1)}, bf16[1,2,112,1024]{3,2,1,0:T(8,128)(2,1)S(1)}, u32[]{:S(2)}, u32[]{:S(2)}) %collective-permute-start.38) | collective-permute-done | bytes 458784 | tf_op jit(solution)/shard_map/ppermute | solution.py:576
  378.2 1.3 bitcast_add_fusion.1
  380.4 1.4 collective-permute-start.39
  384.6 2.9 collective-permute-done.39
  388.7 1.8 collective-permute-done.37
  390.6 35.0 %collective-permute-done.40 = bf16[2,256,896]{2,1,0:T(8,128)(2,1)} collective-permute-done((bf16[2,256,896]{2,1,0:T(8,128)(2,1)}, bf16[2,256,896]{2,1,0:T(8,128)(2,1)}, u32[]{:S(2)}, u32[]{:S(2)}) %collective-permute-start.40) | collective-permute-done | bytes 917536 | tf_op jit(solution)/shard_map/ppermute | solution.py:428
  426.6 3.0 collective-permute-start.43
  429.6 3.7 fusion.4
  434.2 5.0 %collective-permute-done.42 = bf16[28,2176]{1,0:T(8,128)(2,1)S(1)} collective-permute-done((bf16[28,2176]{1,0:T(8,128)(2,1)S(1)}, bf16[28,2176]{1,0:T(8,128)(2,1)S(1)}, u32[]{:S(2)}, u32[]{:S(2)}) %collective-permute-start.42) | collective-permute-done | bytes 121888 | tf_op jit(solution)/shard_map/ppermute | solution.py:428
  442.1 1.3 convert_element_type.135
  (177 shorter events, 39.9 us)
Async XLA Ops:
  7.2 62.2 %all-gather.3.cloned.1.call-start = ((), (), s32[]{:S(2)}) async-start(), calls=%async_computation.1 | async-start | bytes 4386816 | tf_op jit(solution)/shard_map/all_gather | solution.py:459
  11.8 9.2 %collective-permute-start = (bf16[28,2176]{1,0:T(8,128)(2,1)S(1)}, bf16[28,2176]{1,0:T(8,128)(2,1)S(1)}, u32[]{:S(2)}, u32[]{:S(2)}) collective-permute-start(bf16[28,2176]{1,0:T(8,128)(2,1)S(1)} %constant_dynamic-update-slice_fusion), channel_id=1, source_target_pairs={{0,3},{1,0},{2,1},{3,2},{4,7},{5,4},{6,5},{7,6},{8,11},{9,8},{10,9... | collective-permute-start | bytes 365576 | tf_op jit(solution)/shard_map/ppermute | solution.py:428
  16.9 11.8 %collective-permute-start.1 = (bf16[28,2176]{1,0:T(8,128)(2,1)S(1)}, bf16[28,2176]{1,0:T(8,128)(2,1)S(1)}, u32[]{:S(2)}, u32[]{:S(2)}) collective-permute-start(bf16[28,2176]{1,0:T(8,128)(2,1)S(1)} %constant_dynamic-update-slice_fusion), channel_id=1, source_target_pairs={{0,2},{1,3},{2,0},{3,1},{4,6},{5,7},{6,4},{7,5},{8,10},{9,11},{10,... | collective-permute-start | bytes 365576 | tf_op jit(solution)/shard_map/ppermute | solution.py:428
  16.9 11.8 %collective-permute-start.2 = (bf16[28,2176]{1,0:T(8,128)(2,1)S(1)}, bf16[28,2176]{1,0:T(8,128)(2,1)S(1)}, u32[]{:S(2)}, u32[]{:S(2)}) collective-permute-start(bf16[28,2176]{1,0:T(8,128)(2,1)S(1)} %constant_dynamic-update-slice_fusion), channel_id=1, source_target_pairs={{0,1},{1,2},{2,3},{3,0},{4,5},{5,6},{6,7},{7,4},{8,9},{9,10},{10,1... | collective-permute-start | bytes 365576 | tf_op jit(solution)/shard_map/ppermute | solution.py:428
  29.9 141.5 %all-gather.5.cloned.1.call-start = ((), (), s32[]{:S(2)}) async-start(), calls=%async_computation.2 | async-start | bytes 7741440 | tf_op jit(solution)/shard_map/all_gather | solution.py:462
  30.0 11.5 %copy-start.39 = (s32[1,2,1,1024]{3,2,1,0:T(1,128)S(1)}, s32[1,2,1,1024]{3,2,1,0:T(1,128)}, u32[]{:S(2)}) copy-start(s32[1,2,1,1024]{3,2,1,0:T(1,128)} %param.16) | copy-start | bytes 24580
  31.0 411.1 %reduce-scatter.2.cloned.1.call-start = ((), (), s32[]{:S(2)}) async-start(), calls=%async_computation.3 | async-start | bytes 7741440 | tf_op jit(solution)/shard_map/reduce_scatter | solution.py:553
  31.1 43.9 %copy-start.8 = (bf16[256,896]{1,0:T(8,128)(2,1)}, bf16[256,896]{1,0:T(8,128)(2,1)S(1)}, u32[]{:S(2)}) copy-start(bf16[256,896]{1,0:T(8,128)(2,1)S(1)} %get-tuple-element.251.refs_4_) | copy-start | bytes 1376260
  31.1 43.9 %copy-start.9 = (bf16[256,896]{1,0:T(8,128)(2,1)}, bf16[256,896]{1,0:T(8,128)(2,1)S(1)}, u32[]{:S(2)}) copy-start(bf16[256,896]{1,0:T(8,128)(2,1)S(1)} %get-tuple-element.252.refs_4_) | copy-start | bytes 1376260
  31.1 13.7 %collective-permute-start.3 = (bf16[256,896]{1,0:T(8,128)(2,1)S(1)}, bf16[256,896]{1,0:T(8,128)(2,1)S(1)}, u32[]{:S(2)}, u32[]{:S(2)}) collective-permute-start(bf16[256,896]{1,0:T(8,128)(2,1)S(1)} %get-tuple-element.252.refs_4_), channel_id=1, source_target_pairs={{0,1},{1,2},{2,3},{4,5},{5,6},{6,7},{8,9},{9,10},{10,11},{12,13},{... | collective-permute-start | bytes 1376264 | tf_op jit(solution)/shard_map/ppermute | solution.py:441
  33.9 15.9 %collective-permute-start.5 = (bf16[256,896]{1,0:T(8,128)(2,1)S(1)}, bf16[256,896]{1,0:T(8,128)(2,1)}, u32[]{:S(2)}, u32[]{:S(2)}) collective-permute-start(bf16[256,896]{1,0:T(8,128)(2,1)S(1)} %get-tuple-element.252.refs_4_), channel_id=1, source_target_pairs={{1,0},{2,1},{3,2},{5,4},{6,5},{7,6},{9,8},{10,9},{11,10},{13,12},{... | collective-permute-start | bytes 1376264 | tf_op jit(solution)/shard_map/ppermute | solution.py:444
  35.2 25.6 %collective-permute-start.7 = (bf16[256,896]{1,0:T(8,128)(2,1)S(1)}, bf16[256,896]{1,0:T(8,128)(2,1)S(1)}, u32[]{:S(2)}, u32[]{:S(2)}) collective-permute-start(bf16[256,896]{1,0:T(8,128)(2,1)S(1)} %get-tuple-element.251.refs_4_), channel_id=1, source_target_pairs={{0,1},{1,2},{2,3},{4,5},{5,6},{6,7},{8,9},{9,10},{10,11},{12,13},{... | collective-permute-start | bytes 1376264 | tf_op jit(solution)/shard_map/ppermute | solution.py:441
  40.2 19.3 %collective-permute-start.8 = (bf16[256,896]{1,0:T(8,128)(2,1)S(1)}, bf16[256,896]{1,0:T(8,128)(2,1)S(1)}, u32[]{:S(2)}, u32[]{:S(2)}) collective-permute-start(bf16[256,896]{1,0:T(8,128)(2,1)S(1)} %get-tuple-element.251.refs_4_), channel_id=1, source_target_pairs={{1,0},{2,1},{3,2},{5,4},{6,5},{7,6},{9,8},{10,9},{11,10},{13,12},{... | collective-permute-start | bytes 1376264 | tf_op jit(solution)/shard_map/ppermute | solution.py:444
  44.8 30.2 %copy-start.22 = (bf16[256,896]{1,0:T(8,128)(2,1)}, bf16[256,896]{1,0:T(8,128)(2,1)S(1)}, u32[]{:S(2)}) copy-start(bf16[256,896]{1,0:T(8,128)(2,1)S(1)} %collective-permute-done.3.refs_5_) | copy-start | bytes 1376260
  44.8 22.9 %collective-permute-start.4 = (bf16[256,896]{1,0:T(8,128)(2,1)S(1)}, bf16[256,896]{1,0:T(8,128)(2,1)S(1)}, u32[]{:S(2)}, u32[]{:S(2)}) collective-permute-start(bf16[256,896]{1,0:T(8,128)(2,1)S(1)} %collective-permute-done.3.refs_5_), channel_id=1, source_target_pairs={{0,1},{1,2},{2,3},{4,5},{5,6},{6,7},{8,9},{9,10},{10,11},{12,13},{... | collective-permute-start | bytes 1376264 | tf_op jit(solution)/shard_map/ppermute | solution.py:441
  49.8 19.7 %collective-permute-start.6 = (bf16[256,896]{1,0:T(8,128)(2,1)}, bf16[256,896]{1,0:T(8,128)(2,1)}, u32[]{:S(2)}, u32[]{:S(2)}) collective-permute-start(bf16[256,896]{1,0:T(8,128)(2,1)} %collective-permute-done.5.refs_6_), channel_id=1, source_target_pairs={{1,0},{2,1},{3,2},{5,4},{6,5},{7,6},{9,8},{10,9},{11,10},{13,12},{... | collective-permute-start | bytes 1376264 | tf_op jit(solution)/shard_map/ppermute | solution.py:444
  59.5 15.5 %copy-start.14 = (bf16[256,896]{1,0:T(8,128)(2,1)}, bf16[256,896]{1,0:T(8,128)(2,1)S(1)}, u32[]{:S(2)}) copy-start(bf16[256,896]{1,0:T(8,128)(2,1)S(1)} %collective-permute-done.8.refs_6_) | copy-start | bytes 1376260
  59.5 17.9 %collective-permute-start.10 = (bf16[256,896]{1,0:T(8,128)(2,1)S(1)}, bf16[256,896]{1,0:T(8,128)(2,1)S(1)}, u32[]{:S(2)}, u32[]{:S(2)}) collective-permute-start(bf16[256,896]{1,0:T(8,128)(2,1)S(1)} %collective-permute-done.8.refs_6_), channel_id=1, source_target_pairs={{1,0},{2,1},{3,2},{5,4},{6,5},{7,6},{9,8},{10,9},{11,10},{13,12},{... | collective-permute-start | bytes 1376264 | tf_op jit(solution)/shard_map/ppermute | solution.py:444
  60.8 14.2 %copy-start.13 = (bf16[256,896]{1,0:T(8,128)(2,1)}, bf16[256,896]{1,0:T(8,128)(2,1)S(1)}, u32[]{:S(2)}) copy-start(bf16[256,896]{1,0:T(8,128)(2,1)S(1)} %collective-permute-done.7.refs_5_) | copy-start | bytes 1376260
  60.8 16.6 %collective-permute-start.9 = (bf16[256,896]{1,0:T(8,128)(2,1)S(1)}, bf16[256,896]{1,0:T(8,128)(2,1)S(1)}, u32[]{:S(2)}, u32[]{:S(2)}) collective-permute-start(bf16[256,896]{1,0:T(8,128)(2,1)S(1)} %collective-permute-done.7.refs_5_), channel_id=1, source_target_pairs={{0,1},{1,2},{2,3},{4,5},{5,6},{6,7},{8,9},{9,10},{10,11},{12,13},{... | collective-permute-start | bytes 1376264 | tf_op jit(solution)/shard_map/ppermute | solution.py:441
  69.4 21.3 %copy-start.24 = (bf16[256,896]{1,0:T(8,128)(2,1)S(1)}, bf16[256,896]{1,0:T(8,128)(2,1)}, u32[]{:S(2)}) copy-start(bf16[256,896]{1,0:T(8,128)(2,1)} %copy-done.23) | copy-start | bytes 1376260
  77.3 61.0 %copy-start.15 = (bf16[256,896]{1,0:T(8,128)(2,1)}, bf16[256,896]{1,0:T(8,128)(2,1)S(1)}, u32[]{:S(2)}) copy-start(bf16[256,896]{1,0:T(8,128)(2,1)S(1)} %collective-permute-done.10.refs_8_) | copy-start | bytes 1376260
  77.3 61.0 %copy-start.16 = (bf16[256,896]{1,0:T(8,128)(2,1)}, bf16[256,896]{1,0:T(8,128)(2,1)S(1)}, u32[]{:S(2)}) copy-start(bf16[256,896]{1,0:T(8,128)(2,1)S(1)} %collective-permute-done.9.refs_7_) | copy-start | bytes 1376260
  77.3 10.5 %collective-permute-start.11 = (bf16[2,256,256]{2,1,0:T(8,128)(2,1)}, bf16[2,256,256]{2,1,0:T(8,128)(2,1)S(1)}, u32[]{:S(2)}, u32[]{:S(2)}) collective-permute-start(bf16[2,256,256]{2,1,0:T(8,128)(2,1)} %get-tuple-element.110.kv0_ref), channel_id=1, source_target_pairs={{0,1},{1,2},{2,3},{4,5},{5,6},{6,7},{8,9},{9,10},{10,11},{12,13},{... | collective-permute-start | bytes 786440 | tf_op jit(solution)/shard_map/ppermute | solution.py:501
  81.0 9.7 %collective-permute-start.12 = (bf16[2,256,256]{2,1,0:T(8,128)(2,1)}, bf16[2,256,256]{2,1,0:T(8,128)(2,1)S(1)}, u32[]{:S(2)}, u32[]{:S(2)}) collective-permute-start(bf16[2,256,256]{2,1,0:T(8,128)(2,1)} %get-tuple-element.110.kv0_ref), channel_id=1, source_target_pairs={{0,2},{1,3},{4,6},{5,7},{8,10},{9,11},{12,14},{13,15},{16,18},{17,... | collective-permute-start | bytes 786440 | tf_op jit(solution)/shard_map/ppermute | solution.py:501
  87.9 18.8 %copy-start.5 = (bf16[2,256,256]{2,1,0:T(8,128)(2,1)}, bf16[2,256,256]{2,1,0:T(8,128)(2,1)S(1)}, u32[]{:S(2)}) copy-start(bf16[2,256,256]{2,1,0:T(8,128)(2,1)S(1)} %collective-permute-done.11.kv1_ref) | copy-start | bytes 786436
  90.7 16.0 %copy-start.6 = (bf16[2,256,256]{2,1,0:T(8,128)(2,1)}, bf16[2,256,256]{2,1,0:T(8,128)(2,1)S(1)}, u32[]{:S(2)}) copy-start(bf16[2,256,256]{2,1,0:T(8,128)(2,1)S(1)} %collective-permute-done.12.kv2_ref) | copy-start | bytes 786436
  90.7 28.1 %collective-permute-start.13 = (bf16[256,896]{1,0:T(8,128)(2,1)S(1)}, bf16[256,896]{1,0:T(8,128)(2,1)S(1)}, u32[]{:S(2)}, u32[]{:S(2)}) collective-permute-start(bf16[256,896]{1,0:T(8,128)(2,1)S(1)} %copy-done.24), channel_id=1, source_target_pairs={{0,1},{1,2},{2,3},{4,5},{5,6},{6,7},{8,9},{9,10},{10,11},{12,13},{... | collective-permute-start | bytes 1376264 | tf_op jit(solution)/shard_map/ppermute | solution.py:441
  98.9 23.0 %collective-permute-start.14 = (bf16[256,896]{1,0:T(8,128)(2,1)}, bf16[256,896]{1,0:T(8,128)(2,1)S(1)}, u32[]{:S(2)}, u32[]{:S(2)}) collective-permute-start(bf16[256,896]{1,0:T(8,128)(2,1)} %collective-permute-done.6.refs_8_), channel_id=1, source_target_pairs={{1,0},{2,1},{3,2},{5,4},{6,5},{7,6},{9,8},{10,9},{11,10},{13,12},{... | collective-permute-start | bytes 1376264 | tf_op jit(solution)/shard_map/ppermute | solution.py:444
  100.2 22.8 %collective-permute-start.15 = (bf16[256,896]{1,0:T(8,128)(2,1)S(1)}, bf16[256,896]{1,0:T(8,128)(2,1)S(1)}, u32[]{:S(2)}, u32[]{:S(2)}) collective-permute-start(bf16[256,896]{1,0:T(8,128)(2,1)S(1)} %collective-permute-done.9.refs_7_), channel_id=1, source_target_pairs={{0,1},{1,2},{2,3},{4,5},{5,6},{6,7},{8,9},{9,10},{10,11},{12,13},{... | collective-permute-start | bytes 1376264 | tf_op jit(solution)/shard_map/ppermute | solution.py:441
  104.8 24.1 %collective-permute-start.16 = (bf16[256,896]{1,0:T(8,128)(2,1)S(1)}, bf16[256,896]{1,0:T(8,128)(2,1)S(1)}, u32[]{:S(2)}, u32[]{:S(2)}) collective-permute-start(bf16[256,896]{1,0:T(8,128)(2,1)S(1)} %collective-permute-done.10.refs_8_), channel_id=1, source_target_pairs={{1,0},{2,1},{3,2},{5,4},{6,5},{7,6},{9,8},{10,9},{11,10},{13,12},{... | collective-permute-start | bytes 1376264 | tf_op jit(solution)/shard_map/ppermute | solution.py:444
  116.0 35.8 %collective-permute-start.20 = (bf16[256,896]{1,0:T(8,128)(2,1)}, bf16[256,896]{1,0:T(8,128)(2,1)}, u32[]{:S(2)}, u32[]{:S(2)}) collective-permute-start(bf16[256,896]{1,0:T(8,128)(2,1)} %get-tuple-element.119.refs_0_), channel_id=1, source_target_pairs={{0,1},{1,2},{2,3},{3,0},{4,5},{5,6},{6,7},{7,4},{8,9},{9,10},{10,1... | collective-permute-start | bytes 1376264 | tf_op jit(solution)/shard_map/ppermute | solution.py:428
  118.7 19.6 %copy-start.25 = (bf16[256,896]{1,0:T(8,128)(2,1)}, bf16[256,896]{1,0:T(8,128)(2,1)S(1)}, u32[]{:S(2)}) copy-start(bf16[256,896]{1,0:T(8,128)(2,1)S(1)} %collective-permute-done.13.refs_9_) | copy-start | bytes 1376260
  118.7 52.6 %collective-permute-start.21 = (bf16[256,896]{1,0:T(8,128)(2,1)}, bf16[256,896]{1,0:T(8,128)(2,1)}, u32[]{:S(2)}, u32[]{:S(2)}) collective-permute-start(bf16[256,896]{1,0:T(8,128)(2,1)} %get-tuple-element.119.refs_0_), channel_id=1, source_target_pairs={{0,2},{1,3},{2,0},{3,1},{4,6},{5,7},{6,4},{7,5},{8,10},{9,11},{10,... | collective-permute-start | bytes 1376264 | tf_op jit(solution)/shard_map/ppermute | solution.py:428
  121.9 16.4 %copy-start.27 = (bf16[256,896]{1,0:T(8,128)(2,1)}, bf16[256,896]{1,0:T(8,128)(2,1)S(1)}, u32[]{:S(2)}) copy-start(bf16[256,896]{1,0:T(8,128)(2,1)S(1)} %collective-permute-done.14.refs_10_) | copy-start | bytes 1376260
  121.9 49.4 %collective-permute-start.22 = (bf16[256,896]{1,0:T(8,128)(2,1)}, bf16[256,896]{1,0:T(8,128)(2,1)}, u32[]{:S(2)}, u32[]{:S(2)}) collective-permute-start(bf16[256,896]{1,0:T(8,128)(2,1)} %get-tuple-element.119.refs_0_), channel_id=1, source_target_pairs={{0,3},{1,0},{2,1},{3,2},{4,7},{5,4},{6,5},{7,6},{8,11},{9,8},{10,9... | collective-permute-start | bytes 1376264 | tf_op jit(solution)/shard_map/ppermute | solution.py:428
  123.0 15.3 %copy-start.17 = (bf16[256,896]{1,0:T(8,128)(2,1)}, bf16[256,896]{1,0:T(8,128)(2,1)S(1)}, u32[]{:S(2)}) copy-start(bf16[256,896]{1,0:T(8,128)(2,1)S(1)} %collective-permute-done.15.refs_9_) | copy-start | bytes 1376260
  138.4 73.5 %collective-permute-start.17 = (bf16[256,896]{1,0:T(8,128)(2,1)}, bf16[256,896]{1,0:T(8,128)(2,1)S(1)}, u32[]{:S(2)}, u32[]{:S(2)}) collective-permute-start(bf16[256,896]{1,0:T(8,128)(2,1)} %get-tuple-element.118.refs_0_), channel_id=1, source_target_pairs={{0,1},{1,2},{2,3},{3,0},{4,5},{5,6},{6,7},{7,4},{8,9},{9,10},{10,1... | collective-permute-start | bytes 1376264 | tf_op jit(solution)/shard_map/ppermute | solution.py:428
  151.8 60.0 %collective-permute-start.18 = (bf16[256,896]{1,0:T(8,128)(2,1)}, bf16[256,896]{1,0:T(8,128)(2,1)S(1)}, u32[]{:S(2)}, u32[]{:S(2)}) collective-permute-start(bf16[256,896]{1,0:T(8,128)(2,1)} %get-tuple-element.118.refs_0_), channel_id=1, source_target_pairs={{0,2},{1,3},{2,0},{3,1},{4,6},{5,7},{6,4},{7,5},{8,10},{9,11},{10,... | collective-permute-start | bytes 1376264 | tf_op jit(solution)/shard_map/ppermute | solution.py:428
  151.8 60.0 %collective-permute-start.19 = (bf16[256,896]{1,0:T(8,128)(2,1)}, bf16[256,896]{1,0:T(8,128)(2,1)S(1)}, u32[]{:S(2)}, u32[]{:S(2)}) collective-permute-start(bf16[256,896]{1,0:T(8,128)(2,1)} %get-tuple-element.118.refs_0_), channel_id=1, source_target_pairs={{0,3},{1,0},{2,1},{3,2},{4,7},{5,4},{6,5},{7,6},{8,11},{9,8},{10,9... | collective-permute-start | bytes 1376264 | tf_op jit(solution)/shard_map/ppermute | solution.py:428
  197.4 45.3 %collective-permute-start.26 = (bf16[256,896]{1,0:T(8,128)(2,1)}, bf16[256,896]{1,0:T(8,128)(2,1)S(1)}, u32[]{:S(2)}, u32[]{:S(2)}) collective-permute-start(bf16[256,896]{1,0:T(8,128)(2,1)} %get-tuple-element.139), channel_id=1, source_target_pairs={{0,3},{1,0},{2,1},{3,2},{4,7},{5,4},{6,5},{7,6},{8,11},{9,8},{10,9... | collective-permute-start | bytes 1376264 | tf_op jit(solution)/shard_map/ppermute | solution.py:428
  209.9 60.8 %collective-permute-start.27 = (bf16[256,896]{1,0:T(8,128)(2,1)}, bf16[256,896]{1,0:T(8,128)(2,1)S(1)}, u32[]{:S(2)}, u32[]{:S(2)}) collective-permute-start(bf16[256,896]{1,0:T(8,128)(2,1)} %get-tuple-element.140), channel_id=1, source_target_pairs={{0,2},{1,3},{2,0},{3,1},{4,6},{5,7},{6,4},{7,5},{8,10},{9,11},{10,... | collective-permute-start | bytes 1376264 | tf_op jit(solution)/shard_map/ppermute | solution.py:428
  211.8 58.8 %collective-permute-start.28 = (bf16[256,896]{1,0:T(8,128)(2,1)}, bf16[256,896]{1,0:T(8,128)(2,1)}, u32[]{:S(2)}, u32[]{:S(2)}) collective-permute-start(bf16[256,896]{1,0:T(8,128)(2,1)} %get-tuple-element.141), channel_id=1, source_target_pairs={{0,1},{1,2},{2,3},{3,0},{4,5},{5,6},{6,7},{7,4},{8,9},{9,10},{10,1... | collective-permute-start | bytes 1376264 | tf_op jit(solution)/shard_map/ppermute | solution.py:428
  239.0 48.2 %collective-permute-start.23 = (bf16[256,896]{1,0:T(8,128)(2,1)}, bf16[256,896]{1,0:T(8,128)(2,1)S(1)}, u32[]{:S(2)}, u32[]{:S(2)}) collective-permute-start(bf16[256,896]{1,0:T(8,128)(2,1)} %get-tuple-element.131), channel_id=1, source_target_pairs={{0,3},{1,0},{2,1},{3,2},{4,7},{5,4},{6,5},{7,6},{8,11},{9,8},{10,9... | collective-permute-start | bytes 1376264 | tf_op jit(solution)/shard_map/ppermute | solution.py:428
  242.7 47.3 %collective-permute-start.24 = (bf16[256,896]{1,0:T(8,128)(2,1)}, bf16[256,896]{1,0:T(8,128)(2,1)S(1)}, u32[]{:S(2)}, u32[]{:S(2)}) collective-permute-start(bf16[256,896]{1,0:T(8,128)(2,1)} %get-tuple-element.132), channel_id=1, source_target_pairs={{0,2},{1,3},{2,0},{3,1},{4,6},{5,7},{6,4},{7,5},{8,10},{9,11},{10,... | collective-permute-start | bytes 1376264 | tf_op jit(solution)/shard_map/ppermute | solution.py:428
  242.7 26.4 %copy-start.29 = (bf16[256,896]{1,0:T(8,128)(2,1)}, bf16[256,896]{1,0:T(8,128)(2,1)S(1)}, u32[]{:S(2)}) copy-start(bf16[256,896]{1,0:T(8,128)(2,1)S(1)} %collective-permute-done.26.refs_1_) | copy-start | bytes 1376260
  242.7 47.3 %collective-permute-start.25 = (bf16[256,896]{1,0:T(8,128)(2,1)}, bf16[256,896]{1,0:T(8,128)(2,1)S(1)}, u32[]{:S(2)}, u32[]{:S(2)}) collective-permute-start(bf16[256,896]{1,0:T(8,128)(2,1)} %get-tuple-element.133), channel_id=1, source_target_pairs={{0,1},{1,2},{2,3},{3,0},{4,5},{5,6},{6,7},{7,4},{8,9},{9,10},{10,1... | collective-permute-start | bytes 1376264 | tf_op jit(solution)/shard_map/ppermute | solution.py:428
  284.6 7.1 %collective-permute-start.29 = (bf16[256,256]{1,0:T(8,128)(2,1)}, bf16[256,256]{1,0:T(8,128)(2,1)S(1)}, u32[]{:S(2)}, u32[]{:S(2)}) collective-permute-start(bf16[256,256]{1,0:T(8,128)(2,1)} %get-tuple-element.151), channel_id=1, source_target_pairs={{1,0},{2,1},{3,2},{5,4},{6,5},{7,6},{9,8},{10,9},{11,10},{13,12},{... | collective-permute-start | bytes 393224 | tf_op jit(solution)/shard_map/ppermute | solution.py:549
  285.9 10.7 %collective-permute-start.30 = (bf16[256,256]{1,0:T(8,128)(2,1)}, bf16[256,256]{1,0:T(8,128)(2,1)S(1)}, u32[]{:S(2)}, u32[]{:S(2)}) collective-permute-start(bf16[256,256]{1,0:T(8,128)(2,1)} %get-tuple-element.152), channel_id=1, source_target_pairs={{2,0},{3,1},{6,4},{7,5},{10,8},{11,9},{14,12},{15,13},{18,16},{19,... | collective-permute-start | bytes 393224 | tf_op jit(solution)/shard_map/ppermute | solution.py:549
  297.8 18.6 %collective-permute-start.31 = (bf16[2,256,896]{2,1,0:T(8,128)(2,1)S(1)}, bf16[2,256,896]{2,1,0:T(8,128)(2,1)}, u32[]{:S(2)}, u32[]{:S(2)}) collective-permute-start(bf16[2,256,896]{2,1,0:T(8,128)(2,1)S(1)} %copy-done.11), channel_id=1, source_target_pairs={{0,3},{1,0},{2,1},{3,2},{4,7},{5,4},{6,5},{7,6},{8,11},{9,8},{10,9... | collective-permute-start | bytes 2752520 | tf_op jit(solution)/shard_map/ppermute | solution.py:428
  316.4 7.8 %collective-permute-start.32 = (bf16[256,256]{1,0:T(8,128)(2,1)}, bf16[256,256]{1,0:T(8,128)(2,1)S(1)}, u32[]{:S(2)}, u32[]{:S(2)}) collective-permute-start(bf16[256,256]{1,0:T(8,128)(2,1)} %get-tuple-element.176), channel_id=1, source_target_pairs={{1,0},{2,1},{3,2},{5,4},{6,5},{7,6},{9,8},{10,9},{11,10},{13,12},{... | collective-permute-start | bytes 393224 | tf_op jit(solution)/shard_map/ppermute | solution.py:549
  317.7 9.4 %collective-permute-start.33 = (bf16[256,256]{1,0:T(8,128)(2,1)}, bf16[256,256]{1,0:T(8,128)(2,1)S(1)}, u32[]{:S(2)}, u32[]{:S(2)}) collective-permute-start(bf16[256,256]{1,0:T(8,128)(2,1)} %get-tuple-element.177), channel_id=1, source_target_pairs={{2,0},{3,1},{6,4},{7,5},{10,8},{11,9},{14,12},{15,13},{18,16},{19,... | collective-permute-start | bytes 393224 | tf_op jit(solution)/shard_map/ppermute | solution.py:549
  339.2 4.2 collective-permute-start.34
  339.3 24.5 %collective-permute-start.35 = (bf16[2,256,896]{2,1,0:T(8,128)(2,1)S(1)}, bf16[2,256,896]{2,1,0:T(8,128)(2,1)S(1)}, u32[]{:S(2)}, u32[]{:S(2)}) collective-permute-start(bf16[2,256,896]{2,1,0:T(8,128)(2,1)S(1)} %copy-done.12), channel_id=1, source_target_pairs={{0,1},{1,2},{2,3},{3,0},{4,5},{5,6},{6,7},{7,4},{8,9},{9,10},{10,1... | collective-permute-start | bytes 2752520 | tf_op jit(solution)/shard_map/ppermute | solution.py:428
  345.3 18.5 %copy-start.1 = (f32[448,2176]{1,0:T(8,128)}, f32[448,2176]{1,0:T(8,128)S(1)}, u32[]{:S(2)}) copy-start(f32[448,2176]{1,0:T(8,128)S(1)} %convert_add_fusion) | copy-start | bytes 11698180
  366.1 12.1 %collective-permute-start.38 = (bf16[1,2,112,1024]{3,2,1,0:T(8,128)(2,1)S(1)}, bf16[1,2,112,1024]{3,2,1,0:T(8,128)(2,1)S(1)}, u32[]{:S(2)}, u32[]{:S(2)}) collective-permute-start(bf16[1,2,112,1024]{3,2,1,0:T(8,128)(2,1)S(1)} %fusion.8), channel_id=1, source_target_pairs={{0,16},{4,20},{8,24},{12,28},{16,0},{20,4},{24,8},{28,12},{1,17},{... | collective-permute-start | bytes 1376264 | tf_op jit(solution)/shard_map/ppermute | solution.py:576
  369.4 13.5 %collective-permute-start.36 = (bf16[2,1,112,1152]{3,2,0,1:T(8,128)(2,1)S(1)}, bf16[2,1,112,1152]{3,2,0,1:T(8,128)(2,1)}, u32[]{:S(2)}, u32[]{:S(2)}) collective-permute-start(bf16[2,1,112,1152]{3,2,0,1:T(8,128)(2,1)S(1)} %fusion.7), channel_id=1, source_target_pairs={{0,8},{4,12},{8,0},{12,4},{16,24},{20,28},{24,16},{28,20},{1,9},{5... | collective-permute-start | bytes 1548296 | tf_op jit(solution)/shard_map/ppermute | solution.py:576
  380.4 7.1 %collective-permute-start.39 = (bf16[1,1,112,1024]{3,2,1,0:T(8,128)(2,1)}, bf16[1,1,112,1024]{3,2,1,0:T(8,128)(2,1)}, u32[]{:S(2)}, u32[]{:S(2)}) collective-permute-start(bf16[1,1,112,1024]{3,2,1,0:T(8,128)(2,1)} %dynamic-slice_convert_fusion.3), channel_id=1, source_target_pairs={{0,8},{4,12},{8,0},{12,4},{16,24},{20,28},{24,16},{28,20},{1,9},{5... | collective-permute-start | bytes 688136 | tf_op jit(solution)/shard_map/ppermute | solution.py:576
  384.1 6.4 %collective-permute-start.37 = (bf16[1,1,112,1152]{3,2,0,1:T(8,128)(2,1)S(1)}, bf16[1,1,112,1152]{3,2,0,1:T(8,128)(2,1)S(1)}, u32[]{:S(2)}, u32[]{:S(2)}) collective-permute-start(bf16[1,1,112,1152]{3,2,0,1:T(8,128)(2,1)S(1)} %dynamic-slice_convert_fusion.2), channel_id=1, source_target_pairs={{0,16},{4,20},{8,24},{12,28},{16,0},{20,4},{24,8},{28,12},{1,17},{... | collective-permute-start | bytes 774152 | tf_op jit(solution)/shard_map/ppermute | solution.py:576
  384.5 41.0 %collective-permute-start.40 = (bf16[2,256,896]{2,1,0:T(8,128)(2,1)}, bf16[2,256,896]{2,1,0:T(8,128)(2,1)}, u32[]{:S(2)}, u32[]{:S(2)}) collective-permute-start(bf16[2,256,896]{2,1,0:T(8,128)(2,1)} %get-tuple-element.184), channel_id=1, source_target_pairs={{0,2},{1,3},{2,0},{3,1},{4,6},{5,7},{6,4},{7,5},{8,10},{9,11},{10,... | collective-permute-start | bytes 2752520 | tf_op jit(solution)/shard_map/ppermute | solution.py:428
  388.7 40.9 %copy-start = (f32[2,256,896]{2,1,0:T(8,128)S(1)}, f32[2,256,896]{2,1,0:T(8,128)}, u32[]{:S(2)}) copy-start(f32[2,256,896]{2,1,0:T(8,128)} %get-tuple-element.117.middle_ref) | copy-start | bytes 5505028
  425.7 8.5 %collective-permute-start.41 = (bf16[28,2176]{1,0:T(8,128)(2,1)S(1)}, bf16[28,2176]{1,0:T(8,128)(2,1)S(1)}, u32[]{:S(2)}, u32[]{:S(2)}) collective-permute-start(bf16[28,2176]{1,0:T(8,128)(2,1)S(1)} %get-tuple-element.255), channel_id=1, source_target_pairs={{0,1},{1,2},{2,3},{3,0},{4,5},{5,6},{6,7},{7,4},{8,9},{9,10},{10,1... | collective-permute-start | bytes 365576 | tf_op jit(solution)/shard_map/ppermute | solution.py:428
  425.8 13.5 %collective-permute-start.42 = (bf16[28,2176]{1,0:T(8,128)(2,1)S(1)}, bf16[28,2176]{1,0:T(8,128)(2,1)S(1)}, u32[]{:S(2)}, u32[]{:S(2)}) collective-permute-start(bf16[28,2176]{1,0:T(8,128)(2,1)S(1)} %get-tuple-element.257), channel_id=1, source_target_pairs={{0,2},{1,3},{2,0},{3,1},{4,6},{5,7},{6,4},{7,5},{8,10},{9,11},{10,... | collective-permute-start | bytes 365576 | tf_op jit(solution)/shard_map/ppermute | solution.py:428
  426.6 12.6 %collective-permute-start.43 = (bf16[28,2176]{1,0:T(8,128)(2,1)S(1)}, bf16[28,2176]{1,0:T(8,128)(2,1)S(1)}, u32[]{:S(2)}, u32[]{:S(2)}) collective-permute-start(bf16[28,2176]{1,0:T(8,128)(2,1)S(1)} %get-tuple-element.256), channel_id=1, source_target_pairs={{0,3},{1,0},{2,1},{3,2},{4,7},{5,4},{6,5},{7,6},{8,11},{9,8},{10,9... | collective-permute-start | bytes 365576 | tf_op jit(solution)/shard_map/ppermute | solution.py:428
  (23 other events, 70.6 us)
Sparse Core Ops, SparseCore 0:
  30.0 35.8 all-gather.2
  68.3 48.0 all-gather.4
  296.8 63.5 reduce-scatter.1

commit v3 on v2

--- a/solution.py
+++ b/solution.py
@@ -24,42 +24,51 @@
 def scaled(v):
     return lax.rsqrt(jnp.mean(v*v, axis=-1, keepdims=True)+epsilon)
 
-def project_kernel(x_ref, wq_ref, wkv_ref, ws_ref, spread_ref, cos_ref, sin_ref, rq_ref, kv_ref, n1_ref, rows_ref, bias_ref):
+def pairs_kernel(x_ref, wkv_ref, ws_ref, spread_ref, cos_ref, sin_ref, kv_ref, n1_ref, rows_ref, bias_ref):
     @pl.when(pl.program_id(0)==0)
     def _():
         table = ws_ref[...].astype(f32).T[:8]
         rows_ref[...] = table
         close = dot(table.astype(bf16), spread_ref[...],1,0)
-        bias_ref[:, :QW] = table[2:3]
-        bias_ref[:, QW:QW+KW] = close[3:4]
-        bias_ref[:, QW+KW:] = close[4:5]
-    x = x_ref[0].astype(f32)
+        bias_ref[:, :KW] = close[3:4]
+        bias_ref[:, KW:] = close[4:5]
+    x = x_ref[...].astype(f32)
     n1 = (x*scaled(x)*rows_ref[0:1]).astype(bf16)
-    n1_ref[0] = n1
-    cos = cos_ref[0]; sin = sin_ref[0]
-    q = dot(n1, wq_ref[...],1,0) + bias_ref[:, :QW]
+    n1_ref[...] = n1
+    kv = dot(n1, wkv_ref[...],1,0) + bias_ref[...]
+    v = kv[:, :KW]
+    kv_ref[:, :KW] = (v*cos_ref[...] + half_turn(v,False)*sin_ref[...]).astype(bf16)
+    kv_ref[:, KW:] = kv[:, KW:].astype(bf16)
+
+def queries_kernel(n1_ref, wq_ref, rows_ref, cos_ref, sin_ref, rq_ref):
+    q = dot(n1_ref[...], wq_ref[...],1,0) + rows_ref[2:3]
+    cos = cos_ref[...]; sin = sin_ref[...]
     for b in range(QW//LANES):
         v = q[:, b*LANES:(b+1)*LANES]
         r = (v*cos + half_turn(v,False)*sin).astype(bf16)
-        rq_ref[0,:, b*LANES:(b+1)*LANES] = (r.astype(f32)*HEAD**-0.5).astype(bf16)
-    kv = dot(n1, wkv_ref[...],1,0) + bias_ref[:, QW:]
-    v = kv[:, :KW]
-    kv_ref[0,:, :KW] = (v*cos + half_turn(v,False)*sin).astype(bf16)
-    kv_ref[0,:, KW:] = kv[:, KW:].astype(bf16)
+        rq_ref[:, b*LANES:(b+1)*LANES] = (r.astype(f32)*HEAD**-0.5).astype(bf16)
 
 def project(x, first_set, spread, cos, sin):
     m, rows, _ = x.shape
     full=lambda shape,idx: pl.BlockSpec(shape, lambda i: idx)
-    blk=lambda w: pl.BlockSpec((1,rows,w), lambda i:(i,0,0))
-    return pl.pallas_call(
-        project_kernel, grid=(m,),
-        in_specs=[blk(D), full((D,QW),(0,1)), full((D,2*KW),(0,7)), full((D,LANES),(0,16)), full((D,LANES),(0,0)), blk(LANES), blk(LANES)],
-        out_specs=[blk(QW), blk(2*KW), blk(D), full((8,D),(0,0))],
-        out_shape=[jax.ShapeDtypeStruct((m,rows,QW),bf16), jax.ShapeDtypeStruct((m,rows,2*KW),bf16), jax.ShapeDtypeStruct((m,rows,D),bf16), jax.ShapeDtypeStruct((8,D),f32)],
-        scratch_shapes=[pltpu.VMEM((1,QW+2*KW),f32)],
-        compiler_params=pltpu.CompilerParams(vmem_limit_bytes=LIMIT), cost_estimate=COST,
-        name="project",
-    )(x, first_set, first_set, first_set, spread, cos, sin)
+    blk=lambda w: pl.BlockSpec((None,rows,w), lambda i:(i,0,0))
+    sd=jax.ShapeDtypeStruct
+    params=dict(compiler_params=pltpu.CompilerParams(vmem_limit_bytes=LIMIT), cost_estimate=COST)
+    pair, n1, table = pl.pallas_call(
+        pairs_kernel, grid=(m,),
+        in_specs=[blk(D), full((D,2*KW),(0,7)), full((D,LANES),(0,16)), full((D,LANES),(0,0)), blk(LANES), blk(LANES)],
+        out_specs=[blk(2*KW), blk(D), full((8,D),(0,0))],
+        out_shape=[sd((m,rows,2*KW),bf16), sd((m,rows,D),bf16), sd((8,D),f32)],
+        scratch_shapes=[pltpu.VMEM((1,2*KW),f32)],
+        name="pairs", **params,
+    )(x, first_set, first_set, spread, cos, sin)
+    rq = pl.pallas_call(
+        queries_kernel, grid=(m,),
+        in_specs=[blk(D), full((D,QW),(0,1)), full((8,D),(0,0)), blk(LANES), blk(LANES)],
+        out_specs=blk(QW), out_shape=sd((m,rows,QW),bf16),
+        name="queries", **params,
+    )(n1, first_set, table, cos, sin)
+    return rq, pair, n1, table
 
 BLOCK=128
 def units():
@@ -215,7 +224,7 @@
     at=12+len(gs)
     return pl.pallas_call(
         functools.partial(attend_back_kernel,count=len(gs)), grid=(nq,),
-        in_specs=[pl.BlockSpec(memory_space=pltpu.SMEM), blk(QW)]+[one(rows,2*KW)]*3+[pl.BlockSpec((None,1,BLOCK),lambda i:(m,0,i)), full((D,QW)), full((8,D)),
+        in_specs=[pl.BlockSpec(memory_space=pltpu.SMEM), blk(QW)]+[pl.BlockSpec((None,rows,2*KW),lambda i:(m,0,0))]*3+[pl.BlockSpec((None,1,BLOCK),lambda i:(m,0,i)), full((D,QW)), full((8,D)),
             pl.BlockSpec((None,1,16,BLOCK),lambda i:(m,i,0,0)), blk(D), blk(D)]+[blk(LANES)]*2+[pl.BlockSpec((BLOCK,D),lambda i:(i,0))]*len(gs)+[pl.BlockSpec(memory_space=pl.ANY)]*len(before),
         out_specs=[full((rows,2*KW)), full((rows,2*KW)), blk(D), blk(D), blk(QW), one(rows,2*KW), one(8,D)],
         out_shape=[sd((rows,2*KW),bf16), sd((rows,2*KW),bf16), sd((micros,rows,D),f32), sd((micros,rows,D),bf16), sd((micros,rows,QW),bf16), sd((micros,rows,2*KW),f32), sd((micros,8,D),f32)],
@@ -227,73 +236,90 @@
 
 CHUNK=256
 
-class Tokens:
-    def __init__(self, kind, arrays, micro=None):
-        self.kind, self.arrays, self.micro = kind, tuple(arrays), micro
-    def specs(self, rows):
-        if self.kind=="whole":
-            return [pl.BlockSpec((rows,D), lambda i: (i,0))]
-        if self.micro is None:
-            return [pl.BlockSpec((rows,D), lambda i: (0,0), pipeline_mode=pl.Buffered(1))]*len(self.arrays)
-        return [pl.BlockSpec((None,rows,D), lambda i: (self.micro,0,0), pipeline_mode=pl.Buffered(1))]*len(self.arrays)
-    def take(self, refs, i, rank, parts, into):
-        if self.kind=="whole":
-            into[...]=refs[0][...]
-        elif self.kind=="around":
-            for k in range(parts):
-                @pl.when(lax.rem(rank-i+parts,parts)==k)
-                def _(k=k): into[...]=refs[k][...]
-        else:
-            for k in range(-(parts-1),parts):
-                ref = refs[0] if k==0 else refs[2*k-1] if k>0 else refs[-2*k]
-                @pl.when(rank-i==k)
-                def _(ref=ref): into[...]=ref[...]
-
-def feed_kernel(rank_ref, *refs, parts, kept, toks, grads):
-    n_t=len(toks.arrays); n_g=len(grads.arrays)
-    ts=refs[:n_t]; gs=refs[n_t:n_t+n_g]; refs=refs[n_t+n_g:]
-    wg_ref,wu_ref,wd_ref=refs[:3]
-    refs=refs[3+kept:]
+def feed_kernel(own_ref, *refs, parts, micro, kept):
+    ts=refs[:parts]; gs=refs[parts:2*parts]; sets=refs[2*parts:2*parts+2]
+    refs=refs[2*parts+2+kept:]
     backs=refs[:parts]; outs=refs[parts:2*parts]
-    x_ref,y_ref,pair_ref,act_ref=refs[2*parts:]
-    i=pl.program_id(0); rank=rank_ref[0]
-    toks.take(ts,i,rank,parts,x_ref); grads.take(gs,i,rank,parts,y_ref)
-    x=x_ref[...]; y=y_ref[...]
-    width=wg_ref.shape[1]
-    for j in range(width//CHUNK):
-        c=slice(j*CHUNK,(j+1)*CHUNK); c2=slice(width+j*CHUNK,width+(j+1)*CHUNK)
-        g=dot(x,wg_ref[:,c],1,0); u=dot(x,wu_ref[:,c],1,0); da=dot(y,wd_ref[:,c],1,0)
+    left_ref,pair_ref,act_ref,x_ref,y_ref,w_ref,own_buf,far_buf,w_sem,in_sem,out_sem=refs[2*parts:]
+    i=pl.program_id(0)
+    width=w_ref.shape[1]//3
+    chunks=width//CHUNK
+    def tokens(k):
+        return (pltpu.make_async_copy(ts[k],x_ref.at[k],in_sem.at[0,k]),
+                pltpu.make_async_copy(gs[k].at[micro],y_ref.at[k],in_sem.at[1,k]))
+    def columns(which,j,p):
+        c=slice(p*width+j*CHUNK,p*width+(j+1)*CHUNK)
+        return pltpu.make_async_copy(sets[which].at[:,c],w_ref.at[:,c],w_sem.at[p,j])
+    def results(k):
+        if k==0:
+            return (pltpu.make_async_copy(own_buf.at[0],outs[0].at[micro],out_sem.at[0,0]),
+                    pltpu.make_async_copy(own_buf.at[1],backs[0],out_sem.at[1,0]))
+        return (pltpu.make_async_copy(far_buf.at[0,k-1],outs[k].at[micro],out_sem.at[0,k]),
+                pltpu.make_async_copy(far_buf.at[1,k-1],backs[k],out_sem.at[1,k]))
+    @pl.when(i==0)
+    def _():
+        for copy in tokens(0): copy.start()
+        for which in range(2):
+            @pl.when(own_ref[0]==1-which)
+            def _(which=which):
+                for j in range(chunks):
+                    for p in range(3): columns(which,j,p).start()
+        for k in range(1,parts):
+            for copy in tokens(k): copy.start()
+    for k in range(parts):
+        @pl.when(i==k)
+        def _(k=k):
+            for copy in tokens(k): copy.wait()
+    @pl.when(i==0)
+    def _():
+        for j in range(chunks):
+            for p in range(3): columns(0,j,p).wait()
+    x=x_ref[i]; y=y_ref[i]
+    left_ref[0]=x; left_ref[1]=y
+    for j in range(chunks):
+        c=slice(j*CHUNK,(j+1)*CHUNK); c2=slice(width+j*CHUNK,width+(j+1)*CHUNK); c3=slice(2*width+j*CHUNK,2*width+(j+1)*CHUNK)
+        g=dot(x,w_ref[:,c],1,0); u=dot(x,w_ref[:,c2],1,0); da=dot(y,w_ref[:,c3],1,0)
         s=jax.nn.sigmoid(g)
         gs_=g*s
         act_ref[:,c]=(gs_*u).astype(bf16)
         pair_ref[:,c]=(da*u*s*(1.0+g*(1.0-s))).astype(bf16)
         pair_ref[:,c2]=(da*gs_).astype(bf16)
-    out=dot(act_ref[...],wd_ref[...],1,1)
-    res=dot(pair_ref[:,:width],wg_ref[...],1,1)+dot(pair_ref[:,width:],wu_ref[...],1,1)
-    for value,places in ((out,outs),(res,backs)):
+    out=dot(act_ref[...],w_ref[:,2*width:],1,1)
+    res=dot(pair_ref[...],w_ref[:,:2*width],1,1)
+    for k in range(parts):
+        @pl.when(i==k)
+        def _(k=k):
+            if k==0:
+                own_buf[0]=out; own_buf[1]=res
+            else:
+                far_buf[0,k-1]=out.astype(bf16); far_buf[1,k-1]=res.astype(bf16)
+            for copy in results(k): copy.start()
+    @pl.when(i==parts-1)
+    def _():
         for k in range(parts):
-            @pl.when(lax.rem(rank-i+parts,parts)==k)
-            def _(k=k,value=value,places=places):
-                places[k][...]=value.astype(places[k].dtype)
-
-def feed(rank, toks, grads, rest_set, hidden_pad, micro, micros, parts, rows, before):
-    full=lambda shape,idx=(0,0): pl.BlockSpec(shape, lambda i: idx)
-    blk=lambda w,first=0: pl.BlockSpec((rows,w), lambda i:(first+i,0))
+            for copy in results(k): copy.wait()
+
+def feed(own, toks, grads, sets, micro, micros, before):
+    parts=len(toks); rows=toks[0].shape[0]; hidden_pad=sets[0].shape[1]//3
+    blk=lambda w: pl.BlockSpec((rows,w), lambda i:(micro*parts+i,0))
     sd=jax.ShapeDtypeStruct
     everything=rows*parts*micros
     kept=len(before)
-    specs=[full((rows,D))]*parts+[pl.BlockSpec((None,rows,D),lambda i:(micro,0,0))]*parts
+    hold=pl.BlockSpec(memory_space=pl.ANY)
     shapes=[sd((rows,D),f32)]+[sd((rows,D),bf16)]*(parts-1)+[sd((micros,rows,D),f32)]+[sd((micros,rows,D),bf16)]*(parts-1)
-    n_in=1+len(toks.arrays)+len(grads.arrays)+3
+    n_in=1+2*parts+2
+    dma=pltpu.SemaphoreType.DMA
     out=pl.pallas_call(
-        functools.partial(feed_kernel,parts=parts,kept=kept,toks=toks,grads=grads), grid=(parts,),
-        in_specs=[pl.BlockSpec(memory_space=pltpu.SMEM)]+toks.specs(rows)+grads.specs(rows)+[pl.BlockSpec((D,hidden_pad),lambda i,k=k:(0,k),pipeline_mode=pl.Buffered(1)) for k in range(3)]+[pl.BlockSpec(memory_space=pl.ANY)]*kept,
-        out_specs=specs+[blk(w,micro*parts) for w in (D,D,2*hidden_pad,hidden_pad)],
-        out_shape=shapes+[sd((everything,w),bf16) for w in (D,D,2*hidden_pad,hidden_pad)],
+        functools.partial(feed_kernel,parts=parts,micro=micro,kept=kept), grid=(parts,),
+        in_specs=[pl.BlockSpec(memory_space=pltpu.SMEM)]+[hold]*(2*parts+2+kept),
+        out_specs=[hold]*(2*parts)+[pl.BlockSpec((2,rows,D), lambda i:(0,micro*parts+i,0)),blk(2*hidden_pad),blk(hidden_pad)],
+        out_shape=shapes+[sd((2,everything,D),bf16)]+[sd((everything,w),bf16) for w in (2*hidden_pad,hidden_pad)],
+        scratch_shapes=[pltpu.VMEM((parts,rows,D),bf16)]*2+[pltpu.VMEM(sets[0].shape,bf16),pltpu.VMEM((2,rows,D),f32),pltpu.VMEM((2,parts-1,rows,D),bf16),
+            dma((3,hidden_pad//CHUNK)),dma((2,parts)),dma((2,parts))],
         input_output_aliases={n_in+k:parts+k for k in range(kept)},
         compiler_params=pltpu.CompilerParams(vmem_limit_bytes=LIMIT), cost_estimate=COST,
         name="feed",
-    )(rank,*toks.arrays,*grads.arrays,rest_set,rest_set,rest_set,*before)
+    )(own,*toks,*grads,*sets,*before)
     return out[:parts], out[parts:]
 
 def finish_kernel(bit_ref, dq_ref, own_ref, cos_ref, sin_ref, wq_ref, wkv_ref, rows_ref, x_ref, n1_ref, dmid_ref, mixed_ref, dmb_ref, spread_ref, gain2_ref, *refs, near, block):
@@ -363,28 +389,25 @@
         name="finish",
     )(bit,dq,own,cos,sin,first_set,first_set,rows_table,x,n1,dmid,mixed,dmb,spread,gain2,*far)
 
-def weights_kernel(x_ref, y_ref, pair_ref, act_ref, out_ref, left_ref, *, split):
+def weights_kernel(left_ref, pair_ref, act_ref, out_ref, turned_ref, *, split):
     j=pl.program_id(0)
-    @pl.when(j==0)
-    def _(): left_ref[...]=x_ref[...].T
-    @pl.when(j==split)
-    def _(): left_ref[...]=y_ref[...].T
+    @pl.when((j==0)|(j==split))
+    def _(): turned_ref[...]=left_ref[...].T
     @pl.when(j<split)
-    def _(): out_ref[...]=dot(left_ref[...],pair_ref[...],1,0).astype(bf16)
+    def _(): out_ref[...]=dot(turned_ref[...],pair_ref[...],1,0).astype(bf16)
     @pl.when(j>=split)
-    def _(): out_ref[...]=dot(left_ref[...],act_ref[...],1,0).astype(bf16)
-
-def weights(x,y,pair,act,chunk=256):
-    rows=x.shape[0]; width=pair.shape[1]+act.shape[1]; split=pair.shape[1]//chunk
-    one=pl.BlockSpec((rows,D),lambda j:(0,0),pipeline_mode=pl.Buffered(1))
+    def _(): out_ref[...]=dot(turned_ref[...],act_ref[...],1,0).astype(bf16)
+
+def weights(left,pair,act,chunk=256):
+    rows=left.shape[1]; width=pair.shape[1]+act.shape[1]; split=pair.shape[1]//chunk
     return pl.pallas_call(
         functools.partial(weights_kernel,split=split), grid=(width//chunk,),
-        in_specs=[one,one,pl.BlockSpec((rows,chunk),lambda j:(0,jnp.minimum(j,split-1))),pl.BlockSpec((rows,chunk),lambda j:(0,jnp.maximum(j-split,0)))],
+        in_specs=[pl.BlockSpec((None,rows,D),lambda j:(jnp.where(j<split,0,1),0,0)),pl.BlockSpec((rows,chunk),lambda j:(0,jnp.minimum(j,split-1))),pl.BlockSpec((rows,chunk),lambda j:(0,jnp.maximum(j-split,0)))],
         out_specs=pl.BlockSpec((D,chunk),lambda j:(0,j)), out_shape=jax.ShapeDtypeStruct((D,width),bf16),
         scratch_shapes=[pltpu.VMEM((D,rows),bf16)],
         compiler_params=pltpu.CompilerParams(vmem_limit_bytes=LIMIT), cost_estimate=COST,
         name="weights",
-    )(x,y,pair,act)
+    )(left,pair,act)
 
 
 LONGEST = 512
@@ -414,8 +437,10 @@
     up_weight,
     down_weight,
 ):
-    parts = lax.axis_size("ctx")
-    rank = lax.axis_index("ctx")
+    ctx = ("zh", "zb")
+    dp = ("grp", "core")
+    parts = lax.axis_size(ctx)
+    rank = lax.axis_index(ctx)
     micros = layer_in.shape[1]
     shard_rows = layer_in.shape[3]
     hidden = gate_weight.shape[1]
@@ -423,32 +448,37 @@
     weight_rows = query_weight.shape[0]
     bias_rows = key_bias.shape[0]
     reach_parts = -(-LONGEST // shard_rows)
+    core = lax.axis_index("core")
+    far_half = lax.axis_index("zh")
 
     def around(values_in, steps):
-        return lax.ppermute(values_in, "ctx", [(s, (s + steps) % parts) for s in range(parts)])
-
-    def pieces_of(values_in):
-        return [values_in] + [around(values_in, d) for d in range(1, parts)]
+        return lax.ppermute(values_in, ctx, [(s, (s + steps) % parts) for s in range(parts)])
+
+    def other(values_in, axis):
+        return lax.ppermute(values_in, axis, [(0, 1), (1, 0)])
+
+    def corner(values_in):
+        return lax.ppermute(values_in, ("core", "zb"), [(s, 3 - s) for s in range(4)])
+
+    def shared(values_in):
+        beside = other(values_in, "zb")
+        return [values_in, other(values_in, "core"), beside, other(beside, "core")]
 
     def collected(values_in):
-        pieces = pieces_of(values_in)
+        pieces = [values_in] + [around(values_in, d) for d in range(1, parts)]
         ordered = [pieces[d] for d in range(parts - 1, -1, -1)]
         ordered = jnp.stack(ordered + ordered[:-1])
         taken = lax.dynamic_slice_in_dim(ordered, parts - 1 - rank, parts, 0)
         return taken.reshape((-1,) + values_in.shape[1:])
 
-    def ahead(values_in):
-        return lax.ppermute(values_in, "ctx", [(s, s + 1) for s in range(parts - 1)])
-
-    def behind(values_in):
-        return lax.ppermute(values_in, "ctx", [(s + 1, s) for s in range(parts - 1)])
-
     def column(values_in):
         return jnp.pad(values_in, (0, weight_rows - values_in.shape[0]))[:, None]
 
     def wide(values_in):
         return jnp.pad(values_in, ((0, 0), (0, hidden_pad - hidden)))
 
+    own_block = jnp.concatenate([wide(gate_weight), wide(up_weight), wide(down_weight.T)], axis=1)
+    own_set = lax.all_gather(own_block, dp, axis=0, tiled=True)
     small = jnp.concatenate(
         [column(v) for v in (first_gain, second_gain, query_bias, key_bias, value_bias)], axis=1
     )
@@ -456,10 +486,15 @@
     own_attention = jnp.concatenate(
         [out_weight, query_weight, key_weight, value_weight, small], axis=1
     )
-    first_set = lax.all_gather(collected(own_attention), "dp", axis=0, tiled=True)
-    rest_block = jnp.concatenate([wide(gate_weight), wide(up_weight), wide(down_weight.T)], axis=1)
-    rest_block = lax.optimization_barrier((rest_block, first_set[0, 0]))[0]
-    rest_set = lax.all_gather(rest_block, "dp", axis=0, tiled=True)
+    first_block = collected(own_attention)
+    own_block, first_block = after((own_block, first_block))
+    other_block = other(own_block, "zh")
+    first_block, other_block, own_set, upstream = after(
+        (first_block, other_block, own_set, cotangent[0, :, 0])
+    )
+    first_set = lax.all_gather(first_block, dp, axis=0, tiled=True)
+    upstream_pieces = shared(upstream)
+    own_quarter = (core == far_half).astype(jnp.int32).reshape(1)
 
     row = jnp.arange(D, dtype=jnp.int32)[:, None]
     place = row // weight_rows * bias_rows + row % weight_rows
@@ -480,80 +515,72 @@
     base = (rank * shard_rows).reshape(1)
 
     tokens = layer_in[0, :, 0]
-    upstream = cotangent[0, :, 0]
-    chains = [[upstream[m]] for m in range(micros)]
-    moving = [(upstream[m], upstream[m]) for m in range(micros)]
-
-    def next_round(m):
-        moving[m] = (ahead(moving[m][0]), behind(moving[m][1]))
-        chains[m] += list(moving[m])
-
-    for m in range(micros):
-        next_round(m)
-    next_round(0)
-    first_set = after(first_set, moving)
-    for m in range(1, micros):
-        next_round(m)
+    first_set, other_block, upstream_pieces, spread, cosines, sines, begins = after(
+        (first_set, other_block, upstream_pieces, spread, cosines, sines, begins)
+    )
+    other_set = lax.all_gather(other_block, dp, axis=0, tiled=True)
+    sets = (own_set, other_set)
 
     rot_query, pairs, normed_one, rows_table = project(tokens, first_set, spread, cosines, sines)
-    pairs = after(pairs, moving)
     kvs = [pairs] + [
-        lax.ppermute(pairs, "ctx", [(s, s + d) for s in range(parts - d)])
+        lax.ppermute(pairs, ctx, [(s, s + d) for s in range(parts - d)])
         for d in range(1, reach_parts + 1)
     ]
-    moving = after(moving, kvs[1:])
-    while len(chains[0]) < 2 * parts - 1:
-        for m in range(micros):
-            next_round(m)
 
     begins = begins[:, None, :]
     exchanged = []
     held = ()
     for m in range(micros):
-        if m == 1:
-            kvs = after(kvs, moving)
         normed_two, *held = attend(
             m, base, rot_query, kvs, begins, first_set, tokens, rows_table, held
         )
-        exchanged.append(Tokens("around", pieces_of(normed_two)))
+        pieces = [normed_two, other(normed_two, "core"), other(normed_two, "zb")]
+        if m < micros - 1:
+            exchanged.append(pieces)
+        else:
+            exchanged.append(pieces + [corner(normed_two)])
+            exchanged[:-1], normed_two = after((exchanged[:-1], normed_two))
+            exchanged[-1][0] = normed_two
+            for early in exchanged[:-1]:
+                early.append(other(early[2], "core"))
     mixed, middle, log_sums = held
 
     backs = []
     before = ()
-    rank_one = rank.reshape(1)
     for m in range(micros):
         back, before = feed(
-            rank_one, exchanged[m], Tokens("chain", chains[m]), rest_set, hidden_pad, m, micros,
-            parts, shard_rows, before,
-        )
-        backs.append([back[0]] + [around(back[d], parts - d) for d in range(1, parts)])
-    partials = before[:parts]
-
-    feed_local = weights(*before[parts:])
-    backs[0] = after(backs[0], feed_local)
+            own_quarter, exchanged[m], upstream_pieces, sets, m, micros, before
+        )
+        backs.append([back[0], other(back[1], "core"), other(back[2], "zb"), corner(back[3])])
+    partials = before[:4]
+    out_near = other(partials[1], "core")
+    out_far = other(partials[3], "core")
+
+    feed_local = weights(*after(before[4:], backs[0]))
+    backs, feed_local, out_near, out_far = after((backs, feed_local, out_near, out_far))
     far = []
     ended = ()
-    arrived = {}
+    out_beside = []
     for m in range(micros):
-        if m == micros - 1:
-            backs[m], feed_local, ended, far = after((backs[m], feed_local, ended, far))
-            arrived[1] = around(after(partials[1], backs[m]), parts - 1)
+        out_sum = (partials[2][m].astype(f32) + out_far[m].astype(f32)).astype(bf16)
+        out_beside.append(other(out_sum, "zb"))
         far1, far2, *ended = attend_back(
             m, base, rot_query, kvs, begins, first_set, rows_table, log_sums, middle, upstream,
             backs[m], cosines, sines, ended,
         )
-        if m == micros - 1:
-            far1, far2, arrived[1] = after((far1, far2, arrived[1]))
+        far1, far2, ended, out_beside = after((far1, far2, ended, out_beside))
         far.append(
             [
-                lax.ppermute(part, "ctx", [(s, s - d) for s in range(d, parts)])
+                lax.ppermute(part, ctx, [(s, s - d) for s in range(d, parts)])
                 for d, part in ((1, far1), (2, far2))
             ]
         )
-    feed_sum = lax.psum_scatter(feed_local, "dp", scatter_dimension=0, tiled=True).astype(f32)
-
-    group_rank = lax.axis_index("dp")
-    groups = lax.axis_size("dp")
+        if m < micros - 1:
+            out_far, ended = after((out_far, ended))
+    feed_half = lax.psum_scatter(feed_local, "grp", scatter_dimension=0, tiled=True)
+
+    group_rank = lax.axis_index(dp)
+    groups = lax.axis_size(dp)
     bits = [1 << k for k in range(groups.bit_length() - 1)]
     block_rows = parts * weight_rows
     even = block_rows % 16 == 0
@@ -570,32 +597,42 @@
             for v in (group_rank % 2, 1 - group_rank % 2)
         )
 
-    arrived[3] = around(after(partials[3], far), parts - 3)
-
     def swapped(values_in, bit):
-        return lax.ppermute(values_in, "dp", [(s, s ^ bit) for s in range(groups)])
-
-    def halved(blocks, order):
-        for k, bit in enumerate(order):
-            size = blocks.shape[0]
-            at = sorted(order[k:]).index(bit)
-            view = blocks.reshape((size >> (at + 1), 2, 1 << at) + blocks.shape[1:])
-            own = (group_rank // bit) % 2
-            kept = lax.dynamic_index_in_dim(view, own, 1, keepdims=False)
-            sent = lax.dynamic_index_in_dim(view, 1 - own, 1, keepdims=False)
-            got = swapped(sent.astype(bf16), bit)
-            blocks = (kept.astype(f32) + got.astype(f32)).reshape((size // 2,) + blocks.shape[1:])
-        return blocks
-
+        return lax.ppermute(values_in, dp, [(s, s ^ bit) for s in range(groups)])
+
+    def halved(blocks, order, k):
+        bit = order[k]
+        size = blocks.shape[0]
+        at = sorted(order[k:]).index(bit)
+        view = blocks.reshape((size >> (at + 1), 2, 1 << at) + blocks.shape[1:])
+        own = (group_rank // bit) % 2
+        kept = lax.dynamic_index_in_dim(view, own, 1, keepdims=False)
+        sent = lax.dynamic_index_in_dim(view, 1 - own, 1, keepdims=False)
+        got = swapped(sent.astype(bf16), bit)
+        return (kept.astype(f32) + got.astype(f32)).reshape((size // 2,) + blocks.shape[1:])
+
+    def delivered(k):
+        part = lax.dynamic_index_in_dim(
+            feed_half, (core + far_half + k) % 2, 0, keepdims=False
+        )
+        return lax.ppermute(
+            part, ("core", "zh"), [(2 * s + a, 2 * (s ^ a ^ k) + s) for s in range(2) for a in range(2)]
+        )
+
+    feed_half = feed_half.reshape((2, -1) + feed_half.shape[1:])
     blocks = keep.astype(f32) + swapped(send, 1).astype(f32)
-    blocks, arrived[3] = after((blocks, arrived[3]))
-    arrived[2] = around(after(partials[2], blocks), parts - 2)
     blocks = blocks.reshape(groups // 2, block_rows, -1)
     cut = QW + 2 * LANES
-    attention_block = jnp.concatenate(
-        [halved(blocks[:, :, :cut], bits[1:])[0], halved(blocks[:, :, cut:], bits[:0:-1])[0]], axis=1
-    ).astype(bf16)
-    attention_block, arrived[2] = after((attention_block, arrived[2]))
+    sides = [blocks[:, :, :cut], blocks[:, :, cut:]]
+    orders = [bits[1:], bits[:0:-1]]
+    for k in range(len(bits) - 1):
+        sides = [halved(side, order, k) for side, order in zip(sides, orders)]
+        if k == len(bits) - 3:
+            sides, feed_half = after((sides, feed_half))
+            feed_first = delivered(0)
+    sides, feed_first = after((sides, feed_first))
+    attention_block = jnp.concatenate([side[0] for side in sides], axis=1).astype(bf16)
+    feed_last = delivered(1)
     attention_block = attention_block.reshape(parts, weight_rows, -1)
 
     def block_for(steps):
@@ -607,9 +644,9 @@
     for d in range(1, parts):
         sums = sums + around(block_for(d), d).astype(f32)
 
-    total = middle + partials[0]
-    for d in range(1, parts):
-        total = total + arrived[d].astype(f32)
+    feed_sum = feed_first.astype(f32) + feed_last.astype(f32)
+
+    total = middle + partials[0] + out_near.astype(f32) + jnp.stack(out_beside).astype(f32)
 
     edge = 2 * QW + 2 * KW
     return (
@@ -631,20 +668,26 @@
 
 
 def solution(mesh):
-    both = ("dp", "ctx")
-    rows = P(both, None)
-    line = P(both)
-    tokens = P("dp", None, None, "ctx", None)
+    groups, parts = mesh.devices.shape
+    split = jax.sharding.Mesh(
+        mesh.devices.reshape(groups // 2, 2, parts // 2, 2), ("grp", "core", "zh", "zb")
+    )
+    dp = ("grp", "core")
+    ctx = ("zh", "zb")
+    rows = P(dp + ctx, None)
+    line = P(dp + ctx)
+    tokens = P(dp, None, None, ctx, None)
+    up = P(dp, ctx)
     return jax.shard_map(
         body,
-        mesh=mesh,
+        mesh=split,
         in_specs=(
-            tokens, P("dp", None, None, None), tokens, line, rows, line, rows, line, rows, line,
-            rows, line, P("dp", "ctx"), P("dp", "ctx"), P("ctx", "dp"),
+            tokens, P(dp, None, None, None), tokens, line, rows, line, rows, line, rows, line,
+            rows, line, up, up, P(ctx, dp),
         ),
         out_specs=(
             tokens, tokens, line, rows, line, rows, line, rows, line, rows, line,
-            P("dp", "ctx"), P("dp", "ctx"), P("ctx", "dp"),
+            up, up, P(ctx, dp),
         ),
         check_vma=False,
     )

time: 461 us -> 395 us (0.86)
  starting transfers between devices: 107 us -> 76.3 us
  waiting for transfers between devices: 154 us -> 129 us
    ppermute x44 -> x39, waiting for transfers between devices: 154 us -> 120 us  [the longest x17 61.1 us: other(): return lax.ppermute(values_in, axis, [(0, 1), (1, 0)])]
    ppermute x44 -> x39, starting transfers between devices: 107 us -> 76.2 us  [the longest x6 33 us: around(): lax.ppermute(values_in, ctx, [(s, (s + steps) % parts) for s in range(par...]
    all_gather x2 -> x3, waiting for transfers between devices: 0.01 us -> 8.83 us  [the longest x1 8.19 us: body(): first_set = lax.all_gather(first_block, dp, axis=0, tiled=True)]
    unnamed x93 -> x84, local copies, waits for them, and re-layouts: 9.82 us -> 6.37 us
    pallas_call x3 -> x4, Pallas kernels: 57.7 us -> 56.1 us  [the longest x2 48.5 us: feed(): pl.pallas_call(functools.partial(feed_kernel, parts=parts, micro=micro, k...]
  transfers between devices with their start and end apart: 47 -> 43, of which waited for: 27 -> 15; matrix products, arithmetic and copies ran while one was open for 5% -> 5% of each run, Pallas kernels for 31% -> 35%
where the time goes in v3:
time: 395 us; the launch traced here: 390 us
  Pallas kernels  139 us (35%)
  waiting for transfers between devices  129 us (33%)
  starting transfers between devices  76.3 us (19%)
  local copies, waits for them, and re-layouts  16.1 us (4%)
  other arithmetic  15.8 us (4%)
  between operations  14.9 us (4%)
    ppermute x17, waiting for transfers between devices, other(): return lax.ppermute(values_in, axis, [(0, 1), (1, 0)])  61.1 us
    pallas_call x2, Pallas kernels, feed(): pl.pallas_call(functools.partial(feed_kernel, parts=parts, micro=micro, k...  48.5 us
    ppermute x6, starting transfers between devices, around(): lax.ppermute(values_in, ctx, [(s, (s + steps) % parts) for s in range(par...  33 us
    pallas_call x2, Pallas kernels, attend_back(): pl.pallas_call(functools.partial(attend_back_kernel, count=len(gs)), grid...  27.1 us
    pallas_call x1, Pallas kernels, weights(): pl.pallas_call(functools.partial(weights_kernel, split=split), grid=(widt...  25.4 us
    ppermute x17, starting transfers between devices, other(): return lax.ppermute(values_in, axis, [(0, 1), (1, 0)])  20.1 us
    pallas_call x2, Pallas kernels, attend(): pl.pallas_call(attend_kernel, grid=(nq,), in_specs=[pl.BlockSpec(memory_s...  18.5 us
    ppermute x5, waiting for transfers between devices, swapped(): return lax.ppermute(values_in, dp, [(s, s ^ bit) for s in range(groups)])  17.4 us
  transfers between devices with their start and end apart: 43, of which 15 were waited for; matrix products, arithmetic and copies ran while one was open for 5% of the time, Pallas kernels for 35%

profile of v3, /device:TPU:0, one launch (start us, length us, event | category | flops | bytes accessed | tf_op | source)
XLA Modules:
  0.0 390.5 jit_solution(16377204041507674639)
XLA Ops:
  7.3 2.1 fusion.8
  9.8 5.1 %collective-permute-start = (bf16[28,2176]{1,0:T(8,128)(2,1)S(1)}, bf16[28,2176]{1,0:T(8,128)(2,1)S(1)}, u32[]{:S(2)}, u32[]{:S(2)}) collective-permute-start(bf16[28,2176]{1,0:T(8,128)(2,1)S(1)} %constant_dynamic-update-slice_fusion), channel_id=1, source_target_pairs={{0,3},{1,0},{2,1},{3,2},{4,7},{5,4},{6,5},{7,6},{8,11},{9,8},{10,9... | collective-permute-start | bytes 365576 | tf_op jit(solution)/shard_map/ppermute | solution.py:455
  14.9 1.0 collective-permute-start.2
  15.9 3.1 collective-permute-done
  19.0 7.7 %collective-permute-done.1 = bf16[28,2176]{1,0:T(8,128)(2,1)S(1)} collective-permute-done((bf16[28,2176]{1,0:T(8,128)(2,1)S(1)}, bf16[28,2176]{1,0:T(8,128)(2,1)S(1)}, u32[]{:S(2)}, u32[]{:S(2)}) %collective-permute-start.1) | collective-permute-done | bytes 121888 | tf_op jit(solution)/shard_map/ppermute | solution.py:455
  27.0 0.9 reshape.217
  27.9 2.6 collective-permute-start.3
  30.6 37.2 %collective-permute-done.3 = bf16[112,3840]{1,0:T(8,128)(2,1)} collective-permute-done((bf16[112,3840]{1,0:T(8,128)(2,1)S(1)}, bf16[112,3840]{1,0:T(8,128)(2,1)}, u32[]{:S(2)}, u32[]{:S(2)}) %collective-permute-start.3) | collective-permute-done | bytes 860192 | tf_op jit(solution)/shard_map/ppermute | solution.py:458
  68.5 21.7 %collective-permute-done.5.refs_6_ = bf16[2,256,896]{2,1,0:T(8,128)(2,1)S(1)} collective-permute-done((bf16[2,256,896]{2,1,0:T(8,128)(2,1)S(1)}, bf16[2,256,896]{2,1,0:T(8,128)(2,1)S(1)}, u32[]{:S(2)}, u32[]{:S(2)}) %collective-permute-start.5) | collective-permute-done | bytes 917536 | tf_op jit(solution)/shard_map/ppermute | solution.py:458
  90.2 1.0 fusion.21
  91.2 1.3 pad_maximum_fusion
  92.4 1.0 fusion.16.spread_ref
  93.4 8.2 %all-gather.6.cloned.1.call-done.wkv_ref.ws_ref.wq_ref.wo_ref = bf16[896,2176]{1,0:T(8,128)(2,1)} async-done(((bf16[112,2176]{1,0:T(8,128)(2,1)}), bf16[896,2176]{1,0:T(8,128)(2,1)}) %all-gather.6.cloned.1.call-update) | async-done | bytes 3899408 | tf_op jit(solution)/shard_map/all_gather | solution.py:495
  101.7 3.3 pairs.1
  105.0 3.4 collective-permute-start.7
  108.5 4.8 %collective-permute-start.8 = (bf16[2,256,256]{2,1,0:T(8,128)(2,1)}, bf16[2,256,256]{2,1,0:T(8,128)(2,1)S(1)}, u32[]{:S(2)}, u32[]{:S(2)}) collective-permute-start(bf16[2,256,256]{2,1,0:T(8,128)(2,1)} %get-tuple-element.138.kv0_ref), channel_id=1, source_target_pairs={{0,2},{1,3},{4,6},{5,7},{8,10},{9,11},{12,14},{13,15},{16,18},{17,... | collective-permute-start | bytes 786440 | tf_op jit(solution)/shard_map/ppermute | solution.py:526
  113.3 4.3 %queries.1.rq_ref = bf16[2,256,896]{2,1,0:T(8,128)(2,1)} custom-call(bf16[2,256,896]{2,1,0:T(8,128)(2,1)} %get-tuple-element.136.n1_ref, bf16[896,2176]{1,0:T(8,128)(2,1)} %all-gather.6.cloned.1.call-done.wkv_ref.ws_ref.wq_ref.wo_ref, f32[8,896]{1,0:T(8,128)} %get-tuple-element.137.rows_ref, f32[2,256,128]{2,1,0:T(8,128)} %get-tuple-element.134.cos_ref, ...), custom_call_target="tpu_custom_call" | custom-call | flops 1 | bytes 1 | tf_op jit(solution)/shard_map/queries/pallas_call | solution.py:65
  118.2 2.2 collective-permute-done.8.kv2_ref
  121.1 9.2 %attend.2 = (bf16[256,896]{1,0:T(8,128)(2,1)}, bf16[2,256,896]{2,1,0:T(8,128)(2,1)}, f32[2,256,896]{2,1,0:T(8,128)}, f32[2,2,16,128]{3,2,1,0:T(8,128)}) custom-call(s32[1]{0:T(128)} %bitcast.base_ref, bf16[2,256,896]{2,1,0:T(8,128)(2,1)} %queries.1.rq_ref, bf16[2,256,256]{2,1,0:T(8,128)(2,1)} %get-tuple-element.138.kv0_ref, bf16[2,256,256]{2,1,0:T(8,128)(2,1)} %copy-done.4, ...), custom_call_target="tpu_custom_call" | custom-call | flops 1 | bytes 1 | tf_op jit(solution)/shard_map/attend/pallas_call | solution.py:144
  130.4 7.1 %collective-permute-start.10 = (bf16[256,896]{1,0:T(8,128)(2,1)}, bf16[256,896]{1,0:T(8,128)(2,1)S(1)}, u32[]{:S(2)}, u32[]{:S(2)}) collective-permute-start(bf16[256,896]{1,0:T(8,128)(2,1)} %get-tuple-element.153.refs_0_), channel_id=1, source_target_pairs={{0,1},{1,0},{2,3},{3,2},{4,5},{5,4},{6,7},{7,6},{8,9},{9,8},{10,11... | collective-permute-start | bytes 1376264 | tf_op jit(solution)/shard_map/ppermute | solution.py:458
  137.6 9.2 %attend.3 = (bf16[256,896]{1,0:T(8,128)(2,1)}, bf16[2,256,896]{2,1,0:T(8,128)(2,1)}, f32[2,256,896]{2,1,0:T(8,128)}, f32[2,2,16,128]{3,2,1,0:T(8,128)}) custom-call(s32[1]{0:T(128)} %bitcast.base_ref, bf16[2,256,896]{2,1,0:T(8,128)(2,1)} %queries.1.rq_ref, ...), custom_call_target="tpu_custom_call", output_to_operand_aliasing={{1}: (9, {}), {2}: (10, {}), {3}: (11, {})} | custom-call | flops 1 | bytes 1 | tf_op jit(solution)/shard_map/attend/pallas_call | solution.py:144
  146.8 2.0 collective-permute-done.10.refs_2_
  149.4 1.8 collective-permute-start.12
  152.1 24.2 %feed.2 = (f32[256,896]{1,0:T(8,128)}, bf16[256,896]{1,0:T(8,128)(2,1)}, bf16[256,896]{1,0:T(8,128)(2,1)}, bf16[256,896]{1,0:T(8,128)(2,1)}, f32[2,256,896]{2,1,...) custom-call(s32[1]{0:T(128)} %bitcast.13.own_ref, ...), custom_call_target="tpu_custom_call" | custom-call | flops 1 | bytes 1 | tf_op jit(solution)/shard_map/feed/pallas_call | solution.py:312
  176.3 0.8 collective-permute-start.15
  177.0 1.8 collective-permute-start.16
  179.9 24.3 %feed.3 = (f32[256,896]{1,0:T(8,128)}, bf16[256,896]{1,0:T(8,128)(2,1)}, bf16[256,896]{1,0:T(8,128)(2,1)}, bf16[256,896]{1,0:T(8,128)(2,1)}, f32[2,256,896]{2,1,...) custom-call(s32[1]{0:T(128)} %bitcast.13.own_ref, ...), custom_call_target="tpu_custom_call", output_to_operand_aliasing={{4}: (11, {}), {5}: (12, {}), {6}: (13, {}), {7}: (14, {}),... | custom-call | flops 1 | bytes 1 | tf_op jit(solution)/shard_map/feed/pallas_call | solution.py:312
  204.2 0.9 collective-permute-start.21
  205.6 1.8 collective-permute-start.19
  207.4 25.4 %weights.1 = bf16[896,3840]{1,0:T(8,128)(2,1)} custom-call(bf16[2,2048,896]{2,1,0:T(8,128)(2,1)} %get-tuple-element.175.left_ref, bf16[2048,2560]{1,0:T(8,128)(2,1)} %get-tuple-element.176.pair_ref, bf16[2048,1280]{1,0:T(8,128)(2,1)} %get-tuple-element.177.act_ref), custom_call_target="tpu_custom_call" | custom-call | flops 1 | bytes 1 | tf_op jit(solution)/shard_map/weights/pallas_call | solution.py:403
  232.9 1.0 copy-done.11
  233.9 1.1 copy-done.8
  235.2 1.5 collective-permute-start.23
  236.7 13.4 %attend_back.2 = (bf16[256,256]{1,0:T(8,128)(2,1)}, bf16[256,256]{1,0:T(8,128)(2,1)}, f32[2,256,896]{2,1,0:T(8,128)}, bf16[2,256,896]{2,1,0:T(8,128)(2,1)}, bf16...) custom-call(s32[1]{0:T(128)} %bitcast.base_ref, bf16[2,256,896]{2,1,0:T(8,128)(2,1)} %queries.1.rq_ref, ...), custom_call_target="tpu_custom_call" | custom-call | flops 1 | bytes 1 | tf_op jit(solution)/shard_map/attend_back/pallas_call | solution.py:225
  250.9 1.3 collective-permute-start.25
  252.2 1.3 collective-permute-start.26
  253.5 13.7 %attend_back.3 = (bf16[256,256]{1,0:T(8,128)(2,1)}, bf16[256,256]{1,0:T(8,128)(2,1)}, f32[2,256,896]{2,1,0:T(8,128)}, bf16[2,256,896]{2,1,0:T(8,128)(2,1)}, bf16...) custom-call(s32[1]{0:T(128)} %bitcast.base_ref, ...), custom_call_target="tpu_custom_call", output_to_operand_aliasing={{2}: (17, {}), {3}: (18, {}), {4}: (19, {}), {5}: (20, {}),... | custom-call | flops 1 | bytes 1 | tf_op jit(solution)/shard_map/attend_back/pallas_call | solution.py:225
  267.1 1.3 collective-permute-start.27
  268.4 1.3 collective-permute-start.28
  269.8 5.2 %collective-permute-done.27.refs_2_ = bf16[256,256]{1,0:T(8,128)(2,1)S(1)} collective-permute-done((bf16[256,256]{1,0:T(8,128)(2,1)}, bf16[256,256]{1,0:T(8,128)(2,1)S(1)}, u32[]{:S(2)}, u32[]{:S(2)}) %collective-permute-start.27) | collective-permute-done | bytes 131104 | tf_op jit(solution)/shard_map/ppermute | solution.py:574
  275.0 6.5 %collective-permute-done.28.refs_3_ = bf16[256,256]{1,0:T(8,128)(2,1)S(1)} collective-permute-done((bf16[256,256]{1,0:T(8,128)(2,1)}, bf16[256,256]{1,0:T(8,128)(2,1)S(1)}, u32[]{:S(2)}, u32[]{:S(2)}) %collective-permute-start.28) | collective-permute-done | bytes 131104 | tf_op jit(solution)/shard_map/ppermute | solution.py:574
  282.2 11.5 %finish.1 = (f32[2,256,896]{2,1,0:T(8,128)}, bf16[448,2176]{1,0:T(8,128)(2,1)}, bf16[448,2176]{1,0:T(8,128)(2,1)}) custom-call(s32[1]{0:T(128)} %bitcast.20.bit_ref, bf16[2,256,896]{2,1,0:T(8,128)(2,1)} %get-tuple-element.220.dq_ref, f32[2,256,256]{2,1,0:T(8,128)} %get-tuple-element.221.own_ref, f32[2,256,128]{2,1,0:T(8,128)} %get-tuple-element.134.cos_ref, ...), custom_call_target="tpu_custom_call" | custom-call | flops 1 | bytes 1 | tf_op jit(solution)/shard_map/finish/pallas_call | solution.py:382
  293.8 4.1 %collective-permute-done.29 = bf16[448,2176]{1,0:T(8,128)(2,1)S(1)} collective-permute-done((bf16[448,2176]{1,0:T(8,128)(2,1)}, bf16[448,2176]{1,0:T(8,128)(2,1)S(1)}, u32[]{:S(2)}, u32[]{:S(2)}) %collective-permute-start.29) | collective-permute-done | bytes 1949728 | tf_op jit(solution)/shard_map/ppermute | solution.py:601
  297.9 1.9 convert_add_fusion
  300.2 1.2 copy-done.3
  301.5 0.8 fusion.13
  302.3 1.3 collective-permute-start.31
  303.7 0.8 collective-permute-start.30
  304.5 13.3 %collective-permute-done.31 = bf16[1,2,112,1024]{3,2,1,0:T(8,128)(2,1)S(1)} collective-permute-done((bf16[1,2,112,1024]{3,2,1,0:T(8,128)(2,1)}, bf16[1,2,112,1024]{3,2,1,0:T(8,128)(2,1)S(1)}, u32[]{:S(2)}, u32[]{:S(2)}) %collective-permute-start.31) | collective-permute-done | bytes 458784 | tf_op jit(solution)/shard_map/ppermute | solution.py:601
  317.8 2.3 fusion.6
  320.1 1.1 fusion.4
  321.9 1.2 fusion.20
  323.1 1.6 collective-permute-start.33
  324.7 1.5 dynamic-slice_bitcast_fusion
  326.2 1.6 collective-permute-start.34
  327.8 2.7 fusion.5
  330.5 3.7 collective-permute-start.38
  334.7 7.4 %collective-permute-start.37 = (bf16[28,2176]{1,0:T(8,128)(2,1)S(1)}, bf16[28,2176]{1,0:T(8,128)(2,1)S(1)}, u32[]{:S(2)}, u32[]{:S(2)}) collective-permute-start(bf16[28,2176]{1,0:T(8,128)(2,1)S(1)} %get-tuple-element.307), channel_id=1, source_target_pairs={{0,3},{1,0},{2,1},{3,2},{4,7},{5,4},{6,5},{7,6},{8,11},{9,8},{10,9... | collective-permute-start | bytes 365576 | tf_op jit(solution)/shard_map/ppermute | solution.py:455
  342.0 17.5 %collective-permute-start.36 = (bf16[28,2176]{1,0:T(8,128)(2,1)S(1)}, bf16[28,2176]{1,0:T(8,128)(2,1)S(1)}, u32[]{:S(2)}, u32[]{:S(2)}) collective-permute-start(bf16[28,2176]{1,0:T(8,128)(2,1)S(1)} %get-tuple-element.308), channel_id=1, source_target_pairs={{0,2},{1,3},{2,0},{3,1},{4,6},{5,7},{6,4},{7,5},{8,10},{9,11},{10,... | collective-permute-start | bytes 365576 | tf_op jit(solution)/shard_map/ppermute | solution.py:455
  359.6 1.9 collective-permute-start.35
  361.5 16.4 %collective-permute-done.38 = bf16[112,3840]{1,0:T(8,128)(2,1)} collective-permute-done((bf16[112,3840]{1,0:T(8,128)(2,1)S(1)}, bf16[112,3840]{1,0:T(8,128)(2,1)}, u32[]{:S(2)}, u32[]{:S(2)}) %collective-permute-start.38) | collective-permute-done | bytes 860192 | tf_op jit(solution)/shard_map/ppermute | solution.py:618
  378.0 1.6 convert_add_fusion.1
  379.5 1.2 slice_bitcast_fusion
  380.9 0.7 slice_reduce_fusion
  (164 shorter events, 11.0 us)
Async XLA Ops:
  7.2 2.3 copy-start.30
  7.2 2.3 copy-start.31
  7.2 2.3 copy-start.32
  7.2 2.5 copy-start.25
  7.2 2.5 copy-start.26
  7.3 2.5 copy-start.28
  7.3 2.5 copy-start.29
  7.3 60.5 %all-gather.4.cloned.1.call-start = ((), (), s32[]{:S(2)}) async-start(), calls=%async_computation.1 | async-start | bytes 7741440 | tf_op jit(solution)/shard_map/all_gather | solution.py:481
  9.5 92.2 %all-gather.6.cloned.1.call-start = ((), (), s32[]{:S(2)}) async-start(), calls=%async_computation.2 | async-start | bytes 4386816 | tf_op jit(solution)/shard_map/all_gather | solution.py:495
  9.8 9.2 %collective-permute-start = (bf16[28,2176]{1,0:T(8,128)(2,1)S(1)}, bf16[28,2176]{1,0:T(8,128)(2,1)S(1)}, u32[]{:S(2)}, u32[]{:S(2)}) collective-permute-start(bf16[28,2176]{1,0:T(8,128)(2,1)S(1)} %constant_dynamic-update-slice_fusion), channel_id=1, source_target_pairs={{0,3},{1,0},{2,1},{3,2},{4,7},{5,4},{6,5},{7,6},{8,11},{9,8},{10,9... | collective-permute-start | bytes 365576 | tf_op jit(solution)/shard_map/ppermute | solution.py:455
  14.9 11.8 %collective-permute-start.1 = (bf16[28,2176]{1,0:T(8,128)(2,1)S(1)}, bf16[28,2176]{1,0:T(8,128)(2,1)S(1)}, u32[]{:S(2)}, u32[]{:S(2)}) collective-permute-start(bf16[28,2176]{1,0:T(8,128)(2,1)S(1)} %constant_dynamic-update-slice_fusion), channel_id=1, source_target_pairs={{0,2},{1,3},{2,0},{3,1},{4,6},{5,7},{6,4},{7,5},{8,10},{9,11},{10,... | collective-permute-start | bytes 365576 | tf_op jit(solution)/shard_map/ppermute | solution.py:455
  14.9 11.8 %collective-permute-start.2 = (bf16[28,2176]{1,0:T(8,128)(2,1)S(1)}, bf16[28,2176]{1,0:T(8,128)(2,1)S(1)}, u32[]{:S(2)}, u32[]{:S(2)}) collective-permute-start(bf16[28,2176]{1,0:T(8,128)(2,1)S(1)} %constant_dynamic-update-slice_fusion), channel_id=1, source_target_pairs={{0,1},{1,2},{2,3},{3,0},{4,5},{5,6},{6,7},{7,4},{8,9},{9,10},{10,1... | collective-permute-start | bytes 365576 | tf_op jit(solution)/shard_map/ppermute | solution.py:455
  26.8 41.0 %copy-start.1 = (bf16[1,2,1,256,896]{4,3,2,1,0:T(8,128)(2,1)S(1)}, bf16[1,2,1,256,896]{4,3,2,1,0:T(8,128)(2,1)}, u32[]{:S(2)}) copy-start(bf16[1,2,1,256,896]{4,3,2,1,0:T(8,128)(2,1)} %param.17) | copy-start | bytes 2752516
  26.8 41.1 %copy-start.27 = (s32[1,2,1,1024]{3,2,1,0:T(1,128)S(1)}, s32[1,2,1,1024]{3,2,1,0:T(1,128)}, u32[]{:S(2)}) copy-start(s32[1,2,1,1024]{3,2,1,0:T(1,128)} %param.16) | copy-start | bytes 24580
  27.9 39.8 %collective-permute-start.3 = (bf16[112,3840]{1,0:T(8,128)(2,1)S(1)}, bf16[112,3840]{1,0:T(8,128)(2,1)}, u32[]{:S(2)}, u32[]{:S(2)}) collective-permute-start(bf16[112,3840]{1,0:T(8,128)(2,1)S(1)} %copy-done.9), channel_id=1, source_target_pairs={{0,2},{2,0},{1,3},{3,1},{4,6},{6,4},{5,7},{7,5},{8,10},{10,8},{9,1... | collective-permute-start | bytes 2580488 | tf_op jit(solution)/shard_map/ppermute | solution.py:458
  67.8 84.2 %all-gather.8.cloned.1.call-start = ((), (), s32[]{:S(2)}) async-start(), calls=%async_computation.3 | async-start | bytes 7741440 | tf_op jit(solution)/shard_map/all_gather | solution.py:521
  67.8 22.3 %collective-permute-start.5 = (bf16[2,256,896]{2,1,0:T(8,128)(2,1)S(1)}, bf16[2,256,896]{2,1,0:T(8,128)(2,1)S(1)}, u32[]{:S(2)}, u32[]{:S(2)}) collective-permute-start(bf16[2,256,896]{2,1,0:T(8,128)(2,1)S(1)} %bitcast.104), channel_id=1, source_target_pairs={{0,1},{1,0},{2,3},{3,2},{4,5},{5,4},{6,7},{7,6},{8,9},{9,8},{10,11... | collective-permute-start | bytes 2752520 | tf_op jit(solution)/shard_map/ppermute | solution.py:458
  68.4 25.0 %collective-permute-start.4 = (bf16[2,256,896]{2,1,0:T(8,128)(2,1)S(1)}, bf16[2,256,896]{2,1,0:T(8,128)(2,1)S(1)}, u32[]{:S(2)}, u32[]{:S(2)}) collective-permute-start(bf16[2,256,896]{2,1,0:T(8,128)(2,1)S(1)} %bitcast.105), channel_id=1, source_target_pairs={{0,4},{4,0},{1,5},{5,1},{2,6},{6,2},{3,7},{7,3},{8,12},{12,8},{9,1... | collective-permute-start | bytes 2752520 | tf_op jit(solution)/shard_map/ppermute | solution.py:458
  90.1 14.9 %copy-start.6 = (bf16[2,256,896]{2,1,0:T(8,128)(2,1)}, bf16[2,256,896]{2,1,0:T(8,128)(2,1)S(1)}, u32[]{:S(2)}) copy-start(bf16[2,256,896]{2,1,0:T(8,128)(2,1)S(1)} %collective-permute-done.5.refs_6_) | copy-start | bytes 2752516
  90.1 3.3 collective-permute-start.6
  93.4 11.6 %copy-start.7 = (bf16[2,256,896]{2,1,0:T(8,128)(2,1)}, bf16[2,256,896]{2,1,0:T(8,128)(2,1)S(1)}, u32[]{:S(2)}) copy-start(bf16[2,256,896]{2,1,0:T(8,128)(2,1)S(1)} %collective-permute-done.4.refs_5_) | copy-start | bytes 2752516
  101.6 219.6 %reduce-scatter.2.cloned.1.call-start = ((), (), s32[]{:S(2)}) async-start(), calls=%async_computation.4 | async-start | bytes 8601600 | tf_op jit(solution)/shard_map/reduce_scatter | solution.py:580
  105.0 13.2 %collective-permute-start.7 = (bf16[2,256,256]{2,1,0:T(8,128)(2,1)}, bf16[2,256,256]{2,1,0:T(8,128)(2,1)S(1)}, u32[]{:S(2)}, u32[]{:S(2)}) collective-permute-start(bf16[2,256,256]{2,1,0:T(8,128)(2,1)} %get-tuple-element.138.kv0_ref), channel_id=1, source_target_pairs={{0,1},{1,2},{2,3},{4,5},{5,6},{6,7},{8,9},{9,10},{10,11},{12,13},{... | collective-permute-start | bytes 786440 | tf_op jit(solution)/shard_map/ppermute | solution.py:526
  108.5 11.9 %collective-permute-start.8 = (bf16[2,256,256]{2,1,0:T(8,128)(2,1)}, bf16[2,256,256]{2,1,0:T(8,128)(2,1)S(1)}, u32[]{:S(2)}, u32[]{:S(2)}) collective-permute-start(bf16[2,256,256]{2,1,0:T(8,128)(2,1)} %get-tuple-element.138.kv0_ref), channel_id=1, source_target_pairs={{0,2},{1,3},{4,6},{5,7},{8,10},{9,11},{12,14},{13,15},{16,18},{17,... | collective-permute-start | bytes 786440 | tf_op jit(solution)/shard_map/ppermute | solution.py:526
  130.3 16.5 %collective-permute-start.9 = (bf16[256,896]{1,0:T(8,128)(2,1)}, bf16[256,896]{1,0:T(8,128)(2,1)S(1)}, u32[]{:S(2)}, u32[]{:S(2)}) collective-permute-start(bf16[256,896]{1,0:T(8,128)(2,1)} %get-tuple-element.153.refs_0_), channel_id=1, source_target_pairs={{0,4},{4,0},{1,5},{5,1},{2,6},{6,2},{3,7},{7,3},{8,12},{12,8},{9,1... | collective-permute-start | bytes 1376264 | tf_op jit(solution)/shard_map/ppermute | solution.py:458
  130.4 18.4 %collective-permute-start.10 = (bf16[256,896]{1,0:T(8,128)(2,1)}, bf16[256,896]{1,0:T(8,128)(2,1)S(1)}, u32[]{:S(2)}, u32[]{:S(2)}) collective-permute-start(bf16[256,896]{1,0:T(8,128)(2,1)} %get-tuple-element.153.refs_0_), channel_id=1, source_target_pairs={{0,1},{1,0},{2,3},{3,2},{4,5},{5,4},{6,7},{7,6},{8,9},{9,8},{10,11... | collective-permute-start | bytes 1376264 | tf_op jit(solution)/shard_map/ppermute | solution.py:458
  146.8 5.1 %copy-start.18 = (bf16[256,896]{1,0:T(8,128)(2,1)}, bf16[256,896]{1,0:T(8,128)(2,1)S(1)}, u32[]{:S(2)}) copy-start(bf16[256,896]{1,0:T(8,128)(2,1)S(1)} %collective-permute-done.9.refs_1_) | copy-start | bytes 1376260
  148.9 3.1 copy-start.19
  148.9 2.4 collective-permute-start.14
  148.9 29.9 %collective-permute-start.11 = (bf16[256,896]{1,0:T(8,128)(2,1)}, bf16[256,896]{1,0:T(8,128)(2,1)S(1)}, u32[]{:S(2)}, u32[]{:S(2)}) collective-permute-start(bf16[256,896]{1,0:T(8,128)(2,1)} %get-tuple-element.146.refs_0_), channel_id=1, source_target_pairs={{0,4},{4,0},{1,5},{5,1},{2,6},{6,2},{3,7},{7,3},{8,12},{12,8},{9,1... | collective-permute-start | bytes 1376264 | tf_op jit(solution)/shard_map/ppermute | solution.py:458
  149.4 29.4 %collective-permute-start.12 = (bf16[256,896]{1,0:T(8,128)(2,1)}, bf16[256,896]{1,0:T(8,128)(2,1)S(1)}, u32[]{:S(2)}, u32[]{:S(2)}) collective-permute-start(bf16[256,896]{1,0:T(8,128)(2,1)} %get-tuple-element.146.refs_0_), channel_id=1, source_target_pairs={{0,1},{1,0},{2,3},{3,2},{4,5},{5,4},{6,7},{7,6},{8,9},{9,8},{10,11... | collective-permute-start | bytes 1376264 | tf_op jit(solution)/shard_map/ppermute | solution.py:458
  151.1 27.7 %collective-permute-start.13 = (bf16[256,896]{1,0:T(8,128)(2,1)}, bf16[256,896]{1,0:T(8,128)(2,1)S(1)}, u32[]{:S(2)}, u32[]{:S(2)}) collective-permute-start(bf16[256,896]{1,0:T(8,128)(2,1)} %get-tuple-element.146.refs_0_), channel_id=1, source_target_pairs={{0,5},{1,4},{4,1},{5,0},{2,7},{3,6},{6,3},{7,2},{8,13},{9,12},{12,... | collective-permute-start | bytes 1376264 | tf_op jit(solution)/shard_map/ppermute | solution.py:461
  176.3 28.9 %collective-permute-start.15 = (bf16[256,896]{1,0:T(8,128)(2,1)}, bf16[256,896]{1,0:T(8,128)(2,1)S(1)}, u32[]{:S(2)}, u32[]{:S(2)}) collective-permute-start(bf16[256,896]{1,0:T(8,128)(2,1)} %get-tuple-element.165), channel_id=1, source_target_pairs={{0,4},{4,0},{1,5},{5,1},{2,6},{6,2},{3,7},{7,3},{8,12},{12,8},{9,1... | collective-permute-start | bytes 1376264 | tf_op jit(solution)/shard_map/ppermute | solution.py:458
  177.0 28.6 %collective-permute-start.16 = (bf16[256,896]{1,0:T(8,128)(2,1)}, bf16[256,896]{1,0:T(8,128)(2,1)S(1)}, u32[]{:S(2)}, u32[]{:S(2)}) collective-permute-start(bf16[256,896]{1,0:T(8,128)(2,1)} %get-tuple-element.166), channel_id=1, source_target_pairs={{0,1},{1,0},{2,3},{3,2},{4,5},{5,4},{6,7},{7,6},{8,9},{9,8},{10,11... | collective-permute-start | bytes 1376264 | tf_op jit(solution)/shard_map/ppermute | solution.py:458
  178.8 28.6 %collective-permute-start.17 = (bf16[256,896]{1,0:T(8,128)(2,1)}, bf16[256,896]{1,0:T(8,128)(2,1)}, u32[]{:S(2)}, u32[]{:S(2)}) collective-permute-start(bf16[256,896]{1,0:T(8,128)(2,1)} %get-tuple-element.167), channel_id=1, source_target_pairs={{0,5},{1,4},{4,1},{5,0},{2,7},{3,6},{6,3},{7,2},{8,13},{9,12},{12,... | collective-permute-start | bytes 1376264 | tf_op jit(solution)/shard_map/ppermute | solution.py:461
  204.2 28.7 %collective-permute-start.21 = (bf16[2,256,896]{2,1,0:T(8,128)(2,1)}, bf16[2,256,896]{2,1,0:T(8,128)(2,1)S(1)}, u32[]{:S(2)}, u32[]{:S(2)}) collective-permute-start(bf16[2,256,896]{2,1,0:T(8,128)(2,1)} %get-tuple-element.178), channel_id=1, source_target_pairs={{0,4},{4,0},{1,5},{5,1},{2,6},{6,2},{3,7},{7,3},{8,12},{12,8},{9,1... | collective-permute-start | bytes 2752520 | tf_op jit(solution)/shard_map/ppermute | solution.py:458
  205.1 27.7 %collective-permute-start.22 = (bf16[2,256,896]{2,1,0:T(8,128)(2,1)}, bf16[2,256,896]{2,1,0:T(8,128)(2,1)S(1)}, u32[]{:S(2)}, u32[]{:S(2)}) collective-permute-start(bf16[2,256,896]{2,1,0:T(8,128)(2,1)} %get-tuple-element.179), channel_id=1, source_target_pairs={{0,4},{4,0},{1,5},{5,1},{2,6},{6,2},{3,7},{7,3},{8,12},{12,8},{9,1... | collective-permute-start | bytes 2752520 | tf_op jit(solution)/shard_map/ppermute | solution.py:458
  205.2 27.6 %copy-start.15 = (bf16[256,896]{1,0:T(8,128)(2,1)}, bf16[256,896]{1,0:T(8,128)(2,1)S(1)}, u32[]{:S(2)}) copy-start(bf16[256,896]{1,0:T(8,128)(2,1)S(1)} %collective-permute-done.15.refs_1_) | copy-start | bytes 1376260
  205.2 27.6 %collective-permute-start.18 = (bf16[256,896]{1,0:T(8,128)(2,1)}, bf16[256,896]{1,0:T(8,128)(2,1)S(1)}, u32[]{:S(2)}, u32[]{:S(2)}) collective-permute-start(bf16[256,896]{1,0:T(8,128)(2,1)} %get-tuple-element.169), channel_id=1, source_target_pairs={{0,4},{4,0},{1,5},{5,1},{2,6},{6,2},{3,7},{7,3},{8,12},{12,8},{9,1... | collective-permute-start | bytes 1376264 | tf_op jit(solution)/shard_map/ppermute | solution.py:458
  205.6 27.2 %copy-start.16 = (bf16[256,896]{1,0:T(8,128)(2,1)}, bf16[256,896]{1,0:T(8,128)(2,1)S(1)}, u32[]{:S(2)}) copy-start(bf16[256,896]{1,0:T(8,128)(2,1)S(1)} %collective-permute-done.16.refs_2_) | copy-start | bytes 1376260
  205.6 27.2 %collective-permute-start.19 = (bf16[256,896]{1,0:T(8,128)(2,1)}, bf16[256,896]{1,0:T(8,128)(2,1)}, u32[]{:S(2)}, u32[]{:S(2)}) collective-permute-start(bf16[256,896]{1,0:T(8,128)(2,1)} %get-tuple-element.170), channel_id=1, source_target_pairs={{0,1},{1,0},{2,3},{3,2},{4,5},{5,4},{6,7},{7,6},{8,9},{9,8},{10,11... | collective-permute-start | bytes 1376264 | tf_op jit(solution)/shard_map/ppermute | solution.py:458
  207.4 25.4 %collective-permute-start.20 = (bf16[256,896]{1,0:T(8,128)(2,1)}, bf16[256,896]{1,0:T(8,128)(2,1)}, u32[]{:S(2)}, u32[]{:S(2)}) collective-permute-start(bf16[256,896]{1,0:T(8,128)(2,1)} %get-tuple-element.171), channel_id=1, source_target_pairs={{0,5},{1,4},{4,1},{5,0},{2,7},{3,6},{6,3},{7,2},{8,13},{9,12},{12,... | collective-permute-start | bytes 1376264 | tf_op jit(solution)/shard_map/ppermute | solution.py:461
  235.2 14.9 %collective-permute-start.23 = (bf16[256,896]{1,0:T(8,128)(2,1)S(1)}, bf16[256,896]{1,0:T(8,128)(2,1)S(1)}, u32[]{:S(2)}, u32[]{:S(2)}) collective-permute-start(bf16[256,896]{1,0:T(8,128)(2,1)S(1)} %fusion.11), channel_id=1, source_target_pairs={{0,1},{1,0},{2,3},{3,2},{4,5},{5,4},{6,7},{7,6},{8,9},{9,8},{10,11... | collective-permute-start | bytes 1376264 | tf_op jit(solution)/shard_map/ppermute | solution.py:458
  250.2 16.9 %collective-permute-start.24 = (bf16[256,896]{1,0:T(8,128)(2,1)S(1)}, bf16[256,896]{1,0:T(8,128)(2,1)}, u32[]{:S(2)}, u32[]{:S(2)}) collective-permute-start(bf16[256,896]{1,0:T(8,128)(2,1)S(1)} %fusion.12), channel_id=1, source_target_pairs={{0,1},{1,0},{2,3},{3,2},{4,5},{5,4},{6,7},{7,6},{8,9},{9,8},{10,11... | collective-permute-start | bytes 1376264 | tf_op jit(solution)/shard_map/ppermute | solution.py:458
  250.9 18.9 %collective-permute-start.25 = (bf16[256,256]{1,0:T(8,128)(2,1)}, bf16[256,256]{1,0:T(8,128)(2,1)S(1)}, u32[]{:S(2)}, u32[]{:S(2)}) collective-permute-start(bf16[256,256]{1,0:T(8,128)(2,1)} %get-tuple-element.226), channel_id=1, source_target_pairs={{1,0},{2,1},{3,2},{5,4},{6,5},{7,6},{9,8},{10,9},{11,10},{13,12},{... | collective-permute-start | bytes 393224 | tf_op jit(solution)/shard_map/ppermute | solution.py:574
  252.2 17.6 %collective-permute-start.26 = (bf16[256,256]{1,0:T(8,128)(2,1)}, bf16[256,256]{1,0:T(8,128)(2,1)S(1)}, u32[]{:S(2)}, u32[]{:S(2)}) collective-permute-start(bf16[256,256]{1,0:T(8,128)(2,1)} %get-tuple-element.227), channel_id=1, source_target_pairs={{2,0},{3,1},{6,4},{7,5},{10,8},{11,9},{14,12},{15,13},{18,16},{19,... | collective-permute-start | bytes 393224 | tf_op jit(solution)/shard_map/ppermute | solution.py:574
  267.1 7.9 %collective-permute-start.27 = (bf16[256,256]{1,0:T(8,128)(2,1)}, bf16[256,256]{1,0:T(8,128)(2,1)S(1)}, u32[]{:S(2)}, u32[]{:S(2)}) collective-permute-start(bf16[256,256]{1,0:T(8,128)(2,1)} %get-tuple-element.228), channel_id=1, source_target_pairs={{1,0},{2,1},{3,2},{5,4},{6,5},{7,6},{9,8},{10,9},{11,10},{13,12},{... | collective-permute-start | bytes 393224 | tf_op jit(solution)/shard_map/ppermute | solution.py:574
  268.4 13.1 %collective-permute-start.28 = (bf16[256,256]{1,0:T(8,128)(2,1)}, bf16[256,256]{1,0:T(8,128)(2,1)S(1)}, u32[]{:S(2)}, u32[]{:S(2)}) collective-permute-start(bf16[256,256]{1,0:T(8,128)(2,1)} %get-tuple-element.229), channel_id=1, source_target_pairs={{2,0},{3,1},{6,4},{7,5},{10,8},{11,9},{14,12},{15,13},{18,16},{19,... | collective-permute-start | bytes 393224 | tf_op jit(solution)/shard_map/ppermute | solution.py:574
  269.8 11.8 %copy-start.21 = (bf16[256,256]{1,0:T(8,128)(2,1)}, bf16[256,256]{1,0:T(8,128)(2,1)S(1)}, u32[]{:S(2)}) copy-start(bf16[256,256]{1,0:T(8,128)(2,1)S(1)} %collective-permute-done.25.refs_0_) | copy-start | bytes 393220
  269.8 11.8 %copy-start.22 = (bf16[256,256]{1,0:T(8,128)(2,1)}, bf16[256,256]{1,0:T(8,128)(2,1)S(1)}, u32[]{:S(2)}) copy-start(bf16[256,256]{1,0:T(8,128)(2,1)S(1)} %collective-permute-done.26.refs_1_) | copy-start | bytes 393220
  275.0 6.6 %copy-start.23 = (bf16[256,256]{1,0:T(8,128)(2,1)}, bf16[256,256]{1,0:T(8,128)(2,1)S(1)}, u32[]{:S(2)}) copy-start(bf16[256,256]{1,0:T(8,128)(2,1)S(1)} %collective-permute-done.27.refs_2_) | copy-start | bytes 393220
  293.7 4.2 %collective-permute-start.29 = (bf16[448,2176]{1,0:T(8,128)(2,1)}, bf16[448,2176]{1,0:T(8,128)(2,1)S(1)}, u32[]{:S(2)}, u32[]{:S(2)}) collective-permute-start(bf16[448,2176]{1,0:T(8,128)(2,1)} %get-tuple-element.232), channel_id=1, source_target_pairs={{0,4},{4,0},{8,12},{12,8},{16,20},{20,16},{24,28},{28,24},{1,5},{5... | collective-permute-start | bytes 5849096 | tf_op jit(solution)/shard_map/ppermute | solution.py:601
  302.3 15.5 %collective-permute-start.31 = (bf16[1,2,112,1024]{3,2,1,0:T(8,128)(2,1)}, bf16[1,2,112,1024]{3,2,1,0:T(8,128)(2,1)S(1)}, u32[]{:S(2)}, u32[]{:S(2)}) collective-permute-start(bf16[1,2,112,1024]{3,2,1,0:T(8,128)(2,1)} %fusion.13), channel_id=1, source_target_pairs={{0,16},{4,20},{8,24},{12,28},{16,0},{20,4},{24,8},{28,12},{1,17},{... | collective-permute-start | bytes 1376264 | tf_op jit(solution)/shard_map/ppermute | solution.py:601
  303.7 16.4 %collective-permute-start.30 = (bf16[2,1,112,1152]{3,2,0,1:T(8,128)(2,1)S(1)}, bf16[2,1,112,1152]{3,2,0,1:T(8,128)(2,1)}, u32[]{:S(2)}, u32[]{:S(2)}) collective-permute-start(bf16[2,1,112,1152]{3,2,0,1:T(8,128)(2,1)S(1)} %fusion.9), channel_id=1, source_target_pairs={{0,8},{4,12},{8,0},{12,4},{16,24},{20,28},{24,16},{28,20},{1,9},{5... | collective-permute-start | bytes 1548296 | tf_op jit(solution)/shard_map/ppermute | solution.py:601
  321.3 13.1 %collective-permute-start.32 = (bf16[1,1,112,1152]{3,2,1,0:T(8,128)(2,1)S(1)}, bf16[1,1,112,1152]{3,2,1,0:T(8,128)(2,1)S(1)}, u32[]{:S(2)}, u32[]{:S(2)}) collective-permute-start(bf16[1,1,112,1152]{3,2,1,0:T(8,128)(2,1)S(1)} %fusion.19), channel_id=1, source_target_pairs={{0,16},{4,20},{8,24},{12,28},{16,0},{20,4},{24,8},{28,12},{1,17},{... | collective-permute-start | bytes 774152 | tf_op jit(solution)/shard_map/ppermute | solution.py:601
  321.9 5.9 %copy-start.2 = (f32[2,256,896]{2,1,0:T(8,128)S(1)}, f32[2,256,896]{2,1,0:T(8,128)}, u32[]{:S(2)}) copy-start(f32[2,256,896]{2,1,0:T(8,128)} %get-tuple-element.163) | copy-start | bytes 5505028
  323.1 4.7 %copy-start = (f32[2,256,896]{2,1,0:T(8,128)S(1)}, f32[2,256,896]{2,1,0:T(8,128)}, u32[]{:S(2)}) copy-start(f32[2,256,896]{2,1,0:T(8,128)} %get-tuple-element.143.middle_ref) | copy-start | bytes 5505028
  323.1 11.2 %collective-permute-start.33 = (bf16[1,1,112,1024]{3,2,1,0:T(8,128)(2,1)S(1)}, bf16[1,1,112,1024]{3,2,1,0:T(8,128)(2,1)S(1)}, u32[]{:S(2)}, u32[]{:S(2)}) collective-permute-start(bf16[1,1,112,1024]{3,2,1,0:T(8,128)(2,1)S(1)} %fusion.20), channel_id=1, source_target_pairs={{0,8},{4,12},{8,0},{12,4},{16,24},{20,28},{24,16},{28,20},{1,9},{5... | collective-permute-start | bytes 688136 | tf_op jit(solution)/shard_map/ppermute | solution.py:601
  326.2 8.2 %collective-permute-start.34 = (bf16[112,3840]{1,0:T(8,128)(2,1)S(1)}, bf16[112,3840]{1,0:T(8,128)(2,1)}, u32[]{:S(2)}, u32[]{:S(2)}) collective-permute-start(bf16[112,3840]{1,0:T(8,128)(2,1)S(1)} %get-tuple-element.305), channel_id=1, source_target_pairs={{0,0},{2,4},{4,6},{6,2},{1,1},{3,5},{5,7},{7,3},{8,8},{10,12},{12,... | collective-permute-start | bytes 2580488 | tf_op jit(solution)/shard_map/ppermute | solution.py:618
  327.8 6.5 %copy-start.10 = (f32[2,112,1024]{2,1,0:T(8,128)S(1)}, f32[2,112,1024]{2,1,0:T(8,128)}, u32[]{:S(2)}) copy-start(f32[2,112,1024]{2,1,0:T(8,128)} %fusion.6) | copy-start | bytes 2752516
  330.5 47.4 %collective-permute-start.38 = (bf16[112,3840]{1,0:T(8,128)(2,1)S(1)}, bf16[112,3840]{1,0:T(8,128)(2,1)}, u32[]{:S(2)}, u32[]{:S(2)}) collective-permute-start(bf16[112,3840]{1,0:T(8,128)(2,1)S(1)} %get-tuple-element.304), channel_id=1, source_target_pairs={{0,4},{2,0},{4,2},{6,6},{1,5},{3,1},{5,3},{7,7},{8,12},{10,8},{12,... | collective-permute-start | bytes 2580488 | tf_op jit(solution)/shard_map/ppermute | solution.py:618
  334.7 46.1 %collective-permute-start.37 = (bf16[28,2176]{1,0:T(8,128)(2,1)S(1)}, bf16[28,2176]{1,0:T(8,128)(2,1)S(1)}, u32[]{:S(2)}, u32[]{:S(2)}) collective-permute-start(bf16[28,2176]{1,0:T(8,128)(2,1)S(1)} %get-tuple-element.307), channel_id=1, source_target_pairs={{0,3},{1,0},{2,1},{3,2},{4,7},{5,4},{6,5},{7,6},{8,11},{9,8},{10,9... | collective-permute-start | bytes 365576 | tf_op jit(solution)/shard_map/ppermute | solution.py:455
  342.0 38.8 %collective-permute-start.36 = (bf16[28,2176]{1,0:T(8,128)(2,1)S(1)}, bf16[28,2176]{1,0:T(8,128)(2,1)S(1)}, u32[]{:S(2)}, u32[]{:S(2)}) collective-permute-start(bf16[28,2176]{1,0:T(8,128)(2,1)S(1)} %get-tuple-element.308), channel_id=1, source_target_pairs={{0,2},{1,3},{2,0},{3,1},{4,6},{5,7},{6,4},{7,5},{8,10},{9,11},{10,... | collective-permute-start | bytes 365576 | tf_op jit(solution)/shard_map/ppermute | solution.py:455
  359.6 21.3 %collective-permute-start.35 = (bf16[28,2176]{1,0:T(8,128)(2,1)S(1)}, bf16[28,2176]{1,0:T(8,128)(2,1)S(1)}, u32[]{:S(2)}, u32[]{:S(2)}) collective-permute-start(bf16[28,2176]{1,0:T(8,128)(2,1)S(1)} %get-tuple-element.306), channel_id=1, source_target_pairs={{0,1},{1,2},{2,3},{3,0},{4,5},{5,6},{6,7},{7,4},{8,9},{9,10},{10,1... | collective-permute-start | bytes 365576 | tf_op jit(solution)/shard_map/ppermute | solution.py:455
  (14 other events, 17.4 us)
Sparse Core Ops, SparseCore 0:
  10.6 50.7 all-gather.3
  67.9 33.6 all-gather.5
  103.5 48.3 all-gather.7
  234.0 78.4 reduce-scatter.1

commit v4 on v3

--- a/solution.py
+++ b/solution.py
@@ -41,14 +41,14 @@
     kv_ref[:, KW:] = kv[:, KW:].astype(bf16)
 
 def queries_kernel(n1_ref, wq_ref, rows_ref, cos_ref, sin_ref, rq_ref):
-    q = dot(n1_ref[...], wq_ref[...],1,0) + rows_ref[2:3]
+    q = dot(n1_ref[...], wq_ref[:, 2*KW:],1,0) + rows_ref[2:3]
     cos = cos_ref[...]; sin = sin_ref[...]
     for b in range(QW//LANES):
         v = q[:, b*LANES:(b+1)*LANES]
         r = (v*cos + half_turn(v,False)*sin).astype(bf16)
         rq_ref[:, b*LANES:(b+1)*LANES] = (r.astype(f32)*HEAD**-0.5).astype(bf16)
 
-def project(x, first_set, spread, cos, sin):
+def project(x, out_set, in_set, spread, cos, sin):
     m, rows, _ = x.shape
     full=lambda shape,idx: pl.BlockSpec(shape, lambda i: idx)
     blk=lambda w: pl.BlockSpec((None,rows,w), lambda i:(i,0,0))
@@ -56,18 +56,18 @@
     params=dict(compiler_params=pltpu.CompilerParams(vmem_limit_bytes=LIMIT), cost_estimate=COST)
     pair, n1, table = pl.pallas_call(
         pairs_kernel, grid=(m,),
-        in_specs=[blk(D), full((D,2*KW),(0,7)), full((D,LANES),(0,16)), full((D,LANES),(0,0)), blk(LANES), blk(LANES)],
+        in_specs=[blk(D), full((D,2*KW),(0,0)), full((D,LANES),(0,QW//LANES)), full((D,LANES),(0,0)), blk(LANES), blk(LANES)],
         out_specs=[blk(2*KW), blk(D), full((8,D),(0,0))],
         out_shape=[sd((m,rows,2*KW),bf16), sd((m,rows,D),bf16), sd((8,D),f32)],
         scratch_shapes=[pltpu.VMEM((1,2*KW),f32)],
         name="pairs", **params,
-    )(x, first_set, first_set, spread, cos, sin)
+    )(x, in_set, out_set, spread, cos, sin)
     rq = pl.pallas_call(
         queries_kernel, grid=(m,),
-        in_specs=[blk(D), full((D,QW),(0,1)), full((8,D),(0,0)), blk(LANES), blk(LANES)],
+        in_specs=[blk(D), full((D,2*KW+QW),(0,0)), full((8,D),(0,0)), blk(LANES), blk(LANES)],
         out_specs=blk(QW), out_shape=sd((m,rows,QW),bf16),
         name="queries", **params,
-    )(n1, first_set, table, cos, sin)
+    )(n1, in_set, table, cos, sin)
     return rq, pair, n1, table
 
 BLOCK=128
@@ -136,7 +136,7 @@
     middle_ref[...] = middle
     n2_ref[...] = (middle*scaled(middle)*rows_ref[1:2]).astype(bf16)
 
-def attend(m, base, rq, kvs, begins, first_set, x, rows_table, before):
+def attend(m, base, rq, kvs, begins, out_set, x, rows_table, before):
     micros, rows, _ = rq.shape; nq=rows//BLOCK
     full=lambda shape: pl.BlockSpec(shape, lambda i: (0,)*len(shape))
     blk=lambda w: pl.BlockSpec((None,BLOCK,w), lambda i:(m,i,0))
@@ -150,7 +150,7 @@
         input_output_aliases={9+k:1+k for k in range(len(before))},
         compiler_params=pltpu.CompilerParams(vmem_limit_bytes=LIMIT), cost_estimate=COST,
         name="attend",
-    )(base, rq, *kvs, begins, first_set, x, rows_table, *before)
+    )(base, rq, *kvs, begins, out_set, x, rows_table, *before)
 
 def attend_back_kernel(base_ref, rq_ref, kv0_ref, kv1_ref, kv2_ref, begin_ref, wo_ref, rows_ref, lse_ref, middle_ref, dy_ref, cos_ref, sin_ref, *refs, count):
     gs=refs[:count]
@@ -215,7 +215,7 @@
         far1_ref[:, :KW] = dk_ref[rows:2*rows].astype(bf16); far1_ref[:, KW:] = dv_ref[rows:2*rows].astype(bf16)
         far2_ref[:, :KW] = dk_ref[:rows].astype(bf16); far2_ref[:, KW:] = dv_ref[:rows].astype(bf16)
 
-def attend_back(m, base, rq, kvs, begins, first_set, rows_table, lse, middle, dy, gs, cos, sin, before):
+def attend_back(m, base, rq, kvs, begins, out_set, rows_table, lse, middle, dy, gs, cos, sin, before):
     micros, rows, _ = rq.shape; nq=rows//BLOCK
     full=lambda shape: pl.BlockSpec(shape, lambda i: (0,)*len(shape))
     blk=lambda w: pl.BlockSpec((None,BLOCK,w), lambda i:(m,i,0))
@@ -232,7 +232,7 @@
         input_output_aliases={at+1+k:2+k for k in range(len(before))},
         compiler_params=pltpu.CompilerParams(vmem_limit_bytes=LIMIT), cost_estimate=COST,
         name="attend_back",
-    )(base, rq, *kvs, begins, first_set, rows_table, lse, middle, dy, cos, sin, *gs, *before)
+    )(base, rq, *kvs, begins, out_set, rows_table, lse, middle, dy, cos, sin, *gs, *before)
 
 CHUNK=256
 
@@ -246,7 +246,7 @@
     chunks=width//CHUNK
     def tokens(k):
         return (pltpu.make_async_copy(ts[k],x_ref.at[k],in_sem.at[0,k]),
-                pltpu.make_async_copy(gs[k].at[micro],y_ref.at[k],in_sem.at[1,k]))
+                pltpu.make_async_copy(gs[k],y_ref.at[k],in_sem.at[1,k]))
     def columns(which,j,p):
         c=slice(p*width+j*CHUNK,p*width+(j+1)*CHUNK)
         return pltpu.make_async_copy(sets[which].at[:,c],w_ref.at[:,c],w_sem.at[p,j])
@@ -344,7 +344,7 @@
     dv=own[:, KW:].astype(bf16)
     dkv=jnp.concatenate([dk,dv],axis=1)
     dq=dq_ref[...]
-    dn1=dot(dq,wq_ref[...],1,1)+dot(dkv,wkv_ref[...],1,1)
+    dn1=dot(dq,wq_ref[:, 2*KW:],1,1)+dot(dkv,wkv_ref[...],1,1)
     x=x_ref[...].astype(f32); inv=scaled(x)
     small_ref[0:1]+=jnp.sum(dn1*(x*inv),axis=0,keepdims=True)
     small_ref[1:2]+=gain2_ref[0:1]
@@ -371,7 +371,7 @@
             keep_ref[...]=acc_ref[:D//2].astype(bf16)
             send_ref[...]=acc_ref[D//2:].astype(bf16)
 
-def finish(bit,dq,own,far,cos,sin,first_set,rows_table,x,n1,dmid,mixed,dmb,spread,gain2,block):
+def finish(bit,dq,own,far,cos,sin,in_set,rows_table,x,n1,dmid,mixed,dmb,spread,gain2,block):
     m,rows,_=x.shape
     full=lambda shape,idx=(0,0): pl.BlockSpec(shape, lambda i: idx)
     blk=lambda w,h=rows: pl.BlockSpec((None,h,w), lambda i:(i,0,0))
@@ -381,33 +381,48 @@
     far=[f for pieces in far for f in pieces]
     return pl.pallas_call(
         functools.partial(finish_kernel,near=near,block=block), grid=(m,),
-        in_specs=[pl.BlockSpec(memory_space=pltpu.SMEM),blk(QW),blk(2*KW),blk(LANES),blk(LANES),full((D,QW),(0,1)),full((D,2*KW),(0,7)),full((8,D)),blk(D),blk(D),blk(D),blk(QW),blk(D),full((D,LANES)),blk(D,8)]+[full((rows,2*KW))]*len(far),
+        in_specs=[pl.BlockSpec(memory_space=pltpu.SMEM),blk(QW),blk(2*KW),blk(LANES),blk(LANES),full((D,2*KW+QW)),full((D,2*KW)),full((8,D)),blk(D),blk(D),blk(D),blk(QW),blk(D),full((D,LANES)),blk(D,8)]+[full((rows,2*KW))]*len(far),
         out_specs=[blk(D),full((D//2,width)),full((D//2,width))],
         out_shape=[sd((m,rows,D),f32),sd((D//2,width),bf16),sd((D//2,width),bf16)],
         scratch_shapes=[pltpu.VMEM((D,width),f32),pltpu.VMEM((8,D),f32),pltpu.VMEM((rows,2*KW),f32)],
         compiler_params=pltpu.CompilerParams(vmem_limit_bytes=LIMIT), cost_estimate=COST,
         name="finish",
-    )(bit,dq,own,cos,sin,first_set,first_set,rows_table,x,n1,dmid,mixed,dmb,spread,gain2,*far)
-
-def weights_kernel(left_ref, pair_ref, act_ref, out_ref, turned_ref, *, split):
-    j=pl.program_id(0)
-    @pl.when((j==0)|(j==split))
+    )(bit,dq,own,cos,sin,in_set,in_set,rows_table,x,n1,dmid,mixed,dmb,spread,gain2,*far)
+
+def weights_kernel(left_ref, right_ref, out_ref, turned_ref):
+    @pl.when(pl.program_id(0)==0)
     def _(): turned_ref[...]=left_ref[...].T
-    @pl.when(j<split)
-    def _(): out_ref[...]=dot(turned_ref[...],pair_ref[...],1,0).astype(bf16)
-    @pl.when(j>=split)
-    def _(): out_ref[...]=dot(turned_ref[...],act_ref[...],1,0).astype(bf16)
-
-def weights(left,pair,act,chunk=256):
-    rows=left.shape[1]; width=pair.shape[1]+act.shape[1]; split=pair.shape[1]//chunk
+    out_ref[...]=dot(turned_ref[...],right_ref[...],1,0).astype(bf16)
+
+def weights(left,which,right,chunk):
+    rows=left.shape[1]; width=right.shape[1]
     return pl.pallas_call(
-        functools.partial(weights_kernel,split=split), grid=(width//chunk,),
-        in_specs=[pl.BlockSpec((None,rows,D),lambda j:(jnp.where(j<split,0,1),0,0)),pl.BlockSpec((rows,chunk),lambda j:(0,jnp.minimum(j,split-1))),pl.BlockSpec((rows,chunk),lambda j:(0,jnp.maximum(j-split,0)))],
+        weights_kernel, grid=(width//chunk,),
+        in_specs=[pl.BlockSpec((None,rows,D),lambda j:(which,0,0),pipeline_mode=pl.Buffered(1)),pl.BlockSpec((rows,chunk),lambda j:(0,j))],
         out_specs=pl.BlockSpec((D,chunk),lambda j:(0,j)), out_shape=jax.ShapeDtypeStruct((D,width),bf16),
         scratch_shapes=[pltpu.VMEM((D,rows),bf16)],
         compiler_params=pltpu.CompilerParams(vmem_limit_bytes=LIMIT), cost_estimate=COST,
         name="weights",
-    )(left,pair,act)
+    )(left,right)
+
+def woven_kernel(core_ref, *refs):
+    n=len(refs)//3
+    mine=refs[:n]; got=refs[n:2*n]; outs=refs[2*n:]
+    core=core_ref[0]; j=pl.program_id(0)
+    for k in range(n):
+        rows=mine[k].shape[0]
+        outs[k][pl.ds(pl.multiple_of(core*rows,16),rows)]=mine[k][...]
+        outs[k][pl.ds(pl.multiple_of((1-core)*rows,16),rows)]=got[k][...]
+
+def woven(core, mine, got):
+    n=len(mine); blocks,rows,_=mine[0].shape
+    shapes=[jax.ShapeDtypeStruct((2*blocks*rows,v.shape[2]),v.dtype) for v in mine]
+    return pl.pallas_call(
+        woven_kernel, grid=(blocks,), in_specs=[pl.BlockSpec(memory_space=pltpu.SMEM)]+[pl.BlockSpec((None,)+v.shape[1:],lambda j:(j,0,0)) for v in mine+got],
+        out_specs=[pl.BlockSpec((2*rows,v.shape[2]),lambda j:(j,0)) for v in mine], out_shape=shapes,
+        compiler_params=pltpu.CompilerParams(vmem_limit_bytes=LIMIT), cost_estimate=COST,
+        name="woven",
+    )(core,*mine,*got)
 
 
 LONGEST = 512
@@ -451,6 +466,22 @@
     core = lax.axis_index("core")
     far_half = lax.axis_index("zh")
 
+    group_rank = lax.axis_index(dp)
+    groups = lax.axis_size(dp)
+    bits = [1 << k for k in range(groups.bit_length() - 1)]
+    block_rows = parts * weight_rows
+    even = block_rows % 16 == 0
+
+    def swapped(values_in, bit):
+        return lax.ppermute(values_in, dp, [(s, s ^ bit) for s in range(groups)])
+
+    def doubled(blocks, order, k):
+        bit = order[k]
+        got = swapped(blocks, bit)
+        low = (group_rank // bit) % 2 == 0
+        at = sum(earlier > bit for earlier in order[:k])
+        return jnp.stack([jnp.where(low, blocks, got), jnp.where(low, got, blocks)], axis=at)
+
     def around(values_in, steps):
         return lax.ppermute(values_in, ctx, [(s, (s + steps) % parts) for s in range(parts)])
 
@@ -484,18 +515,9 @@
     )
     small = jnp.pad(small, ((0, 0), (0, LANES - small.shape[1])))
     own_attention = jnp.concatenate(
-        [out_weight, query_weight, key_weight, value_weight, small], axis=1
+        [out_weight, small, key_weight, value_weight, query_weight], axis=1
     )
     first_block = collected(own_attention)
-    own_block, first_block = after((own_block, first_block))
-    other_block = other(own_block, "zh")
-    first_block, other_block, own_set, upstream = after(
-        (first_block, other_block, own_set, cotangent[0, :, 0])
-    )
-    first_set = lax.all_gather(first_block, dp, axis=0, tiled=True)
-    upstream_pieces = shared(upstream)
-    own_quarter = (core == far_half).astype(jnp.int32).reshape(1)
-
     row = jnp.arange(D, dtype=jnp.int32)[:, None]
     place = row // weight_rows * bias_rows + row % weight_rows
     spread = (
@@ -514,50 +536,89 @@
     sines = jnp.concatenate([-sines, sines] * (LANES // HEAD), axis=2)
     base = (rank * shard_rows).reshape(1)
 
+    own_block, first_block = after((own_block, first_block))
+    cut = QW + LANES
+    firsts = [first_block[:, :cut], first_block[:, cut:]]
+    gather_orders = [bits[1:] + bits[:1], bits[:0:-1] + bits[:1]]
+    widths = own_block.shape[1] // LANES // 4 * LANES
+    edges = [0, widths, own_block.shape[1] - widths, own_block.shape[1]]
+    other_block = []
+    upstream = [cotangent[0, m, 0] for m in range(micros)]
+    crossed = []
+    for k in range(len(bits)):
+        if k < len(bits) - 1 or not even:
+            firsts = [doubled(side, order, k) for side, order in zip(firsts, gather_orders)]
+        else:
+            gots = [swapped(side, 1) for side in firsts]
+            firsts = [firsts, gots]
+        if k < 3:
+            other_block.append(other(own_block[:, edges[k] : edges[k + 1]], "zh"))
+        firsts, other_block, own_block, spread, cosines, sines, begins, upstream, crossed = after(
+            (firsts, other_block, own_block, spread, cosines, sines, begins, upstream, crossed)
+        )
+    other_set = lax.all_gather(jnp.concatenate(other_block, axis=1), dp, axis=0, tiled=True)
+    if even:
+        firsts, gots = ([v.reshape((-1,) + v.shape[-2:]) for v in part] for part in firsts)
+        out_set, in_set = woven(core.reshape(1), firsts, gots)
+        crossed.append(other(upstream[0], "zb"))
+        out_set, in_set, crossed = after((out_set, in_set, crossed))
+    else:
+        out_set, in_set = (side.reshape(-1, side.shape[-1]) for side in firsts)
+        crossed.append(other(upstream[0], "zb"))
+    sets = (own_set, other_set)
+    own_quarter = (core == far_half).astype(jnp.int32).reshape(1)
+
     tokens = layer_in[0, :, 0]
-    first_set, other_block, upstream_pieces, spread, cosines, sines, begins = after(
-        (first_set, other_block, upstream_pieces, spread, cosines, sines, begins)
-    )
-    other_set = lax.all_gather(other_block, dp, axis=0, tiled=True)
-    sets = (own_set, other_set)
-
-    rot_query, pairs, normed_one, rows_table = project(tokens, first_set, spread, cosines, sines)
+    rot_query, pairs, normed_one, rows_table = project(
+        tokens, out_set, in_set, spread, cosines, sines
+    )
     kvs = [pairs] + [
         lax.ppermute(pairs, ctx, [(s, s + d) for s in range(parts - d)])
         for d in range(1, reach_parts + 1)
     ]
+
+    kvs, rot_query, upstream = after((kvs, rot_query, upstream))
+    crossed += [other(u, "zb") for u in upstream[1:]]
+    upstream_pieces = [[u, other(u, "core"), v] for u, v in zip(upstream, crossed)]
 
     begins = begins[:, None, :]
     exchanged = []
     held = ()
     for m in range(micros):
         normed_two, *held = attend(
-            m, base, rot_query, kvs, begins, first_set, tokens, rows_table, held
-        )
-        pieces = [normed_two, other(normed_two, "core"), other(normed_two, "zb")]
-        if m < micros - 1:
-            exchanged.append(pieces)
-        else:
-            exchanged.append(pieces + [corner(normed_two)])
-            exchanged[:-1], normed_two = after((exchanged[:-1], normed_two))
-            exchanged[-1][0] = normed_two
-            for early in exchanged[:-1]:
-                early.append(other(early[2], "core"))
+            m, base, rot_query, kvs, begins, out_set, tokens, rows_table, held
+        )
+        exchanged.append([normed_two, other(normed_two, "core"), other(normed_two, "zb")])
+    exchanged[-1].append(corner(normed_two))
+    exchanged[:-1], upstream_pieces[0], exchanged[-1][0] = after(
+        (exchanged[:-1], upstream_pieces[0], normed_two)
+    )
+    for early in exchanged[:-1] + upstream_pieces[:1]:
+        early.append(other(early[2], "core"))
     mixed, middle, log_sums = held
 
     backs = []
     before = ()
     for m in range(micros):
         back, before = feed(
-            own_quarter, exchanged[m], upstream_pieces, sets, m, micros, before
-        )
+            own_quarter, exchanged[m], upstream_pieces[m], sets, m, micros, before
+        )
+        if m < micros - 1:
+            back, upstream_pieces[m + 1] = after((back, upstream_pieces[m + 1]))
+            upstream_pieces[m + 1].append(other(upstream_pieces[m + 1][2], "core"))
         backs.append([back[0], other(back[1], "core"), other(back[2], "zb"), corner(back[3])])
     partials = before[:4]
     out_near = other(partials[1], "core")
     out_far = other(partials[3], "core")
 
-    feed_local = weights(*after(before[4:], backs[0]))
-    backs, feed_local, out_near, out_far = after((backs, feed_local, out_near, out_far))
+    left, pair, act = after(before[4:], backs[0])
+    feed_pair = weights(left, 0, pair, 512)
+    feed_down = weights(left, 1, act, 640)
+    backs, feed_pair, feed_down, out_near, out_far = after(
+        (backs, feed_pair, feed_down, out_near, out_far)
+    )
+    feed_pair = lax.psum_scatter(feed_pair, "grp", scatter_dimension=0, tiled=True)
+
     far = []
     ended = ()
     out_beside = []
@@ -565,7 +626,7 @@
         out_sum = (partials[2][m].astype(f32) + out_far[m].astype(f32)).astype(bf16)
         out_beside.append(other(out_sum, "zb"))
         far1, far2, *ended = attend_back(
-            m, base, rot_query, kvs, begins, first_set, rows_table, log_sums, middle, upstream,
+            m, base, rot_query, kvs, begins, out_set, rows_table, log_sums, middle, cotangent[0, :, 0],
             backs[m], cosines, sines, ended,
         )
         far1, far2, ended, out_beside = after((far1, far2, ended, out_beside))
@@ -577,28 +638,20 @@
         )
         if m < micros - 1:
             out_far, ended = after((out_far, ended))
-    feed_half = lax.psum_scatter(feed_local, "grp", scatter_dimension=0, tiled=True)
-
-    group_rank = lax.axis_index(dp)
-    groups = lax.axis_size(dp)
-    bits = [1 << k for k in range(groups.bit_length() - 1)]
-    block_rows = parts * weight_rows
-    even = block_rows % 16 == 0
     grad_middle, branch_low, query_grad, own_pair, gain_sum = ended
     input_grad, keep, send = finish(
-        (group_rank % 2).reshape(1), query_grad, own_pair, far, cosines, sines, first_set,
+        (group_rank % 2).reshape(1), query_grad, own_pair, far, cosines, sines, in_set,
         rows_table, tokens, normed_one, grad_middle, mixed, branch_low, spread, gain_sum,
         block_rows if even else 0,
     )
+    keep, send, feed_pair, feed_down = after((keep, send, feed_pair, feed_down))
+    feed_down = lax.psum_scatter(feed_down, "grp", scatter_dimension=0, tiled=True)
     if not even:
         both = jnp.concatenate([keep, send]).reshape(groups // 2, 2, block_rows, -1)
         keep, send = (
             lax.dynamic_index_in_dim(both, v, 1, keepdims=False)
             for v in (group_rank % 2, 1 - group_rank % 2)
         )
-
-    def swapped(values_in, bit):
-        return lax.ppermute(values_in, dp, [(s, s ^ bit) for s in range(groups)])
 
     def halved(blocks, order, k):
         bit = order[k]
@@ -611,28 +664,29 @@
         got = swapped(sent.astype(bf16), bit)
         return (kept.astype(f32) + got.astype(f32)).reshape((size // 2,) + blocks.shape[1:])
 
-    def delivered(k):
+    def delivered(half, k):
         part = lax.dynamic_index_in_dim(
-            feed_half, (core + far_half + k) % 2, 0, keepdims=False
+            half.reshape((2, -1) + half.shape[1:]), (core + far_half + k) % 2, 0, keepdims=False
         )
         return lax.ppermute(
             part, ("core", "zh"), [(2 * s + a, 2 * (s ^ a ^ k) + s) for s in range(2) for a in range(2)]
         )
 
-    feed_half = feed_half.reshape((2, -1) + feed_half.shape[1:])
     blocks = keep.astype(f32) + swapped(send, 1).astype(f32)
     blocks = blocks.reshape(groups // 2, block_rows, -1)
     cut = QW + 2 * LANES
     sides = [blocks[:, :, :cut], blocks[:, :, cut:]]
     orders = [bits[1:], bits[:0:-1]]
+    pair_parts = []
     for k in range(len(bits) - 1):
+        if k < 2:
+            pair_parts.append(delivered(feed_pair, k))
         sides = [halved(side, order, k) for side, order in zip(sides, orders)]
-        if k == len(bits) - 3:
-            sides, feed_half = after((sides, feed_half))
-            feed_first = delivered(0)
-    sides, feed_first = after((sides, feed_first))
+        if k == len(bits) - 2:
+            sides, feed_down = after((sides, feed_down))
+        sides, pair_parts, feed_pair = after((sides, pair_parts, feed_pair))
+    down_parts = [delivered(feed_down, k) for k in range(2)]
     attention_block = jnp.concatenate([side[0] for side in sides], axis=1).astype(bf16)
-    feed_last = delivered(1)
     attention_block = attention_block.reshape(parts, weight_rows, -1)
 
     def block_for(steps):
@@ -644,7 +698,8 @@
     for d in range(1, parts):
         sums = sums + around(block_for(d), d).astype(f32)
 
-    feed_sum = feed_first.astype(f32) + feed_last.astype(f32)
+    pair_sum = pair_parts[0].astype(f32) + pair_parts[1].astype(f32)
+    down_sum = down_parts[0].astype(f32) + down_parts[1].astype(f32)
 
     total = middle + partials[0] + out_near.astype(f32) + jnp.stack(out_beside).astype(f32)
 
@@ -661,9 +716,9 @@
         sums[:bias_rows, edge + 4],
         sums[:, :QW],
         sums[:, edge + 1],
-        feed_sum[:, :hidden],
-        feed_sum[:, hidden_pad : hidden_pad + hidden],
-        feed_sum[:, 2 * hidden_pad : 2 * hidden_pad + hidden].T,
+        pair_sum[:, :hidden],
+        pair_sum[:, hidden_pad : hidden_pad + hidden],
+        down_sum[:, :hidden].T,
     )
 
 

time: 395 us -> 374 us (0.947)
  the two profiles are of different devices: /device:TPU:0 before, /device:TPU:1 now
where the time goes in v4:
time: 374 us; the launch traced here: 368 us
  Pallas kernels  145 us (39%)
  waiting for transfers between devices  109 us (29%)
  starting transfers between devices  69.8 us (19%)
  between operations  15.1 us (4%)
  local copies, waits for them, and re-layouts  15 us (4%)
  other arithmetic  14 us (4%)
    ppermute x11, waiting for transfers between devices, swapped(): return lax.ppermute(values_in, dp, [(s, s ^ bit) for s in range(groups)])  51.9 us
    pallas_call x2, Pallas kernels, feed(): pl.pallas_call(functools.partial(feed_kernel, parts=parts, micro=micro, k...  49.3 us
    pallas_call x2, Pallas kernels, attend_back(): pl.pallas_call(functools.partial(attend_back_kernel, count=len(gs)), grid...  27.1 us
    pallas_call x2, Pallas kernels, weights(): pl.pallas_call(weights_kernel, grid=(width // chunk,), in_specs=[pl.Block...  26.1 us
    ppermute x22, starting transfers between devices, other(): return lax.ppermute(values_in, axis, [(0, 1), (1, 0)])  20.8 us
    pallas_call x2, Pallas kernels, attend(): pl.pallas_call(attend_kernel, grid=(nq,), in_specs=[pl.BlockSpec(memory_s...  18.5 us
    ppermute x6, waiting for transfers between devices, around(): lax.ppermute(values_in, ctx, [(s, (s + steps) % parts) for s in range(par...  16.3 us
    ppermute x22, waiting for transfers between devices, other(): return lax.ppermute(values_in, axis, [(0, 1), (1, 0)])  15.6 us
  transfers between devices with their start and end apart: 56, of which 21 were waited for; matrix products, arithmetic and copies ran while one was open for 5% of the time, Pallas kernels for 39%

profile of v4, /device:TPU:1, one launch (start us, length us, event | category | flops | bytes accessed | tf_op | source)
XLA Modules:
  0.0 368.4 jit_solution(8756851941671889814)
XLA Ops:
  7.3 2.2 fusion.8
  9.9 4.2 %collective-permute-start = (bf16[28,2176]{1,0:T(8,128)(2,1)S(1)}, bf16[28,2176]{1,0:T(8,128)(2,1)S(1)}, u32[]{:S(2)}, u32[]{:S(2)}) collective-permute-start(bf16[28,2176]{1,0:T(8,128)(2,1)S(1)} %constant_dynamic-update-slice_fusion), channel_id=1, source_target_pairs={{0,3},{1,0},{2,1},{3,2},{4,7},{5,4},{6,5},{7,6},{8,11},{9,8},{10,9... | collective-permute-start | bytes 365576 | tf_op jit(solution)/shard_map/ppermute | solution.py:486
  16.1 1.3 pad_maximum_fusion.5
  17.5 8.3 %collective-permute-done.1 = bf16[28,2176]{1,0:T(8,128)(2,1)S(1)} collective-permute-done((bf16[28,2176]{1,0:T(8,128)(2,1)S(1)}, bf16[28,2176]{1,0:T(8,128)(2,1)S(1)}, u32[]{:S(2)}, u32[]{:S(2)}) %collective-permute-start.1) | collective-permute-done | bytes 121888 | tf_op jit(solution)/shard_map/ppermute | solution.py:486
  26.1 1.3 collective-permute-start.3
  28.4 1.3 collective-permute-start.4
  29.7 2.5 collective-permute-start.5
  32.2 4.2 %collective-permute-done.3 = bf16[112,1024]{1,0:T(8,128)(2,1)S(1)} collective-permute-done((bf16[112,1024]{1,0:T(8,128)(2,1)S(1)}, bf16[112,1024]{1,0:T(8,128)(2,1)S(1)}, u32[]{:S(2)}, u32[]{:S(2)}) %collective-permute-start.3) | collective-permute-done | bytes 229408 | tf_op jit(solution)/shard_map/ppermute | solution.py:476
  37.4 4.4 %collective-permute-done.5 = bf16[112,896]{1,0:T(8,128)(2,1)S(1)} collective-permute-done((bf16[112,896]{1,0:T(8,128)(2,1)S(1)}, bf16[112,896]{1,0:T(8,128)(2,1)S(1)}, u32[]{:S(2)}, u32[]{:S(2)}) %collective-permute-start.5) | collective-permute-done | bytes 200736 | tf_op jit(solution)/shard_map/ppermute | solution.py:489
  42.5 21.4 %collective-permute-done.6 = bf16[2,112,1024]{2,1,0:T(8,128)(2,1)S(1)} collective-permute-done((bf16[2,112,1024]{2,1,0:T(8,128)(2,1)S(1)}, bf16[2,112,1024]{2,1,0:T(8,128)(2,1)S(1)}, u32[]{:S(2)}, u32[]{:S(2)}) %collective-permute-start.6) | collective-permute-done | bytes 458784 | tf_op jit(solution)/shard_map/ppermute | solution.py:476
  64.0 2.3 collective-permute-done.7
  66.6 1.6 collective-permute-start.10
  68.5 7.0 %collective-permute-done.11 = bf16[112,896]{1,0:T(8,128)(2,1)S(1)} collective-permute-done((bf16[112,896]{1,0:T(8,128)(2,1)S(1)}, bf16[112,896]{1,0:T(8,128)(2,1)S(1)}, u32[]{:S(2)}, u32[]{:S(2)}) %collective-permute-start.11) | collective-permute-done | bytes 200736 | tf_op jit(solution)/shard_map/ppermute | solution.py:489
  77.6 1.1 copy.60
  78.7 2.3 copy.61
  81.0 4.7 %woven.1 = (bf16[896,1024]{1,0:T(8,128)(2,1)}, bf16[896,1152]{1,0:T(8,128)(2,1)}) custom-call(s32[1]{0:T(128)} %bitcast.2.core_ref, bf16[4,112,1024]{2,1,0:T(8,128)(2,1)} %bitcast.139, bf16[4,112,1152]{2,1,0:T(8,128)(2,1)} %bitcast.137, bf16[4,112,1024]{2,1,0:T(8,128)(2,1)} %bitcast.142, bf16[4,112,1152]{2,1,0:T(8,128)(2,1)} %bitcast.138), custom_call_target="tpu_custom_call" | custom-call | flops 1 | bytes 1 | tf_op jit(solution)/shard_map/woven/pallas_call | solution.py:420
  85.6 2.7 collective-permute-done.12.refs_6_
  88.3 3.5 pairs.1
  91.8 2.2 collective-permute-start.13
  94.0 4.1 %collective-permute-start.14 = (bf16[2,256,256]{2,1,0:T(8,128)(2,1)}, bf16[2,256,256]{2,1,0:T(8,128)(2,1)S(1)}, u32[]{:S(2)}, u32[]{:S(2)}) collective-permute-start(bf16[2,256,256]{2,1,0:T(8,128)(2,1)} %get-tuple-element.218.kv0_ref), channel_id=1, source_target_pairs={{0,2},{1,3},{4,6},{5,7},{8,10},{9,11},{12,14},{13,15},{16,18},{17,... | collective-permute-start | bytes 786440 | tf_op jit(solution)/shard_map/ppermute | solution.py:576
  98.7 4.5 %queries.1.rq_ref = bf16[2,256,896]{2,1,0:T(8,128)(2,1)} custom-call(bf16[2,256,896]{2,1,0:T(8,128)(2,1)} %get-tuple-element.214.n1_ref, bf16[896,1152]{1,0:T(8,128)(2,1)} %get-tuple-element.208.wkv_ref.wq_ref, f32[8,896]{1,0:T(8,128)} %get-tuple-element.215.rows_ref, f32[2,256,128]{2,1,0:T(8,128)} %get-tuple-element.211.cos_ref, ...), custom_call_target="tpu_custom_call" | custom-call | flops 1 | bytes 1 | tf_op jit(solution)/shard_map/queries/pallas_call | solution.py:65
  103.2 1.3 collective-permute-done.14.kv2_ref
  105.1 9.2 %attend.2 = (bf16[256,896]{1,0:T(8,128)(2,1)}, bf16[2,256,896]{2,1,0:T(8,128)(2,1)}, f32[2,256,896]{2,1,0:T(8,128)}, f32[2,2,16,128]{3,2,1,0:T(8,128)}) custom-call(s32[1]{0:T(128)} %bitcast.base_ref, bf16[2,256,896]{2,1,0:T(8,128)(2,1)} %queries.1.rq_ref, bf16[2,256,256]{2,1,0:T(8,128)(2,1)} %get-tuple-element.218.kv0_ref, bf16[2,256,256]{2,1,0:T(8,128)(2,1)} %copy-done.3, ...), custom_call_target="tpu_custom_call" | custom-call | flops 1 | bytes 1 | tf_op jit(solution)/shard_map/attend/pallas_call | solution.py:144
  114.4 2.1 collective-permute-start.15
  116.5 6.7 %collective-permute-start.16 = (bf16[256,896]{1,0:T(8,128)(2,1)}, bf16[256,896]{1,0:T(8,128)(2,1)S(1)}, u32[]{:S(2)}, u32[]{:S(2)}) collective-permute-start(bf16[256,896]{1,0:T(8,128)(2,1)} %get-tuple-element.231.refs_0_), channel_id=1, source_target_pairs={{0,1},{1,0},{2,3},{3,2},{4,5},{5,4},{6,7},{7,6},{8,9},{9,8},{10,11... | collective-permute-start | bytes 1376264 | tf_op jit(solution)/shard_map/ppermute | solution.py:489
  123.5 9.2 %attend.3 = (bf16[256,896]{1,0:T(8,128)(2,1)}, bf16[2,256,896]{2,1,0:T(8,128)(2,1)}, f32[2,256,896]{2,1,0:T(8,128)}, f32[2,2,16,128]{3,2,1,0:T(8,128)}) custom-call(s32[1]{0:T(128)} %bitcast.base_ref, bf16[2,256,896]{2,1,0:T(8,128)(2,1)} %queries.1.rq_ref, ...), custom_call_target="tpu_custom_call", output_to_operand_aliasing={{1}: (9, {}), {2}: (10, {}), {3}: (11, {})} | custom-call | flops 1 | bytes 1 | tf_op jit(solution)/shard_map/attend/pallas_call | solution.py:144
  132.8 1.4 collective-permute-done.16.refs_2_
  135.6 1.5 collective-permute-start.24
  138.2 1.1 collective-permute-start.20
  139.3 24.8 %feed.2 = (f32[256,896]{1,0:T(8,128)}, bf16[256,896]{1,0:T(8,128)(2,1)}, bf16[256,896]{1,0:T(8,128)(2,1)}, bf16[256,896]{1,0:T(8,128)(2,1)}, f32[2,256,896]{2,1,...) custom-call(s32[1]{0:T(128)} %bitcast.27.own_ref, ...), custom_call_target="tpu_custom_call" | custom-call | flops 1 | bytes 1 | tf_op jit(solution)/shard_map/feed/pallas_call | solution.py:312
  165.3 1.2 collective-permute-start.28
  166.5 1.2 collective-permute-done.20.refs_3_
  168.6 24.5 %feed.3 = (f32[256,896]{1,0:T(8,128)}, bf16[256,896]{1,0:T(8,128)(2,1)}, bf16[256,896]{1,0:T(8,128)(2,1)}, bf16[256,896]{1,0:T(8,128)(2,1)}, f32[2,256,896]{2,1,...) custom-call(s32[1]{0:T(128)} %bitcast.27.own_ref, ...), custom_call_target="tpu_custom_call", output_to_operand_aliasing={{4}: (11, {}), {5}: (12, {}), {6}: (13, {}), {7}: (14, {}),... | custom-call | flops 1 | bytes 1 | tf_op jit(solution)/shard_map/feed/pallas_call | solution.py:312
  193.8 1.8 collective-permute-start.30
  196.0 15.1 %weights.2 = bf16[896,2560]{1,0:T(8,128)(2,1)} custom-call(bf16[2,2048,896]{2,1,0:T(8,128)(2,1)} %get-tuple-element.267.left_ref, bf16[2048,2560]{1,0:T(8,128)(2,1)} %get-tuple-element.268.right_ref), custom_call_target="tpu_custom_call" | custom-call | flops 1 | bytes 1 | tf_op jit(solution)/shard_map/weights/pallas_call | solution.py:399
  211.1 11.0 %weights.3 = bf16[896,1280]{1,0:T(8,128)(2,1)} custom-call(bf16[2,2048,896]{2,1,0:T(8,128)(2,1)} %get-tuple-element.267.left_ref, bf16[2048,1280]{1,0:T(8,128)(2,1)} %get-tuple-element.269.right_ref), custom_call_target="tpu_custom_call" | custom-call | flops 1 | bytes 1 | tf_op jit(solution)/shard_map/weights/pallas_call | solution.py:399
  223.1 1.0 copy-done.6
  224.3 1.7 collective-permute-start.34
  226.0 13.6 %attend_back.2 = (bf16[256,256]{1,0:T(8,128)(2,1)}, bf16[256,256]{1,0:T(8,128)(2,1)}, f32[2,256,896]{2,1,0:T(8,128)}, bf16[2,256,896]{2,1,0:T(8,128)(2,1)}, bf16...) custom-call(s32[1]{0:T(128)} %bitcast.base_ref, bf16[2,256,896]{2,1,0:T(8,128)(2,1)} %queries.1.rq_ref, ...), custom_call_target="tpu_custom_call" | custom-call | flops 1 | bytes 1 | tf_op jit(solution)/shard_map/attend_back/pallas_call | solution.py:225
  239.9 1.3 collective-permute-start.36
  241.1 1.3 collective-permute-start.37
  242.4 13.5 %attend_back.3 = (bf16[256,256]{1,0:T(8,128)(2,1)}, bf16[256,256]{1,0:T(8,128)(2,1)}, f32[2,256,896]{2,1,0:T(8,128)}, bf16[2,256,896]{2,1,0:T(8,128)(2,1)}, bf16...) custom-call(s32[1]{0:T(128)} %bitcast.base_ref, ...), custom_call_target="tpu_custom_call", output_to_operand_aliasing={{2}: (17, {}), {3}: (18, {}), {4}: (19, {}), {5}: (20, {}),... | custom-call | flops 1 | bytes 1 | tf_op jit(solution)/shard_map/attend_back/pallas_call | solution.py:225
  256.0 1.3 collective-permute-start.38
  257.3 1.3 collective-permute-start.39
  258.6 4.3 %collective-permute-done.38.refs_2_ = bf16[256,256]{1,0:T(8,128)(2,1)S(1)} collective-permute-done((bf16[256,256]{1,0:T(8,128)(2,1)}, bf16[256,256]{1,0:T(8,128)(2,1)S(1)}, u32[]{:S(2)}, u32[]{:S(2)}) %collective-permute-start.38) | collective-permute-done | bytes 131104 | tf_op jit(solution)/shard_map/ppermute | solution.py:635
  262.9 6.2 %collective-permute-done.39.refs_3_ = bf16[256,256]{1,0:T(8,128)(2,1)S(1)} collective-permute-done((bf16[256,256]{1,0:T(8,128)(2,1)}, bf16[256,256]{1,0:T(8,128)(2,1)S(1)}, u32[]{:S(2)}, u32[]{:S(2)}) %collective-permute-start.39) | collective-permute-done | bytes 131104 | tf_op jit(solution)/shard_map/ppermute | solution.py:635
  269.8 11.7 %finish.1 = (f32[2,256,896]{2,1,0:T(8,128)}, bf16[448,2176]{1,0:T(8,128)(2,1)}, bf16[448,2176]{1,0:T(8,128)(2,1)}) custom-call(s32[1]{0:T(128)} %bitcast.35.bit_ref, bf16[2,256,896]{2,1,0:T(8,128)(2,1)} %get-tuple-element.312.dq_ref, f32[2,256,256]{2,1,0:T(8,128)} %get-tuple-element.313.own_ref, f32[2,256,128]{2,1,0:T(8,128)} %get-tuple-element.211.cos_ref, ...), custom_call_target="tpu_custom_call" | custom-call | flops 1 | bytes 1 | tf_op jit(solution)/shard_map/finish/pallas_call | solution.py:382
  281.6 2.1 collective-permute-start.40
  283.8 3.0 fusion.5
  287.6 1.9 convert_add_fusion
  291.0 1.6 collective-permute-start.41
  292.6 1.9 collective-permute-start.43
  294.5 17.2 %collective-permute-done.42 = bf16[1,2,112,1024]{3,2,1,0:T(8,128)(2,1)S(1)} collective-permute-done((bf16[1,2,112,1024]{3,2,1,0:T(8,128)(2,1)S(1)}, bf16[1,2,112,1024]{3,2,1,0:T(8,128)(2,1)S(1)}, u32[]{:S(2)}, u32[]{:S(2)}) %collective-permute-start.42) | collective-permute-done | bytes 458784 | tf_op jit(solution)/shard_map/ppermute | solution.py:476
  311.9 3.2 collective-permute-done.41
  316.9 3.3 collective-permute-start.46
  320.2 1.5 collective-permute-done.45
  322.3 8.7 %reduce-scatter.5.cloned.1.call-done = bf16[224,1280]{1,0:T(8,128)(2,1)} async-done(((bf16[896,1280]{1,0:T(8,128)(2,1)}), bf16[224,1280]{1,0:T(8,128)(2,1)}) %reduce-scatter.5.cloned.1.call-update) | async-done | bytes 573456 | tf_op jit(solution)/shard_map/reduce_scatter | solution.py:648
  331.2 2.4 collective-permute-start.49
  333.6 2.0 collective-permute-start.48
  335.8 1.1 fusion.32
  336.9 7.6 %collective-permute-start.51 = (bf16[112,1280]{1,0:T(8,128)(2,1)S(1)}, bf16[112,1280]{1,0:T(8,128)(2,1)S(1)}, u32[]{:S(2)}, u32[]{:S(2)}) collective-permute-start(bf16[112,1280]{1,0:T(8,128)(2,1)S(1)} %get-tuple-element.416), channel_id=1, source_target_pairs={{0,4},{2,0},{4,2},{6,6},{1,5},{3,1},{5,3},{7,7},{8,12},{10,8},{12,... | collective-permute-start | bytes 860168 | tf_op jit(solution)/shard_map/ppermute | solution.py:671
  344.5 1.9 collective-permute-start.50
  346.4 8.0 %collective-permute-done.48 = bf16[28,2176]{1,0:T(8,128)(2,1)S(1)} collective-permute-done((bf16[28,2176]{1,0:T(8,128)(2,1)S(1)}, bf16[28,2176]{1,0:T(8,128)(2,1)S(1)}, u32[]{:S(2)}, u32[]{:S(2)}) %collective-permute-start.48) | collective-permute-done | bytes 121888 | tf_op jit(solution)/shard_map/ppermute | solution.py:486
  357.3 3.5 collective-permute-done.50
  (224 shorter events, 26.1 us)
Async XLA Ops:
  7.3 7.3 %copy-start.33 = (s32[1,2,1,1024]{3,2,1,0:T(1,128)S(1)}, s32[1,2,1,1024]{3,2,1,0:T(1,128)}, u32[]{:S(2)}) copy-start(s32[1,2,1,1024]{3,2,1,0:T(1,128)} %param.16) | copy-start | bytes 24580
  7.3 132.1 %all-gather.3.cloned.1.call-start = ((), (), s32[]{:S(2)}) async-start(), calls=%async_computation.2 | async-start | bytes 7741440 | tf_op jit(solution)/shard_map/all_gather | solution.py:512
  7.3 8.7 %copy-start.1 = (bf16[1,2,1,256,896]{4,3,2,1,0:T(8,128)(2,1)S(1)}, bf16[1,2,1,256,896]{4,3,2,1,0:T(8,128)(2,1)}, u32[]{:S(2)}) copy-start(bf16[1,2,1,256,896]{4,3,2,1,0:T(8,128)(2,1)} %param.17) | copy-start | bytes 2752516
  9.5 129.8 %all-gather.5.cloned.1.call-start = ((), (), s32[]{:S(2)}) async-start(), calls=%async_computation.3 | async-start | bytes 7741440 | tf_op jit(solution)/shard_map/all_gather | solution.py:559
  9.9 7.6 %collective-permute-start = (bf16[28,2176]{1,0:T(8,128)(2,1)S(1)}, bf16[28,2176]{1,0:T(8,128)(2,1)S(1)}, u32[]{:S(2)}, u32[]{:S(2)}) collective-permute-start(bf16[28,2176]{1,0:T(8,128)(2,1)S(1)} %constant_dynamic-update-slice_fusion), channel_id=1, source_target_pairs={{0,3},{1,0},{2,1},{3,2},{4,7},{5,4},{6,5},{7,6},{8,11},{9,8},{10,9... | collective-permute-start | bytes 365576 | tf_op jit(solution)/shard_map/ppermute | solution.py:486
  14.1 11.6 %collective-permute-start.1 = (bf16[28,2176]{1,0:T(8,128)(2,1)S(1)}, bf16[28,2176]{1,0:T(8,128)(2,1)S(1)}, u32[]{:S(2)}, u32[]{:S(2)}) collective-permute-start(bf16[28,2176]{1,0:T(8,128)(2,1)S(1)} %constant_dynamic-update-slice_fusion), channel_id=1, source_target_pairs={{0,2},{1,3},{2,0},{3,1},{4,6},{5,7},{6,4},{7,5},{8,10},{9,11},{10,... | collective-permute-start | bytes 365576 | tf_op jit(solution)/shard_map/ppermute | solution.py:486
  14.1 11.6 %collective-permute-start.2 = (bf16[28,2176]{1,0:T(8,128)(2,1)S(1)}, bf16[28,2176]{1,0:T(8,128)(2,1)S(1)}, u32[]{:S(2)}, u32[]{:S(2)}) collective-permute-start(bf16[28,2176]{1,0:T(8,128)(2,1)S(1)} %constant_dynamic-update-slice_fusion), channel_id=1, source_target_pairs={{0,1},{1,2},{2,3},{3,0},{4,5},{5,6},{6,7},{7,4},{8,9},{9,10},{10,1... | collective-permute-start | bytes 365576 | tf_op jit(solution)/shard_map/ppermute | solution.py:486
  16.1 107.1 %copy-start.9 = (bf16[256,896]{1,0:T(8,128)(2,1)}, bf16[256,896]{1,0:T(8,128)(2,1)S(1)}, u32[]{:S(2)}) copy-start(bf16[256,896]{1,0:T(8,128)(2,1)S(1)} %get-tuple-element.234.refs_4_) | copy-start | bytes 1376260
  16.1 119.5 %copy-start.8 = (bf16[256,896]{1,0:T(8,128)(2,1)}, bf16[256,896]{1,0:T(8,128)(2,1)S(1)}, u32[]{:S(2)}) copy-start(bf16[256,896]{1,0:T(8,128)(2,1)S(1)} %get-tuple-element.245.refs_4_) | copy-start | bytes 1376260
  26.1 10.3 %collective-permute-start.3 = (bf16[112,1024]{1,0:T(8,128)(2,1)S(1)}, bf16[112,1024]{1,0:T(8,128)(2,1)S(1)}, u32[]{:S(2)}, u32[]{:S(2)}) collective-permute-start(bf16[112,1024]{1,0:T(8,128)(2,1)S(1)} %slice.75), channel_id=1, source_target_pairs={{0,8},{4,12},{8,0},{12,4},{16,24},{20,28},{24,16},{28,20},{1,9},{5... | collective-permute-start | bytes 688136 | tf_op jit(solution)/shard_map/ppermute | solution.py:476
  28.4 8.9 %collective-permute-start.4 = (bf16[112,1152]{1,0:T(8,128)(2,1)S(1)}, bf16[112,1152]{1,0:T(8,128)(2,1)S(1)}, u32[]{:S(2)}, u32[]{:S(2)}) collective-permute-start(bf16[112,1152]{1,0:T(8,128)(2,1)S(1)} %slice.76), channel_id=1, source_target_pairs={{0,16},{4,20},{8,24},{12,28},{16,0},{20,4},{24,8},{28,12},{1,17},{... | collective-permute-start | bytes 774152 | tf_op jit(solution)/shard_map/ppermute | solution.py:476
  29.7 12.2 %collective-permute-start.5 = (bf16[112,896]{1,0:T(8,128)(2,1)S(1)}, bf16[112,896]{1,0:T(8,128)(2,1)S(1)}, u32[]{:S(2)}, u32[]{:S(2)}) collective-permute-start(bf16[112,896]{1,0:T(8,128)(2,1)S(1)} %slice.77), channel_id=1, source_target_pairs={{0,2},{2,0},{1,3},{3,1},{4,6},{6,4},{5,7},{7,5},{8,10},{10,8},{9,1... | collective-permute-start | bytes 602120 | tf_op jit(solution)/shard_map/ppermute | solution.py:489
  41.9 22.0 %collective-permute-start.6 = (bf16[2,112,1024]{2,1,0:T(8,128)(2,1)S(1)}, bf16[2,112,1024]{2,1,0:T(8,128)(2,1)S(1)}, u32[]{:S(2)}, u32[]{:S(2)}) collective-permute-start(bf16[2,112,1024]{2,1,0:T(8,128)(2,1)S(1)} %pad_maximum_fusion.4), channel_id=1, source_target_pairs={{0,16},{4,20},{8,24},{12,28},{16,0},{20,4},{24,8},{28,12},{1,17},{... | collective-permute-start | bytes 1376264 | tf_op jit(solution)/shard_map/ppermute | solution.py:476
  42.1 24.3 %collective-permute-start.7 = (bf16[2,112,1152]{2,1,0:T(8,128)(2,1)S(1)}, bf16[2,112,1152]{2,1,0:T(8,128)(2,1)S(1)}, u32[]{:S(2)}, u32[]{:S(2)}) collective-permute-start(bf16[2,112,1152]{2,1,0:T(8,128)(2,1)S(1)} %pad_maximum_fusion.3), channel_id=1, source_target_pairs={{0,8},{4,12},{8,0},{12,4},{16,24},{20,28},{24,16},{28,20},{1,9},{5... | collective-permute-start | bytes 1548296 | tf_op jit(solution)/shard_map/ppermute | solution.py:476
  42.4 24.2 %collective-permute-start.8 = (bf16[112,2048]{1,0:T(8,128)(2,1)S(1)}, bf16[112,2048]{1,0:T(8,128)(2,1)S(1)}, u32[]{:S(2)}, u32[]{:S(2)}) collective-permute-start(bf16[112,2048]{1,0:T(8,128)(2,1)S(1)} %slice.80), channel_id=1, source_target_pairs={{0,2},{2,0},{1,3},{3,1},{4,6},{6,4},{5,7},{7,5},{8,10},{10,8},{9,1... | collective-permute-start | bytes 1376264 | tf_op jit(solution)/shard_map/ppermute | solution.py:489
  66.6 9.8 %collective-permute-start.10 = (bf16[2,2,112,1152]{3,2,0,1:T(8,128)(2,1)S(1)}, bf16[2,2,112,1152]{3,2,0,1:T(8,128)(2,1)}, u32[]{:S(2)}, u32[]{:S(2)}) collective-permute-start(bf16[2,2,112,1152]{3,2,0,1:T(8,128)(2,1)S(1)} %pad_maximum_fusion), channel_id=1, source_target_pairs={{0,4},{4,0},{8,12},{12,8},{16,20},{20,16},{24,28},{28,24},{1,5},{5... | collective-permute-start | bytes 3096584 | tf_op jit(solution)/shard_map/ppermute | solution.py:476
  68.3 7.2 %collective-permute-start.9 = (bf16[2,2,112,1024]{3,2,1,0:T(8,128)(2,1)S(1)}, bf16[2,2,112,1024]{3,2,1,0:T(8,128)(2,1)S(1)}, u32[]{:S(2)}, u32[]{:S(2)}) collective-permute-start(bf16[2,2,112,1024]{3,2,1,0:T(8,128)(2,1)S(1)} %pad_maximum_fusion.1), channel_id=1, source_target_pairs={{0,4},{4,0},{8,12},{12,8},{16,20},{20,16},{24,28},{28,24},{1,5},{5... | collective-permute-start | bytes 2752520 | tf_op jit(solution)/shard_map/ppermute | solution.py:476
  68.4 7.1 %collective-permute-start.11 = (bf16[112,896]{1,0:T(8,128)(2,1)S(1)}, bf16[112,896]{1,0:T(8,128)(2,1)S(1)}, u32[]{:S(2)}, u32[]{:S(2)}) collective-permute-start(bf16[112,896]{1,0:T(8,128)(2,1)S(1)} %slice.81), channel_id=1, source_target_pairs={{0,2},{2,0},{1,3},{3,1},{4,6},{6,4},{5,7},{7,5},{8,10},{10,8},{9,1... | collective-permute-start | bytes 602120 | tf_op jit(solution)/shard_map/ppermute | solution.py:489
  77.5 204.1 %reduce-scatter.3.cloned.1.call-start = ((), (), s32[]{:S(2)}) async-start(), calls=%async_computation.4 | async-start | bytes 5734400 | tf_op jit(solution)/shard_map/reduce_scatter | solution.py:620
  77.5 10.8 %collective-permute-start.12 = (bf16[256,896]{1,0:T(8,128)(2,1)S(1)}, bf16[256,896]{1,0:T(8,128)(2,1)S(1)}, u32[]{:S(2)}, u32[]{:S(2)}) collective-permute-start(bf16[256,896]{1,0:T(8,128)(2,1)S(1)} %get-tuple-element.234.refs_4_), channel_id=1, source_target_pairs={{0,1},{1,0},{2,3},{3,2},{4,5},{5,4},{6,7},{7,6},{8,9},{9,8},{10,11... | collective-permute-start | bytes 1376264 | tf_op jit(solution)/shard_map/ppermute | solution.py:489
  88.3 46.6 %copy-start.19 = (bf16[256,896]{1,0:T(8,128)(2,1)}, bf16[256,896]{1,0:T(8,128)(2,1)S(1)}, u32[]{:S(2)}) copy-start(bf16[256,896]{1,0:T(8,128)(2,1)S(1)} %collective-permute-done.12.refs_6_) | copy-start | bytes 1376260
  91.8 11.4 %collective-permute-start.13 = (bf16[2,256,256]{2,1,0:T(8,128)(2,1)}, bf16[2,256,256]{2,1,0:T(8,128)(2,1)S(1)}, u32[]{:S(2)}, u32[]{:S(2)}) collective-permute-start(bf16[2,256,256]{2,1,0:T(8,128)(2,1)} %get-tuple-element.218.kv0_ref), channel_id=1, source_target_pairs={{0,1},{1,2},{2,3},{4,5},{5,6},{6,7},{8,9},{9,10},{10,11},{12,13},{... | collective-permute-start | bytes 786440 | tf_op jit(solution)/shard_map/ppermute | solution.py:576
  94.0 10.4 %collective-permute-start.14 = (bf16[2,256,256]{2,1,0:T(8,128)(2,1)}, bf16[2,256,256]{2,1,0:T(8,128)(2,1)S(1)}, u32[]{:S(2)}, u32[]{:S(2)}) collective-permute-start(bf16[2,256,256]{2,1,0:T(8,128)(2,1)} %get-tuple-element.218.kv0_ref), channel_id=1, source_target_pairs={{0,2},{1,3},{4,6},{5,7},{8,10},{9,11},{12,14},{13,15},{16,18},{17,... | collective-permute-start | bytes 786440 | tf_op jit(solution)/shard_map/ppermute | solution.py:576
  114.4 18.4 %collective-permute-start.15 = (bf16[256,896]{1,0:T(8,128)(2,1)}, bf16[256,896]{1,0:T(8,128)(2,1)S(1)}, u32[]{:S(2)}, u32[]{:S(2)}) collective-permute-start(bf16[256,896]{1,0:T(8,128)(2,1)} %get-tuple-element.231.refs_0_), channel_id=1, source_target_pairs={{0,4},{4,0},{1,5},{5,1},{2,6},{6,2},{3,7},{7,3},{8,12},{12,8},{9,1... | collective-permute-start | bytes 1376264 | tf_op jit(solution)/shard_map/ppermute | solution.py:489
  116.5 17.7 %collective-permute-start.16 = (bf16[256,896]{1,0:T(8,128)(2,1)}, bf16[256,896]{1,0:T(8,128)(2,1)S(1)}, u32[]{:S(2)}, u32[]{:S(2)}) collective-permute-start(bf16[256,896]{1,0:T(8,128)(2,1)} %get-tuple-element.231.refs_0_), channel_id=1, source_target_pairs={{0,1},{1,0},{2,3},{3,2},{4,5},{5,4},{6,7},{7,6},{8,9},{9,8},{10,11... | collective-permute-start | bytes 1376264 | tf_op jit(solution)/shard_map/ppermute | solution.py:489
  123.2 11.0 %collective-permute-start.17 = (bf16[256,896]{1,0:T(8,128)(2,1)S(1)}, bf16[256,896]{1,0:T(8,128)(2,1)S(1)}, u32[]{:S(2)}, u32[]{:S(2)}) collective-permute-start(bf16[256,896]{1,0:T(8,128)(2,1)S(1)} %get-tuple-element.234.refs_4_), channel_id=1, source_target_pairs={{0,4},{4,0},{1,5},{5,1},{2,6},{6,2},{3,7},{7,3},{8,12},{12,8},{9,1... | collective-permute-start | bytes 1376264 | tf_op jit(solution)/shard_map/ppermute | solution.py:489
  134.2 3.2 collective-permute-start.21
  134.9 3.3 collective-permute-start.22
  135.0 29.1 %collective-permute-start.23 = (bf16[256,896]{1,0:T(8,128)(2,1)S(1)}, bf16[256,896]{1,0:T(8,128)(2,1)S(1)}, u32[]{:S(2)}, u32[]{:S(2)}) collective-permute-start(bf16[256,896]{1,0:T(8,128)(2,1)S(1)} %get-tuple-element.245.refs_4_), channel_id=1, source_target_pairs={{0,4},{4,0},{1,5},{5,1},{2,6},{6,2},{3,7},{7,3},{8,12},{12,8},{9,1... | collective-permute-start | bytes 1376264 | tf_op jit(solution)/shard_map/ppermute | solution.py:489
  135.6 28.5 %collective-permute-start.24 = (bf16[256,896]{1,0:T(8,128)(2,1)S(1)}, bf16[256,896]{1,0:T(8,128)(2,1)S(1)}, u32[]{:S(2)}, u32[]{:S(2)}) collective-permute-start(bf16[256,896]{1,0:T(8,128)(2,1)S(1)} %get-tuple-element.245.refs_4_), channel_id=1, source_target_pairs={{0,1},{1,0},{2,3},{3,2},{4,5},{5,4},{6,7},{7,6},{8,9},{9,8},{10,11... | collective-permute-start | bytes 1376264 | tf_op jit(solution)/shard_map/ppermute | solution.py:489
  137.1 27.6 %collective-permute-start.18 = (bf16[256,896]{1,0:T(8,128)(2,1)}, bf16[256,896]{1,0:T(8,128)(2,1)S(1)}, u32[]{:S(2)}, u32[]{:S(2)}) collective-permute-start(bf16[256,896]{1,0:T(8,128)(2,1)} %get-tuple-element.230.refs_0_), channel_id=1, source_target_pairs={{0,4},{4,0},{1,5},{5,1},{2,6},{6,2},{3,7},{7,3},{8,12},{12,8},{9,1... | collective-permute-start | bytes 1376264 | tf_op jit(solution)/shard_map/ppermute | solution.py:489
  137.4 27.9 %collective-permute-start.19 = (bf16[256,896]{1,0:T(8,128)(2,1)}, bf16[256,896]{1,0:T(8,128)(2,1)S(1)}, u32[]{:S(2)}, u32[]{:S(2)}) collective-permute-start(bf16[256,896]{1,0:T(8,128)(2,1)} %get-tuple-element.230.refs_0_), channel_id=1, source_target_pairs={{0,1},{1,0},{2,3},{3,2},{4,5},{5,4},{6,7},{7,6},{8,9},{9,8},{10,11... | collective-permute-start | bytes 1376264 | tf_op jit(solution)/shard_map/ppermute | solution.py:489
  138.2 29.4 %collective-permute-start.20 = (bf16[256,896]{1,0:T(8,128)(2,1)}, bf16[256,896]{1,0:T(8,128)(2,1)S(1)}, u32[]{:S(2)}, u32[]{:S(2)}) collective-permute-start(bf16[256,896]{1,0:T(8,128)(2,1)} %get-tuple-element.230.refs_0_), channel_id=1, source_target_pairs={{0,5},{1,4},{4,1},{5,0},{2,7},{3,6},{6,3},{7,2},{8,13},{9,12},{12,... | collective-permute-start | bytes 1376264 | tf_op jit(solution)/shard_map/ppermute | solution.py:492
  164.2 3.5 collective-permute-start.25
  164.3 29.5 %collective-permute-start.26 = (bf16[256,896]{1,0:T(8,128)(2,1)}, bf16[256,896]{1,0:T(8,128)(2,1)}, u32[]{:S(2)}, u32[]{:S(2)}) collective-permute-start(bf16[256,896]{1,0:T(8,128)(2,1)} %get-tuple-element.257), channel_id=1, source_target_pairs={{0,4},{4,0},{1,5},{5,1},{2,6},{6,2},{3,7},{7,3},{8,12},{12,8},{9,1... | collective-permute-start | bytes 1376264 | tf_op jit(solution)/shard_map/ppermute | solution.py:489
  164.8 29.1 %collective-permute-start.27 = (bf16[256,896]{1,0:T(8,128)(2,1)}, bf16[256,896]{1,0:T(8,128)(2,1)}, u32[]{:S(2)}, u32[]{:S(2)}) collective-permute-start(bf16[256,896]{1,0:T(8,128)(2,1)} %get-tuple-element.258), channel_id=1, source_target_pairs={{0,1},{1,0},{2,3},{3,2},{4,5},{5,4},{6,7},{7,6},{8,9},{9,8},{10,11... | collective-permute-start | bytes 1376264 | tf_op jit(solution)/shard_map/ppermute | solution.py:489
  165.3 30.3 %collective-permute-start.28 = (bf16[256,896]{1,0:T(8,128)(2,1)}, bf16[256,896]{1,0:T(8,128)(2,1)}, u32[]{:S(2)}, u32[]{:S(2)}) collective-permute-start(bf16[256,896]{1,0:T(8,128)(2,1)} %get-tuple-element.259), channel_id=1, source_target_pairs={{0,5},{1,4},{4,1},{5,0},{2,7},{3,6},{6,3},{7,2},{8,13},{9,12},{12,... | collective-permute-start | bytes 1376264 | tf_op jit(solution)/shard_map/ppermute | solution.py:492
  193.2 29.0 %collective-permute-start.32 = (bf16[2,256,896]{2,1,0:T(8,128)(2,1)}, bf16[2,256,896]{2,1,0:T(8,128)(2,1)S(1)}, u32[]{:S(2)}, u32[]{:S(2)}) collective-permute-start(bf16[2,256,896]{2,1,0:T(8,128)(2,1)} %get-tuple-element.270), channel_id=1, source_target_pairs={{0,4},{4,0},{1,5},{5,1},{2,6},{6,2},{3,7},{7,3},{8,12},{12,8},{9,1... | collective-permute-start | bytes 2752520 | tf_op jit(solution)/shard_map/ppermute | solution.py:489
  193.2 28.9 %collective-permute-start.33 = (bf16[2,256,896]{2,1,0:T(8,128)(2,1)}, bf16[2,256,896]{2,1,0:T(8,128)(2,1)S(1)}, u32[]{:S(2)}, u32[]{:S(2)}) collective-permute-start(bf16[2,256,896]{2,1,0:T(8,128)(2,1)} %get-tuple-element.271), channel_id=1, source_target_pairs={{0,4},{4,0},{1,5},{5,1},{2,6},{6,2},{3,7},{7,3},{8,12},{12,8},{9,1... | collective-permute-start | bytes 2752520 | tf_op jit(solution)/shard_map/ppermute | solution.py:489
  193.7 28.3 %collective-permute-start.29 = (bf16[256,896]{1,0:T(8,128)(2,1)}, bf16[256,896]{1,0:T(8,128)(2,1)S(1)}, u32[]{:S(2)}, u32[]{:S(2)}) collective-permute-start(bf16[256,896]{1,0:T(8,128)(2,1)} %get-tuple-element.261), channel_id=1, source_target_pairs={{0,4},{4,0},{1,5},{5,1},{2,6},{6,2},{3,7},{7,3},{8,12},{12,8},{9,1... | collective-permute-start | bytes 1376264 | tf_op jit(solution)/shard_map/ppermute | solution.py:489
  193.8 28.3 %collective-permute-start.30 = (bf16[256,896]{1,0:T(8,128)(2,1)}, bf16[256,896]{1,0:T(8,128)(2,1)S(1)}, u32[]{:S(2)}, u32[]{:S(2)}) collective-permute-start(bf16[256,896]{1,0:T(8,128)(2,1)} %get-tuple-element.262), channel_id=1, source_target_pairs={{0,1},{1,0},{2,3},{3,2},{4,5},{5,4},{6,7},{7,6},{8,9},{9,8},{10,11... | collective-permute-start | bytes 1376264 | tf_op jit(solution)/shard_map/ppermute | solution.py:489
  195.6 26.5 %collective-permute-start.31 = (bf16[256,896]{1,0:T(8,128)(2,1)}, bf16[256,896]{1,0:T(8,128)(2,1)S(1)}, u32[]{:S(2)}, u32[]{:S(2)}) collective-permute-start(bf16[256,896]{1,0:T(8,128)(2,1)} %get-tuple-element.263), channel_id=1, source_target_pairs={{0,5},{1,4},{4,1},{5,0},{2,7},{3,6},{6,3},{7,2},{8,13},{9,12},{12,... | collective-permute-start | bytes 1376264 | tf_op jit(solution)/shard_map/ppermute | solution.py:492
  223.1 107.9 %reduce-scatter.5.cloned.1.call-start = ((), (), s32[]{:S(2)}) async-start(), calls=%async_computation.5 | async-start | bytes 2867200 | tf_op jit(solution)/shard_map/reduce_scatter | solution.py:648
  224.3 15.3 %collective-permute-start.34 = (bf16[256,896]{1,0:T(8,128)(2,1)S(1)}, bf16[256,896]{1,0:T(8,128)(2,1)S(1)}, u32[]{:S(2)}, u32[]{:S(2)}) collective-permute-start(bf16[256,896]{1,0:T(8,128)(2,1)S(1)} %fusion.11), channel_id=1, source_target_pairs={{0,1},{1,0},{2,3},{3,2},{4,5},{5,4},{6,7},{7,6},{8,9},{9,8},{10,11... | collective-permute-start | bytes 1376264 | tf_op jit(solution)/shard_map/ppermute | solution.py:489
  239.8 16.2 %collective-permute-start.35 = (bf16[256,896]{1,0:T(8,128)(2,1)S(1)}, bf16[256,896]{1,0:T(8,128)(2,1)}, u32[]{:S(2)}, u32[]{:S(2)}) collective-permute-start(bf16[256,896]{1,0:T(8,128)(2,1)S(1)} %fusion.12), channel_id=1, source_target_pairs={{0,1},{1,0},{2,3},{3,2},{4,5},{5,4},{6,7},{7,6},{8,9},{9,8},{10,11... | collective-permute-start | bytes 1376264 | tf_op jit(solution)/shard_map/ppermute | solution.py:489
  239.9 18.7 %collective-permute-start.36 = (bf16[256,256]{1,0:T(8,128)(2,1)}, bf16[256,256]{1,0:T(8,128)(2,1)S(1)}, u32[]{:S(2)}, u32[]{:S(2)}) collective-permute-start(bf16[256,256]{1,0:T(8,128)(2,1)} %get-tuple-element.318), channel_id=1, source_target_pairs={{1,0},{2,1},{3,2},{5,4},{6,5},{7,6},{9,8},{10,9},{11,10},{13,12},{... | collective-permute-start | bytes 393224 | tf_op jit(solution)/shard_map/ppermute | solution.py:635
  241.1 17.5 %collective-permute-start.37 = (bf16[256,256]{1,0:T(8,128)(2,1)}, bf16[256,256]{1,0:T(8,128)(2,1)S(1)}, u32[]{:S(2)}, u32[]{:S(2)}) collective-permute-start(bf16[256,256]{1,0:T(8,128)(2,1)} %get-tuple-element.319), channel_id=1, source_target_pairs={{2,0},{3,1},{6,4},{7,5},{10,8},{11,9},{14,12},{15,13},{18,16},{19,... | collective-permute-start | bytes 393224 | tf_op jit(solution)/shard_map/ppermute | solution.py:635
  256.0 7.0 %collective-permute-start.38 = (bf16[256,256]{1,0:T(8,128)(2,1)}, bf16[256,256]{1,0:T(8,128)(2,1)S(1)}, u32[]{:S(2)}, u32[]{:S(2)}) collective-permute-start(bf16[256,256]{1,0:T(8,128)(2,1)} %get-tuple-element.320), channel_id=1, source_target_pairs={{1,0},{2,1},{3,2},{5,4},{6,5},{7,6},{9,8},{10,9},{11,10},{13,12},{... | collective-permute-start | bytes 393224 | tf_op jit(solution)/shard_map/ppermute | solution.py:635
  257.3 11.9 %collective-permute-start.39 = (bf16[256,256]{1,0:T(8,128)(2,1)}, bf16[256,256]{1,0:T(8,128)(2,1)S(1)}, u32[]{:S(2)}, u32[]{:S(2)}) collective-permute-start(bf16[256,256]{1,0:T(8,128)(2,1)} %get-tuple-element.321), channel_id=1, source_target_pairs={{2,0},{3,1},{6,4},{7,5},{10,8},{11,9},{14,12},{15,13},{18,16},{19,... | collective-permute-start | bytes 393224 | tf_op jit(solution)/shard_map/ppermute | solution.py:635
  258.6 10.6 %copy-start.27 = (bf16[256,256]{1,0:T(8,128)(2,1)}, bf16[256,256]{1,0:T(8,128)(2,1)S(1)}, u32[]{:S(2)}) copy-start(bf16[256,256]{1,0:T(8,128)(2,1)S(1)} %collective-permute-done.36.refs_0_) | copy-start | bytes 393220
  258.6 10.6 %copy-start.28 = (bf16[256,256]{1,0:T(8,128)(2,1)}, bf16[256,256]{1,0:T(8,128)(2,1)S(1)}, u32[]{:S(2)}) copy-start(bf16[256,256]{1,0:T(8,128)(2,1)S(1)} %collective-permute-done.37.refs_1_) | copy-start | bytes 393220
  262.9 6.2 %copy-start.29 = (bf16[256,256]{1,0:T(8,128)(2,1)}, bf16[256,256]{1,0:T(8,128)(2,1)S(1)}, u32[]{:S(2)}) copy-start(bf16[256,256]{1,0:T(8,128)(2,1)S(1)} %collective-permute-done.38.refs_2_) | copy-start | bytes 393220
  281.6 6.0 %collective-permute-start.40 = (bf16[448,2176]{1,0:T(8,128)(2,1)}, bf16[448,2176]{1,0:T(8,128)(2,1)}, u32[]{:S(2)}, u32[]{:S(2)}) collective-permute-start(bf16[448,2176]{1,0:T(8,128)(2,1)} %get-tuple-element.328), channel_id=1, source_target_pairs={{0,4},{4,0},{8,12},{12,8},{16,20},{20,16},{24,28},{28,24},{1,5},{5... | collective-permute-start | bytes 5849096 | tf_op jit(solution)/shard_map/ppermute | solution.py:476
  290.0 21.8 %collective-permute-start.42 = (bf16[1,2,112,1024]{3,2,1,0:T(8,128)(2,1)S(1)}, bf16[1,2,112,1024]{3,2,1,0:T(8,128)(2,1)S(1)}, u32[]{:S(2)}, u32[]{:S(2)}) collective-permute-start(bf16[1,2,112,1024]{3,2,1,0:T(8,128)(2,1)S(1)} %fusion.13), channel_id=1, source_target_pairs={{0,16},{4,20},{8,24},{12,28},{16,0},{20,4},{24,8},{28,12},{1,17},{... | collective-permute-start | bytes 1376264 | tf_op jit(solution)/shard_map/ppermute | solution.py:476
  291.0 24.1 %collective-permute-start.41 = (bf16[2,1,112,1152]{3,2,0,1:T(8,128)(2,1)S(1)}, bf16[2,1,112,1152]{3,2,0,1:T(8,128)(2,1)S(1)}, u32[]{:S(2)}, u32[]{:S(2)}) collective-permute-start(bf16[2,1,112,1152]{3,2,0,1:T(8,128)(2,1)S(1)} %fusion.9), channel_id=1, source_target_pairs={{0,8},{4,12},{8,0},{12,4},{16,24},{20,28},{24,16},{28,20},{1,9},{5... | collective-permute-start | bytes 1548296 | tf_op jit(solution)/shard_map/ppermute | solution.py:476
  292.6 22.5 %collective-permute-start.43 = (bf16[112,2560]{1,0:T(8,128)(2,1)S(1)}, bf16[112,2560]{1,0:T(8,128)(2,1)S(1)}, u32[]{:S(2)}, u32[]{:S(2)}) collective-permute-start(bf16[112,2560]{1,0:T(8,128)(2,1)S(1)} %dynamic-slice_bitcast_fusion.1), channel_id=1, source_target_pairs={{0,0},{2,4},{4,6},{6,2},{1,1},{3,5},{5,7},{7,3},{8,8},{10,12},{12,... | collective-permute-start | bytes 1720328 | tf_op jit(solution)/shard_map/ppermute | solution.py:671
  315.2 7.0 %collective-permute-start.44 = (bf16[1,1,112,1152]{3,2,1,0:T(8,128)(2,1)S(1)}, bf16[1,1,112,1152]{3,2,1,0:T(8,128)(2,1)S(1)}, u32[]{:S(2)}, u32[]{:S(2)}) collective-permute-start(bf16[1,1,112,1152]{3,2,1,0:T(8,128)(2,1)S(1)} %fusion.19), channel_id=1, source_target_pairs={{0,16},{4,20},{8,24},{12,28},{16,0},{20,4},{24,8},{28,12},{1,17},{... | collective-permute-start | bytes 774152 | tf_op jit(solution)/shard_map/ppermute | solution.py:476
  316.0 5.6 %collective-permute-start.45 = (bf16[1,1,112,1024]{3,2,1,0:T(8,128)(2,1)S(1)}, bf16[1,1,112,1024]{3,2,1,0:T(8,128)(2,1)S(1)}, u32[]{:S(2)}, u32[]{:S(2)}) collective-permute-start(bf16[1,1,112,1024]{3,2,1,0:T(8,128)(2,1)S(1)} %fusion.20), channel_id=1, source_target_pairs={{0,8},{4,12},{8,0},{12,4},{16,24},{20,28},{24,16},{28,20},{1,9},{5... | collective-permute-start | bytes 688136 | tf_op jit(solution)/shard_map/ppermute | solution.py:476
  316.9 14.1 %collective-permute-start.46 = (bf16[112,2560]{1,0:T(8,128)(2,1)S(1)}, bf16[112,2560]{1,0:T(8,128)(2,1)S(1)}, u32[]{:S(2)}, u32[]{:S(2)}) collective-permute-start(bf16[112,2560]{1,0:T(8,128)(2,1)S(1)} %dynamic-slice_bitcast_fusion), channel_id=1, source_target_pairs={{0,4},{2,0},{4,2},{6,6},{1,5},{3,1},{5,3},{7,7},{8,12},{10,8},{12,... | collective-permute-start | bytes 1720328 | tf_op jit(solution)/shard_map/ppermute | solution.py:671
  331.2 15.2 %collective-permute-start.49 = (bf16[28,2176]{1,0:T(8,128)(2,1)S(1)}, bf16[28,2176]{1,0:T(8,128)(2,1)S(1)}, u32[]{:S(2)}, u32[]{:S(2)}) collective-permute-start(bf16[28,2176]{1,0:T(8,128)(2,1)S(1)} %get-tuple-element.418), channel_id=1, source_target_pairs={{0,3},{1,0},{2,1},{3,2},{4,7},{5,4},{6,5},{7,6},{8,11},{9,8},{10,9... | collective-permute-start | bytes 365576 | tf_op jit(solution)/shard_map/ppermute | solution.py:486
  333.6 20.8 %collective-permute-start.48 = (bf16[28,2176]{1,0:T(8,128)(2,1)S(1)}, bf16[28,2176]{1,0:T(8,128)(2,1)S(1)}, u32[]{:S(2)}, u32[]{:S(2)}) collective-permute-start(bf16[28,2176]{1,0:T(8,128)(2,1)S(1)} %get-tuple-element.419), channel_id=1, source_target_pairs={{0,2},{1,3},{2,0},{3,1},{4,6},{5,7},{6,4},{7,5},{8,10},{9,11},{10,... | collective-permute-start | bytes 365576 | tf_op jit(solution)/shard_map/ppermute | solution.py:486
  335.6 18.8 %collective-permute-start.47 = (bf16[28,2176]{1,0:T(8,128)(2,1)S(1)}, bf16[28,2176]{1,0:T(8,128)(2,1)S(1)}, u32[]{:S(2)}, u32[]{:S(2)}) collective-permute-start(bf16[28,2176]{1,0:T(8,128)(2,1)S(1)} %get-tuple-element.417), channel_id=1, source_target_pairs={{0,1},{1,2},{2,3},{3,0},{4,5},{5,6},{6,7},{7,4},{8,9},{9,10},{10,1... | collective-permute-start | bytes 365576 | tf_op jit(solution)/shard_map/ppermute | solution.py:486
  336.9 20.4 %collective-permute-start.51 = (bf16[112,1280]{1,0:T(8,128)(2,1)S(1)}, bf16[112,1280]{1,0:T(8,128)(2,1)S(1)}, u32[]{:S(2)}, u32[]{:S(2)}) collective-permute-start(bf16[112,1280]{1,0:T(8,128)(2,1)S(1)} %get-tuple-element.416), channel_id=1, source_target_pairs={{0,4},{2,0},{4,2},{6,6},{1,5},{3,1},{5,3},{7,7},{8,12},{10,8},{12,... | collective-permute-start | bytes 860168 | tf_op jit(solution)/shard_map/ppermute | solution.py:671
  344.5 16.3 %collective-permute-start.50 = (bf16[112,1280]{1,0:T(8,128)(2,1)S(1)}, bf16[112,1280]{1,0:T(8,128)(2,1)S(1)}, u32[]{:S(2)}, u32[]{:S(2)}) collective-permute-start(bf16[112,1280]{1,0:T(8,128)(2,1)S(1)} %get-tuple-element.415), channel_id=1, source_target_pairs={{0,0},{2,4},{4,6},{6,2},{1,1},{3,5},{5,7},{7,3},{8,8},{10,12},{12,... | collective-permute-start | bytes 860168 | tf_op jit(solution)/shard_map/ppermute | solution.py:671
  (33 other events, 68.9 us)
Sparse Core Ops, SparseCore 0:
  10.0 65.5 all-gather.2
  77.6 48.7 all-gather.4
  223.1 57.1 reduce-scatter.2
  283.8 47.1 reduce-scatter.4

commit v5 on v4

--- a/solution.py
+++ b/solution.py
@@ -416,9 +416,13 @@
 
 def woven(core, mine, got):
     n=len(mine); blocks,rows,_=mine[0].shape
+    size=blocks.bit_length()-1
+    def turned(j):
+        return sum(((j>>k)&1)<<(size-1-k) for k in range(size))
+    places=[lambda j:(j,0,0), lambda j:(turned(j),0,0)]
     shapes=[jax.ShapeDtypeStruct((2*blocks*rows,v.shape[2]),v.dtype) for v in mine]
     return pl.pallas_call(
-        woven_kernel, grid=(blocks,), in_specs=[pl.BlockSpec(memory_space=pltpu.SMEM)]+[pl.BlockSpec((None,)+v.shape[1:],lambda j:(j,0,0)) for v in mine+got],
+        woven_kernel, grid=(blocks,), in_specs=[pl.BlockSpec(memory_space=pltpu.SMEM)]+[pl.BlockSpec((None,)+v.shape[1:],places[k%n]) for k,v in enumerate(mine+got)],
         out_specs=[pl.BlockSpec((2*rows,v.shape[2]),lambda j:(j,0)) for v in mine], out_shape=shapes,
         compiler_params=pltpu.CompilerParams(vmem_limit_bytes=LIMIT), cost_estimate=COST,
         name="woven",
@@ -479,8 +483,7 @@
         bit = order[k]
         got = swapped(blocks, bit)
         low = (group_rank // bit) % 2 == 0
-        at = sum(earlier > bit for earlier in order[:k])
-        return jnp.stack([jnp.where(low, blocks, got), jnp.where(low, got, blocks)], axis=at)
+        return jnp.stack([jnp.where(low, blocks, got), jnp.where(low, got, blocks)])
 
     def around(values_in, steps):
         return lax.ppermute(values_in, ctx, [(s, (s + steps) % parts) for s in range(parts)])
@@ -560,11 +563,13 @@
     if even:
         firsts, gots = ([v.reshape((-1,) + v.shape[-2:]) for v in part] for part in firsts)
         out_set, in_set = woven(core.reshape(1), firsts, gots)
-        crossed.append(other(upstream[0], "zb"))
-        out_set, in_set, crossed = after((out_set, in_set, crossed))
     else:
-        out_set, in_set = (side.reshape(-1, side.shape[-1]) for side in firsts)
-        crossed.append(other(upstream[0], "zb"))
+        out_set, in_set = (
+            jnp.transpose(
+                side, [list(reversed(order)).index(bit) for bit in reversed(bits)] + [-2, -1]
+            ).reshape(-1, side.shape[-1])
+            for side, order in zip(firsts, gather_orders)
+        )
     sets = (own_set, other_set)
     own_quarter = (core == far_half).astype(jnp.int32).reshape(1)
 
@@ -578,8 +583,7 @@
     ]
 
     kvs, rot_query, upstream = after((kvs, rot_query, upstream))
-    crossed += [other(u, "zb") for u in upstream[1:]]
-    upstream_pieces = [[u, other(u, "core"), v] for u, v in zip(upstream, crossed)]
+    crossed.append(other(upstream[0], "zb"))
 
     begins = begins[:, None, :]
     exchanged = []
@@ -588,7 +592,12 @@
         normed_two, *held = attend(
             m, base, rot_query, kvs, begins, out_set, tokens, rows_table, held
         )
+        if m == 0:
+            upstream, crossed, normed_two = after((upstream, crossed, normed_two))
         exchanged.append([normed_two, other(normed_two, "core"), other(normed_two, "zb")])
+        if m == 0:
+            crossed += [other(u, "zb") for u in upstream[1:]]
+            upstream_pieces = [[u, other(u, "core"), v] for u, v in zip(upstream, crossed)]
     exchanged[-1].append(corner(normed_two))
     exchanged[:-1], upstream_pieces[0], exchanged[-1][0] = after(
         (exchanged[:-1], upstream_pieces[0], normed_two)
@@ -612,11 +621,11 @@
     out_far = other(partials[3], "core")
 
     left, pair, act = after(before[4:], backs[0])
+    feed_down = weights(left, 1, act, 256)
+    backs[-1][1:3], left, pair, feed_down = after((backs[-1][1:3], left, pair, feed_down))
     feed_pair = weights(left, 0, pair, 512)
-    feed_down = weights(left, 1, act, 640)
-    backs, feed_pair, feed_down, out_near, out_far = after(
-        (backs, feed_pair, feed_down, out_near, out_far)
-    )
+    backs, feed_pair, out_near, out_far = after((backs, feed_pair, out_near, out_far))
+    feed_down = lax.psum_scatter(feed_down, "grp", scatter_dimension=0, tiled=True)
     feed_pair = lax.psum_scatter(feed_pair, "grp", scatter_dimension=0, tiled=True)
 
     far = []
@@ -638,14 +647,23 @@
         )
         if m < micros - 1:
             out_far, ended = after((out_far, ended))
+    def delivered(half, k):
+        part = lax.dynamic_index_in_dim(
+            half.reshape((2, -1) + half.shape[1:]), (core + far_half + k) % 2, 0, keepdims=False
+        )
+        return lax.ppermute(
+            part, ("core", "zh"), [(2 * s + a, 2 * (s ^ a ^ k) + s) for s in range(2) for a in range(2)]
+        )
+
+    far, feed_down = after((far, feed_down))
+    down_parts = [delivered(feed_down, k) for k in range(2)]
     grad_middle, branch_low, query_grad, own_pair, gain_sum = ended
     input_grad, keep, send = finish(
         (group_rank % 2).reshape(1), query_grad, own_pair, far, cosines, sines, in_set,
         rows_table, tokens, normed_one, grad_middle, mixed, branch_low, spread, gain_sum,
         block_rows if even else 0,
     )
-    keep, send, feed_pair, feed_down = after((keep, send, feed_pair, feed_down))
-    feed_down = lax.psum_scatter(feed_down, "grp", scatter_dimension=0, tiled=True)
+    keep, send, down_parts = after((keep, send, down_parts))
     if not even:
         both = jnp.concatenate([keep, send]).reshape(groups // 2, 2, block_rows, -1)
         keep, send = (
@@ -664,28 +682,18 @@
         got = swapped(sent.astype(bf16), bit)
         return (kept.astype(f32) + got.astype(f32)).reshape((size // 2,) + blocks.shape[1:])
 
-    def delivered(half, k):
-        part = lax.dynamic_index_in_dim(
-            half.reshape((2, -1) + half.shape[1:]), (core + far_half + k) % 2, 0, keepdims=False
-        )
-        return lax.ppermute(
-            part, ("core", "zh"), [(2 * s + a, 2 * (s ^ a ^ k) + s) for s in range(2) for a in range(2)]
-        )
-
     blocks = keep.astype(f32) + swapped(send, 1).astype(f32)
     blocks = blocks.reshape(groups // 2, block_rows, -1)
     cut = QW + 2 * LANES
     sides = [blocks[:, :, :cut], blocks[:, :, cut:]]
     orders = [bits[1:], bits[:0:-1]]
-    pair_parts = []
+    pair_parts = [delivered(feed_pair, 0)]
     for k in range(len(bits) - 1):
-        if k < 2:
-            pair_parts.append(delivered(feed_pair, k))
         sides = [halved(side, order, k) for side, order in zip(sides, orders)]
-        if k == len(bits) - 2:
-            sides, feed_down = after((sides, feed_down))
-        sides, pair_parts, feed_pair = after((sides, pair_parts, feed_pair))
-    down_parts = [delivered(feed_down, k) for k in range(2)]
+        if k == len(bits) - 3:
+            sides, pair_parts, feed_pair = after((sides, pair_parts, feed_pair))
+            pair_parts.append(delivered(feed_pair, 1))
+    sides, pair_parts = after((sides, pair_parts))
     attention_block = jnp.concatenate([side[0] for side in sides], axis=1).astype(bf16)
     attention_block = attention_block.reshape(parts, weight_rows, -1)
 

time: 374 us -> 363 us (0.971)
  the two profiles are of different devices: /device:TPU:1 before, /device:TPU:0 now
where the time goes in v5:
time: 363 us; the launch traced here: 357 us
  Pallas kernels  144 us (40%)
  waiting for transfers between devices  95 us (26%)
  starting transfers between devices  66.4 us (18%)
  other arithmetic  19.5 us (5%)
  local copies, waits for them, and re-layouts  17.8 us (5%)
  between operations  15 us (4%)
    pallas_call x2, Pallas kernels, feed(): pl.pallas_call(functools.partial(feed_kernel, parts=parts, micro=micro, k...  48.5 us
    ppermute x11, waiting for transfers between devices, swapped(): return lax.ppermute(values_in, dp, [(s, s ^ bit) for s in range(groups)])  38.7 us
    pallas_call x2, Pallas kernels, attend_back(): pl.pallas_call(functools.partial(attend_back_kernel, count=len(gs)), grid...  26.6 us
    pallas_call x2, Pallas kernels, weights(): pl.pallas_call(weights_kernel, grid=(width // chunk,), in_specs=[pl.Block...  25.6 us
    ppermute x22, starting transfers between devices, other(): return lax.ppermute(values_in, axis, [(0, 1), (1, 0)])  21 us
    pallas_call x2, Pallas kernels, attend(): pl.pallas_call(attend_kernel, grid=(nq,), in_specs=[pl.BlockSpec(memory_s...  18.6 us
    ppermute x6, waiting for transfers between devices, around(): lax.ppermute(values_in, ctx, [(s, (s + steps) % parts) for s in range(par...  15.1 us
    ppermute x22, waiting for transfers between devices, other(): return lax.ppermute(values_in, axis, [(0, 1), (1, 0)])  14.5 us
  transfers between devices with their start and end apart: 56, of which 19 were waited for; matrix products, arithmetic and copies ran while one was open for 7% of the time, Pallas kernels for 40%

profile of v5, /device:TPU:0, one launch (start us, length us, event | category | flops | bytes accessed | tf_op | source)
XLA Modules:
  0.0 357.2 jit_solution(14239302927930183782)
XLA Ops:
  7.3 2.2 fusion.8
  9.9 5.1 %collective-permute-start = (bf16[28,2176]{1,0:T(8,128)(2,1)S(1)}, bf16[28,2176]{1,0:T(8,128)(2,1)S(1)}, u32[]{:S(2)}, u32[]{:S(2)}) collective-permute-start(bf16[28,2176]{1,0:T(8,128)(2,1)S(1)} %constant_dynamic-update-slice_fusion), channel_id=1, source_target_pairs={{0,3},{1,0},{2,1},{3,2},{4,7},{5,4},{6,5},{7,6},{8,11},{9,8},{10,9... | collective-permute-start | bytes 365576 | tf_op jit(solution)/shard_map/ppermute | solution.py:489
  18.4 1.3 pad_maximum_fusion.5
  19.7 7.2 %collective-permute-done.1 = bf16[28,2176]{1,0:T(8,128)(2,1)S(1)} collective-permute-done((bf16[28,2176]{1,0:T(8,128)(2,1)S(1)}, bf16[28,2176]{1,0:T(8,128)(2,1)S(1)}, u32[]{:S(2)}, u32[]{:S(2)}) %collective-permute-start.1) | collective-permute-done | bytes 121888 | tf_op jit(solution)/shard_map/ppermute | solution.py:489
  27.2 1.6 collective-permute-start.3
  29.7 1.6 collective-permute-start.4
  31.4 2.8 collective-permute-start.5
  34.1 3.1 collective-permute-done.3
  38.4 3.9 %collective-permute-done.5 = bf16[112,896]{1,0:T(8,128)(2,1)S(1)} collective-permute-done((bf16[112,896]{1,0:T(8,128)(2,1)S(1)}, bf16[112,896]{1,0:T(8,128)(2,1)S(1)}, u32[]{:S(2)}, u32[]{:S(2)}) %collective-permute-start.5) | collective-permute-done | bytes 200736 | tf_op jit(solution)/shard_map/ppermute | solution.py:492
  43.5 21.4 %collective-permute-done.6 = bf16[2,112,1024]{2,1,0:T(8,128)(2,1)S(1)} collective-permute-done((bf16[2,112,1024]{2,1,0:T(8,128)(2,1)S(1)}, bf16[2,112,1024]{2,1,0:T(8,128)(2,1)S(1)}, u32[]{:S(2)}, u32[]{:S(2)}) %collective-permute-start.6) | collective-permute-done | bytes 458784 | tf_op jit(solution)/shard_map/ppermute | solution.py:480
  65.1 2.8 collective-permute-done.7
  68.9 7.9 %collective-permute-done.11 = bf16[112,896]{1,0:T(8,128)(2,1)S(1)} collective-permute-done((bf16[112,896]{1,0:T(8,128)(2,1)S(1)}, bf16[112,896]{1,0:T(8,128)(2,1)S(1)}, u32[]{:S(2)}, u32[]{:S(2)}) %collective-permute-start.11) | collective-permute-done | bytes 200736 | tf_op jit(solution)/shard_map/ppermute | solution.py:492
  77.7 1.0 pad_maximum_fusion.2
  78.8 4.7 %woven.1 = (bf16[896,1024]{1,0:T(8,128)(2,1)}, bf16[896,1152]{1,0:T(8,128)(2,1)}) custom-call(s32[1]{0:T(128)} %bitcast.2.core_ref, bf16[4,112,1024]{2,1,0:T(8,128)(2,1)} %bitcast.138, bf16[4,112,1152]{2,1,0:T(8,128)(2,1)} %bitcast.137, bf16[4,112,1024]{2,1,0:T(8,128)(2,1)} %bitcast.141, bf16[4,112,1152]{2,1,0:T(8,128)(2,1)} %bitcast.26.refs_3_), custom_call_target="tpu_custom_call" | custom-call | flops 1 | bytes 1 | tf_op jit(solution)/shard_map/woven/pallas_call | solution.py:424
  83.5 3.3 pairs.1
  86.8 1.3 collective-permute-start.12
  88.2 5.3 %collective-permute-start.13 = (bf16[2,256,256]{2,1,0:T(8,128)(2,1)}, bf16[2,256,256]{2,1,0:T(8,128)(2,1)S(1)}, u32[]{:S(2)}, u32[]{:S(2)}) collective-permute-start(bf16[2,256,256]{2,1,0:T(8,128)(2,1)} %get-tuple-element.223.kv0_ref), channel_id=1, source_target_pairs={{0,2},{1,3},{4,6},{5,7},{8,10},{9,11},{12,14},{13,15},{16,18},{17,... | collective-permute-start | bytes 786440 | tf_op jit(solution)/shard_map/ppermute | solution.py:581
  93.5 4.7 %queries.1.rq_ref = bf16[2,256,896]{2,1,0:T(8,128)(2,1)} custom-call(bf16[2,256,896]{2,1,0:T(8,128)(2,1)} %get-tuple-element.218.n1_ref, bf16[896,1152]{1,0:T(8,128)(2,1)} %get-tuple-element.212.wkv_ref.wq_ref, f32[8,896]{1,0:T(8,128)} %get-tuple-element.219.rows_ref, f32[2,256,128]{2,1,0:T(8,128)} %get-tuple-element.215.cos_ref, ...), custom_call_target="tpu_custom_call" | custom-call | flops 1 | bytes 1 | tf_op jit(solution)/shard_map/queries/pallas_call | solution.py:65
  98.2 1.2 collective-permute-done.13.kv2_ref
  99.3 7.1 %collective-permute-start.14 = (bf16[256,896]{1,0:T(8,128)(2,1)S(1)}, bf16[256,896]{1,0:T(8,128)(2,1)S(1)}, u32[]{:S(2)}, u32[]{:S(2)}) collective-permute-start(bf16[256,896]{1,0:T(8,128)(2,1)S(1)} %copy-done.11), channel_id=1, source_target_pairs={{0,1},{1,0},{2,3},{3,2},{4,5},{5,4},{6,7},{7,6},{8,9},{9,8},{10,11... | collective-permute-start | bytes 1376264 | tf_op jit(solution)/shard_map/ppermute | solution.py:492
  107.0 9.3 %attend.2 = (bf16[256,896]{1,0:T(8,128)(2,1)}, bf16[2,256,896]{2,1,0:T(8,128)(2,1)}, f32[2,256,896]{2,1,0:T(8,128)}, f32[2,2,16,128]{3,2,1,0:T(8,128)}) custom-call(s32[1]{0:T(128)} %bitcast.base_ref, bf16[2,256,896]{2,1,0:T(8,128)(2,1)} %queries.1.rq_ref, bf16[2,256,256]{2,1,0:T(8,128)(2,1)} %get-tuple-element.223.kv0_ref, bf16[2,256,256]{2,1,0:T(8,128)(2,1)} %copy-done.4, ...), custom_call_target="tpu_custom_call" | custom-call | flops 1 | bytes 1 | tf_op jit(solution)/shard_map/attend/pallas_call | solution.py:144
  116.4 1.1 collective-permute-start.16
  117.7 9.3 %attend.3 = (bf16[256,896]{1,0:T(8,128)(2,1)}, bf16[2,256,896]{2,1,0:T(8,128)(2,1)}, f32[2,256,896]{2,1,0:T(8,128)}, f32[2,2,16,128]{3,2,1,0:T(8,128)}) custom-call(s32[1]{0:T(128)} %bitcast.base_ref, bf16[2,256,896]{2,1,0:T(8,128)(2,1)} %queries.1.rq_ref, ...), custom_call_target="tpu_custom_call", output_to_operand_aliasing={{1}: (9, {}), {2}: (10, {}), {3}: (11, {})} | custom-call | flops 1 | bytes 1 | tf_op jit(solution)/shard_map/attend/pallas_call | solution.py:144
  127.0 2.5 collective-permute-done.16.refs_2_
  130.4 1.1 collective-permute-start.24
  133.3 24.5 %feed.2 = (f32[256,896]{1,0:T(8,128)}, bf16[256,896]{1,0:T(8,128)(2,1)}, bf16[256,896]{1,0:T(8,128)(2,1)}, bf16[256,896]{1,0:T(8,128)(2,1)}, f32[2,256,896]{2,1,...) custom-call(s32[1]{0:T(128)} %bitcast.27.own_ref, ...), custom_call_target="tpu_custom_call" | custom-call | flops 1 | bytes 1 | tf_op jit(solution)/shard_map/feed/pallas_call | solution.py:312
  157.8 1.1 collective-permute-start.25
  160.8 1.8 collective-permute-done.20.refs_3_
  163.5 24.1 %feed.3 = (f32[256,896]{1,0:T(8,128)}, bf16[256,896]{1,0:T(8,128)(2,1)}, bf16[256,896]{1,0:T(8,128)(2,1)}, bf16[256,896]{1,0:T(8,128)(2,1)}, f32[2,256,896]{2,1,...) custom-call(s32[1]{0:T(128)} %bitcast.27.own_ref, ...), custom_call_target="tpu_custom_call", output_to_operand_aliasing={{4}: (11, {}), {5}: (12, {}), {6}: (13, {}), {7}: (14, {}),... | custom-call | flops 1 | bytes 1 | tf_op jit(solution)/shard_map/feed/pallas_call | solution.py:312
  187.6 1.1 collective-permute-start.29
  188.8 1.1 collective-permute-start.30
  190.9 10.4 %weights.2 = bf16[896,1280]{1,0:T(8,128)(2,1)} custom-call(bf16[2,2048,896]{2,1,0:T(8,128)(2,1)} %get-tuple-element.280.left_ref, bf16[2048,1280]{1,0:T(8,128)(2,1)} %get-tuple-element.276.right_ref), custom_call_target="tpu_custom_call" | custom-call | flops 1 | bytes 1 | tf_op jit(solution)/shard_map/weights/pallas_call | solution.py:399
  204.2 15.1 %weights.3 = bf16[896,2560]{1,0:T(8,128)(2,1)} custom-call(bf16[2,2048,896]{2,1,0:T(8,128)(2,1)} %get-tuple-element.280.left_ref, bf16[2048,2560]{1,0:T(8,128)(2,1)} %get-tuple-element.281.right_ref), custom_call_target="tpu_custom_call" | custom-call | flops 1 | bytes 1 | tf_op jit(solution)/shard_map/weights/pallas_call | solution.py:399
  220.7 1.1 fusion.11
  221.9 1.2 collective-permute-start.34
  223.0 13.2 %attend_back.2 = (bf16[256,256]{1,0:T(8,128)(2,1)}, bf16[256,256]{1,0:T(8,128)(2,1)}, f32[2,256,896]{2,1,0:T(8,128)}, bf16[2,256,896]{2,1,0:T(8,128)(2,1)}, bf16...) custom-call(s32[1]{0:T(128)} %bitcast.base_ref, bf16[2,256,896]{2,1,0:T(8,128)(2,1)} %queries.1.rq_ref, ...), custom_call_target="tpu_custom_call" | custom-call | flops 1 | bytes 1 | tf_op jit(solution)/shard_map/attend_back/pallas_call | solution.py:225
  236.3 1.1 fusion.12
  238.4 1.3 collective-permute-start.36
  239.7 1.3 collective-permute-start.37
  241.0 13.4 %attend_back.3 = (bf16[256,256]{1,0:T(8,128)(2,1)}, bf16[256,256]{1,0:T(8,128)(2,1)}, f32[2,256,896]{2,1,0:T(8,128)}, bf16[2,256,896]{2,1,0:T(8,128)(2,1)}, bf16...) custom-call(s32[1]{0:T(128)} %bitcast.base_ref, ...), custom_call_target="tpu_custom_call", output_to_operand_aliasing={{2}: (17, {}), {3}: (18, {}), {4}: (19, {}), {5}: (20, {}),... | custom-call | flops 1 | bytes 1 | tf_op jit(solution)/shard_map/attend_back/pallas_call | solution.py:225
  254.4 1.3 collective-permute-start.38
  255.7 1.3 collective-permute-start.39
  257.1 5.6 %collective-permute-done.38.refs_2_ = bf16[256,256]{1,0:T(8,128)(2,1)S(1)} collective-permute-done((bf16[256,256]{1,0:T(8,128)(2,1)}, bf16[256,256]{1,0:T(8,128)(2,1)S(1)}, u32[]{:S(2)}, u32[]{:S(2)}) %collective-permute-start.38) | collective-permute-done | bytes 131104 | tf_op jit(solution)/shard_map/ppermute | solution.py:644
  262.7 6.3 %collective-permute-done.39.refs_3_ = bf16[256,256]{1,0:T(8,128)(2,1)S(1)} collective-permute-done((bf16[256,256]{1,0:T(8,128)(2,1)}, bf16[256,256]{1,0:T(8,128)(2,1)S(1)}, u32[]{:S(2)}, u32[]{:S(2)}) %collective-permute-start.39) | collective-permute-done | bytes 131104 | tf_op jit(solution)/shard_map/ppermute | solution.py:644
  269.0 1.9 dynamic-slice_bitcast_fusion.2
  270.9 1.6 collective-permute-start.40
  272.5 1.9 collective-permute-start.41
  274.5 11.6 %finish.1 = (f32[2,256,896]{2,1,0:T(8,128)}, bf16[448,2176]{1,0:T(8,128)(2,1)}, bf16[448,2176]{1,0:T(8,128)(2,1)}) custom-call(s32[1]{0:T(128)} %bitcast.35.bit_ref, bf16[2,256,896]{2,1,0:T(8,128)(2,1)} %get-tuple-element.324.dq_ref, f32[2,256,256]{2,1,0:T(8,128)} %get-tuple-element.325.own_ref, f32[2,256,128]{2,1,0:T(8,128)} %get-tuple-element.215.cos_ref, ...), custom_call_target="tpu_custom_call" | custom-call | flops 1 | bytes 1 | tf_op jit(solution)/shard_map/finish/pallas_call | solution.py:382
  286.6 3.1 fusion.5
  289.7 1.8 add_bitcast_fusion
  291.5 1.9 convert_add_fusion
  293.8 1.2 copy-done.3
  295.9 1.6 collective-permute-start.44
  298.0 1.1 dynamic-slice_bitcast_fusion.1
  299.8 9.3 %collective-permute-done.44 = bf16[1,2,112,1024]{3,2,1,0:T(8,128)(2,1)} collective-permute-done((bf16[1,2,112,1024]{3,2,1,0:T(8,128)(2,1)}, bf16[1,2,112,1024]{3,2,1,0:T(8,128)(2,1)}, u32[]{:S(2)}, u32[]{:S(2)}) %collective-permute-start.44) | collective-permute-done | bytes 458784 | tf_op jit(solution)/shard_map/ppermute | solution.py:480
  309.2 1.5 fusion.6
  310.7 1.0 collective-permute-done.43
  311.7 1.1 fusion.4
  314.5 6.4 %collective-permute-start.48 = (bf16[112,2560]{1,0:T(8,128)(2,1)S(1)}, bf16[112,2560]{1,0:T(8,128)(2,1)S(1)}, u32[]{:S(2)}, u32[]{:S(2)}) collective-permute-start(bf16[112,2560]{1,0:T(8,128)(2,1)S(1)} %dynamic-slice_bitcast_fusion), channel_id=1, source_target_pairs={{0,4},{2,0},{4,2},{6,6},{1,5},{3,1},{5,3},{7,7},{8,12},{10,8},{12,... | collective-permute-start | bytes 1720328 | tf_op jit(solution)/shard_map/ppermute | solution.py:654
  321.0 11.3 %collective-permute-done.48 = bf16[112,2560]{1,0:T(8,128)(2,1)S(1)} collective-permute-done((bf16[112,2560]{1,0:T(8,128)(2,1)S(1)}, bf16[112,2560]{1,0:T(8,128)(2,1)S(1)}, u32[]{:S(2)}, u32[]{:S(2)}) %collective-permute-start.48) | collective-permute-done | bytes 573472 | tf_op jit(solution)/shard_map/ppermute | solution.py:654
  332.5 5.4 %collective-permute-start.51 = (bf16[28,2176]{1,0:T(8,128)(2,1)S(1)}, bf16[28,2176]{1,0:T(8,128)(2,1)S(1)}, u32[]{:S(2)}, u32[]{:S(2)}) collective-permute-start(bf16[28,2176]{1,0:T(8,128)(2,1)S(1)} %get-tuple-element.432), channel_id=1, source_target_pairs={{0,3},{1,0},{2,1},{3,2},{4,7},{5,4},{6,5},{7,6},{8,11},{9,8},{10,9... | collective-permute-start | bytes 365576 | tf_op jit(solution)/shard_map/ppermute | solution.py:489
  338.7 1.1 fusion.32
  339.8 1.3 collective-permute-done.51
  341.0 6.7 %collective-permute-done.50 = bf16[28,2176]{1,0:T(8,128)(2,1)S(1)} collective-permute-done((bf16[28,2176]{1,0:T(8,128)(2,1)S(1)}, bf16[28,2176]{1,0:T(8,128)(2,1)S(1)}, u32[]{:S(2)}, u32[]{:S(2)}) %collective-permute-start.50) | collective-permute-done | bytes 121888 | tf_op jit(solution)/shard_map/ppermute | solution.py:489
  (232 shorter events, 30.6 us)
Async XLA Ops:
  7.3 126.0 %all-gather.3.cloned.1.call-start = ((), (), s32[]{:S(2)}) async-start(), calls=%async_computation.2 | async-start | bytes 7741440 | tf_op jit(solution)/shard_map/all_gather | solution.py:515
  7.3 10.2 %copy-start.1 = (bf16[1,2,1,256,896]{4,3,2,1,0:T(8,128)(2,1)S(1)}, bf16[1,2,1,256,896]{4,3,2,1,0:T(8,128)(2,1)}, u32[]{:S(2)}) copy-start(bf16[1,2,1,256,896]{4,3,2,1,0:T(8,128)(2,1)} %param.17) | copy-start | bytes 2752516
  9.5 123.8 %all-gather.5.cloned.1.call-start = ((), (), s32[]{:S(2)}) async-start(), calls=%async_computation.3 | async-start | bytes 7741440 | tf_op jit(solution)/shard_map/all_gather | solution.py:562
  9.9 9.7 %collective-permute-start = (bf16[28,2176]{1,0:T(8,128)(2,1)S(1)}, bf16[28,2176]{1,0:T(8,128)(2,1)S(1)}, u32[]{:S(2)}, u32[]{:S(2)}) collective-permute-start(bf16[28,2176]{1,0:T(8,128)(2,1)S(1)} %constant_dynamic-update-slice_fusion), channel_id=1, source_target_pairs={{0,3},{1,0},{2,1},{3,2},{4,7},{5,4},{6,5},{7,6},{8,11},{9,8},{10,9... | collective-permute-start | bytes 365576 | tf_op jit(solution)/shard_map/ppermute | solution.py:489
  15.0 11.8 %collective-permute-start.1 = (bf16[28,2176]{1,0:T(8,128)(2,1)S(1)}, bf16[28,2176]{1,0:T(8,128)(2,1)S(1)}, u32[]{:S(2)}, u32[]{:S(2)}) collective-permute-start(bf16[28,2176]{1,0:T(8,128)(2,1)S(1)} %constant_dynamic-update-slice_fusion), channel_id=1, source_target_pairs={{0,2},{1,3},{2,0},{3,1},{4,6},{5,7},{6,4},{7,5},{8,10},{9,11},{10,... | collective-permute-start | bytes 365576 | tf_op jit(solution)/shard_map/ppermute | solution.py:489
  15.0 11.8 %collective-permute-start.2 = (bf16[28,2176]{1,0:T(8,128)(2,1)S(1)}, bf16[28,2176]{1,0:T(8,128)(2,1)S(1)}, u32[]{:S(2)}, u32[]{:S(2)}) collective-permute-start(bf16[28,2176]{1,0:T(8,128)(2,1)S(1)} %constant_dynamic-update-slice_fusion), channel_id=1, source_target_pairs={{0,1},{1,2},{2,3},{3,0},{4,5},{5,6},{6,7},{7,4},{8,9},{9,10},{10,1... | collective-permute-start | bytes 365576 | tf_op jit(solution)/shard_map/ppermute | solution.py:489
  18.4 112.0 %copy-start.10 = (bf16[256,896]{1,0:T(8,128)(2,1)}, bf16[256,896]{1,0:T(8,128)(2,1)S(1)}, u32[]{:S(2)}) copy-start(bf16[256,896]{1,0:T(8,128)(2,1)S(1)} %get-tuple-element.253.refs_4_) | copy-start | bytes 1376260
  27.2 10.0 %collective-permute-start.3 = (bf16[112,1024]{1,0:T(8,128)(2,1)S(1)}, bf16[112,1024]{1,0:T(8,128)(2,1)S(1)}, u32[]{:S(2)}, u32[]{:S(2)}) collective-permute-start(bf16[112,1024]{1,0:T(8,128)(2,1)S(1)} %slice.75), channel_id=1, source_target_pairs={{0,8},{4,12},{8,0},{12,4},{16,24},{20,28},{24,16},{28,20},{1,9},{5... | collective-permute-start | bytes 688136 | tf_op jit(solution)/shard_map/ppermute | solution.py:480
  29.7 8.6 %collective-permute-start.4 = (bf16[112,1152]{1,0:T(8,128)(2,1)S(1)}, bf16[112,1152]{1,0:T(8,128)(2,1)S(1)}, u32[]{:S(2)}, u32[]{:S(2)}) collective-permute-start(bf16[112,1152]{1,0:T(8,128)(2,1)S(1)} %slice.76), channel_id=1, source_target_pairs={{0,16},{4,20},{8,24},{12,28},{16,0},{20,4},{24,8},{28,12},{1,17},{... | collective-permute-start | bytes 774152 | tf_op jit(solution)/shard_map/ppermute | solution.py:480
  31.4 11.0 %collective-permute-start.5 = (bf16[112,896]{1,0:T(8,128)(2,1)S(1)}, bf16[112,896]{1,0:T(8,128)(2,1)S(1)}, u32[]{:S(2)}, u32[]{:S(2)}) collective-permute-start(bf16[112,896]{1,0:T(8,128)(2,1)S(1)} %slice.77), channel_id=1, source_target_pairs={{0,2},{2,0},{1,3},{3,1},{4,6},{6,4},{5,7},{7,5},{8,10},{10,8},{9,1... | collective-permute-start | bytes 602120 | tf_op jit(solution)/shard_map/ppermute | solution.py:492
  42.4 22.6 %collective-permute-start.6 = (bf16[2,112,1024]{2,1,0:T(8,128)(2,1)S(1)}, bf16[2,112,1024]{2,1,0:T(8,128)(2,1)S(1)}, u32[]{:S(2)}, u32[]{:S(2)}) collective-permute-start(bf16[2,112,1024]{2,1,0:T(8,128)(2,1)S(1)} %pad_maximum_fusion.4), channel_id=1, source_target_pairs={{0,16},{4,20},{8,24},{12,28},{16,0},{20,4},{24,8},{28,12},{1,17},{... | collective-permute-start | bytes 1376264 | tf_op jit(solution)/shard_map/ppermute | solution.py:480
  42.9 25.1 %collective-permute-start.7 = (bf16[2,112,1152]{2,1,0:T(8,128)(2,1)S(1)}, bf16[2,112,1152]{2,1,0:T(8,128)(2,1)S(1)}, u32[]{:S(2)}, u32[]{:S(2)}) collective-permute-start(bf16[2,112,1152]{2,1,0:T(8,128)(2,1)S(1)} %pad_maximum_fusion.3), channel_id=1, source_target_pairs={{0,8},{4,12},{8,0},{12,4},{16,24},{20,28},{24,16},{28,20},{1,9},{5... | collective-permute-start | bytes 1548296 | tf_op jit(solution)/shard_map/ppermute | solution.py:480
  43.4 24.7 %collective-permute-start.8 = (bf16[112,2048]{1,0:T(8,128)(2,1)S(1)}, bf16[112,2048]{1,0:T(8,128)(2,1)S(1)}, u32[]{:S(2)}, u32[]{:S(2)}) collective-permute-start(bf16[112,2048]{1,0:T(8,128)(2,1)S(1)} %slice.80), channel_id=1, source_target_pairs={{0,2},{2,0},{1,3},{3,1},{4,6},{6,4},{5,7},{7,5},{8,10},{10,8},{9,1... | collective-permute-start | bytes 1376264 | tf_op jit(solution)/shard_map/ppermute | solution.py:492
  68.2 10.6 %copy-start.6 = (bf16[2,2,112,1152]{3,2,1,0:T(8,128)(2,1)}, bf16[2,2,112,1152]{3,2,1,0:T(8,128)(2,1)S(1)}, u32[]{:S(2)}) copy-start(bf16[2,2,112,1152]{3,2,1,0:T(8,128)(2,1)S(1)} %pad_maximum_fusion) | copy-start | bytes 3096580
  68.2 9.5 %collective-permute-start.10 = (bf16[2,2,112,1152]{3,2,1,0:T(8,128)(2,1)S(1)}, bf16[2,2,112,1152]{3,2,1,0:T(8,128)(2,1)}, u32[]{:S(2)}, u32[]{:S(2)}) collective-permute-start(bf16[2,2,112,1152]{3,2,1,0:T(8,128)(2,1)S(1)} %pad_maximum_fusion), channel_id=1, source_target_pairs={{0,4},{4,0},{8,12},{12,8},{16,20},{20,16},{24,28},{28,24},{1,5},{5... | collective-permute-start | bytes 3096584 | tf_op jit(solution)/shard_map/ppermute | solution.py:480
  68.3 8.5 %collective-permute-start.9 = (bf16[2,2,112,1024]{3,2,1,0:T(8,128)(2,1)S(1)}, bf16[2,2,112,1024]{3,2,1,0:T(8,128)(2,1)S(1)}, u32[]{:S(2)}, u32[]{:S(2)}) collective-permute-start(bf16[2,2,112,1024]{3,2,1,0:T(8,128)(2,1)S(1)} %pad_maximum_fusion.1), channel_id=1, source_target_pairs={{0,4},{4,0},{8,12},{12,8},{16,20},{20,16},{24,28},{28,24},{1,5},{5... | collective-permute-start | bytes 2752520 | tf_op jit(solution)/shard_map/ppermute | solution.py:480
  68.8 7.9 %collective-permute-start.11 = (bf16[112,896]{1,0:T(8,128)(2,1)S(1)}, bf16[112,896]{1,0:T(8,128)(2,1)S(1)}, u32[]{:S(2)}, u32[]{:S(2)}) collective-permute-start(bf16[112,896]{1,0:T(8,128)(2,1)S(1)} %slice.81), channel_id=1, source_target_pairs={{0,2},{2,0},{1,3},{3,1},{4,6},{6,4},{5,7},{7,5},{8,10},{10,8},{9,1... | collective-permute-start | bytes 602120 | tf_op jit(solution)/shard_map/ppermute | solution.py:492
  78.7 190.2 %reduce-scatter.3.cloned.1.call-start = ((), (), s32[]{:S(2)}) async-start(), calls=%async_computation.4 | async-start | bytes 2867200 | tf_op jit(solution)/shard_map/reduce_scatter | solution.py:628
  86.8 11.3 %collective-permute-start.12 = (bf16[2,256,256]{2,1,0:T(8,128)(2,1)}, bf16[2,256,256]{2,1,0:T(8,128)(2,1)S(1)}, u32[]{:S(2)}, u32[]{:S(2)}) collective-permute-start(bf16[2,256,256]{2,1,0:T(8,128)(2,1)} %get-tuple-element.223.kv0_ref), channel_id=1, source_target_pairs={{0,1},{1,2},{2,3},{4,5},{5,6},{6,7},{8,9},{9,10},{10,11},{12,13},{... | collective-permute-start | bytes 786440 | tf_op jit(solution)/shard_map/ppermute | solution.py:581
  88.2 11.2 %collective-permute-start.13 = (bf16[2,256,256]{2,1,0:T(8,128)(2,1)}, bf16[2,256,256]{2,1,0:T(8,128)(2,1)S(1)}, u32[]{:S(2)}, u32[]{:S(2)}) collective-permute-start(bf16[2,256,256]{2,1,0:T(8,128)(2,1)} %get-tuple-element.223.kv0_ref), channel_id=1, source_target_pairs={{0,2},{1,3},{4,6},{5,7},{8,10},{9,11},{12,14},{13,15},{16,18},{17,... | collective-permute-start | bytes 786440 | tf_op jit(solution)/shard_map/ppermute | solution.py:581
  99.3 17.0 %collective-permute-start.14 = (bf16[256,896]{1,0:T(8,128)(2,1)S(1)}, bf16[256,896]{1,0:T(8,128)(2,1)S(1)}, u32[]{:S(2)}, u32[]{:S(2)}) collective-permute-start(bf16[256,896]{1,0:T(8,128)(2,1)S(1)} %copy-done.11), channel_id=1, source_target_pairs={{0,1},{1,0},{2,3},{3,2},{4,5},{5,4},{6,7},{7,6},{8,9},{9,8},{10,11... | collective-permute-start | bytes 1376264 | tf_op jit(solution)/shard_map/ppermute | solution.py:492
  116.3 13.3 %copy-start.27 = (bf16[256,896]{1,0:T(8,128)(2,1)}, bf16[256,896]{1,0:T(8,128)(2,1)S(1)}, u32[]{:S(2)}) copy-start(bf16[256,896]{1,0:T(8,128)(2,1)S(1)} %collective-permute-done.14.refs_6_) | copy-start | bytes 1376260
  116.3 10.7 %collective-permute-start.15 = (bf16[256,896]{1,0:T(8,128)(2,1)}, bf16[256,896]{1,0:T(8,128)(2,1)S(1)}, u32[]{:S(2)}, u32[]{:S(2)}) collective-permute-start(bf16[256,896]{1,0:T(8,128)(2,1)} %get-tuple-element.239.refs_0_), channel_id=1, source_target_pairs={{0,4},{4,0},{1,5},{5,1},{2,6},{6,2},{3,7},{7,3},{8,12},{12,8},{9,1... | collective-permute-start | bytes 1376264 | tf_op jit(solution)/shard_map/ppermute | solution.py:492
  116.4 13.1 %collective-permute-start.16 = (bf16[256,896]{1,0:T(8,128)(2,1)}, bf16[256,896]{1,0:T(8,128)(2,1)S(1)}, u32[]{:S(2)}, u32[]{:S(2)}) collective-permute-start(bf16[256,896]{1,0:T(8,128)(2,1)} %get-tuple-element.239.refs_0_), channel_id=1, source_target_pairs={{0,1},{1,0},{2,3},{3,2},{4,5},{5,4},{6,7},{7,6},{8,9},{9,8},{10,11... | collective-permute-start | bytes 1376264 | tf_op jit(solution)/shard_map/ppermute | solution.py:492
  117.5 12.1 %collective-permute-start.17 = (bf16[256,896]{1,0:T(8,128)(2,1)S(1)}, bf16[256,896]{1,0:T(8,128)(2,1)S(1)}, u32[]{:S(2)}, u32[]{:S(2)}) collective-permute-start(bf16[256,896]{1,0:T(8,128)(2,1)S(1)} %copy-done.11), channel_id=1, source_target_pairs={{0,4},{4,0},{1,5},{5,1},{2,6},{6,2},{3,7},{7,3},{8,12},{12,8},{9,1... | collective-permute-start | bytes 1376264 | tf_op jit(solution)/shard_map/ppermute | solution.py:492
  129.6 2.1 collective-permute-start.21
  129.7 3.0 collective-permute-start.22
  130.4 27.4 %collective-permute-start.23 = (bf16[256,896]{1,0:T(8,128)(2,1)S(1)}, bf16[256,896]{1,0:T(8,128)(2,1)S(1)}, u32[]{:S(2)}, u32[]{:S(2)}) collective-permute-start(bf16[256,896]{1,0:T(8,128)(2,1)S(1)} %get-tuple-element.253.refs_4_), channel_id=1, source_target_pairs={{0,4},{4,0},{1,5},{5,1},{2,6},{6,2},{3,7},{7,3},{8,12},{12,8},{9,1... | collective-permute-start | bytes 1376264 | tf_op jit(solution)/shard_map/ppermute | solution.py:492
  130.4 27.5 %collective-permute-start.24 = (bf16[256,896]{1,0:T(8,128)(2,1)S(1)}, bf16[256,896]{1,0:T(8,128)(2,1)S(1)}, u32[]{:S(2)}, u32[]{:S(2)}) collective-permute-start(bf16[256,896]{1,0:T(8,128)(2,1)S(1)} %get-tuple-element.253.refs_4_), channel_id=1, source_target_pairs={{0,1},{1,0},{2,3},{3,2},{4,5},{5,4},{6,7},{7,6},{8,9},{9,8},{10,11... | collective-permute-start | bytes 1376264 | tf_op jit(solution)/shard_map/ppermute | solution.py:492
  131.4 27.5 %collective-permute-start.18 = (bf16[256,896]{1,0:T(8,128)(2,1)}, bf16[256,896]{1,0:T(8,128)(2,1)S(1)}, u32[]{:S(2)}, u32[]{:S(2)}) collective-permute-start(bf16[256,896]{1,0:T(8,128)(2,1)} %get-tuple-element.238.refs_0_), channel_id=1, source_target_pairs={{0,4},{4,0},{1,5},{5,1},{2,6},{6,2},{3,7},{7,3},{8,12},{12,8},{9,1... | collective-permute-start | bytes 1376264 | tf_op jit(solution)/shard_map/ppermute | solution.py:492
  131.7 28.3 %collective-permute-start.19 = (bf16[256,896]{1,0:T(8,128)(2,1)}, bf16[256,896]{1,0:T(8,128)(2,1)S(1)}, u32[]{:S(2)}, u32[]{:S(2)}) collective-permute-start(bf16[256,896]{1,0:T(8,128)(2,1)} %get-tuple-element.238.refs_0_), channel_id=1, source_target_pairs={{0,1},{1,0},{2,3},{3,2},{4,5},{5,4},{6,7},{7,6},{8,9},{9,8},{10,11... | collective-permute-start | bytes 1376264 | tf_op jit(solution)/shard_map/ppermute | solution.py:492
  132.7 29.9 %collective-permute-start.20 = (bf16[256,896]{1,0:T(8,128)(2,1)}, bf16[256,896]{1,0:T(8,128)(2,1)S(1)}, u32[]{:S(2)}, u32[]{:S(2)}) collective-permute-start(bf16[256,896]{1,0:T(8,128)(2,1)} %get-tuple-element.238.refs_0_), channel_id=1, source_target_pairs={{0,5},{1,4},{4,1},{5,0},{2,7},{3,6},{6,3},{7,2},{8,13},{9,12},{12,... | collective-permute-start | bytes 1376264 | tf_op jit(solution)/shard_map/ppermute | solution.py:495
  157.8 4.7 %collective-permute-start.25 = (bf16[256,896]{1,0:T(8,128)(2,1)S(1)}, bf16[256,896]{1,0:T(8,128)(2,1)S(1)}, u32[]{:S(2)}, u32[]{:S(2)}) collective-permute-start(bf16[256,896]{1,0:T(8,128)(2,1)S(1)} %collective-permute-done.24.refs_6_), channel_id=1, source_target_pairs={{0,4},{4,0},{1,5},{5,1},{2,6},{6,2},{3,7},{7,3},{8,12},{12,8},{9,1... | collective-permute-start | bytes 1376264 | tf_op jit(solution)/shard_map/ppermute | solution.py:492
  158.9 30.9 %collective-permute-start.26 = (bf16[256,896]{1,0:T(8,128)(2,1)}, bf16[256,896]{1,0:T(8,128)(2,1)S(1)}, u32[]{:S(2)}, u32[]{:S(2)}) collective-permute-start(bf16[256,896]{1,0:T(8,128)(2,1)} %get-tuple-element.265), channel_id=1, source_target_pairs={{0,4},{4,0},{1,5},{5,1},{2,6},{6,2},{3,7},{7,3},{8,12},{12,8},{9,1... | collective-permute-start | bytes 1376264 | tf_op jit(solution)/shard_map/ppermute | solution.py:492
  159.0 30.9 %collective-permute-start.27 = (bf16[256,896]{1,0:T(8,128)(2,1)}, bf16[256,896]{1,0:T(8,128)(2,1)S(1)}, u32[]{:S(2)}, u32[]{:S(2)}) collective-permute-start(bf16[256,896]{1,0:T(8,128)(2,1)} %get-tuple-element.266), channel_id=1, source_target_pairs={{0,1},{1,0},{2,3},{3,2},{4,5},{5,4},{6,7},{7,6},{8,9},{9,8},{10,11... | collective-permute-start | bytes 1376264 | tf_op jit(solution)/shard_map/ppermute | solution.py:492
  160.0 29.9 %collective-permute-start.28 = (bf16[256,896]{1,0:T(8,128)(2,1)}, bf16[256,896]{1,0:T(8,128)(2,1)S(1)}, u32[]{:S(2)}, u32[]{:S(2)}) collective-permute-start(bf16[256,896]{1,0:T(8,128)(2,1)} %get-tuple-element.267), channel_id=1, source_target_pairs={{0,5},{1,4},{4,1},{5,0},{2,7},{3,6},{6,3},{7,2},{8,13},{9,12},{12,... | collective-permute-start | bytes 1376264 | tf_op jit(solution)/shard_map/ppermute | solution.py:495
  187.6 13.7 %collective-permute-start.29 = (bf16[256,896]{1,0:T(8,128)(2,1)}, bf16[256,896]{1,0:T(8,128)(2,1)S(1)}, u32[]{:S(2)}, u32[]{:S(2)}) collective-permute-start(bf16[256,896]{1,0:T(8,128)(2,1)} %get-tuple-element.269), channel_id=1, source_target_pairs={{0,4},{4,0},{1,5},{5,1},{2,6},{6,2},{3,7},{7,3},{8,12},{12,8},{9,1... | collective-permute-start | bytes 1376264 | tf_op jit(solution)/shard_map/ppermute | solution.py:492
  188.8 12.7 %collective-permute-start.30 = (bf16[256,896]{1,0:T(8,128)(2,1)}, bf16[256,896]{1,0:T(8,128)(2,1)S(1)}, u32[]{:S(2)}, u32[]{:S(2)}) collective-permute-start(bf16[256,896]{1,0:T(8,128)(2,1)} %get-tuple-element.270), channel_id=1, source_target_pairs={{0,1},{1,0},{2,3},{3,2},{4,5},{5,4},{6,7},{7,6},{8,9},{9,8},{10,11... | collective-permute-start | bytes 1376264 | tf_op jit(solution)/shard_map/ppermute | solution.py:492
  201.5 96.5 %reduce-scatter.5.cloned.1.call-start = ((), (), s32[]{:S(2)}) async-start(), calls=%async_computation.5 | async-start | bytes 5734400 | tf_op jit(solution)/shard_map/reduce_scatter | solution.py:629
  202.9 16.5 %collective-permute-start.32 = (bf16[2,256,896]{2,1,0:T(8,128)(2,1)S(1)}, bf16[2,256,896]{2,1,0:T(8,128)(2,1)S(1)}, u32[]{:S(2)}, u32[]{:S(2)}) collective-permute-start(bf16[2,256,896]{2,1,0:T(8,128)(2,1)S(1)} %copy-done.13), channel_id=1, source_target_pairs={{0,4},{4,0},{1,5},{5,1},{2,6},{6,2},{3,7},{7,3},{8,12},{12,8},{9,1... | collective-permute-start | bytes 2752520 | tf_op jit(solution)/shard_map/ppermute | solution.py:492
  203.2 16.2 %collective-permute-start.33 = (bf16[2,256,896]{2,1,0:T(8,128)(2,1)S(1)}, bf16[2,256,896]{2,1,0:T(8,128)(2,1)}, u32[]{:S(2)}, u32[]{:S(2)}) collective-permute-start(bf16[2,256,896]{2,1,0:T(8,128)(2,1)S(1)} %copy-done.14), channel_id=1, source_target_pairs={{0,4},{4,0},{1,5},{5,1},{2,6},{6,2},{3,7},{7,3},{8,12},{12,8},{9,1... | collective-permute-start | bytes 2752520 | tf_op jit(solution)/shard_map/ppermute | solution.py:492
  203.4 16.0 %collective-permute-start.31 = (bf16[256,896]{1,0:T(8,128)(2,1)}, bf16[256,896]{1,0:T(8,128)(2,1)S(1)}, u32[]{:S(2)}, u32[]{:S(2)}) collective-permute-start(bf16[256,896]{1,0:T(8,128)(2,1)} %get-tuple-element.279), channel_id=1, source_target_pairs={{0,5},{1,4},{4,1},{5,0},{2,7},{3,6},{6,3},{7,2},{8,13},{9,12},{12,... | collective-permute-start | bytes 1376264 | tf_op jit(solution)/shard_map/ppermute | solution.py:495
  221.9 14.4 %collective-permute-start.34 = (bf16[256,896]{1,0:T(8,128)(2,1)S(1)}, bf16[256,896]{1,0:T(8,128)(2,1)S(1)}, u32[]{:S(2)}, u32[]{:S(2)}) collective-permute-start(bf16[256,896]{1,0:T(8,128)(2,1)S(1)} %fusion.11), channel_id=1, source_target_pairs={{0,1},{1,0},{2,3},{3,2},{4,5},{5,4},{6,7},{7,6},{8,9},{9,8},{10,11... | collective-permute-start | bytes 1376264 | tf_op jit(solution)/shard_map/ppermute | solution.py:492
  237.4 17.0 %collective-permute-start.35 = (bf16[256,896]{1,0:T(8,128)(2,1)S(1)}, bf16[256,896]{1,0:T(8,128)(2,1)}, u32[]{:S(2)}, u32[]{:S(2)}) collective-permute-start(bf16[256,896]{1,0:T(8,128)(2,1)S(1)} %fusion.12), channel_id=1, source_target_pairs={{0,1},{1,0},{2,3},{3,2},{4,5},{5,4},{6,7},{7,6},{8,9},{9,8},{10,11... | collective-permute-start | bytes 1376264 | tf_op jit(solution)/shard_map/ppermute | solution.py:492
  238.4 18.6 %collective-permute-start.36 = (bf16[256,256]{1,0:T(8,128)(2,1)}, bf16[256,256]{1,0:T(8,128)(2,1)S(1)}, u32[]{:S(2)}, u32[]{:S(2)}) collective-permute-start(bf16[256,256]{1,0:T(8,128)(2,1)} %get-tuple-element.330), channel_id=1, source_target_pairs={{1,0},{2,1},{3,2},{5,4},{6,5},{7,6},{9,8},{10,9},{11,10},{13,12},{... | collective-permute-start | bytes 393224 | tf_op jit(solution)/shard_map/ppermute | solution.py:644
  239.7 17.3 %collective-permute-start.37 = (bf16[256,256]{1,0:T(8,128)(2,1)}, bf16[256,256]{1,0:T(8,128)(2,1)S(1)}, u32[]{:S(2)}, u32[]{:S(2)}) collective-permute-start(bf16[256,256]{1,0:T(8,128)(2,1)} %get-tuple-element.331), channel_id=1, source_target_pairs={{2,0},{3,1},{6,4},{7,5},{10,8},{11,9},{14,12},{15,13},{18,16},{19,... | collective-permute-start | bytes 393224 | tf_op jit(solution)/shard_map/ppermute | solution.py:644
  254.4 8.3 %collective-permute-start.38 = (bf16[256,256]{1,0:T(8,128)(2,1)}, bf16[256,256]{1,0:T(8,128)(2,1)S(1)}, u32[]{:S(2)}, u32[]{:S(2)}) collective-permute-start(bf16[256,256]{1,0:T(8,128)(2,1)} %get-tuple-element.332), channel_id=1, source_target_pairs={{1,0},{2,1},{3,2},{5,4},{6,5},{7,6},{9,8},{10,9},{11,10},{13,12},{... | collective-permute-start | bytes 393224 | tf_op jit(solution)/shard_map/ppermute | solution.py:644
  255.7 13.3 %collective-permute-start.39 = (bf16[256,256]{1,0:T(8,128)(2,1)}, bf16[256,256]{1,0:T(8,128)(2,1)S(1)}, u32[]{:S(2)}, u32[]{:S(2)}) collective-permute-start(bf16[256,256]{1,0:T(8,128)(2,1)} %get-tuple-element.333), channel_id=1, source_target_pairs={{2,0},{3,1},{6,4},{7,5},{10,8},{11,9},{14,12},{15,13},{18,16},{19,... | collective-permute-start | bytes 393224 | tf_op jit(solution)/shard_map/ppermute | solution.py:644
  257.0 17.4 %copy-start.32 = (bf16[256,256]{1,0:T(8,128)(2,1)}, bf16[256,256]{1,0:T(8,128)(2,1)S(1)}, u32[]{:S(2)}) copy-start(bf16[256,256]{1,0:T(8,128)(2,1)S(1)} %collective-permute-done.36.refs_0_) | copy-start | bytes 393220
  257.1 17.4 %copy-start.33 = (bf16[256,256]{1,0:T(8,128)(2,1)}, bf16[256,256]{1,0:T(8,128)(2,1)S(1)}, u32[]{:S(2)}) copy-start(bf16[256,256]{1,0:T(8,128)(2,1)S(1)} %collective-permute-done.37.refs_1_) | copy-start | bytes 393220
  262.7 11.8 %copy-start.34 = (bf16[256,256]{1,0:T(8,128)(2,1)}, bf16[256,256]{1,0:T(8,128)(2,1)S(1)}, u32[]{:S(2)}) copy-start(bf16[256,256]{1,0:T(8,128)(2,1)S(1)} %collective-permute-done.38.refs_2_) | copy-start | bytes 393220
  270.9 15.2 %collective-permute-start.40 = (bf16[112,1280]{1,0:T(8,128)(2,1)}, bf16[112,1280]{1,0:T(8,128)(2,1)S(1)}, u32[]{:S(2)}, u32[]{:S(2)}) collective-permute-start(bf16[112,1280]{1,0:T(8,128)(2,1)} %get-tuple-element.430), channel_id=1, source_target_pairs={{0,0},{2,4},{4,6},{6,2},{1,1},{3,5},{5,7},{7,3},{8,8},{10,12},{12,... | collective-permute-start | bytes 860168 | tf_op jit(solution)/shard_map/ppermute | solution.py:654
  272.5 14.1 %collective-permute-start.41 = (bf16[112,1280]{1,0:T(8,128)(2,1)}, bf16[112,1280]{1,0:T(8,128)(2,1)}, u32[]{:S(2)}, u32[]{:S(2)}) collective-permute-start(bf16[112,1280]{1,0:T(8,128)(2,1)} %get-tuple-element.429), channel_id=1, source_target_pairs={{0,4},{2,0},{4,2},{6,6},{1,5},{3,1},{5,3},{7,7},{8,12},{10,8},{12,... | collective-permute-start | bytes 860168 | tf_op jit(solution)/shard_map/ppermute | solution.py:654
  274.5 12.1 %copy-start = (f32[2,256,896]{2,1,0:T(8,128)S(1)}, f32[2,256,896]{2,1,0:T(8,128)}, u32[]{:S(2)}) copy-start(f32[2,256,896]{2,1,0:T(8,128)} %get-tuple-element.230.middle_ref) | copy-start | bytes 5505028
  286.6 4.9 %collective-permute-start.42 = (bf16[448,2176]{1,0:T(8,128)(2,1)}, bf16[448,2176]{1,0:T(8,128)(2,1)}, u32[]{:S(2)}, u32[]{:S(2)}) collective-permute-start(bf16[448,2176]{1,0:T(8,128)(2,1)} %get-tuple-element.344), channel_id=1, source_target_pairs={{0,4},{4,0},{8,12},{12,8},{16,20},{20,16},{24,28},{28,24},{1,5},{5... | collective-permute-start | bytes 5849096 | tf_op jit(solution)/shard_map/ppermute | solution.py:480
  295.9 13.3 %collective-permute-start.44 = (bf16[1,2,112,1024]{3,2,1,0:T(8,128)(2,1)}, bf16[1,2,112,1024]{3,2,1,0:T(8,128)(2,1)}, u32[]{:S(2)}, u32[]{:S(2)}) collective-permute-start(bf16[1,2,112,1024]{3,2,1,0:T(8,128)(2,1)} %fusion.13), channel_id=1, source_target_pairs={{0,16},{4,20},{8,24},{12,28},{16,0},{20,4},{24,8},{28,12},{1,17},{... | collective-permute-start | bytes 1376264 | tf_op jit(solution)/shard_map/ppermute | solution.py:480
  297.5 14.1 %collective-permute-start.43 = (bf16[2,1,112,1152]{3,2,0,1:T(8,128)(2,1)S(1)}, bf16[2,1,112,1152]{3,2,0,1:T(8,128)(2,1)}, u32[]{:S(2)}, u32[]{:S(2)}) collective-permute-start(bf16[2,1,112,1152]{3,2,0,1:T(8,128)(2,1)S(1)} %fusion.9), channel_id=1, source_target_pairs={{0,8},{4,12},{8,0},{12,4},{16,24},{20,28},{24,16},{28,20},{1,9},{5... | collective-permute-start | bytes 1548296 | tf_op jit(solution)/shard_map/ppermute | solution.py:480
  299.1 13.7 %collective-permute-start.45 = (bf16[112,2560]{1,0:T(8,128)(2,1)S(1)}, bf16[112,2560]{1,0:T(8,128)(2,1)S(1)}, u32[]{:S(2)}, u32[]{:S(2)}) collective-permute-start(bf16[112,2560]{1,0:T(8,128)(2,1)S(1)} %dynamic-slice_bitcast_fusion.1), channel_id=1, source_target_pairs={{0,0},{2,4},{4,6},{6,2},{1,1},{3,5},{5,7},{7,3},{8,8},{10,12},{12,... | collective-permute-start | bytes 1720328 | tf_op jit(solution)/shard_map/ppermute | solution.py:654
  312.9 8.1 %collective-permute-start.46 = (bf16[1,1,112,1152]{3,2,1,0:T(8,128)(2,1)S(1)}, bf16[1,1,112,1152]{3,2,1,0:T(8,128)(2,1)S(1)}, u32[]{:S(2)}, u32[]{:S(2)}) collective-permute-start(bf16[1,1,112,1152]{3,2,1,0:T(8,128)(2,1)S(1)} %fusion.19), channel_id=1, source_target_pairs={{0,16},{4,20},{8,24},{12,28},{16,0},{20,4},{24,8},{28,12},{1,17},{... | collective-permute-start | bytes 774152 | tf_op jit(solution)/shard_map/ppermute | solution.py:480
  313.7 7.2 %collective-permute-start.47 = (bf16[1,1,112,1024]{3,2,1,0:T(8,128)(2,1)S(1)}, bf16[1,1,112,1024]{3,2,1,0:T(8,128)(2,1)S(1)}, u32[]{:S(2)}, u32[]{:S(2)}) collective-permute-start(bf16[1,1,112,1024]{3,2,1,0:T(8,128)(2,1)S(1)} %fusion.20), channel_id=1, source_target_pairs={{0,8},{4,12},{8,0},{12,4},{16,24},{20,28},{24,16},{28,20},{1,9},{5... | collective-permute-start | bytes 688136 | tf_op jit(solution)/shard_map/ppermute | solution.py:480
  314.5 17.8 %collective-permute-start.48 = (bf16[112,2560]{1,0:T(8,128)(2,1)S(1)}, bf16[112,2560]{1,0:T(8,128)(2,1)S(1)}, u32[]{:S(2)}, u32[]{:S(2)}) collective-permute-start(bf16[112,2560]{1,0:T(8,128)(2,1)S(1)} %dynamic-slice_bitcast_fusion), channel_id=1, source_target_pairs={{0,4},{2,0},{4,2},{6,6},{1,5},{3,1},{5,3},{7,7},{8,12},{10,8},{12,... | collective-permute-start | bytes 1720328 | tf_op jit(solution)/shard_map/ppermute | solution.py:654
  332.5 8.5 %collective-permute-start.51 = (bf16[28,2176]{1,0:T(8,128)(2,1)S(1)}, bf16[28,2176]{1,0:T(8,128)(2,1)S(1)}, u32[]{:S(2)}, u32[]{:S(2)}) collective-permute-start(bf16[28,2176]{1,0:T(8,128)(2,1)S(1)} %get-tuple-element.432), channel_id=1, source_target_pairs={{0,3},{1,0},{2,1},{3,2},{4,7},{5,4},{6,5},{7,6},{8,11},{9,8},{10,9... | collective-permute-start | bytes 365576 | tf_op jit(solution)/shard_map/ppermute | solution.py:489
  337.9 9.8 %collective-permute-start.50 = (bf16[28,2176]{1,0:T(8,128)(2,1)S(1)}, bf16[28,2176]{1,0:T(8,128)(2,1)S(1)}, u32[]{:S(2)}, u32[]{:S(2)}) collective-permute-start(bf16[28,2176]{1,0:T(8,128)(2,1)S(1)} %get-tuple-element.433), channel_id=1, source_target_pairs={{0,2},{1,3},{2,0},{3,1},{4,6},{5,7},{6,4},{7,5},{8,10},{9,11},{10,... | collective-permute-start | bytes 365576 | tf_op jit(solution)/shard_map/ppermute | solution.py:489
  337.9 9.8 %collective-permute-start.49 = (bf16[28,2176]{1,0:T(8,128)(2,1)S(1)}, bf16[28,2176]{1,0:T(8,128)(2,1)S(1)}, u32[]{:S(2)}, u32[]{:S(2)}) collective-permute-start(bf16[28,2176]{1,0:T(8,128)(2,1)S(1)} %get-tuple-element.431), channel_id=1, source_target_pairs={{0,1},{1,2},{2,3},{3,0},{4,5},{5,6},{6,7},{7,4},{8,9},{9,10},{10,1... | collective-permute-start | bytes 365576 | tf_op jit(solution)/shard_map/ppermute | solution.py:489
  (38 other events, 112.2 us)
Sparse Core Ops, SparseCore 0:
  10.0 65.7 all-gather.2
  78.9 47.7 all-gather.4
  201.6 37.1 reduce-scatter.2
  241.8 55.9 reduce-scatter.4

commit v6 on v5

--- a/solution.py
+++ b/solution.py
@@ -275,7 +275,7 @@
         for j in range(chunks):
             for p in range(3): columns(0,j,p).wait()
     x=x_ref[i]; y=y_ref[i]
-    left_ref[0]=x; left_ref[1]=y
+    left_ref[0]=x.T; left_ref[1]=y.T
     for j in range(chunks):
         c=slice(j*CHUNK,(j+1)*CHUNK); c2=slice(width+j*CHUNK,width+(j+1)*CHUNK); c3=slice(2*width+j*CHUNK,2*width+(j+1)*CHUNK)
         g=dot(x,w_ref[:,c],1,0); u=dot(x,w_ref[:,c2],1,0); da=dot(y,w_ref[:,c3],1,0)
@@ -312,8 +312,8 @@
     out=pl.pallas_call(
         functools.partial(feed_kernel,parts=parts,micro=micro,kept=kept), grid=(parts,),
         in_specs=[pl.BlockSpec(memory_space=pltpu.SMEM)]+[hold]*(2*parts+2+kept),
-        out_specs=[hold]*(2*parts)+[pl.BlockSpec((2,rows,D), lambda i:(0,micro*parts+i,0)),blk(2*hidden_pad),blk(hidden_pad)],
-        out_shape=shapes+[sd((2,everything,D),bf16)]+[sd((everything,w),bf16) for w in (2*hidden_pad,hidden_pad)],
+        out_specs=[hold]*(2*parts)+[pl.BlockSpec((2,None,D,rows), lambda i:(0,micro*parts+i,0,0)),blk(2*hidden_pad),blk(hidden_pad)],
+        out_shape=shapes+[sd((2,parts*micros,D,rows),bf16)]+[sd((everything,w),bf16) for w in (2*hidden_pad,hidden_pad)],
         scratch_shapes=[pltpu.VMEM((parts,rows,D),bf16)]*2+[pltpu.VMEM(sets[0].shape,bf16),pltpu.VMEM((2,rows,D),f32),pltpu.VMEM((2,parts-1,rows,D),bf16),
             dma((3,hidden_pad//CHUNK)),dma((2,parts)),dma((2,parts))],
         input_output_aliases={n_in+k:parts+k for k in range(kept)},
@@ -389,18 +389,16 @@
         name="finish",
     )(bit,dq,own,cos,sin,in_set,in_set,rows_table,x,n1,dmid,mixed,dmb,spread,gain2,*far)
 
-def weights_kernel(left_ref, right_ref, out_ref, turned_ref):
-    @pl.when(pl.program_id(0)==0)
-    def _(): turned_ref[...]=left_ref[...].T
-    out_ref[...]=dot(turned_ref[...],right_ref[...],1,0).astype(bf16)
+def weights_kernel(left_ref, right_ref, out_ref):
+    left=jnp.concatenate([left_ref[k] for k in range(left_ref.shape[0])],axis=1)
+    out_ref[...]=dot(left,right_ref[...],1,0).astype(bf16)
 
 def weights(left,which,right,chunk):
-    rows=left.shape[1]; width=right.shape[1]
+    rows,width=right.shape
     return pl.pallas_call(
         weights_kernel, grid=(width//chunk,),
-        in_specs=[pl.BlockSpec((None,rows,D),lambda j:(which,0,0),pipeline_mode=pl.Buffered(1)),pl.BlockSpec((rows,chunk),lambda j:(0,j))],
+        in_specs=[pl.BlockSpec((None,)+left.shape[1:],lambda j:(which,0,0,0),pipeline_mode=pl.Buffered(1)),pl.BlockSpec((rows,chunk),lambda j:(0,j))],
         out_specs=pl.BlockSpec((D,chunk),lambda j:(0,j)), out_shape=jax.ShapeDtypeStruct((D,width),bf16),
-        scratch_shapes=[pltpu.VMEM((D,rows),bf16)],
         compiler_params=pltpu.CompilerParams(vmem_limit_bytes=LIMIT), cost_estimate=COST,
         name="weights",
     )(left,right)
@@ -693,7 +691,7 @@
         if k == len(bits) - 3:
             sides, pair_parts, feed_pair = after((sides, pair_parts, feed_pair))
             pair_parts.append(delivered(feed_pair, 1))
-    sides, pair_parts = after((sides, pair_parts))
+    sides, down_parts = after((sides, down_parts))
     attention_block = jnp.concatenate([side[0] for side in sides], axis=1).astype(bf16)
     attention_block = attention_block.reshape(parts, weight_rows, -1)
 
@@ -702,9 +700,11 @@
             attention_block, (rank + steps) % parts, 0, keepdims=False
         )
 
+    ends = [around(block_for(d), d) for d in range(1, parts)]
+    ends, pair_parts = after((ends, pair_parts))
     sums = block_for(0).astype(f32)
-    for d in range(1, parts):
-        sums = sums + around(block_for(d), d).astype(f32)
+    for end in ends:
+        sums = sums + end.astype(f32)
 
     pair_sum = pair_parts[0].astype(f32) + pair_parts[1].astype(f32)
     down_sum = down_parts[0].astype(f32) + down_parts[1].astype(f32)

time: 363 us -> 359 us (0.989)
  waiting for transfers between devices: 95 us -> 90.7 us
    ppermute x4, waiting for transfers between devices: 11.8 us -> 0.89 us  [delivered(): lax.ppermute(part, ('core', 'zh'), [(2 * s + a, 2 * (s ^ a ^ k) + s) for...]
    ppermute x6, waiting for transfers between devices: 15.1 us -> 19.6 us  [around(): lax.ppermute(values_in, ctx, [(s, (s + steps) % parts) for s in range(par...]
where the time goes in v6:
time: 359 us; the launch traced here: 353 us
  Pallas kernels  141 us (39%)
  waiting for transfers between devices  90.7 us (25%)
  starting transfers between devices  69.2 us (19%)
  other arithmetic  19.4 us (5%)
  local copies, waits for them, and re-layouts  17 us (5%)
  between operations  15 us (4%)
    pallas_call x2, Pallas kernels, feed(): pl.pallas_call(functools.partial(feed_kernel, parts=parts, micro=micro, k...  48.6 us
    ppermute x11, waiting for transfers between devices, swapped(): return lax.ppermute(values_in, dp, [(s, s ^ bit) for s in range(groups)])  38.6 us
    pallas_call x2, Pallas kernels, attend_back(): pl.pallas_call(functools.partial(attend_back_kernel, count=len(gs)), grid...  26.6 us
    pallas_call x2, Pallas kernels, weights(): pl.pallas_call(weights_kernel, grid=(width // chunk,), in_specs=[pl.Block...  23.4 us
    ppermute x22, starting transfers between devices, other(): return lax.ppermute(values_in, axis, [(0, 1), (1, 0)])  21.3 us
    ppermute x6, waiting for transfers between devices, around(): lax.ppermute(values_in, ctx, [(s, (s + steps) % parts) for s in range(par...  19.6 us
    pallas_call x2, Pallas kernels, attend(): pl.pallas_call(attend_kernel, grid=(nq,), in_specs=[pl.BlockSpec(memory_s...  18.6 us
    ppermute x22, waiting for transfers between devices, other(): return lax.ppermute(values_in, axis, [(0, 1), (1, 0)])  15.6 us
  transfers between devices with their start and end apart: 56, of which 19 were waited for; matrix products, arithmetic and copies ran while one was open for 7% of the time, Pallas kernels for 40%

profile of v6, /device:TPU:0, one launch (start us, length us, event | category | flops | bytes accessed | tf_op | source)
XLA Modules:
  0.0 352.6 jit_solution(14660722102096620530)
XLA Ops:
  7.3 2.2 fusion.8
  9.9 5.1 %collective-permute-start = (bf16[28,2176]{1,0:T(8,128)(2,1)S(1)}, bf16[28,2176]{1,0:T(8,128)(2,1)S(1)}, u32[]{:S(2)}, u32[]{:S(2)}) collective-permute-start(bf16[28,2176]{1,0:T(8,128)(2,1)S(1)} %constant_dynamic-update-slice_fusion), channel_id=1, source_target_pairs={{0,3},{1,0},{2,1},{3,2},{4,7},{5,4},{6,5},{7,6},{8,11},{9,8},{10,9... | collective-permute-start | bytes 365576 | tf_op jit(solution)/shard_map/ppermute | solution.py:487
  18.4 1.3 pad_maximum_fusion.5
  19.7 7.2 %collective-permute-done.1 = bf16[28,2176]{1,0:T(8,128)(2,1)S(1)} collective-permute-done((bf16[28,2176]{1,0:T(8,128)(2,1)S(1)}, bf16[28,2176]{1,0:T(8,128)(2,1)S(1)}, u32[]{:S(2)}, u32[]{:S(2)}) %collective-permute-start.1) | collective-permute-done | bytes 121888 | tf_op jit(solution)/shard_map/ppermute | solution.py:487
  27.2 1.6 collective-permute-start.3
  29.7 1.6 collective-permute-start.4
  31.4 2.8 collective-permute-start.5
  34.1 3.1 collective-permute-done.3
  38.4 3.9 %collective-permute-done.5 = bf16[112,896]{1,0:T(8,128)(2,1)S(1)} collective-permute-done((bf16[112,896]{1,0:T(8,128)(2,1)S(1)}, bf16[112,896]{1,0:T(8,128)(2,1)S(1)}, u32[]{:S(2)}, u32[]{:S(2)}) %collective-permute-start.5) | collective-permute-done | bytes 200736 | tf_op jit(solution)/shard_map/ppermute | solution.py:490
  43.5 21.4 %collective-permute-done.6 = bf16[2,112,1024]{2,1,0:T(8,128)(2,1)S(1)} collective-permute-done((bf16[2,112,1024]{2,1,0:T(8,128)(2,1)S(1)}, bf16[2,112,1024]{2,1,0:T(8,128)(2,1)S(1)}, u32[]{:S(2)}, u32[]{:S(2)}) %collective-permute-start.6) | collective-permute-done | bytes 458784 | tf_op jit(solution)/shard_map/ppermute | solution.py:478
  65.1 2.8 collective-permute-done.7
  68.8 7.9 %collective-permute-done.11 = bf16[112,896]{1,0:T(8,128)(2,1)S(1)} collective-permute-done((bf16[112,896]{1,0:T(8,128)(2,1)S(1)}, bf16[112,896]{1,0:T(8,128)(2,1)S(1)}, u32[]{:S(2)}, u32[]{:S(2)}) %collective-permute-start.11) | collective-permute-done | bytes 200736 | tf_op jit(solution)/shard_map/ppermute | solution.py:490
  78.8 4.7 %woven.1 = (bf16[896,1024]{1,0:T(8,128)(2,1)}, bf16[896,1152]{1,0:T(8,128)(2,1)}) custom-call(s32[1]{0:T(128)} %bitcast.2.core_ref, bf16[4,112,1024]{2,1,0:T(8,128)(2,1)} %bitcast.138, bf16[4,112,1152]{2,1,0:T(8,128)(2,1)} %bitcast.137, bf16[4,112,1024]{2,1,0:T(8,128)(2,1)} %bitcast.141, bf16[4,112,1152]{2,1,0:T(8,128)(2,1)} %bitcast.26.refs_3_), custom_call_target="tpu_custom_call" | custom-call | flops 1 | bytes 1 | tf_op jit(solution)/shard_map/woven/pallas_call | solution.py:422
  83.5 3.3 pairs.1
  86.8 1.3 collective-permute-start.12
  88.2 5.5 %collective-permute-start.13 = (bf16[2,256,256]{2,1,0:T(8,128)(2,1)}, bf16[2,256,256]{2,1,0:T(8,128)(2,1)S(1)}, u32[]{:S(2)}, u32[]{:S(2)}) collective-permute-start(bf16[2,256,256]{2,1,0:T(8,128)(2,1)} %get-tuple-element.228.kv0_ref), channel_id=1, source_target_pairs={{0,2},{1,3},{4,6},{5,7},{8,10},{9,11},{12,14},{13,15},{16,18},{17,... | collective-permute-start | bytes 786440 | tf_op jit(solution)/shard_map/ppermute | solution.py:579
  93.6 4.5 %queries.1.rq_ref = bf16[2,256,896]{2,1,0:T(8,128)(2,1)} custom-call(bf16[2,256,896]{2,1,0:T(8,128)(2,1)} %get-tuple-element.223.n1_ref, bf16[896,1152]{1,0:T(8,128)(2,1)} %get-tuple-element.217.wkv_ref.wq_ref, f32[8,896]{1,0:T(8,128)} %get-tuple-element.224.rows_ref, f32[2,256,128]{2,1,0:T(8,128)} %get-tuple-element.220.cos_ref, ...), custom_call_target="tpu_custom_call" | custom-call | flops 1 | bytes 1 | tf_op jit(solution)/shard_map/queries/pallas_call | solution.py:65
  98.2 1.2 collective-permute-done.13.kv2_ref
  99.3 7.1 %collective-permute-start.14 = (bf16[256,896]{1,0:T(8,128)(2,1)S(1)}, bf16[256,896]{1,0:T(8,128)(2,1)S(1)}, u32[]{:S(2)}, u32[]{:S(2)}) collective-permute-start(bf16[256,896]{1,0:T(8,128)(2,1)S(1)} %copy-done.11), channel_id=1, source_target_pairs={{0,1},{1,0},{2,3},{3,2},{4,5},{5,4},{6,7},{7,6},{8,9},{9,8},{10,11... | collective-permute-start | bytes 1376264 | tf_op jit(solution)/shard_map/ppermute | solution.py:490
  107.0 9.3 %attend.2 = (bf16[256,896]{1,0:T(8,128)(2,1)}, bf16[2,256,896]{2,1,0:T(8,128)(2,1)}, f32[2,256,896]{2,1,0:T(8,128)}, f32[2,2,16,128]{3,2,1,0:T(8,128)}) custom-call(s32[1]{0:T(128)} %bitcast.base_ref, bf16[2,256,896]{2,1,0:T(8,128)(2,1)} %queries.1.rq_ref, bf16[2,256,256]{2,1,0:T(8,128)(2,1)} %get-tuple-element.228.kv0_ref, bf16[2,256,256]{2,1,0:T(8,128)(2,1)} %copy-done.4, ...), custom_call_target="tpu_custom_call" | custom-call | flops 1 | bytes 1 | tf_op jit(solution)/shard_map/attend/pallas_call | solution.py:144
  116.4 1.1 collective-permute-start.16
  117.7 9.3 %attend.3 = (bf16[256,896]{1,0:T(8,128)(2,1)}, bf16[2,256,896]{2,1,0:T(8,128)(2,1)}, f32[2,256,896]{2,1,0:T(8,128)}, f32[2,2,16,128]{3,2,1,0:T(8,128)}) custom-call(s32[1]{0:T(128)} %bitcast.base_ref, bf16[2,256,896]{2,1,0:T(8,128)(2,1)} %queries.1.rq_ref, ...), custom_call_target="tpu_custom_call", output_to_operand_aliasing={{1}: (9, {}), {2}: (10, {}), {3}: (11, {})} | custom-call | flops 1 | bytes 1 | tf_op jit(solution)/shard_map/attend/pallas_call | solution.py:144
  127.0 2.5 collective-permute-done.16.refs_2_
  130.4 1.1 collective-permute-start.24
  133.3 24.5 %feed.2 = (f32[256,896]{1,0:T(8,128)}, bf16[256,896]{1,0:T(8,128)(2,1)}, bf16[256,896]{1,0:T(8,128)(2,1)}, bf16[256,896]{1,0:T(8,128)(2,1)}, f32[2,256,896]{2,1,...) custom-call(s32[1]{0:T(128)} %bitcast.27.own_ref, ...), custom_call_target="tpu_custom_call" | custom-call | flops 1 | bytes 1 | tf_op jit(solution)/shard_map/feed/pallas_call | solution.py:312
  157.9 1.1 collective-permute-start.25
  160.8 1.8 collective-permute-done.20.refs_3_
  163.5 24.1 %feed.3 = (f32[256,896]{1,0:T(8,128)}, bf16[256,896]{1,0:T(8,128)(2,1)}, bf16[256,896]{1,0:T(8,128)(2,1)}, bf16[256,896]{1,0:T(8,128)(2,1)}, f32[2,256,896]{2,1,...) custom-call(s32[1]{0:T(128)} %bitcast.27.own_ref, ...), custom_call_target="tpu_custom_call", output_to_operand_aliasing={{4}: (11, {}), {5}: (12, {}), {6}: (13, {}), {7}: (14, {}),... | custom-call | flops 1 | bytes 1 | tf_op jit(solution)/shard_map/feed/pallas_call | solution.py:312
  187.6 1.2 collective-permute-start.29
  188.8 1.1 collective-permute-start.30
  190.9 9.3 %weights.2 = bf16[896,1280]{1,0:T(8,128)(2,1)} custom-call(bf16[2,8,896,256]{3,2,1,0:T(8,128)(2,1)} %get-tuple-element.285.left_ref, bf16[2048,1280]{1,0:T(8,128)(2,1)} %get-tuple-element.281.right_ref), custom_call_target="tpu_custom_call" | custom-call | flops 1 | bytes 1 | tf_op jit(solution)/shard_map/weights/pallas_call | solution.py:398
  200.3 1.2 collective-permute-done.30.refs_2_
  203.5 14.1 %weights.3 = bf16[896,2560]{1,0:T(8,128)(2,1)} custom-call(bf16[2,8,896,256]{3,2,1,0:T(8,128)(2,1)} %get-tuple-element.285.left_ref, bf16[2048,2560]{1,0:T(8,128)(2,1)} %get-tuple-element.286.right_ref), custom_call_target="tpu_custom_call" | custom-call | flops 1 | bytes 1 | tf_op jit(solution)/shard_map/weights/pallas_call | solution.py:398
  219.0 1.1 fusion.11
  220.2 1.1 collective-permute-start.34
  221.3 13.2 %attend_back.2 = (bf16[256,256]{1,0:T(8,128)(2,1)}, bf16[256,256]{1,0:T(8,128)(2,1)}, f32[2,256,896]{2,1,0:T(8,128)}, bf16[2,256,896]{2,1,0:T(8,128)(2,1)}, bf16...) custom-call(s32[1]{0:T(128)} %bitcast.base_ref, bf16[2,256,896]{2,1,0:T(8,128)(2,1)} %queries.1.rq_ref, ...), custom_call_target="tpu_custom_call" | custom-call | flops 1 | bytes 1 | tf_op jit(solution)/shard_map/attend_back/pallas_call | solution.py:225
  234.6 1.1 fusion.12
  235.7 1.1 collective-permute-start.35
  236.8 1.3 collective-permute-start.36
  238.1 1.3 collective-permute-start.37
  239.4 13.4 %attend_back.3 = (bf16[256,256]{1,0:T(8,128)(2,1)}, bf16[256,256]{1,0:T(8,128)(2,1)}, f32[2,256,896]{2,1,0:T(8,128)}, bf16[2,256,896]{2,1,0:T(8,128)(2,1)}, bf16...) custom-call(s32[1]{0:T(128)} %bitcast.base_ref, ...), custom_call_target="tpu_custom_call", output_to_operand_aliasing={{2}: (17, {}), {3}: (18, {}), {4}: (19, {}), {5}: (20, {}),... | custom-call | flops 1 | bytes 1 | tf_op jit(solution)/shard_map/attend_back/pallas_call | solution.py:225
  252.8 1.3 collective-permute-start.38
  254.1 1.3 collective-permute-start.39
  255.4 5.2 %collective-permute-done.38.refs_2_ = bf16[256,256]{1,0:T(8,128)(2,1)S(1)} collective-permute-done((bf16[256,256]{1,0:T(8,128)(2,1)}, bf16[256,256]{1,0:T(8,128)(2,1)S(1)}, u32[]{:S(2)}, u32[]{:S(2)}) %collective-permute-start.38) | collective-permute-done | bytes 131104 | tf_op jit(solution)/shard_map/ppermute | solution.py:642
  260.6 7.1 %collective-permute-done.39.refs_3_ = bf16[256,256]{1,0:T(8,128)(2,1)S(1)} collective-permute-done((bf16[256,256]{1,0:T(8,128)(2,1)}, bf16[256,256]{1,0:T(8,128)(2,1)S(1)}, u32[]{:S(2)}, u32[]{:S(2)}) %collective-permute-start.39) | collective-permute-done | bytes 131104 | tf_op jit(solution)/shard_map/ppermute | solution.py:642
  267.7 1.9 dynamic-slice_bitcast_fusion.2
  269.7 1.6 collective-permute-start.40
  271.3 1.9 collective-permute-start.41
  273.3 11.5 %finish.1 = (f32[2,256,896]{2,1,0:T(8,128)}, bf16[448,2176]{1,0:T(8,128)(2,1)}, bf16[448,2176]{1,0:T(8,128)(2,1)}) custom-call(s32[1]{0:T(128)} %bitcast.35.bit_ref, bf16[2,256,896]{2,1,0:T(8,128)(2,1)} %get-tuple-element.329.dq_ref, f32[2,256,256]{2,1,0:T(8,128)} %get-tuple-element.330.own_ref, f32[2,256,128]{2,1,0:T(8,128)} %get-tuple-element.220.cos_ref, ...), custom_call_target="tpu_custom_call" | custom-call | flops 1 | bytes 1 | tf_op jit(solution)/shard_map/finish/pallas_call | solution.py:382
  285.7 1.1 collective-permute-start.42
  286.8 3.0 fusion.5
  290.7 2.0 convert_add_fusion
  293.0 1.2 copy-done.3
  295.1 1.5 collective-permute-start.44
  297.9 1.1 dynamic-slice_bitcast_fusion.1
  299.7 8.5 %collective-permute-done.44 = bf16[1,2,112,1024]{3,2,1,0:T(8,128)(2,1)} collective-permute-done((bf16[1,2,112,1024]{3,2,1,0:T(8,128)(2,1)}, bf16[1,2,112,1024]{3,2,1,0:T(8,128)(2,1)}, u32[]{:S(2)}, u32[]{:S(2)}) %collective-permute-start.44) | collective-permute-done | bytes 458784 | tf_op jit(solution)/shard_map/ppermute | solution.py:478
  308.2 1.5 fusion.6
  310.5 1.1 fusion.4
  313.1 7.4 %collective-permute-start.51 = (bf16[112,2560]{1,0:T(8,128)(2,1)S(1)}, bf16[112,2560]{1,0:T(8,128)(2,1)S(1)}, u32[]{:S(2)}, u32[]{:S(2)}) collective-permute-start(bf16[112,2560]{1,0:T(8,128)(2,1)S(1)} %dynamic-slice_bitcast_fusion), channel_id=1, source_target_pairs={{0,4},{2,0},{4,2},{6,6},{1,5},{3,1},{5,3},{7,7},{8,12},{10,8},{12,... | collective-permute-start | bytes 1720328 | tf_op jit(solution)/shard_map/ppermute | solution.py:652
  321.1 3.6 %collective-permute-start.49 = (bf16[28,2176]{1,0:T(8,128)(2,1)S(1)}, bf16[28,2176]{1,0:T(8,128)(2,1)S(1)}, u32[]{:S(2)}, u32[]{:S(2)}) collective-permute-start(bf16[28,2176]{1,0:T(8,128)(2,1)S(1)} %get-tuple-element.442), channel_id=1, source_target_pairs={{0,2},{1,3},{2,0},{3,1},{4,6},{5,7},{6,4},{7,5},{8,10},{9,11},{10,... | collective-permute-start | bytes 365576 | tf_op jit(solution)/shard_map/ppermute | solution.py:487
  324.7 2.8 collective-permute-start.50
  327.6 1.8 add_bitcast_fusion
  329.4 12.5 %collective-permute-done.49 = bf16[28,2176]{1,0:T(8,128)(2,1)S(1)} collective-permute-done((bf16[28,2176]{1,0:T(8,128)(2,1)S(1)}, bf16[28,2176]{1,0:T(8,128)(2,1)S(1)}, u32[]{:S(2)}, u32[]{:S(2)}) %collective-permute-start.49) | collective-permute-done | bytes 121888 | tf_op jit(solution)/shard_map/ppermute | solution.py:487
  344.8 1.1 fusion.32
  (232 shorter events, 32.1 us)
Async XLA Ops:
  7.3 126.0 %all-gather.3.cloned.1.call-start = ((), (), s32[]{:S(2)}) async-start(), calls=%async_computation.2 | async-start | bytes 7741440 | tf_op jit(solution)/shard_map/all_gather | solution.py:513
  7.3 10.2 %copy-start.1 = (bf16[1,2,1,256,896]{4,3,2,1,0:T(8,128)(2,1)S(1)}, bf16[1,2,1,256,896]{4,3,2,1,0:T(8,128)(2,1)}, u32[]{:S(2)}) copy-start(bf16[1,2,1,256,896]{4,3,2,1,0:T(8,128)(2,1)} %param.17) | copy-start | bytes 2752516
  9.5 123.8 %all-gather.5.cloned.1.call-start = ((), (), s32[]{:S(2)}) async-start(), calls=%async_computation.3 | async-start | bytes 7741440 | tf_op jit(solution)/shard_map/all_gather | solution.py:560
  9.9 9.7 %collective-permute-start = (bf16[28,2176]{1,0:T(8,128)(2,1)S(1)}, bf16[28,2176]{1,0:T(8,128)(2,1)S(1)}, u32[]{:S(2)}, u32[]{:S(2)}) collective-permute-start(bf16[28,2176]{1,0:T(8,128)(2,1)S(1)} %constant_dynamic-update-slice_fusion), channel_id=1, source_target_pairs={{0,3},{1,0},{2,1},{3,2},{4,7},{5,4},{6,5},{7,6},{8,11},{9,8},{10,9... | collective-permute-start | bytes 365576 | tf_op jit(solution)/shard_map/ppermute | solution.py:487
  15.0 11.8 %collective-permute-start.1 = (bf16[28,2176]{1,0:T(8,128)(2,1)S(1)}, bf16[28,2176]{1,0:T(8,128)(2,1)S(1)}, u32[]{:S(2)}, u32[]{:S(2)}) collective-permute-start(bf16[28,2176]{1,0:T(8,128)(2,1)S(1)} %constant_dynamic-update-slice_fusion), channel_id=1, source_target_pairs={{0,2},{1,3},{2,0},{3,1},{4,6},{5,7},{6,4},{7,5},{8,10},{9,11},{10,... | collective-permute-start | bytes 365576 | tf_op jit(solution)/shard_map/ppermute | solution.py:487
  15.0 11.8 %collective-permute-start.2 = (bf16[28,2176]{1,0:T(8,128)(2,1)S(1)}, bf16[28,2176]{1,0:T(8,128)(2,1)S(1)}, u32[]{:S(2)}, u32[]{:S(2)}) collective-permute-start(bf16[28,2176]{1,0:T(8,128)(2,1)S(1)} %constant_dynamic-update-slice_fusion), channel_id=1, source_target_pairs={{0,1},{1,2},{2,3},{3,0},{4,5},{5,6},{6,7},{7,4},{8,9},{9,10},{10,1... | collective-permute-start | bytes 365576 | tf_op jit(solution)/shard_map/ppermute | solution.py:487
  18.4 112.0 %copy-start.10 = (bf16[256,896]{1,0:T(8,128)(2,1)}, bf16[256,896]{1,0:T(8,128)(2,1)S(1)}, u32[]{:S(2)}) copy-start(bf16[256,896]{1,0:T(8,128)(2,1)S(1)} %get-tuple-element.258.refs_4_) | copy-start | bytes 1376260
  27.2 10.0 %collective-permute-start.3 = (bf16[112,1024]{1,0:T(8,128)(2,1)S(1)}, bf16[112,1024]{1,0:T(8,128)(2,1)S(1)}, u32[]{:S(2)}, u32[]{:S(2)}) collective-permute-start(bf16[112,1024]{1,0:T(8,128)(2,1)S(1)} %slice.75), channel_id=1, source_target_pairs={{0,8},{4,12},{8,0},{12,4},{16,24},{20,28},{24,16},{28,20},{1,9},{5... | collective-permute-start | bytes 688136 | tf_op jit(solution)/shard_map/ppermute | solution.py:478
  29.7 8.6 %collective-permute-start.4 = (bf16[112,1152]{1,0:T(8,128)(2,1)S(1)}, bf16[112,1152]{1,0:T(8,128)(2,1)S(1)}, u32[]{:S(2)}, u32[]{:S(2)}) collective-permute-start(bf16[112,1152]{1,0:T(8,128)(2,1)S(1)} %slice.76), channel_id=1, source_target_pairs={{0,16},{4,20},{8,24},{12,28},{16,0},{20,4},{24,8},{28,12},{1,17},{... | collective-permute-start | bytes 774152 | tf_op jit(solution)/shard_map/ppermute | solution.py:478
  31.4 11.0 %collective-permute-start.5 = (bf16[112,896]{1,0:T(8,128)(2,1)S(1)}, bf16[112,896]{1,0:T(8,128)(2,1)S(1)}, u32[]{:S(2)}, u32[]{:S(2)}) collective-permute-start(bf16[112,896]{1,0:T(8,128)(2,1)S(1)} %slice.77), channel_id=1, source_target_pairs={{0,2},{2,0},{1,3},{3,1},{4,6},{6,4},{5,7},{7,5},{8,10},{10,8},{9,1... | collective-permute-start | bytes 602120 | tf_op jit(solution)/shard_map/ppermute | solution.py:490
  42.4 22.6 %collective-permute-start.6 = (bf16[2,112,1024]{2,1,0:T(8,128)(2,1)S(1)}, bf16[2,112,1024]{2,1,0:T(8,128)(2,1)S(1)}, u32[]{:S(2)}, u32[]{:S(2)}) collective-permute-start(bf16[2,112,1024]{2,1,0:T(8,128)(2,1)S(1)} %pad_maximum_fusion.4), channel_id=1, source_target_pairs={{0,16},{4,20},{8,24},{12,28},{16,0},{20,4},{24,8},{28,12},{1,17},{... | collective-permute-start | bytes 1376264 | tf_op jit(solution)/shard_map/ppermute | solution.py:478
  42.9 25.1 %collective-permute-start.7 = (bf16[2,112,1152]{2,1,0:T(8,128)(2,1)S(1)}, bf16[2,112,1152]{2,1,0:T(8,128)(2,1)S(1)}, u32[]{:S(2)}, u32[]{:S(2)}) collective-permute-start(bf16[2,112,1152]{2,1,0:T(8,128)(2,1)S(1)} %pad_maximum_fusion.3), channel_id=1, source_target_pairs={{0,8},{4,12},{8,0},{12,4},{16,24},{20,28},{24,16},{28,20},{1,9},{5... | collective-permute-start | bytes 1548296 | tf_op jit(solution)/shard_map/ppermute | solution.py:478
  43.4 24.7 %collective-permute-start.8 = (bf16[112,2048]{1,0:T(8,128)(2,1)S(1)}, bf16[112,2048]{1,0:T(8,128)(2,1)S(1)}, u32[]{:S(2)}, u32[]{:S(2)}) collective-permute-start(bf16[112,2048]{1,0:T(8,128)(2,1)S(1)} %slice.80), channel_id=1, source_target_pairs={{0,2},{2,0},{1,3},{3,1},{4,6},{6,4},{5,7},{7,5},{8,10},{10,8},{9,1... | collective-permute-start | bytes 1376264 | tf_op jit(solution)/shard_map/ppermute | solution.py:490
  68.2 10.6 %copy-start.6 = (bf16[2,2,112,1152]{3,2,1,0:T(8,128)(2,1)}, bf16[2,2,112,1152]{3,2,1,0:T(8,128)(2,1)S(1)}, u32[]{:S(2)}) copy-start(bf16[2,2,112,1152]{3,2,1,0:T(8,128)(2,1)S(1)} %pad_maximum_fusion) | copy-start | bytes 3096580
  68.2 9.5 %collective-permute-start.10 = (bf16[2,2,112,1152]{3,2,1,0:T(8,128)(2,1)S(1)}, bf16[2,2,112,1152]{3,2,1,0:T(8,128)(2,1)}, u32[]{:S(2)}, u32[]{:S(2)}) collective-permute-start(bf16[2,2,112,1152]{3,2,1,0:T(8,128)(2,1)S(1)} %pad_maximum_fusion), channel_id=1, source_target_pairs={{0,4},{4,0},{8,12},{12,8},{16,20},{20,16},{24,28},{28,24},{1,5},{5... | collective-permute-start | bytes 3096584 | tf_op jit(solution)/shard_map/ppermute | solution.py:478
  68.3 8.5 %collective-permute-start.9 = (bf16[2,2,112,1024]{3,2,1,0:T(8,128)(2,1)S(1)}, bf16[2,2,112,1024]{3,2,1,0:T(8,128)(2,1)S(1)}, u32[]{:S(2)}, u32[]{:S(2)}) collective-permute-start(bf16[2,2,112,1024]{3,2,1,0:T(8,128)(2,1)S(1)} %pad_maximum_fusion.1), channel_id=1, source_target_pairs={{0,4},{4,0},{8,12},{12,8},{16,20},{20,16},{24,28},{28,24},{1,5},{5... | collective-permute-start | bytes 2752520 | tf_op jit(solution)/shard_map/ppermute | solution.py:478
  68.8 7.9 %collective-permute-start.11 = (bf16[112,896]{1,0:T(8,128)(2,1)S(1)}, bf16[112,896]{1,0:T(8,128)(2,1)S(1)}, u32[]{:S(2)}, u32[]{:S(2)}) collective-permute-start(bf16[112,896]{1,0:T(8,128)(2,1)S(1)} %slice.81), channel_id=1, source_target_pairs={{0,2},{2,0},{1,3},{3,1},{4,6},{6,4},{5,7},{7,5},{8,10},{10,8},{9,1... | collective-permute-start | bytes 602120 | tf_op jit(solution)/shard_map/ppermute | solution.py:490
  78.7 189.0 %reduce-scatter.3.cloned.1.call-start = ((), (), s32[]{:S(2)}) async-start(), calls=%async_computation.4 | async-start | bytes 2867200 | tf_op jit(solution)/shard_map/reduce_scatter | solution.py:626
  86.8 11.3 %collective-permute-start.12 = (bf16[2,256,256]{2,1,0:T(8,128)(2,1)}, bf16[2,256,256]{2,1,0:T(8,128)(2,1)S(1)}, u32[]{:S(2)}, u32[]{:S(2)}) collective-permute-start(bf16[2,256,256]{2,1,0:T(8,128)(2,1)} %get-tuple-element.228.kv0_ref), channel_id=1, source_target_pairs={{0,1},{1,2},{2,3},{4,5},{5,6},{6,7},{8,9},{9,10},{10,11},{12,13},{... | collective-permute-start | bytes 786440 | tf_op jit(solution)/shard_map/ppermute | solution.py:579
  88.2 11.2 %collective-permute-start.13 = (bf16[2,256,256]{2,1,0:T(8,128)(2,1)}, bf16[2,256,256]{2,1,0:T(8,128)(2,1)S(1)}, u32[]{:S(2)}, u32[]{:S(2)}) collective-permute-start(bf16[2,256,256]{2,1,0:T(8,128)(2,1)} %get-tuple-element.228.kv0_ref), channel_id=1, source_target_pairs={{0,2},{1,3},{4,6},{5,7},{8,10},{9,11},{12,14},{13,15},{16,18},{17,... | collective-permute-start | bytes 786440 | tf_op jit(solution)/shard_map/ppermute | solution.py:579
  99.3 17.0 %collective-permute-start.14 = (bf16[256,896]{1,0:T(8,128)(2,1)S(1)}, bf16[256,896]{1,0:T(8,128)(2,1)S(1)}, u32[]{:S(2)}, u32[]{:S(2)}) collective-permute-start(bf16[256,896]{1,0:T(8,128)(2,1)S(1)} %copy-done.11), channel_id=1, source_target_pairs={{0,1},{1,0},{2,3},{3,2},{4,5},{5,4},{6,7},{7,6},{8,9},{9,8},{10,11... | collective-permute-start | bytes 1376264 | tf_op jit(solution)/shard_map/ppermute | solution.py:490
  116.3 13.3 %copy-start.27 = (bf16[256,896]{1,0:T(8,128)(2,1)}, bf16[256,896]{1,0:T(8,128)(2,1)S(1)}, u32[]{:S(2)}) copy-start(bf16[256,896]{1,0:T(8,128)(2,1)S(1)} %collective-permute-done.14.refs_6_) | copy-start | bytes 1376260
  116.3 10.7 %collective-permute-start.15 = (bf16[256,896]{1,0:T(8,128)(2,1)}, bf16[256,896]{1,0:T(8,128)(2,1)S(1)}, u32[]{:S(2)}, u32[]{:S(2)}) collective-permute-start(bf16[256,896]{1,0:T(8,128)(2,1)} %get-tuple-element.244.refs_0_), channel_id=1, source_target_pairs={{0,4},{4,0},{1,5},{5,1},{2,6},{6,2},{3,7},{7,3},{8,12},{12,8},{9,1... | collective-permute-start | bytes 1376264 | tf_op jit(solution)/shard_map/ppermute | solution.py:490
  116.4 13.1 %collective-permute-start.16 = (bf16[256,896]{1,0:T(8,128)(2,1)}, bf16[256,896]{1,0:T(8,128)(2,1)S(1)}, u32[]{:S(2)}, u32[]{:S(2)}) collective-permute-start(bf16[256,896]{1,0:T(8,128)(2,1)} %get-tuple-element.244.refs_0_), channel_id=1, source_target_pairs={{0,1},{1,0},{2,3},{3,2},{4,5},{5,4},{6,7},{7,6},{8,9},{9,8},{10,11... | collective-permute-start | bytes 1376264 | tf_op jit(solution)/shard_map/ppermute | solution.py:490
  117.5 12.1 %collective-permute-start.17 = (bf16[256,896]{1,0:T(8,128)(2,1)S(1)}, bf16[256,896]{1,0:T(8,128)(2,1)S(1)}, u32[]{:S(2)}, u32[]{:S(2)}) collective-permute-start(bf16[256,896]{1,0:T(8,128)(2,1)S(1)} %copy-done.11), channel_id=1, source_target_pairs={{0,4},{4,0},{1,5},{5,1},{2,6},{6,2},{3,7},{7,3},{8,12},{12,8},{9,1... | collective-permute-start | bytes 1376264 | tf_op jit(solution)/shard_map/ppermute | solution.py:490
  129.6 2.1 collective-permute-start.21
  129.7 3.0 collective-permute-start.22
  130.4 27.5 %collective-permute-start.23 = (bf16[256,896]{1,0:T(8,128)(2,1)S(1)}, bf16[256,896]{1,0:T(8,128)(2,1)S(1)}, u32[]{:S(2)}, u32[]{:S(2)}) collective-permute-start(bf16[256,896]{1,0:T(8,128)(2,1)S(1)} %get-tuple-element.258.refs_4_), channel_id=1, source_target_pairs={{0,4},{4,0},{1,5},{5,1},{2,6},{6,2},{3,7},{7,3},{8,12},{12,8},{9,1... | collective-permute-start | bytes 1376264 | tf_op jit(solution)/shard_map/ppermute | solution.py:490
  130.4 27.5 %collective-permute-start.24 = (bf16[256,896]{1,0:T(8,128)(2,1)S(1)}, bf16[256,896]{1,0:T(8,128)(2,1)S(1)}, u32[]{:S(2)}, u32[]{:S(2)}) collective-permute-start(bf16[256,896]{1,0:T(8,128)(2,1)S(1)} %get-tuple-element.258.refs_4_), channel_id=1, source_target_pairs={{0,1},{1,0},{2,3},{3,2},{4,5},{5,4},{6,7},{7,6},{8,9},{9,8},{10,11... | collective-permute-start | bytes 1376264 | tf_op jit(solution)/shard_map/ppermute | solution.py:490
  131.4 27.6 %collective-permute-start.18 = (bf16[256,896]{1,0:T(8,128)(2,1)}, bf16[256,896]{1,0:T(8,128)(2,1)S(1)}, u32[]{:S(2)}, u32[]{:S(2)}) collective-permute-start(bf16[256,896]{1,0:T(8,128)(2,1)} %get-tuple-element.243.refs_0_), channel_id=1, source_target_pairs={{0,4},{4,0},{1,5},{5,1},{2,6},{6,2},{3,7},{7,3},{8,12},{12,8},{9,1... | collective-permute-start | bytes 1376264 | tf_op jit(solution)/shard_map/ppermute | solution.py:490
  131.7 28.3 %collective-permute-start.19 = (bf16[256,896]{1,0:T(8,128)(2,1)}, bf16[256,896]{1,0:T(8,128)(2,1)S(1)}, u32[]{:S(2)}, u32[]{:S(2)}) collective-permute-start(bf16[256,896]{1,0:T(8,128)(2,1)} %get-tuple-element.243.refs_0_), channel_id=1, source_target_pairs={{0,1},{1,0},{2,3},{3,2},{4,5},{5,4},{6,7},{7,6},{8,9},{9,8},{10,11... | collective-permute-start | bytes 1376264 | tf_op jit(solution)/shard_map/ppermute | solution.py:490
  132.7 29.9 %collective-permute-start.20 = (bf16[256,896]{1,0:T(8,128)(2,1)}, bf16[256,896]{1,0:T(8,128)(2,1)S(1)}, u32[]{:S(2)}, u32[]{:S(2)}) collective-permute-start(bf16[256,896]{1,0:T(8,128)(2,1)} %get-tuple-element.243.refs_0_), channel_id=1, source_target_pairs={{0,5},{1,4},{4,1},{5,0},{2,7},{3,6},{6,3},{7,2},{8,13},{9,12},{12,... | collective-permute-start | bytes 1376264 | tf_op jit(solution)/shard_map/ppermute | solution.py:493
  157.9 4.7 %collective-permute-start.25 = (bf16[256,896]{1,0:T(8,128)(2,1)S(1)}, bf16[256,896]{1,0:T(8,128)(2,1)S(1)}, u32[]{:S(2)}, u32[]{:S(2)}) collective-permute-start(bf16[256,896]{1,0:T(8,128)(2,1)S(1)} %collective-permute-done.24.refs_6_), channel_id=1, source_target_pairs={{0,4},{4,0},{1,5},{5,1},{2,6},{6,2},{3,7},{7,3},{8,12},{12,8},{9,1... | collective-permute-start | bytes 1376264 | tf_op jit(solution)/shard_map/ppermute | solution.py:490
  158.9 31.0 %collective-permute-start.26 = (bf16[256,896]{1,0:T(8,128)(2,1)}, bf16[256,896]{1,0:T(8,128)(2,1)S(1)}, u32[]{:S(2)}, u32[]{:S(2)}) collective-permute-start(bf16[256,896]{1,0:T(8,128)(2,1)} %get-tuple-element.270), channel_id=1, source_target_pairs={{0,4},{4,0},{1,5},{5,1},{2,6},{6,2},{3,7},{7,3},{8,12},{12,8},{9,1... | collective-permute-start | bytes 1376264 | tf_op jit(solution)/shard_map/ppermute | solution.py:490
  159.0 30.9 %collective-permute-start.27 = (bf16[256,896]{1,0:T(8,128)(2,1)}, bf16[256,896]{1,0:T(8,128)(2,1)S(1)}, u32[]{:S(2)}, u32[]{:S(2)}) collective-permute-start(bf16[256,896]{1,0:T(8,128)(2,1)} %get-tuple-element.271), channel_id=1, source_target_pairs={{0,1},{1,0},{2,3},{3,2},{4,5},{5,4},{6,7},{7,6},{8,9},{9,8},{10,11... | collective-permute-start | bytes 1376264 | tf_op jit(solution)/shard_map/ppermute | solution.py:490
  160.0 29.9 %collective-permute-start.28 = (bf16[256,896]{1,0:T(8,128)(2,1)}, bf16[256,896]{1,0:T(8,128)(2,1)S(1)}, u32[]{:S(2)}, u32[]{:S(2)}) collective-permute-start(bf16[256,896]{1,0:T(8,128)(2,1)} %get-tuple-element.272), channel_id=1, source_target_pairs={{0,5},{1,4},{4,1},{5,0},{2,7},{3,6},{6,3},{7,2},{8,13},{9,12},{12,... | collective-permute-start | bytes 1376264 | tf_op jit(solution)/shard_map/ppermute | solution.py:493
  187.6 12.7 %collective-permute-start.29 = (bf16[256,896]{1,0:T(8,128)(2,1)}, bf16[256,896]{1,0:T(8,128)(2,1)S(1)}, u32[]{:S(2)}, u32[]{:S(2)}) collective-permute-start(bf16[256,896]{1,0:T(8,128)(2,1)} %get-tuple-element.274), channel_id=1, source_target_pairs={{0,4},{4,0},{1,5},{5,1},{2,6},{6,2},{3,7},{7,3},{8,12},{12,8},{9,1... | collective-permute-start | bytes 1376264 | tf_op jit(solution)/shard_map/ppermute | solution.py:490
  188.8 12.7 %collective-permute-start.30 = (bf16[256,896]{1,0:T(8,128)(2,1)}, bf16[256,896]{1,0:T(8,128)(2,1)S(1)}, u32[]{:S(2)}, u32[]{:S(2)}) collective-permute-start(bf16[256,896]{1,0:T(8,128)(2,1)} %get-tuple-element.275), channel_id=1, source_target_pairs={{0,1},{1,0},{2,3},{3,2},{4,5},{5,4},{6,7},{7,6},{8,9},{9,8},{10,11... | collective-permute-start | bytes 1376264 | tf_op jit(solution)/shard_map/ppermute | solution.py:490
  201.5 96.3 %reduce-scatter.5.cloned.1.call-start = ((), (), s32[]{:S(2)}) async-start(), calls=%async_computation.5 | async-start | bytes 5734400 | tf_op jit(solution)/shard_map/reduce_scatter | solution.py:627
  202.3 15.3 %collective-permute-start.32 = (bf16[2,256,896]{2,1,0:T(8,128)(2,1)S(1)}, bf16[2,256,896]{2,1,0:T(8,128)(2,1)S(1)}, u32[]{:S(2)}, u32[]{:S(2)}) collective-permute-start(bf16[2,256,896]{2,1,0:T(8,128)(2,1)S(1)} %copy-done.13), channel_id=1, source_target_pairs={{0,4},{4,0},{1,5},{5,1},{2,6},{6,2},{3,7},{7,3},{8,12},{12,8},{9,1... | collective-permute-start | bytes 2752520 | tf_op jit(solution)/shard_map/ppermute | solution.py:490
  202.3 15.3 %collective-permute-start.33 = (bf16[2,256,896]{2,1,0:T(8,128)(2,1)S(1)}, bf16[2,256,896]{2,1,0:T(8,128)(2,1)}, u32[]{:S(2)}, u32[]{:S(2)}) collective-permute-start(bf16[2,256,896]{2,1,0:T(8,128)(2,1)S(1)} %copy-done.14), channel_id=1, source_target_pairs={{0,4},{4,0},{1,5},{5,1},{2,6},{6,2},{3,7},{7,3},{8,12},{12,8},{9,1... | collective-permute-start | bytes 2752520 | tf_op jit(solution)/shard_map/ppermute | solution.py:490
  202.8 14.8 %collective-permute-start.31 = (bf16[256,896]{1,0:T(8,128)(2,1)}, bf16[256,896]{1,0:T(8,128)(2,1)S(1)}, u32[]{:S(2)}, u32[]{:S(2)}) collective-permute-start(bf16[256,896]{1,0:T(8,128)(2,1)} %get-tuple-element.284), channel_id=1, source_target_pairs={{0,5},{1,4},{4,1},{5,0},{2,7},{3,6},{6,3},{7,2},{8,13},{9,12},{12,... | collective-permute-start | bytes 1376264 | tf_op jit(solution)/shard_map/ppermute | solution.py:493
  220.2 14.4 %collective-permute-start.34 = (bf16[256,896]{1,0:T(8,128)(2,1)S(1)}, bf16[256,896]{1,0:T(8,128)(2,1)S(1)}, u32[]{:S(2)}, u32[]{:S(2)}) collective-permute-start(bf16[256,896]{1,0:T(8,128)(2,1)S(1)} %fusion.11), channel_id=1, source_target_pairs={{0,1},{1,0},{2,3},{3,2},{4,5},{5,4},{6,7},{7,6},{8,9},{9,8},{10,11... | collective-permute-start | bytes 1376264 | tf_op jit(solution)/shard_map/ppermute | solution.py:490
  235.7 17.1 %collective-permute-start.35 = (bf16[256,896]{1,0:T(8,128)(2,1)S(1)}, bf16[256,896]{1,0:T(8,128)(2,1)}, u32[]{:S(2)}, u32[]{:S(2)}) collective-permute-start(bf16[256,896]{1,0:T(8,128)(2,1)S(1)} %fusion.12), channel_id=1, source_target_pairs={{0,1},{1,0},{2,3},{3,2},{4,5},{5,4},{6,7},{7,6},{8,9},{9,8},{10,11... | collective-permute-start | bytes 1376264 | tf_op jit(solution)/shard_map/ppermute | solution.py:490
  236.8 18.6 %collective-permute-start.36 = (bf16[256,256]{1,0:T(8,128)(2,1)}, bf16[256,256]{1,0:T(8,128)(2,1)S(1)}, u32[]{:S(2)}, u32[]{:S(2)}) collective-permute-start(bf16[256,256]{1,0:T(8,128)(2,1)} %get-tuple-element.335), channel_id=1, source_target_pairs={{1,0},{2,1},{3,2},{5,4},{6,5},{7,6},{9,8},{10,9},{11,10},{13,12},{... | collective-permute-start | bytes 393224 | tf_op jit(solution)/shard_map/ppermute | solution.py:642
  238.1 17.4 %collective-permute-start.37 = (bf16[256,256]{1,0:T(8,128)(2,1)}, bf16[256,256]{1,0:T(8,128)(2,1)S(1)}, u32[]{:S(2)}, u32[]{:S(2)}) collective-permute-start(bf16[256,256]{1,0:T(8,128)(2,1)} %get-tuple-element.336), channel_id=1, source_target_pairs={{2,0},{3,1},{6,4},{7,5},{10,8},{11,9},{14,12},{15,13},{18,16},{19,... | collective-permute-start | bytes 393224 | tf_op jit(solution)/shard_map/ppermute | solution.py:642
  252.8 7.9 %collective-permute-start.38 = (bf16[256,256]{1,0:T(8,128)(2,1)}, bf16[256,256]{1,0:T(8,128)(2,1)S(1)}, u32[]{:S(2)}, u32[]{:S(2)}) collective-permute-start(bf16[256,256]{1,0:T(8,128)(2,1)} %get-tuple-element.337), channel_id=1, source_target_pairs={{1,0},{2,1},{3,2},{5,4},{6,5},{7,6},{9,8},{10,9},{11,10},{13,12},{... | collective-permute-start | bytes 393224 | tf_op jit(solution)/shard_map/ppermute | solution.py:642
  254.1 13.7 %collective-permute-start.39 = (bf16[256,256]{1,0:T(8,128)(2,1)}, bf16[256,256]{1,0:T(8,128)(2,1)S(1)}, u32[]{:S(2)}, u32[]{:S(2)}) collective-permute-start(bf16[256,256]{1,0:T(8,128)(2,1)} %get-tuple-element.338), channel_id=1, source_target_pairs={{2,0},{3,1},{6,4},{7,5},{10,8},{11,9},{14,12},{15,13},{18,16},{19,... | collective-permute-start | bytes 393224 | tf_op jit(solution)/shard_map/ppermute | solution.py:642
  255.4 17.8 %copy-start.32 = (bf16[256,256]{1,0:T(8,128)(2,1)}, bf16[256,256]{1,0:T(8,128)(2,1)S(1)}, u32[]{:S(2)}) copy-start(bf16[256,256]{1,0:T(8,128)(2,1)S(1)} %collective-permute-done.36.refs_0_) | copy-start | bytes 393220
  255.4 17.8 %copy-start.33 = (bf16[256,256]{1,0:T(8,128)(2,1)}, bf16[256,256]{1,0:T(8,128)(2,1)S(1)}, u32[]{:S(2)}) copy-start(bf16[256,256]{1,0:T(8,128)(2,1)S(1)} %collective-permute-done.37.refs_1_) | copy-start | bytes 393220
  260.6 12.6 %copy-start.34 = (bf16[256,256]{1,0:T(8,128)(2,1)}, bf16[256,256]{1,0:T(8,128)(2,1)S(1)}, u32[]{:S(2)}) copy-start(bf16[256,256]{1,0:T(8,128)(2,1)S(1)} %collective-permute-done.38.refs_2_) | copy-start | bytes 393220
  269.7 15.1 %collective-permute-start.40 = (bf16[112,1280]{1,0:T(8,128)(2,1)}, bf16[112,1280]{1,0:T(8,128)(2,1)S(1)}, u32[]{:S(2)}, u32[]{:S(2)}) collective-permute-start(bf16[112,1280]{1,0:T(8,128)(2,1)} %get-tuple-element.440), channel_id=1, source_target_pairs={{0,0},{2,4},{4,6},{6,2},{1,1},{3,5},{5,7},{7,3},{8,8},{10,12},{12,... | collective-permute-start | bytes 860168 | tf_op jit(solution)/shard_map/ppermute | solution.py:652
  271.3 14.4 %collective-permute-start.41 = (bf16[112,1280]{1,0:T(8,128)(2,1)}, bf16[112,1280]{1,0:T(8,128)(2,1)}, u32[]{:S(2)}, u32[]{:S(2)}) collective-permute-start(bf16[112,1280]{1,0:T(8,128)(2,1)} %get-tuple-element.439), channel_id=1, source_target_pairs={{0,4},{2,0},{4,2},{6,6},{1,5},{3,1},{5,3},{7,7},{8,12},{10,8},{12,... | collective-permute-start | bytes 860168 | tf_op jit(solution)/shard_map/ppermute | solution.py:652
  273.2 13.5 %copy-start = (f32[2,256,896]{2,1,0:T(8,128)S(1)}, f32[2,256,896]{2,1,0:T(8,128)}, u32[]{:S(2)}) copy-start(f32[2,256,896]{2,1,0:T(8,128)} %get-tuple-element.235.middle_ref) | copy-start | bytes 5505028
  285.7 5.0 %collective-permute-start.42 = (bf16[448,2176]{1,0:T(8,128)(2,1)}, bf16[448,2176]{1,0:T(8,128)(2,1)}, u32[]{:S(2)}, u32[]{:S(2)}) collective-permute-start(bf16[448,2176]{1,0:T(8,128)(2,1)} %get-tuple-element.349), channel_id=1, source_target_pairs={{0,4},{4,0},{8,12},{12,8},{16,20},{20,16},{24,28},{28,24},{1,5},{5... | collective-permute-start | bytes 5849096 | tf_op jit(solution)/shard_map/ppermute | solution.py:478
  295.1 13.1 %collective-permute-start.44 = (bf16[1,2,112,1024]{3,2,1,0:T(8,128)(2,1)}, bf16[1,2,112,1024]{3,2,1,0:T(8,128)(2,1)}, u32[]{:S(2)}, u32[]{:S(2)}) collective-permute-start(bf16[1,2,112,1024]{3,2,1,0:T(8,128)(2,1)} %fusion.13), channel_id=1, source_target_pairs={{0,16},{4,20},{8,24},{12,28},{16,0},{20,4},{24,8},{28,12},{1,17},{... | collective-permute-start | bytes 1376264 | tf_op jit(solution)/shard_map/ppermute | solution.py:478
  296.6 13.9 %collective-permute-start.43 = (bf16[2,1,112,1152]{3,2,0,1:T(8,128)(2,1)S(1)}, bf16[2,1,112,1152]{3,2,0,1:T(8,128)(2,1)}, u32[]{:S(2)}, u32[]{:S(2)}) collective-permute-start(bf16[2,1,112,1152]{3,2,0,1:T(8,128)(2,1)S(1)} %fusion.9), channel_id=1, source_target_pairs={{0,8},{4,12},{8,0},{12,4},{16,24},{20,28},{24,16},{28,20},{1,9},{5... | collective-permute-start | bytes 1548296 | tf_op jit(solution)/shard_map/ppermute | solution.py:478
  299.0 12.7 %collective-permute-start.45 = (bf16[112,2560]{1,0:T(8,128)(2,1)S(1)}, bf16[112,2560]{1,0:T(8,128)(2,1)S(1)}, u32[]{:S(2)}, u32[]{:S(2)}) collective-permute-start(bf16[112,2560]{1,0:T(8,128)(2,1)S(1)} %dynamic-slice_bitcast_fusion.1), channel_id=1, source_target_pairs={{0,0},{2,4},{4,6},{6,2},{1,1},{3,5},{5,7},{7,3},{8,8},{10,12},{12,... | collective-permute-start | bytes 1720328 | tf_op jit(solution)/shard_map/ppermute | solution.py:652
  311.7 8.9 %collective-permute-start.46 = (bf16[1,1,112,1152]{3,2,1,0:T(8,128)(2,1)S(1)}, bf16[1,1,112,1152]{3,2,1,0:T(8,128)(2,1)S(1)}, u32[]{:S(2)}, u32[]{:S(2)}) collective-permute-start(bf16[1,1,112,1152]{3,2,1,0:T(8,128)(2,1)S(1)} %fusion.19), channel_id=1, source_target_pairs={{0,16},{4,20},{8,24},{12,28},{16,0},{20,4},{24,8},{28,12},{1,17},{... | collective-permute-start | bytes 774152 | tf_op jit(solution)/shard_map/ppermute | solution.py:478
  312.5 8.0 %collective-permute-start.47 = (bf16[1,1,112,1024]{3,2,1,0:T(8,128)(2,1)S(1)}, bf16[1,1,112,1024]{3,2,1,0:T(8,128)(2,1)S(1)}, u32[]{:S(2)}, u32[]{:S(2)}) collective-permute-start(bf16[1,1,112,1024]{3,2,1,0:T(8,128)(2,1)S(1)} %fusion.20), channel_id=1, source_target_pairs={{0,8},{4,12},{8,0},{12,4},{16,24},{20,28},{24,16},{28,20},{1,9},{5... | collective-permute-start | bytes 688136 | tf_op jit(solution)/shard_map/ppermute | solution.py:478
  313.1 28.7 %collective-permute-start.51 = (bf16[112,2560]{1,0:T(8,128)(2,1)S(1)}, bf16[112,2560]{1,0:T(8,128)(2,1)S(1)}, u32[]{:S(2)}, u32[]{:S(2)}) collective-permute-start(bf16[112,2560]{1,0:T(8,128)(2,1)S(1)} %dynamic-slice_bitcast_fusion), channel_id=1, source_target_pairs={{0,4},{2,0},{4,2},{6,6},{1,5},{3,1},{5,3},{7,7},{8,12},{10,8},{12,... | collective-permute-start | bytes 1720328 | tf_op jit(solution)/shard_map/ppermute | solution.py:652
  320.9 8.5 %collective-permute-start.48 = (bf16[28,2176]{1,0:T(8,128)(2,1)S(1)}, bf16[28,2176]{1,0:T(8,128)(2,1)S(1)}, u32[]{:S(2)}, u32[]{:S(2)}) collective-permute-start(bf16[28,2176]{1,0:T(8,128)(2,1)S(1)} %get-tuple-element.443), channel_id=1, source_target_pairs={{0,1},{1,2},{2,3},{3,0},{4,5},{5,6},{6,7},{7,4},{8,9},{9,10},{10,1... | collective-permute-start | bytes 365576 | tf_op jit(solution)/shard_map/ppermute | solution.py:487
  321.1 20.7 %collective-permute-start.49 = (bf16[28,2176]{1,0:T(8,128)(2,1)S(1)}, bf16[28,2176]{1,0:T(8,128)(2,1)S(1)}, u32[]{:S(2)}, u32[]{:S(2)}) collective-permute-start(bf16[28,2176]{1,0:T(8,128)(2,1)S(1)} %get-tuple-element.442), channel_id=1, source_target_pairs={{0,2},{1,3},{2,0},{3,1},{4,6},{5,7},{6,4},{7,5},{8,10},{9,11},{10,... | collective-permute-start | bytes 365576 | tf_op jit(solution)/shard_map/ppermute | solution.py:487
  324.7 17.1 %collective-permute-start.50 = (bf16[28,2176]{1,0:T(8,128)(2,1)S(1)}, bf16[28,2176]{1,0:T(8,128)(2,1)S(1)}, u32[]{:S(2)}, u32[]{:S(2)}) collective-permute-start(bf16[28,2176]{1,0:T(8,128)(2,1)S(1)} %get-tuple-element.441), channel_id=1, source_target_pairs={{0,3},{1,0},{2,1},{3,2},{4,7},{5,4},{6,5},{7,6},{8,11},{9,8},{10,9... | collective-permute-start | bytes 365576 | tf_op jit(solution)/shard_map/ppermute | solution.py:487
  (38 other events, 111.8 us)
Sparse Core Ops, SparseCore 0:
  10.0 65.7 all-gather.2
  78.8 47.7 all-gather.4
  201.7 37.2 reduce-scatter.2
  241.9 55.9 reduce-scatter.4

commit v7 on v6

--- a/solution.py
+++ b/solution.py
@@ -24,7 +24,8 @@
 def scaled(v):
     return lax.rsqrt(jnp.mean(v*v, axis=-1, keepdims=True)+epsilon)
 
-def pairs_kernel(x_ref, wkv_ref, ws_ref, spread_ref, cos_ref, sin_ref, kv_ref, n1_ref, rows_ref, bias_ref):
+def pairs_kernel(x_ref, wkv_ref, ws_ref, spread_ref, cos_ref, sin_ref, n1_ref, rows_ref, *refs):
+    kv_refs=refs[:-1]; bias_ref=refs[-1]
     @pl.when(pl.program_id(0)==0)
     def _():
         table = ws_ref[...].astype(f32).T[:8]
@@ -37,8 +38,10 @@
     n1_ref[...] = n1
     kv = dot(n1, wkv_ref[...],1,0) + bias_ref[...]
     v = kv[:, :KW]
-    kv_ref[:, :KW] = (v*cos_ref[...] + half_turn(v,False)*sin_ref[...]).astype(bf16)
-    kv_ref[:, KW:] = kv[:, KW:].astype(bf16)
+    pair = jnp.concatenate([v*cos_ref[...] + half_turn(v,False)*sin_ref[...], kv[:, KW:]],axis=1).astype(bf16)
+    for m,kv_ref in enumerate(kv_refs):
+        @pl.when(pl.program_id(0)==m)
+        def _(kv_ref=kv_ref): kv_ref[...] = pair
 
 def queries_kernel(n1_ref, wq_ref, rows_ref, cos_ref, sin_ref, rq_ref):
     q = dot(n1_ref[...], wq_ref[:, 2*KW:],1,0) + rows_ref[2:3]
@@ -54,11 +57,11 @@
     blk=lambda w: pl.BlockSpec((None,rows,w), lambda i:(i,0,0))
     sd=jax.ShapeDtypeStruct
     params=dict(compiler_params=pltpu.CompilerParams(vmem_limit_bytes=LIMIT), cost_estimate=COST)
-    pair, n1, table = pl.pallas_call(
+    n1, table, *pair = pl.pallas_call(
         pairs_kernel, grid=(m,),
         in_specs=[blk(D), full((D,2*KW),(0,0)), full((D,LANES),(0,QW//LANES)), full((D,LANES),(0,0)), blk(LANES), blk(LANES)],
-        out_specs=[blk(2*KW), blk(D), full((8,D),(0,0))],
-        out_shape=[sd((m,rows,2*KW),bf16), sd((m,rows,D),bf16), sd((8,D),f32)],
+        out_specs=[blk(D), full((8,D),(0,0))]+[full((rows,2*KW),(0,0))]*m,
+        out_shape=[sd((m,rows,D),bf16), sd((8,D),f32)]+[sd((rows,2*KW),bf16)]*m,
         scratch_shapes=[pltpu.VMEM((1,2*KW),f32)],
         name="pairs", **params,
     )(x, in_set, out_set, spread, cos, sin)
@@ -143,7 +146,7 @@
     sd=jax.ShapeDtypeStruct
     return pl.pallas_call(
         attend_kernel, grid=(nq,),
-        in_specs=[pl.BlockSpec(memory_space=pltpu.SMEM), blk(QW)]+[pl.BlockSpec((None,rows,2*KW),lambda i:(m,0,0))]*3+[pl.BlockSpec((None,1,BLOCK),lambda i:(m,0,i)), full((D,QW)), blk(D), full((8,D))]+[pl.BlockSpec(memory_space=pl.ANY)]*len(before),
+        in_specs=[pl.BlockSpec(memory_space=pltpu.SMEM), blk(QW)]+[full((rows,2*KW))]*3+[pl.BlockSpec((None,1,BLOCK),lambda i:(m,0,i)), full((D,QW)), blk(D), full((8,D))]+[pl.BlockSpec(memory_space=pl.ANY)]*len(before),
         out_specs=[pl.BlockSpec((BLOCK,D),lambda i:(i,0)), blk(QW), blk(D), pl.BlockSpec((None,1,16,BLOCK),lambda i:(m,i,0,0))],
         out_shape=[sd((rows,D),bf16), sd((micros,rows,QW),bf16), sd((micros,rows,D),f32), sd((micros,nq,16,BLOCK),f32)],
         scratch_shapes=[pltpu.VMEM((4,3*rows,LANES),bf16), pltpu.VMEM((4,3*rows,LANES),bf16)],
@@ -224,7 +227,7 @@
     at=12+len(gs)
     return pl.pallas_call(
         functools.partial(attend_back_kernel,count=len(gs)), grid=(nq,),
-        in_specs=[pl.BlockSpec(memory_space=pltpu.SMEM), blk(QW)]+[pl.BlockSpec((None,rows,2*KW),lambda i:(m,0,0))]*3+[pl.BlockSpec((None,1,BLOCK),lambda i:(m,0,i)), full((D,QW)), full((8,D)),
+        in_specs=[pl.BlockSpec(memory_space=pltpu.SMEM), blk(QW)]+[full((rows,2*KW))]*3+[pl.BlockSpec((None,1,BLOCK),lambda i:(m,0,i)), full((D,QW)), full((8,D)),
             pl.BlockSpec((None,1,16,BLOCK),lambda i:(m,i,0,0)), blk(D), blk(D)]+[blk(LANES)]*2+[pl.BlockSpec((BLOCK,D),lambda i:(i,0))]*len(gs)+[pl.BlockSpec(memory_space=pl.ANY)]*len(before),
         out_specs=[full((rows,2*KW)), full((rows,2*KW)), blk(D), blk(D), blk(QW), one(rows,2*KW), one(8,D)],
         out_shape=[sd((rows,2*KW),bf16), sd((rows,2*KW),bf16), sd((micros,rows,D),f32), sd((micros,rows,D),bf16), sd((micros,rows,QW),bf16), sd((micros,rows,2*KW),f32), sd((micros,8,D),f32)],
@@ -554,6 +557,8 @@
             firsts = [firsts, gots]
         if k < 3:
             other_block.append(other(own_block[:, edges[k] : edges[k + 1]], "zh"))
+        if k == 1:
+            crossed.append(other(upstream[0], "zb"))
         firsts, other_block, own_block, spread, cosines, sines, begins, upstream, crossed = after(
             (firsts, other_block, own_block, spread, cosines, sines, begins, upstream, crossed)
         )
@@ -575,23 +580,25 @@
     rot_query, pairs, normed_one, rows_table = project(
         tokens, out_set, in_set, spread, cosines, sines
     )
-    kvs = [pairs] + [
-        lax.ppermute(pairs, ctx, [(s, s + d) for s in range(parts - d)])
-        for d in range(1, reach_parts + 1)
-    ]
-
-    kvs, rot_query, upstream = after((kvs, rot_query, upstream))
-    crossed.append(other(upstream[0], "zb"))
+    def earlier(pair):
+        return [pair] + [
+            lax.ppermute(pair, ctx, [(s, s + d) for s in range(parts - d)])
+            for d in range(1, reach_parts + 1)
+        ]
+
+    kvs = [earlier(pairs[0])]
+    rot_query, pairs[1:] = after((rot_query, pairs[1:]))
+    kvs += [earlier(pair) for pair in pairs[1:]]
 
     begins = begins[:, None, :]
     exchanged = []
     held = ()
     for m in range(micros):
         normed_two, *held = attend(
-            m, base, rot_query, kvs, begins, out_set, tokens, rows_table, held
+            m, base, rot_query, kvs[m], begins, out_set, tokens, rows_table, held
         )
         if m == 0:
-            upstream, crossed, normed_two = after((upstream, crossed, normed_two))
+            upstream, crossed, normed_two, kvs[1:] = after((upstream, crossed, normed_two, kvs[1:]))
         exchanged.append([normed_two, other(normed_two, "core"), other(normed_two, "zb")])
         if m == 0:
             crossed += [other(u, "zb") for u in upstream[1:]]
@@ -633,7 +640,7 @@
         out_sum = (partials[2][m].astype(f32) + out_far[m].astype(f32)).astype(bf16)
         out_beside.append(other(out_sum, "zb"))
         far1, far2, *ended = attend_back(
-            m, base, rot_query, kvs, begins, out_set, rows_table, log_sums, middle, cotangent[0, :, 0],
+            m, base, rot_query, kvs[m], begins, out_set, rows_table, log_sums, middle, cotangent[0, :, 0],
             backs[m], cosines, sines, ended,
         )
         far1, far2, ended, out_beside = after((far1, far2, ended, out_beside))

time: 359 us -> 354 us (0.986)
  starting transfers between devices: 69.2 us -> 62.4 us
    ppermute x22, starting transfers between devices: 21.3 us -> 13.9 us  [other(): return lax.ppermute(values_in, axis, [(0, 1), (1, 0)])]
    ppermute x22, waiting for transfers between devices: 15.6 us -> 19.4 us  [other(): return lax.ppermute(values_in, axis, [(0, 1), (1, 0)])]
    ppermute x2 -> x4, starting transfers between devices: 6.77 us -> 8.84 us  [earlier(): lax.ppermute(pair, ctx, [(s, s + d) for s in range(parts - d)])]
    unnamed x106 -> x112, local copies, waits for them, and re-layouts: 6.86 us -> 7.37 us
  transfers between devices with their start and end apart: 56 -> 58, of which waited for: 19 -> 19; matrix products, arithmetic and copies ran while one was open for 7% -> 7% of each run, Pallas kernels for 40% -> 41%
where the time goes in v7:
time: 354 us; the launch traced here: 348 us
  Pallas kernels  142 us (40%)
  waiting for transfers between devices  91.1 us (26%)
  starting transfers between devices  62.4 us (18%)
  other arithmetic  19.4 us (5%)
  local copies, waits for them, and re-layouts  17.5 us (5%)
  between operations  15.4 us (4%)
    pallas_call x2, Pallas kernels, feed(): pl.pallas_call(functools.partial(feed_kernel, parts=parts, micro=micro, k...  48.5 us
    ppermute x11, waiting for transfers between devices, swapped(): return lax.ppermute(values_in, dp, [(s, s ^ bit) for s in range(groups)])  36.6 us
    pallas_call x2, Pallas kernels, attend_back(): pl.pallas_call(functools.partial(attend_back_kernel, count=len(gs)), grid...  26.7 us
    pallas_call x2, Pallas kernels, weights(): pl.pallas_call(weights_kernel, grid=(width // chunk,), in_specs=[pl.Block...  23.4 us
    ppermute x6, waiting for transfers between devices, around(): lax.ppermute(values_in, ctx, [(s, (s + steps) % parts) for s in range(par...  20.8 us
    ppermute x22, waiting for transfers between devices, other(): return lax.ppermute(values_in, axis, [(0, 1), (1, 0)])  19.4 us
    pallas_call x2, Pallas kernels, attend(): pl.pallas_call(attend_kernel, grid=(nq,), in_specs=[pl.BlockSpec(memory_s...  18.9 us
    ppermute x22, starting transfers between devices, other(): return lax.ppermute(values_in, axis, [(0, 1), (1, 0)])  13.9 us
  transfers between devices with their start and end apart: 58, of which 19 were waited for; matrix products, arithmetic and copies ran while one was open for 7% of the time, Pallas kernels for 41%

profile of v7, /device:TPU:0, one launch (start us, length us, event | category | flops | bytes accessed | tf_op | source)
XLA Modules:
  0.0 347.7 jit_solution(11513826848224067443)
XLA Ops:
  7.3 2.2 fusion.8
  9.9 5.1 %collective-permute-start = (bf16[28,2176]{1,0:T(8,128)(2,1)S(1)}, bf16[28,2176]{1,0:T(8,128)(2,1)S(1)}, u32[]{:S(2)}, u32[]{:S(2)}) collective-permute-start(bf16[28,2176]{1,0:T(8,128)(2,1)S(1)} %constant_dynamic-update-slice_fusion), channel_id=1, source_target_pairs={{0,3},{1,0},{2,1},{3,2},{4,7},{5,4},{6,5},{7,6},{8,11},{9,8},{10,9... | collective-permute-start | bytes 365576 | tf_op jit(solution)/shard_map/ppermute | solution.py:490
  18.4 1.3 pad_maximum_fusion.5
  19.6 7.2 %collective-permute-done.1 = bf16[28,2176]{1,0:T(8,128)(2,1)S(1)} collective-permute-done((bf16[28,2176]{1,0:T(8,128)(2,1)S(1)}, bf16[28,2176]{1,0:T(8,128)(2,1)S(1)}, u32[]{:S(2)}, u32[]{:S(2)}) %collective-permute-start.1) | collective-permute-done | bytes 121888 | tf_op jit(solution)/shard_map/ppermute | solution.py:490
  27.2 1.6 collective-permute-start.3
  29.7 1.6 collective-permute-start.4
  31.4 2.8 collective-permute-start.5
  34.1 3.1 collective-permute-done.3
  38.4 3.9 %collective-permute-done.5 = bf16[112,896]{1,0:T(8,128)(2,1)S(1)} collective-permute-done((bf16[112,896]{1,0:T(8,128)(2,1)S(1)}, bf16[112,896]{1,0:T(8,128)(2,1)S(1)}, u32[]{:S(2)}, u32[]{:S(2)}) %collective-permute-start.5) | collective-permute-done | bytes 200736 | tf_op jit(solution)/shard_map/ppermute | solution.py:493
  43.5 1.9 collective-permute-start.9
  45.5 19.5 %collective-permute-done.6 = bf16[2,112,1024]{2,1,0:T(8,128)(2,1)S(1)} collective-permute-done((bf16[2,112,1024]{2,1,0:T(8,128)(2,1)S(1)}, bf16[2,112,1024]{2,1,0:T(8,128)(2,1)S(1)}, u32[]{:S(2)}, u32[]{:S(2)}) %collective-permute-start.6) | collective-permute-done | bytes 458784 | tf_op jit(solution)/shard_map/ppermute | solution.py:481
  65.1 2.8 collective-permute-done.7
  68.9 8.8 %collective-permute-done.12 = bf16[112,896]{1,0:T(8,128)(2,1)S(1)} collective-permute-done((bf16[112,896]{1,0:T(8,128)(2,1)S(1)}, bf16[112,896]{1,0:T(8,128)(2,1)S(1)}, u32[]{:S(2)}, u32[]{:S(2)}) %collective-permute-start.12) | collective-permute-done | bytes 200736 | tf_op jit(solution)/shard_map/ppermute | solution.py:493
  79.7 4.7 %woven.1 = (bf16[896,1024]{1,0:T(8,128)(2,1)}, bf16[896,1152]{1,0:T(8,128)(2,1)}) custom-call(s32[1]{0:T(128)} %bitcast.2.core_ref, bf16[4,112,1024]{2,1,0:T(8,128)(2,1)} %bitcast.138, bf16[4,112,1152]{2,1,0:T(8,128)(2,1)} %bitcast.137, bf16[4,112,1024]{2,1,0:T(8,128)(2,1)} %bitcast.141, bf16[4,112,1152]{2,1,0:T(8,128)(2,1)} %bitcast.26.refs_3_), custom_call_target="tpu_custom_call" | custom-call | flops 1 | bytes 1 | tf_op jit(solution)/shard_map/woven/pallas_call | solution.py:425
  84.4 3.7 %pairs.1 = (bf16[2,256,896]{2,1,0:T(8,128)(2,1)}, f32[8,896]{1,0:T(8,128)}, bf16[256,256]{1,0:T(8,128)(2,1)}, bf16[256,256]{1,0:T(8,128)(2,1)}) custom-call(bf16[2,256,896]{2,1,0:T(8,128)(2,1)} %bitcast.127, bf16[896,1152]{1,0:T(8,128)(2,1)} %get-tuple-element.220.wkv_ref.wq_ref, bf16[896,1024]{1,0:T(8,128)(2,1)} %get-tuple-element.221.ws_ref.wo_ref, ...), custom_call_target="tpu_custom_call" | custom-call | flops 1 | bytes 1 | tf_op jit(solution)/shard_map/pairs/pallas_call | solution.py:60
  88.1 1.3 collective-permute-start.13
  89.4 4.2 %collective-permute-start.14 = (bf16[256,256]{1,0:T(8,128)(2,1)}, bf16[256,256]{1,0:T(8,128)(2,1)S(1)}, u32[]{:S(2)}, u32[]{:S(2)}) collective-permute-start(bf16[256,256]{1,0:T(8,128)(2,1)} %get-tuple-element.232.kv0_ref), channel_id=1, source_target_pairs={{0,2},{1,3},{4,6},{5,7},{8,10},{9,11},{12,14},{13,15},{16,18},{17,... | collective-permute-start | bytes 393224 | tf_op jit(solution)/shard_map/ppermute | solution.py:585
  93.6 4.5 %queries.1.rq_ref = bf16[2,256,896]{2,1,0:T(8,128)(2,1)} custom-call(bf16[2,256,896]{2,1,0:T(8,128)(2,1)} %get-tuple-element.225.n1_ref, bf16[896,1152]{1,0:T(8,128)(2,1)} %get-tuple-element.220.wkv_ref.wq_ref, f32[8,896]{1,0:T(8,128)} %get-tuple-element.226.rows_ref, f32[2,256,128]{2,1,0:T(8,128)} %get-tuple-element.223.cos_ref, ...), custom_call_target="tpu_custom_call" | custom-call | flops 1 | bytes 1 | tf_op jit(solution)/shard_map/queries/pallas_call | solution.py:68
  98.1 1.3 collective-permute-start.15
  99.4 2.1 collective-permute-start.16
  102.8 9.5 %attend.2 = (bf16[256,896]{1,0:T(8,128)(2,1)}, bf16[2,256,896]{2,1,0:T(8,128)(2,1)}, f32[2,256,896]{2,1,0:T(8,128)}, f32[2,2,16,128]{3,2,1,0:T(8,128)}) custom-call(s32[1]{0:T(128)} %bitcast.base_ref, bf16[2,256,896]{2,1,0:T(8,128)(2,1)} %queries.1.rq_ref, bf16[256,256]{1,0:T(8,128)(2,1)} %get-tuple-element.232.kv0_ref, bf16[256,256]{1,0:T(8,128)(2,1)} %copy-done.13, ...), custom_call_target="tpu_custom_call" | custom-call | flops 1 | bytes 1 | tf_op jit(solution)/shard_map/attend/pallas_call | solution.py:147
  113.1 9.3 %attend.3 = (bf16[256,896]{1,0:T(8,128)(2,1)}, bf16[2,256,896]{2,1,0:T(8,128)(2,1)}, f32[2,256,896]{2,1,0:T(8,128)}, f32[2,2,16,128]{3,2,1,0:T(8,128)}) custom-call(s32[1]{0:T(128)} %bitcast.base_ref, bf16[2,256,896]{2,1,0:T(8,128)(2,1)} %queries.1.rq_ref, ...), custom_call_target="tpu_custom_call", output_to_operand_aliasing={{1}: (9, {}), {2}: (10, {}), {3}: (11, {})} | custom-call | flops 1 | bytes 1 | tf_op jit(solution)/shard_map/attend/pallas_call | solution.py:147
  122.5 3.2 collective-permute-done.18.refs_2_
  127.6 1.1 collective-permute-start.21
  129.4 24.1 %feed.2 = (f32[256,896]{1,0:T(8,128)}, bf16[256,896]{1,0:T(8,128)(2,1)}, bf16[256,896]{1,0:T(8,128)(2,1)}, bf16[256,896]{1,0:T(8,128)(2,1)}, f32[2,256,896]{2,1,...) custom-call(s32[1]{0:T(128)} %bitcast.27.own_ref, ...), custom_call_target="tpu_custom_call" | custom-call | flops 1 | bytes 1 | tf_op jit(solution)/shard_map/feed/pallas_call | solution.py:315
  154.6 1.3 collective-permute-start.29
  156.4 2.0 collective-permute-done.22.refs_3_
  159.3 24.4 %feed.3 = (f32[256,896]{1,0:T(8,128)}, bf16[256,896]{1,0:T(8,128)(2,1)}, bf16[256,896]{1,0:T(8,128)(2,1)}, bf16[256,896]{1,0:T(8,128)(2,1)}, f32[2,256,896]{2,1,...) custom-call(s32[1]{0:T(128)} %bitcast.27.own_ref, ...), custom_call_target="tpu_custom_call", output_to_operand_aliasing={{4}: (11, {}), {5}: (12, {}), {6}: (13, {}), {7}: (14, {}),... | custom-call | flops 1 | bytes 1 | tf_op jit(solution)/shard_map/feed/pallas_call | solution.py:315
  183.7 1.3 collective-permute-start.31
  186.1 9.3 %weights.2 = bf16[896,1280]{1,0:T(8,128)(2,1)} custom-call(bf16[2,8,896,256]{3,2,1,0:T(8,128)(2,1)} %get-tuple-element.289.left_ref, bf16[2048,1280]{1,0:T(8,128)(2,1)} %get-tuple-element.285.right_ref), custom_call_target="tpu_custom_call" | custom-call | flops 1 | bytes 1 | tf_op jit(solution)/shard_map/weights/pallas_call | solution.py:401
  195.5 2.3 collective-permute-done.32.refs_2_
  199.4 14.1 %weights.3 = bf16[896,2560]{1,0:T(8,128)(2,1)} custom-call(bf16[2,8,896,256]{3,2,1,0:T(8,128)(2,1)} %get-tuple-element.289.left_ref, bf16[2048,2560]{1,0:T(8,128)(2,1)} %get-tuple-element.290.right_ref), custom_call_target="tpu_custom_call" | custom-call | flops 1 | bytes 1 | tf_op jit(solution)/shard_map/weights/pallas_call | solution.py:401
  214.8 1.1 fusion.11
  216.0 1.4 collective-permute-start.36
  217.4 13.2 %attend_back.2 = (bf16[256,256]{1,0:T(8,128)(2,1)}, bf16[256,256]{1,0:T(8,128)(2,1)}, f32[2,256,896]{2,1,0:T(8,128)}, bf16[2,256,896]{2,1,0:T(8,128)(2,1)}, bf16...) custom-call(s32[1]{0:T(128)} %bitcast.base_ref, bf16[2,256,896]{2,1,0:T(8,128)(2,1)} %queries.1.rq_ref, ...), custom_call_target="tpu_custom_call" | custom-call | flops 1 | bytes 1 | tf_op jit(solution)/shard_map/attend_back/pallas_call | solution.py:228
  230.6 1.1 fusion.12
  232.5 1.3 collective-permute-start.38
  233.8 1.3 collective-permute-start.39
  235.1 13.5 %attend_back.3 = (bf16[256,256]{1,0:T(8,128)(2,1)}, bf16[256,256]{1,0:T(8,128)(2,1)}, f32[2,256,896]{2,1,0:T(8,128)}, bf16[2,256,896]{2,1,0:T(8,128)(2,1)}, bf16...) custom-call(s32[1]{0:T(128)} %bitcast.base_ref, ...), custom_call_target="tpu_custom_call", output_to_operand_aliasing={{2}: (17, {}), {3}: (18, {}), {4}: (19, {}), {5}: (20, {}),... | custom-call | flops 1 | bytes 1 | tf_op jit(solution)/shard_map/attend_back/pallas_call | solution.py:228
  248.6 1.3 collective-permute-start.40
  249.9 1.3 collective-permute-start.41
  251.3 5.7 %collective-permute-done.40.refs_2_ = bf16[256,256]{1,0:T(8,128)(2,1)S(1)} collective-permute-done((bf16[256,256]{1,0:T(8,128)(2,1)}, bf16[256,256]{1,0:T(8,128)(2,1)S(1)}, u32[]{:S(2)}, u32[]{:S(2)}) %collective-permute-start.40) | collective-permute-done | bytes 131104 | tf_op jit(solution)/shard_map/ppermute | solution.py:649
  256.9 6.1 %collective-permute-done.41.refs_3_ = bf16[256,256]{1,0:T(8,128)(2,1)S(1)} collective-permute-done((bf16[256,256]{1,0:T(8,128)(2,1)}, bf16[256,256]{1,0:T(8,128)(2,1)S(1)}, u32[]{:S(2)}, u32[]{:S(2)}) %collective-permute-start.41) | collective-permute-done | bytes 131104 | tf_op jit(solution)/shard_map/ppermute | solution.py:649
  263.1 1.9 dynamic-slice_bitcast_fusion.2
  265.0 1.6 collective-permute-start.42
  266.6 1.9 collective-permute-start.43
  268.6 11.6 %finish.1 = (f32[2,256,896]{2,1,0:T(8,128)}, bf16[448,2176]{1,0:T(8,128)(2,1)}, bf16[448,2176]{1,0:T(8,128)(2,1)}) custom-call(s32[1]{0:T(128)} %bitcast.35.bit_ref, bf16[2,256,896]{2,1,0:T(8,128)(2,1)} %get-tuple-element.333.dq_ref, f32[2,256,256]{2,1,0:T(8,128)} %get-tuple-element.334.own_ref, f32[2,256,128]{2,1,0:T(8,128)} %get-tuple-element.223.cos_ref, ...), custom_call_target="tpu_custom_call" | custom-call | flops 1 | bytes 1 | tf_op jit(solution)/shard_map/finish/pallas_call | solution.py:385
  280.7 3.0 fusion.5
  283.7 1.3 collective-permute-done.44
  285.0 2.0 convert_add_fusion
  287.4 1.2 copy-done.3
  289.4 1.1 collective-permute-start.46
  290.6 1.4 collective-permute-start.45
  292.0 1.1 dynamic-slice_bitcast_fusion.1
  293.8 8.4 %collective-permute-done.46 = bf16[1,2,112,1024]{3,2,1,0:T(8,128)(2,1)} collective-permute-done((bf16[1,2,112,1024]{3,2,1,0:T(8,128)(2,1)}, bf16[1,2,112,1024]{3,2,1,0:T(8,128)(2,1)}, u32[]{:S(2)}, u32[]{:S(2)}) %collective-permute-start.46) | collective-permute-done | bytes 458784 | tf_op jit(solution)/shard_map/ppermute | solution.py:481
  302.2 1.5 fusion.6
  304.2 1.1 fusion.4
  306.4 1.3 collective-permute-start.49
  307.8 6.5 %collective-permute-start.53 = (bf16[112,2560]{1,0:T(8,128)(2,1)S(1)}, bf16[112,2560]{1,0:T(8,128)(2,1)S(1)}, u32[]{:S(2)}, u32[]{:S(2)}) collective-permute-start(bf16[112,2560]{1,0:T(8,128)(2,1)S(1)} %dynamic-slice_bitcast_fusion), channel_id=1, source_target_pairs={{0,4},{2,0},{4,2},{6,6},{1,5},{3,1},{5,3},{7,7},{8,12},{10,8},{12,... | collective-permute-start | bytes 1720328 | tf_op jit(solution)/shard_map/ppermute | solution.py:659
  314.7 3.6 %collective-permute-start.51 = (bf16[28,2176]{1,0:T(8,128)(2,1)S(1)}, bf16[28,2176]{1,0:T(8,128)(2,1)S(1)}, u32[]{:S(2)}, u32[]{:S(2)}) collective-permute-start(bf16[28,2176]{1,0:T(8,128)(2,1)S(1)} %get-tuple-element.446), channel_id=1, source_target_pairs={{0,2},{1,3},{2,0},{3,1},{4,6},{5,7},{6,4},{7,5},{8,10},{9,11},{10,... | collective-permute-start | bytes 365576 | tf_op jit(solution)/shard_map/ppermute | solution.py:490
  318.4 2.8 collective-permute-start.52
  321.2 1.8 add_bitcast_fusion
  323.0 13.6 %collective-permute-done.51 = bf16[28,2176]{1,0:T(8,128)(2,1)S(1)} collective-permute-done((bf16[28,2176]{1,0:T(8,128)(2,1)S(1)}, bf16[28,2176]{1,0:T(8,128)(2,1)S(1)}, u32[]{:S(2)}, u32[]{:S(2)}) %collective-permute-start.51) | collective-permute-done | bytes 121888 | tf_op jit(solution)/shard_map/ppermute | solution.py:490
  339.6 1.1 fusion.32
  (242 shorter events, 29.8 us)
Async XLA Ops:
  7.3 122.1 %all-gather.3.cloned.1.call-start = ((), (), s32[]{:S(2)}) async-start(), calls=%async_computation.2 | async-start | bytes 7741440 | tf_op jit(solution)/shard_map/all_gather | solution.py:516
  9.6 119.8 %all-gather.5.cloned.1.call-start = ((), (), s32[]{:S(2)}) async-start(), calls=%async_computation.3 | async-start | bytes 7741440 | tf_op jit(solution)/shard_map/all_gather | solution.py:565
  9.9 9.7 %collective-permute-start = (bf16[28,2176]{1,0:T(8,128)(2,1)S(1)}, bf16[28,2176]{1,0:T(8,128)(2,1)S(1)}, u32[]{:S(2)}, u32[]{:S(2)}) collective-permute-start(bf16[28,2176]{1,0:T(8,128)(2,1)S(1)} %constant_dynamic-update-slice_fusion), channel_id=1, source_target_pairs={{0,3},{1,0},{2,1},{3,2},{4,7},{5,4},{6,5},{7,6},{8,11},{9,8},{10,9... | collective-permute-start | bytes 365576 | tf_op jit(solution)/shard_map/ppermute | solution.py:490
  15.0 11.8 %collective-permute-start.1 = (bf16[28,2176]{1,0:T(8,128)(2,1)S(1)}, bf16[28,2176]{1,0:T(8,128)(2,1)S(1)}, u32[]{:S(2)}, u32[]{:S(2)}) collective-permute-start(bf16[28,2176]{1,0:T(8,128)(2,1)S(1)} %constant_dynamic-update-slice_fusion), channel_id=1, source_target_pairs={{0,2},{1,3},{2,0},{3,1},{4,6},{5,7},{6,4},{7,5},{8,10},{9,11},{10,... | collective-permute-start | bytes 365576 | tf_op jit(solution)/shard_map/ppermute | solution.py:490
  15.0 11.8 %collective-permute-start.2 = (bf16[28,2176]{1,0:T(8,128)(2,1)S(1)}, bf16[28,2176]{1,0:T(8,128)(2,1)S(1)}, u32[]{:S(2)}, u32[]{:S(2)}) collective-permute-start(bf16[28,2176]{1,0:T(8,128)(2,1)S(1)} %constant_dynamic-update-slice_fusion), channel_id=1, source_target_pairs={{0,1},{1,2},{2,3},{3,0},{4,5},{5,6},{6,7},{7,4},{8,9},{9,10},{10,1... | collective-permute-start | bytes 365576 | tf_op jit(solution)/shard_map/ppermute | solution.py:490
  18.4 107.9 %copy-start.8 = (bf16[256,896]{1,0:T(8,128)(2,1)}, bf16[256,896]{1,0:T(8,128)(2,1)S(1)}, u32[]{:S(2)}) copy-start(bf16[256,896]{1,0:T(8,128)(2,1)S(1)} %get-tuple-element.262.refs_4_) | copy-start | bytes 1376260
  27.2 10.0 %collective-permute-start.3 = (bf16[112,1024]{1,0:T(8,128)(2,1)S(1)}, bf16[112,1024]{1,0:T(8,128)(2,1)S(1)}, u32[]{:S(2)}, u32[]{:S(2)}) collective-permute-start(bf16[112,1024]{1,0:T(8,128)(2,1)S(1)} %slice.75), channel_id=1, source_target_pairs={{0,8},{4,12},{8,0},{12,4},{16,24},{20,28},{24,16},{28,20},{1,9},{5... | collective-permute-start | bytes 688136 | tf_op jit(solution)/shard_map/ppermute | solution.py:481
  29.7 8.6 %collective-permute-start.4 = (bf16[112,1152]{1,0:T(8,128)(2,1)S(1)}, bf16[112,1152]{1,0:T(8,128)(2,1)S(1)}, u32[]{:S(2)}, u32[]{:S(2)}) collective-permute-start(bf16[112,1152]{1,0:T(8,128)(2,1)S(1)} %slice.76), channel_id=1, source_target_pairs={{0,16},{4,20},{8,24},{12,28},{16,0},{20,4},{24,8},{28,12},{1,17},{... | collective-permute-start | bytes 774152 | tf_op jit(solution)/shard_map/ppermute | solution.py:481
  31.4 11.0 %collective-permute-start.5 = (bf16[112,896]{1,0:T(8,128)(2,1)S(1)}, bf16[112,896]{1,0:T(8,128)(2,1)S(1)}, u32[]{:S(2)}, u32[]{:S(2)}) collective-permute-start(bf16[112,896]{1,0:T(8,128)(2,1)S(1)} %slice.77), channel_id=1, source_target_pairs={{0,2},{2,0},{1,3},{3,1},{4,6},{6,4},{5,7},{7,5},{8,10},{10,8},{9,1... | collective-permute-start | bytes 602120 | tf_op jit(solution)/shard_map/ppermute | solution.py:493
  42.4 22.6 %collective-permute-start.6 = (bf16[2,112,1024]{2,1,0:T(8,128)(2,1)S(1)}, bf16[2,112,1024]{2,1,0:T(8,128)(2,1)S(1)}, u32[]{:S(2)}, u32[]{:S(2)}) collective-permute-start(bf16[2,112,1024]{2,1,0:T(8,128)(2,1)S(1)} %pad_maximum_fusion.4), channel_id=1, source_target_pairs={{0,16},{4,20},{8,24},{12,28},{16,0},{20,4},{24,8},{28,12},{1,17},{... | collective-permute-start | bytes 1376264 | tf_op jit(solution)/shard_map/ppermute | solution.py:481
  42.9 25.1 %collective-permute-start.7 = (bf16[2,112,1152]{2,1,0:T(8,128)(2,1)S(1)}, bf16[2,112,1152]{2,1,0:T(8,128)(2,1)S(1)}, u32[]{:S(2)}, u32[]{:S(2)}) collective-permute-start(bf16[2,112,1152]{2,1,0:T(8,128)(2,1)S(1)} %pad_maximum_fusion.3), channel_id=1, source_target_pairs={{0,8},{4,12},{8,0},{12,4},{16,24},{20,28},{24,16},{28,20},{1,9},{5... | collective-permute-start | bytes 1548296 | tf_op jit(solution)/shard_map/ppermute | solution.py:481
  43.4 24.7 %collective-permute-start.8 = (bf16[112,2048]{1,0:T(8,128)(2,1)S(1)}, bf16[112,2048]{1,0:T(8,128)(2,1)S(1)}, u32[]{:S(2)}, u32[]{:S(2)}) collective-permute-start(bf16[112,2048]{1,0:T(8,128)(2,1)S(1)} %slice.80), channel_id=1, source_target_pairs={{0,2},{2,0},{1,3},{3,1},{4,6},{6,4},{5,7},{7,5},{8,10},{10,8},{9,1... | collective-permute-start | bytes 1376264 | tf_op jit(solution)/shard_map/ppermute | solution.py:493
  43.5 24.7 %collective-permute-start.9 = (bf16[256,896]{1,0:T(8,128)(2,1)}, bf16[256,896]{1,0:T(8,128)(2,1)S(1)}, u32[]{:S(2)}, u32[]{:S(2)}) collective-permute-start(bf16[256,896]{1,0:T(8,128)(2,1)} %get-tuple-element.251.refs_4_), channel_id=1, source_target_pairs={{0,1},{1,0},{2,3},{3,2},{4,5},{5,4},{6,7},{7,6},{8,9},{9,8},{10,11... | collective-permute-start | bytes 1376264 | tf_op jit(solution)/shard_map/ppermute | solution.py:493
  68.2 10.4 %collective-permute-start.11 = (bf16[2,2,112,1152]{3,2,1,0:T(8,128)(2,1)S(1)}, bf16[2,2,112,1152]{3,2,1,0:T(8,128)(2,1)}, u32[]{:S(2)}, u32[]{:S(2)}) collective-permute-start(bf16[2,2,112,1152]{3,2,1,0:T(8,128)(2,1)S(1)} %pad_maximum_fusion), channel_id=1, source_target_pairs={{0,4},{4,0},{8,12},{12,8},{16,20},{20,16},{24,28},{28,24},{1,5},{5... | collective-permute-start | bytes 3096584 | tf_op jit(solution)/shard_map/ppermute | solution.py:481
  68.3 9.4 %collective-permute-start.10 = (bf16[2,2,112,1024]{3,2,1,0:T(8,128)(2,1)S(1)}, bf16[2,2,112,1024]{3,2,1,0:T(8,128)(2,1)S(1)}, u32[]{:S(2)}, u32[]{:S(2)}) collective-permute-start(bf16[2,2,112,1024]{3,2,1,0:T(8,128)(2,1)S(1)} %pad_maximum_fusion.1), channel_id=1, source_target_pairs={{0,4},{4,0},{8,12},{12,8},{16,20},{20,16},{24,28},{28,24},{1,5},{5... | collective-permute-start | bytes 2752520 | tf_op jit(solution)/shard_map/ppermute | solution.py:481
  68.8 8.9 %collective-permute-start.12 = (bf16[112,896]{1,0:T(8,128)(2,1)S(1)}, bf16[112,896]{1,0:T(8,128)(2,1)S(1)}, u32[]{:S(2)}, u32[]{:S(2)}) collective-permute-start(bf16[112,896]{1,0:T(8,128)(2,1)S(1)} %slice.81), channel_id=1, source_target_pairs={{0,2},{2,0},{1,3},{3,1},{4,6},{6,4},{5,7},{7,5},{8,10},{10,8},{9,1... | collective-permute-start | bytes 602120 | tf_op jit(solution)/shard_map/ppermute | solution.py:493
  79.7 183.4 %reduce-scatter.3.cloned.1.call-start = ((), (), s32[]{:S(2)}) async-start(), calls=%async_computation.4 | async-start | bytes 2867200 | tf_op jit(solution)/shard_map/reduce_scatter | solution.py:633
  88.1 14.0 %collective-permute-start.13 = (bf16[256,256]{1,0:T(8,128)(2,1)}, bf16[256,256]{1,0:T(8,128)(2,1)S(1)}, u32[]{:S(2)}, u32[]{:S(2)}) collective-permute-start(bf16[256,256]{1,0:T(8,128)(2,1)} %get-tuple-element.232.kv0_ref), channel_id=1, source_target_pairs={{0,1},{1,2},{2,3},{4,5},{5,6},{6,7},{8,9},{9,10},{10,11},{12,13},{... | collective-permute-start | bytes 393224 | tf_op jit(solution)/shard_map/ppermute | solution.py:585
  89.4 12.7 %collective-permute-start.14 = (bf16[256,256]{1,0:T(8,128)(2,1)}, bf16[256,256]{1,0:T(8,128)(2,1)S(1)}, u32[]{:S(2)}, u32[]{:S(2)}) collective-permute-start(bf16[256,256]{1,0:T(8,128)(2,1)} %get-tuple-element.232.kv0_ref), channel_id=1, source_target_pairs={{0,2},{1,3},{4,6},{5,7},{8,10},{9,11},{12,14},{13,15},{16,18},{17,... | collective-permute-start | bytes 393224 | tf_op jit(solution)/shard_map/ppermute | solution.py:585
  98.1 14.2 %collective-permute-start.15 = (bf16[256,256]{1,0:T(8,128)(2,1)S(1)}, bf16[256,256]{1,0:T(8,128)(2,1)S(1)}, u32[]{:S(2)}, u32[]{:S(2)}) collective-permute-start(bf16[256,256]{1,0:T(8,128)(2,1)S(1)} %copy-done.15), channel_id=1, source_target_pairs={{0,1},{1,2},{2,3},{4,5},{5,6},{6,7},{8,9},{9,10},{10,11},{12,13},{... | collective-permute-start | bytes 393224 | tf_op jit(solution)/shard_map/ppermute | solution.py:585
  99.4 13.0 %collective-permute-start.16 = (bf16[256,256]{1,0:T(8,128)(2,1)S(1)}, bf16[256,256]{1,0:T(8,128)(2,1)S(1)}, u32[]{:S(2)}, u32[]{:S(2)}) collective-permute-start(bf16[256,256]{1,0:T(8,128)(2,1)S(1)} %copy-done.15), channel_id=1, source_target_pairs={{0,2},{1,3},{4,6},{5,7},{8,10},{9,11},{12,14},{13,15},{16,18},{17,... | collective-permute-start | bytes 393224 | tf_op jit(solution)/shard_map/ppermute | solution.py:585
  112.4 10.0 %collective-permute-start.17 = (bf16[256,896]{1,0:T(8,128)(2,1)}, bf16[256,896]{1,0:T(8,128)(2,1)S(1)}, u32[]{:S(2)}, u32[]{:S(2)}) collective-permute-start(bf16[256,896]{1,0:T(8,128)(2,1)} %get-tuple-element.248.refs_0_), channel_id=1, source_target_pairs={{0,4},{4,0},{1,5},{5,1},{2,6},{6,2},{3,7},{7,3},{8,12},{12,8},{9,1... | collective-permute-start | bytes 1376264 | tf_op jit(solution)/shard_map/ppermute | solution.py:493
  112.5 13.1 %collective-permute-start.18 = (bf16[256,896]{1,0:T(8,128)(2,1)}, bf16[256,896]{1,0:T(8,128)(2,1)S(1)}, u32[]{:S(2)}, u32[]{:S(2)}) collective-permute-start(bf16[256,896]{1,0:T(8,128)(2,1)} %get-tuple-element.248.refs_0_), channel_id=1, source_target_pairs={{0,1},{1,0},{2,3},{3,2},{4,5},{5,4},{6,7},{7,6},{8,9},{9,8},{10,11... | collective-permute-start | bytes 1376264 | tf_op jit(solution)/shard_map/ppermute | solution.py:493
  112.6 13.1 %collective-permute-start.19 = (bf16[256,896]{1,0:T(8,128)(2,1)}, bf16[256,896]{1,0:T(8,128)(2,1)S(1)}, u32[]{:S(2)}, u32[]{:S(2)}) collective-permute-start(bf16[256,896]{1,0:T(8,128)(2,1)} %get-tuple-element.251.refs_4_), channel_id=1, source_target_pairs={{0,4},{4,0},{1,5},{5,1},{2,6},{6,2},{3,7},{7,3},{8,12},{12,8},{9,1... | collective-permute-start | bytes 1376264 | tf_op jit(solution)/shard_map/ppermute | solution.py:493
  113.1 12.6 %copy-start.25 = (bf16[256,896]{1,0:T(8,128)(2,1)S(1)}, bf16[256,896]{1,0:T(8,128)(2,1)}, u32[]{:S(2)}) copy-start(bf16[256,896]{1,0:T(8,128)(2,1)} %copy-done.24) | copy-start | bytes 1376260
  125.6 2.0 collective-permute-start.23
  125.7 3.2 collective-permute-start.24
  126.2 27.3 %collective-permute-start.25 = (bf16[256,896]{1,0:T(8,128)(2,1)S(1)}, bf16[256,896]{1,0:T(8,128)(2,1)S(1)}, u32[]{:S(2)}, u32[]{:S(2)}) collective-permute-start(bf16[256,896]{1,0:T(8,128)(2,1)S(1)} %get-tuple-element.262.refs_4_), channel_id=1, source_target_pairs={{0,4},{4,0},{1,5},{5,1},{2,6},{6,2},{3,7},{7,3},{8,12},{12,8},{9,1... | collective-permute-start | bytes 1376264 | tf_op jit(solution)/shard_map/ppermute | solution.py:493
  126.3 27.2 %collective-permute-start.26 = (bf16[256,896]{1,0:T(8,128)(2,1)S(1)}, bf16[256,896]{1,0:T(8,128)(2,1)S(1)}, u32[]{:S(2)}, u32[]{:S(2)}) collective-permute-start(bf16[256,896]{1,0:T(8,128)(2,1)S(1)} %get-tuple-element.262.refs_4_), channel_id=1, source_target_pairs={{0,1},{1,0},{2,3},{3,2},{4,5},{5,4},{6,7},{7,6},{8,9},{9,8},{10,11... | collective-permute-start | bytes 1376264 | tf_op jit(solution)/shard_map/ppermute | solution.py:493
  126.6 28.0 %collective-permute-start.20 = (bf16[256,896]{1,0:T(8,128)(2,1)}, bf16[256,896]{1,0:T(8,128)(2,1)S(1)}, u32[]{:S(2)}, u32[]{:S(2)}) collective-permute-start(bf16[256,896]{1,0:T(8,128)(2,1)} %get-tuple-element.247.refs_0_), channel_id=1, source_target_pairs={{0,4},{4,0},{1,5},{5,1},{2,6},{6,2},{3,7},{7,3},{8,12},{12,8},{9,1... | collective-permute-start | bytes 1376264 | tf_op jit(solution)/shard_map/ppermute | solution.py:493
  127.6 28.3 %collective-permute-start.21 = (bf16[256,896]{1,0:T(8,128)(2,1)}, bf16[256,896]{1,0:T(8,128)(2,1)S(1)}, u32[]{:S(2)}, u32[]{:S(2)}) collective-permute-start(bf16[256,896]{1,0:T(8,128)(2,1)} %get-tuple-element.247.refs_0_), channel_id=1, source_target_pairs={{0,1},{1,0},{2,3},{3,2},{4,5},{5,4},{6,7},{7,6},{8,9},{9,8},{10,11... | collective-permute-start | bytes 1376264 | tf_op jit(solution)/shard_map/ppermute | solution.py:493
  129.0 29.4 %collective-permute-start.22 = (bf16[256,896]{1,0:T(8,128)(2,1)}, bf16[256,896]{1,0:T(8,128)(2,1)S(1)}, u32[]{:S(2)}, u32[]{:S(2)}) collective-permute-start(bf16[256,896]{1,0:T(8,128)(2,1)} %get-tuple-element.247.refs_0_), channel_id=1, source_target_pairs={{0,5},{1,4},{4,1},{5,0},{2,7},{3,6},{6,3},{7,2},{8,13},{9,12},{12,... | collective-permute-start | bytes 1376264 | tf_op jit(solution)/shard_map/ppermute | solution.py:496
  153.6 4.8 %collective-permute-start.27 = (bf16[256,896]{1,0:T(8,128)(2,1)S(1)}, bf16[256,896]{1,0:T(8,128)(2,1)S(1)}, u32[]{:S(2)}, u32[]{:S(2)}) collective-permute-start(bf16[256,896]{1,0:T(8,128)(2,1)S(1)} %collective-permute-done.26.refs_6_), channel_id=1, source_target_pairs={{0,4},{4,0},{1,5},{5,1},{2,6},{6,2},{3,7},{7,3},{8,12},{12,8},{9,1... | collective-permute-start | bytes 1376264 | tf_op jit(solution)/shard_map/ppermute | solution.py:493
  154.5 30.6 %collective-permute-start.28 = (bf16[256,896]{1,0:T(8,128)(2,1)}, bf16[256,896]{1,0:T(8,128)(2,1)S(1)}, u32[]{:S(2)}, u32[]{:S(2)}) collective-permute-start(bf16[256,896]{1,0:T(8,128)(2,1)} %get-tuple-element.274), channel_id=1, source_target_pairs={{0,4},{4,0},{1,5},{5,1},{2,6},{6,2},{3,7},{7,3},{8,12},{12,8},{9,1... | collective-permute-start | bytes 1376264 | tf_op jit(solution)/shard_map/ppermute | solution.py:493
  154.6 30.5 %collective-permute-start.29 = (bf16[256,896]{1,0:T(8,128)(2,1)}, bf16[256,896]{1,0:T(8,128)(2,1)S(1)}, u32[]{:S(2)}, u32[]{:S(2)}) collective-permute-start(bf16[256,896]{1,0:T(8,128)(2,1)} %get-tuple-element.275), channel_id=1, source_target_pairs={{0,1},{1,0},{2,3},{3,2},{4,5},{5,4},{6,7},{7,6},{8,9},{9,8},{10,11... | collective-permute-start | bytes 1376264 | tf_op jit(solution)/shard_map/ppermute | solution.py:493
  155.9 29.2 %collective-permute-start.30 = (bf16[256,896]{1,0:T(8,128)(2,1)}, bf16[256,896]{1,0:T(8,128)(2,1)S(1)}, u32[]{:S(2)}, u32[]{:S(2)}) collective-permute-start(bf16[256,896]{1,0:T(8,128)(2,1)} %get-tuple-element.276), channel_id=1, source_target_pairs={{0,5},{1,4},{4,1},{5,0},{2,7},{3,6},{6,3},{7,2},{8,13},{9,12},{12,... | collective-permute-start | bytes 1376264 | tf_op jit(solution)/shard_map/ppermute | solution.py:496
  183.7 11.8 %collective-permute-start.31 = (bf16[256,896]{1,0:T(8,128)(2,1)}, bf16[256,896]{1,0:T(8,128)(2,1)S(1)}, u32[]{:S(2)}, u32[]{:S(2)}) collective-permute-start(bf16[256,896]{1,0:T(8,128)(2,1)} %get-tuple-element.278), channel_id=1, source_target_pairs={{0,4},{4,0},{1,5},{5,1},{2,6},{6,2},{3,7},{7,3},{8,12},{12,8},{9,1... | collective-permute-start | bytes 1376264 | tf_op jit(solution)/shard_map/ppermute | solution.py:493
  185.0 12.7 %collective-permute-start.32 = (bf16[256,896]{1,0:T(8,128)(2,1)}, bf16[256,896]{1,0:T(8,128)(2,1)S(1)}, u32[]{:S(2)}, u32[]{:S(2)}) collective-permute-start(bf16[256,896]{1,0:T(8,128)(2,1)} %get-tuple-element.279), channel_id=1, source_target_pairs={{0,1},{1,0},{2,3},{3,2},{4,5},{5,4},{6,7},{7,6},{8,9},{9,8},{10,11... | collective-permute-start | bytes 1376264 | tf_op jit(solution)/shard_map/ppermute | solution.py:493
  197.8 94.2 %reduce-scatter.5.cloned.1.call-start = ((), (), s32[]{:S(2)}) async-start(), calls=%async_computation.5 | async-start | bytes 5734400 | tf_op jit(solution)/shard_map/reduce_scatter | solution.py:634
  198.5 14.9 %collective-permute-start.34 = (bf16[2,256,896]{2,1,0:T(8,128)(2,1)S(1)}, bf16[2,256,896]{2,1,0:T(8,128)(2,1)S(1)}, u32[]{:S(2)}, u32[]{:S(2)}) collective-permute-start(bf16[2,256,896]{2,1,0:T(8,128)(2,1)S(1)} %copy-done.10), channel_id=1, source_target_pairs={{0,4},{4,0},{1,5},{5,1},{2,6},{6,2},{3,7},{7,3},{8,12},{12,8},{9,1... | collective-permute-start | bytes 2752520 | tf_op jit(solution)/shard_map/ppermute | solution.py:493
  198.5 14.9 %collective-permute-start.35 = (bf16[2,256,896]{2,1,0:T(8,128)(2,1)S(1)}, bf16[2,256,896]{2,1,0:T(8,128)(2,1)}, u32[]{:S(2)}, u32[]{:S(2)}) collective-permute-start(bf16[2,256,896]{2,1,0:T(8,128)(2,1)S(1)} %copy-done.11), channel_id=1, source_target_pairs={{0,4},{4,0},{1,5},{5,1},{2,6},{6,2},{3,7},{7,3},{8,12},{12,8},{9,1... | collective-permute-start | bytes 2752520 | tf_op jit(solution)/shard_map/ppermute | solution.py:493
  199.0 14.4 %collective-permute-start.33 = (bf16[256,896]{1,0:T(8,128)(2,1)}, bf16[256,896]{1,0:T(8,128)(2,1)S(1)}, u32[]{:S(2)}, u32[]{:S(2)}) collective-permute-start(bf16[256,896]{1,0:T(8,128)(2,1)} %get-tuple-element.288), channel_id=1, source_target_pairs={{0,5},{1,4},{4,1},{5,0},{2,7},{3,6},{6,3},{7,2},{8,13},{9,12},{12,... | collective-permute-start | bytes 1376264 | tf_op jit(solution)/shard_map/ppermute | solution.py:496
  216.0 14.6 %collective-permute-start.36 = (bf16[256,896]{1,0:T(8,128)(2,1)S(1)}, bf16[256,896]{1,0:T(8,128)(2,1)S(1)}, u32[]{:S(2)}, u32[]{:S(2)}) collective-permute-start(bf16[256,896]{1,0:T(8,128)(2,1)S(1)} %fusion.11), channel_id=1, source_target_pairs={{0,1},{1,0},{2,3},{3,2},{4,5},{5,4},{6,7},{7,6},{8,9},{9,8},{10,11... | collective-permute-start | bytes 1376264 | tf_op jit(solution)/shard_map/ppermute | solution.py:493
  231.7 16.9 %collective-permute-start.37 = (bf16[256,896]{1,0:T(8,128)(2,1)S(1)}, bf16[256,896]{1,0:T(8,128)(2,1)}, u32[]{:S(2)}, u32[]{:S(2)}) collective-permute-start(bf16[256,896]{1,0:T(8,128)(2,1)S(1)} %fusion.12), channel_id=1, source_target_pairs={{0,1},{1,0},{2,3},{3,2},{4,5},{5,4},{6,7},{7,6},{8,9},{9,8},{10,11... | collective-permute-start | bytes 1376264 | tf_op jit(solution)/shard_map/ppermute | solution.py:493
  232.5 18.7 %collective-permute-start.38 = (bf16[256,256]{1,0:T(8,128)(2,1)}, bf16[256,256]{1,0:T(8,128)(2,1)S(1)}, u32[]{:S(2)}, u32[]{:S(2)}) collective-permute-start(bf16[256,256]{1,0:T(8,128)(2,1)} %get-tuple-element.339), channel_id=1, source_target_pairs={{1,0},{2,1},{3,2},{5,4},{6,5},{7,6},{9,8},{10,9},{11,10},{13,12},{... | collective-permute-start | bytes 393224 | tf_op jit(solution)/shard_map/ppermute | solution.py:649
  233.8 17.4 %collective-permute-start.39 = (bf16[256,256]{1,0:T(8,128)(2,1)}, bf16[256,256]{1,0:T(8,128)(2,1)S(1)}, u32[]{:S(2)}, u32[]{:S(2)}) collective-permute-start(bf16[256,256]{1,0:T(8,128)(2,1)} %get-tuple-element.340), channel_id=1, source_target_pairs={{2,0},{3,1},{6,4},{7,5},{10,8},{11,9},{14,12},{15,13},{18,16},{19,... | collective-permute-start | bytes 393224 | tf_op jit(solution)/shard_map/ppermute | solution.py:649
  248.6 8.3 %collective-permute-start.40 = (bf16[256,256]{1,0:T(8,128)(2,1)}, bf16[256,256]{1,0:T(8,128)(2,1)S(1)}, u32[]{:S(2)}, u32[]{:S(2)}) collective-permute-start(bf16[256,256]{1,0:T(8,128)(2,1)} %get-tuple-element.341), channel_id=1, source_target_pairs={{1,0},{2,1},{3,2},{5,4},{6,5},{7,6},{9,8},{10,9},{11,10},{13,12},{... | collective-permute-start | bytes 393224 | tf_op jit(solution)/shard_map/ppermute | solution.py:649
  249.9 13.1 %collective-permute-start.41 = (bf16[256,256]{1,0:T(8,128)(2,1)}, bf16[256,256]{1,0:T(8,128)(2,1)S(1)}, u32[]{:S(2)}, u32[]{:S(2)}) collective-permute-start(bf16[256,256]{1,0:T(8,128)(2,1)} %get-tuple-element.342), channel_id=1, source_target_pairs={{2,0},{3,1},{6,4},{7,5},{10,8},{11,9},{14,12},{15,13},{18,16},{19,... | collective-permute-start | bytes 393224 | tf_op jit(solution)/shard_map/ppermute | solution.py:649
  251.2 17.3 %copy-start.35 = (bf16[256,256]{1,0:T(8,128)(2,1)}, bf16[256,256]{1,0:T(8,128)(2,1)S(1)}, u32[]{:S(2)}) copy-start(bf16[256,256]{1,0:T(8,128)(2,1)S(1)} %collective-permute-done.38.refs_0_) | copy-start | bytes 393220
  251.3 17.3 %copy-start.36 = (bf16[256,256]{1,0:T(8,128)(2,1)}, bf16[256,256]{1,0:T(8,128)(2,1)S(1)}, u32[]{:S(2)}) copy-start(bf16[256,256]{1,0:T(8,128)(2,1)S(1)} %collective-permute-done.39.refs_1_) | copy-start | bytes 393220
  256.9 11.6 %copy-start.37 = (bf16[256,256]{1,0:T(8,128)(2,1)}, bf16[256,256]{1,0:T(8,128)(2,1)S(1)}, u32[]{:S(2)}) copy-start(bf16[256,256]{1,0:T(8,128)(2,1)S(1)} %collective-permute-done.40.refs_2_) | copy-start | bytes 393220
  265.0 15.2 %collective-permute-start.42 = (bf16[112,1280]{1,0:T(8,128)(2,1)}, bf16[112,1280]{1,0:T(8,128)(2,1)S(1)}, u32[]{:S(2)}, u32[]{:S(2)}) collective-permute-start(bf16[112,1280]{1,0:T(8,128)(2,1)} %get-tuple-element.444), channel_id=1, source_target_pairs={{0,0},{2,4},{4,6},{6,2},{1,1},{3,5},{5,7},{7,3},{8,8},{10,12},{12,... | collective-permute-start | bytes 860168 | tf_op jit(solution)/shard_map/ppermute | solution.py:659
  266.6 14.1 %collective-permute-start.43 = (bf16[112,1280]{1,0:T(8,128)(2,1)}, bf16[112,1280]{1,0:T(8,128)(2,1)}, u32[]{:S(2)}, u32[]{:S(2)}) collective-permute-start(bf16[112,1280]{1,0:T(8,128)(2,1)} %get-tuple-element.443), channel_id=1, source_target_pairs={{0,4},{2,0},{4,2},{6,6},{1,5},{3,1},{5,3},{7,7},{8,12},{10,8},{12,... | collective-permute-start | bytes 860168 | tf_op jit(solution)/shard_map/ppermute | solution.py:659
  268.6 12.1 %copy-start = (f32[2,256,896]{2,1,0:T(8,128)S(1)}, f32[2,256,896]{2,1,0:T(8,128)}, u32[]{:S(2)}) copy-start(f32[2,256,896]{2,1,0:T(8,128)} %get-tuple-element.242.middle_ref) | copy-start | bytes 5505028
  280.7 4.3 %collective-permute-start.44 = (bf16[448,2176]{1,0:T(8,128)(2,1)}, bf16[448,2176]{1,0:T(8,128)(2,1)}, u32[]{:S(2)}, u32[]{:S(2)}) collective-permute-start(bf16[448,2176]{1,0:T(8,128)(2,1)} %get-tuple-element.353), channel_id=1, source_target_pairs={{0,4},{4,0},{8,12},{12,8},{16,20},{20,16},{24,28},{28,24},{1,5},{5... | collective-permute-start | bytes 5849096 | tf_op jit(solution)/shard_map/ppermute | solution.py:481
  289.4 12.8 %collective-permute-start.46 = (bf16[1,2,112,1024]{3,2,1,0:T(8,128)(2,1)}, bf16[1,2,112,1024]{3,2,1,0:T(8,128)(2,1)}, u32[]{:S(2)}, u32[]{:S(2)}) collective-permute-start(bf16[1,2,112,1024]{3,2,1,0:T(8,128)(2,1)} %fusion.13), channel_id=1, source_target_pairs={{0,16},{4,20},{8,24},{12,28},{16,0},{20,4},{24,8},{28,12},{1,17},{... | collective-permute-start | bytes 1376264 | tf_op jit(solution)/shard_map/ppermute | solution.py:481
  290.6 13.6 %collective-permute-start.45 = (bf16[2,1,112,1152]{3,2,0,1:T(8,128)(2,1)S(1)}, bf16[2,1,112,1152]{3,2,0,1:T(8,128)(2,1)}, u32[]{:S(2)}, u32[]{:S(2)}) collective-permute-start(bf16[2,1,112,1152]{3,2,0,1:T(8,128)(2,1)S(1)} %fusion.9), channel_id=1, source_target_pairs={{0,8},{4,12},{8,0},{12,4},{16,24},{20,28},{24,16},{28,20},{1,9},{5... | collective-permute-start | bytes 1548296 | tf_op jit(solution)/shard_map/ppermute | solution.py:481
  293.1 12.2 %collective-permute-start.47 = (bf16[112,2560]{1,0:T(8,128)(2,1)S(1)}, bf16[112,2560]{1,0:T(8,128)(2,1)S(1)}, u32[]{:S(2)}, u32[]{:S(2)}) collective-permute-start(bf16[112,2560]{1,0:T(8,128)(2,1)S(1)} %dynamic-slice_bitcast_fusion.1), channel_id=1, source_target_pairs={{0,0},{2,4},{4,6},{6,2},{1,1},{3,5},{5,7},{7,3},{8,8},{10,12},{12,... | collective-permute-start | bytes 1720328 | tf_op jit(solution)/shard_map/ppermute | solution.py:659
  305.4 9.0 %collective-permute-start.48 = (bf16[1,1,112,1152]{3,2,1,0:T(8,128)(2,1)S(1)}, bf16[1,1,112,1152]{3,2,1,0:T(8,128)(2,1)S(1)}, u32[]{:S(2)}, u32[]{:S(2)}) collective-permute-start(bf16[1,1,112,1152]{3,2,1,0:T(8,128)(2,1)S(1)} %fusion.19), channel_id=1, source_target_pairs={{0,16},{4,20},{8,24},{12,28},{16,0},{20,4},{24,8},{28,12},{1,17},{... | collective-permute-start | bytes 774152 | tf_op jit(solution)/shard_map/ppermute | solution.py:481
  306.4 7.8 %collective-permute-start.49 = (bf16[1,1,112,1024]{3,2,1,0:T(8,128)(2,1)S(1)}, bf16[1,1,112,1024]{3,2,1,0:T(8,128)(2,1)S(1)}, u32[]{:S(2)}, u32[]{:S(2)}) collective-permute-start(bf16[1,1,112,1024]{3,2,1,0:T(8,128)(2,1)S(1)} %fusion.20), channel_id=1, source_target_pairs={{0,8},{4,12},{8,0},{12,4},{16,24},{20,28},{24,16},{28,20},{1,9},{5... | collective-permute-start | bytes 688136 | tf_op jit(solution)/shard_map/ppermute | solution.py:481
  307.8 28.9 %collective-permute-start.53 = (bf16[112,2560]{1,0:T(8,128)(2,1)S(1)}, bf16[112,2560]{1,0:T(8,128)(2,1)S(1)}, u32[]{:S(2)}, u32[]{:S(2)}) collective-permute-start(bf16[112,2560]{1,0:T(8,128)(2,1)S(1)} %dynamic-slice_bitcast_fusion), channel_id=1, source_target_pairs={{0,4},{2,0},{4,2},{6,6},{1,5},{3,1},{5,3},{7,7},{8,12},{10,8},{12,... | collective-permute-start | bytes 1720328 | tf_op jit(solution)/shard_map/ppermute | solution.py:659
  314.7 8.4 %collective-permute-start.50 = (bf16[28,2176]{1,0:T(8,128)(2,1)S(1)}, bf16[28,2176]{1,0:T(8,128)(2,1)S(1)}, u32[]{:S(2)}, u32[]{:S(2)}) collective-permute-start(bf16[28,2176]{1,0:T(8,128)(2,1)S(1)} %get-tuple-element.447), channel_id=1, source_target_pairs={{0,1},{1,2},{2,3},{3,0},{4,5},{5,6},{6,7},{7,4},{8,9},{9,10},{10,1... | collective-permute-start | bytes 365576 | tf_op jit(solution)/shard_map/ppermute | solution.py:490
  314.7 21.9 %collective-permute-start.51 = (bf16[28,2176]{1,0:T(8,128)(2,1)S(1)}, bf16[28,2176]{1,0:T(8,128)(2,1)S(1)}, u32[]{:S(2)}, u32[]{:S(2)}) collective-permute-start(bf16[28,2176]{1,0:T(8,128)(2,1)S(1)} %get-tuple-element.446), channel_id=1, source_target_pairs={{0,2},{1,3},{2,0},{3,1},{4,6},{5,7},{6,4},{7,5},{8,10},{9,11},{10,... | collective-permute-start | bytes 365576 | tf_op jit(solution)/shard_map/ppermute | solution.py:490
  318.4 18.3 %collective-permute-start.52 = (bf16[28,2176]{1,0:T(8,128)(2,1)S(1)}, bf16[28,2176]{1,0:T(8,128)(2,1)S(1)}, u32[]{:S(2)}, u32[]{:S(2)}) collective-permute-start(bf16[28,2176]{1,0:T(8,128)(2,1)S(1)} %get-tuple-element.445), channel_id=1, source_target_pairs={{0,3},{1,0},{2,1},{3,2},{4,7},{5,4},{6,5},{7,6},{8,11},{9,8},{10,9... | collective-permute-start | bytes 365576 | tf_op jit(solution)/shard_map/ppermute | solution.py:490
  (43 other events, 134.1 us)
Sparse Core Ops, SparseCore 0:
  10.0 65.7 all-gather.2
  79.8 46.7 all-gather.4
  197.9 34.6 reduce-scatter.2
  235.5 55.9 reduce-scatter.4

commit v8 on v7

--- a/solution.py
+++ b/solution.py
@@ -628,7 +628,7 @@
     left, pair, act = after(before[4:], backs[0])
     feed_down = weights(left, 1, act, 256)
     backs[-1][1:3], left, pair, feed_down = after((backs[-1][1:3], left, pair, feed_down))
-    feed_pair = weights(left, 0, pair, 512)
+    feed_pair = weights(left, 0, pair, 256)
     backs, feed_pair, out_near, out_far = after((backs, feed_pair, out_near, out_far))
     feed_down = lax.psum_scatter(feed_down, "grp", scatter_dimension=0, tiled=True)
     feed_pair = lax.psum_scatter(feed_pair, "grp", scatter_dimension=0, tiled=True)
@@ -652,16 +652,22 @@
         )
         if m < micros - 1:
             out_far, ended = after((out_far, ended))
-    def delivered(half, k):
-        part = lax.dynamic_index_in_dim(
+    def portion(half, k):
+        return lax.dynamic_index_in_dim(
             half.reshape((2, -1) + half.shape[1:]), (core + far_half + k) % 2, 0, keepdims=False
         )
+
+    def handed(part, k):
         return lax.ppermute(
             part, ("core", "zh"), [(2 * s + a, 2 * (s ^ a ^ k) + s) for s in range(2) for a in range(2)]
         )
 
-    far, feed_down = after((far, feed_down))
-    down_parts = [delivered(feed_down, k) for k in range(2)]
+    def delivered(half, k):
+        return handed(portion(half, k), k)
+
+    down_parts = [portion(feed_down, k) for k in range(2)]
+    far, down_parts = after((far, down_parts))
+    down_parts = [handed(part, k) for k, part in enumerate(down_parts)]
     grad_middle, branch_low, query_grad, own_pair, gain_sum = ended
     input_grad, keep, send = finish(
         (group_rank % 2).reshape(1), query_grad, own_pair, far, cosines, sines, in_set,

time: 354 us -> 354 us (level)
    unnamed x112 -> x110, local copies, waits for them, and re-layouts: 7.37 us -> 7.2 us
where the time goes in v8:
time: 354 us; the launch traced here: 347 us
  Pallas kernels  144 us (41%)
  waiting for transfers between devices  89 us (25%)
  starting transfers between devices  62.6 us (18%)
  other arithmetic  19.4 us (5%)
  local copies, waits for them, and re-layouts  17.3 us (5%)
  between operations  15.3 us (4%)
    pallas_call x2, Pallas kernels, feed(): pl.pallas_call(functools.partial(feed_kernel, parts=parts, micro=micro, k...  48.5 us
    ppermute x11, waiting for transfers between devices, swapped(): return lax.ppermute(values_in, dp, [(s, s ^ bit) for s in range(groups)])  36.7 us
    pallas_call x2, Pallas kernels, attend_back(): pl.pallas_call(functools.partial(attend_back_kernel, count=len(gs)), grid...  26.7 us
    pallas_call x2, Pallas kernels, weights(): pl.pallas_call(weights_kernel, grid=(width // chunk,), in_specs=[pl.Block...  25.2 us
    ppermute x6, waiting for transfers between devices, around(): lax.ppermute(values_in, ctx, [(s, (s + steps) % parts) for s in range(par...  20.5 us
    ppermute x22, waiting for transfers between devices, other(): return lax.ppermute(values_in, axis, [(0, 1), (1, 0)])  19.4 us
    pallas_call x2, Pallas kernels, attend(): pl.pallas_call(attend_kernel, grid=(nq,), in_specs=[pl.BlockSpec(memory_s...  18.8 us
    ppermute x22, starting transfers between devices, other(): return lax.ppermute(values_in, axis, [(0, 1), (1, 0)])  13.9 us
  transfers between devices with their start and end apart: 58, of which 19 were waited for; matrix products, arithmetic and copies ran while one was open for 7% of the time, Pallas kernels for 41%

profile of v8, /device:TPU:0, one launch (start us, length us, event | category | flops | bytes accessed | tf_op | source)
XLA Modules:
  0.0 347.3 jit_solution(3416112750226122084)
XLA Ops:
  7.3 2.2 fusion.8
  9.9 5.1 %collective-permute-start = (bf16[28,2176]{1,0:T(8,128)(2,1)S(1)}, bf16[28,2176]{1,0:T(8,128)(2,1)S(1)}, u32[]{:S(2)}, u32[]{:S(2)}) collective-permute-start(bf16[28,2176]{1,0:T(8,128)(2,1)S(1)} %constant_dynamic-update-slice_fusion), channel_id=1, source_target_pairs={{0,3},{1,0},{2,1},{3,2},{4,7},{5,4},{6,5},{7,6},{8,11},{9,8},{10,9... | collective-permute-start | bytes 365576 | tf_op jit(solution)/shard_map/ppermute | solution.py:490
  18.4 1.3 pad_maximum_fusion.5
  19.6 7.2 %collective-permute-done.1 = bf16[28,2176]{1,0:T(8,128)(2,1)S(1)} collective-permute-done((bf16[28,2176]{1,0:T(8,128)(2,1)S(1)}, bf16[28,2176]{1,0:T(8,128)(2,1)S(1)}, u32[]{:S(2)}, u32[]{:S(2)}) %collective-permute-start.1) | collective-permute-done | bytes 121888 | tf_op jit(solution)/shard_map/ppermute | solution.py:490
  27.2 1.6 collective-permute-start.3
  29.7 1.6 collective-permute-start.4
  31.3 2.8 collective-permute-start.5
  34.1 3.1 collective-permute-done.3
  38.4 3.9 %collective-permute-done.5 = bf16[112,896]{1,0:T(8,128)(2,1)S(1)} collective-permute-done((bf16[112,896]{1,0:T(8,128)(2,1)S(1)}, bf16[112,896]{1,0:T(8,128)(2,1)S(1)}, u32[]{:S(2)}, u32[]{:S(2)}) %collective-permute-start.5) | collective-permute-done | bytes 200736 | tf_op jit(solution)/shard_map/ppermute | solution.py:493
  43.5 1.9 collective-permute-start.9
  45.4 19.5 %collective-permute-done.6 = bf16[2,112,1024]{2,1,0:T(8,128)(2,1)S(1)} collective-permute-done((bf16[2,112,1024]{2,1,0:T(8,128)(2,1)S(1)}, bf16[2,112,1024]{2,1,0:T(8,128)(2,1)S(1)}, u32[]{:S(2)}, u32[]{:S(2)}) %collective-permute-start.6) | collective-permute-done | bytes 458784 | tf_op jit(solution)/shard_map/ppermute | solution.py:481
  65.1 2.8 collective-permute-done.7
  68.8 8.8 %collective-permute-done.12 = bf16[112,896]{1,0:T(8,128)(2,1)S(1)} collective-permute-done((bf16[112,896]{1,0:T(8,128)(2,1)S(1)}, bf16[112,896]{1,0:T(8,128)(2,1)S(1)}, u32[]{:S(2)}, u32[]{:S(2)}) %collective-permute-start.12) | collective-permute-done | bytes 200736 | tf_op jit(solution)/shard_map/ppermute | solution.py:493
  79.7 4.7 %woven.1 = (bf16[896,1024]{1,0:T(8,128)(2,1)}, bf16[896,1152]{1,0:T(8,128)(2,1)}) custom-call(s32[1]{0:T(128)} %bitcast.2.core_ref, bf16[4,112,1024]{2,1,0:T(8,128)(2,1)} %bitcast.138, bf16[4,112,1152]{2,1,0:T(8,128)(2,1)} %bitcast.137, bf16[4,112,1024]{2,1,0:T(8,128)(2,1)} %bitcast.141, bf16[4,112,1152]{2,1,0:T(8,128)(2,1)} %bitcast.26.refs_3_), custom_call_target="tpu_custom_call" | custom-call | flops 1 | bytes 1 | tf_op jit(solution)/shard_map/woven/pallas_call | solution.py:425
  84.4 3.7 %pairs.1 = (bf16[2,256,896]{2,1,0:T(8,128)(2,1)}, f32[8,896]{1,0:T(8,128)}, bf16[256,256]{1,0:T(8,128)(2,1)}, bf16[256,256]{1,0:T(8,128)(2,1)}) custom-call(bf16[2,256,896]{2,1,0:T(8,128)(2,1)} %bitcast.127, bf16[896,1152]{1,0:T(8,128)(2,1)} %get-tuple-element.221.wkv_ref.wq_ref, bf16[896,1024]{1,0:T(8,128)(2,1)} %get-tuple-element.222.ws_ref.wo_ref, ...), custom_call_target="tpu_custom_call" | custom-call | flops 1 | bytes 1 | tf_op jit(solution)/shard_map/pairs/pallas_call | solution.py:60
  88.1 1.3 collective-permute-start.13
  89.4 4.2 %collective-permute-start.14 = (bf16[256,256]{1,0:T(8,128)(2,1)}, bf16[256,256]{1,0:T(8,128)(2,1)S(1)}, u32[]{:S(2)}, u32[]{:S(2)}) collective-permute-start(bf16[256,256]{1,0:T(8,128)(2,1)} %get-tuple-element.233.kv0_ref), channel_id=1, source_target_pairs={{0,2},{1,3},{4,6},{5,7},{8,10},{9,11},{12,14},{13,15},{16,18},{17,... | collective-permute-start | bytes 393224 | tf_op jit(solution)/shard_map/ppermute | solution.py:585
  93.6 4.5 %queries.1.rq_ref = bf16[2,256,896]{2,1,0:T(8,128)(2,1)} custom-call(bf16[2,256,896]{2,1,0:T(8,128)(2,1)} %get-tuple-element.226.n1_ref, bf16[896,1152]{1,0:T(8,128)(2,1)} %get-tuple-element.221.wkv_ref.wq_ref, f32[8,896]{1,0:T(8,128)} %get-tuple-element.227.rows_ref, f32[2,256,128]{2,1,0:T(8,128)} %get-tuple-element.224.cos_ref, ...), custom_call_target="tpu_custom_call" | custom-call | flops 1 | bytes 1 | tf_op jit(solution)/shard_map/queries/pallas_call | solution.py:68
  98.1 1.3 collective-permute-start.15
  99.4 2.1 collective-permute-start.16
  102.8 9.5 %attend.2 = (bf16[256,896]{1,0:T(8,128)(2,1)}, bf16[2,256,896]{2,1,0:T(8,128)(2,1)}, f32[2,256,896]{2,1,0:T(8,128)}, f32[2,2,16,128]{3,2,1,0:T(8,128)}) custom-call(s32[1]{0:T(128)} %bitcast.base_ref, bf16[2,256,896]{2,1,0:T(8,128)(2,1)} %queries.1.rq_ref, bf16[256,256]{1,0:T(8,128)(2,1)} %get-tuple-element.233.kv0_ref, bf16[256,256]{1,0:T(8,128)(2,1)} %copy-done.13, ...), custom_call_target="tpu_custom_call" | custom-call | flops 1 | bytes 1 | tf_op jit(solution)/shard_map/attend/pallas_call | solution.py:147
  113.1 9.3 %attend.3 = (bf16[256,896]{1,0:T(8,128)(2,1)}, bf16[2,256,896]{2,1,0:T(8,128)(2,1)}, f32[2,256,896]{2,1,0:T(8,128)}, f32[2,2,16,128]{3,2,1,0:T(8,128)}) custom-call(s32[1]{0:T(128)} %bitcast.base_ref, bf16[2,256,896]{2,1,0:T(8,128)(2,1)} %queries.1.rq_ref, ...), custom_call_target="tpu_custom_call", output_to_operand_aliasing={{1}: (9, {}), {2}: (10, {}), {3}: (11, {})} | custom-call | flops 1 | bytes 1 | tf_op jit(solution)/shard_map/attend/pallas_call | solution.py:147
  122.4 3.2 collective-permute-done.18.refs_2_
  127.6 1.1 collective-permute-start.21
  129.4 24.1 %feed.2 = (f32[256,896]{1,0:T(8,128)}, bf16[256,896]{1,0:T(8,128)(2,1)}, bf16[256,896]{1,0:T(8,128)(2,1)}, bf16[256,896]{1,0:T(8,128)(2,1)}, f32[2,256,896]{2,1,...) custom-call(s32[1]{0:T(128)} %bitcast.27.own_ref, ...), custom_call_target="tpu_custom_call" | custom-call | flops 1 | bytes 1 | tf_op jit(solution)/shard_map/feed/pallas_call | solution.py:315
  154.6 1.3 collective-permute-start.29
  156.4 1.9 collective-permute-done.22.refs_3_
  159.3 24.4 %feed.3 = (f32[256,896]{1,0:T(8,128)}, bf16[256,896]{1,0:T(8,128)(2,1)}, bf16[256,896]{1,0:T(8,128)(2,1)}, bf16[256,896]{1,0:T(8,128)(2,1)}, f32[2,256,896]{2,1,...) custom-call(s32[1]{0:T(128)} %bitcast.27.own_ref, ...), custom_call_target="tpu_custom_call", output_to_operand_aliasing={{4}: (11, {}), {5}: (12, {}), {6}: (13, {}), {7}: (14, {}),... | custom-call | flops 1 | bytes 1 | tf_op jit(solution)/shard_map/feed/pallas_call | solution.py:315
  183.7 1.3 collective-permute-start.31
  186.1 9.4 %weights.2 = bf16[896,1280]{1,0:T(8,128)(2,1)} custom-call(bf16[2,8,896,256]{3,2,1,0:T(8,128)(2,1)} %get-tuple-element.290.left_ref, bf16[2048,1280]{1,0:T(8,128)(2,1)} %get-tuple-element.286.right_ref), custom_call_target="tpu_custom_call" | custom-call | flops 1 | bytes 1 | tf_op jit(solution)/shard_map/weights/pallas_call | solution.py:401
  195.5 2.2 collective-permute-done.32.refs_2_
  199.4 15.8 %weights.3 = bf16[896,2560]{1,0:T(8,128)(2,1)} custom-call(bf16[2,8,896,256]{3,2,1,0:T(8,128)(2,1)} %get-tuple-element.290.left_ref, bf16[2048,2560]{1,0:T(8,128)(2,1)} %get-tuple-element.291.right_ref), custom_call_target="tpu_custom_call" | custom-call | flops 1 | bytes 1 | tf_op jit(solution)/shard_map/weights/pallas_call | solution.py:401
  215.3 1.1 copy-done.6
  216.5 1.1 fusion.11
  217.6 1.4 collective-permute-start.36
  219.0 13.2 %attend_back.2 = (bf16[256,256]{1,0:T(8,128)(2,1)}, bf16[256,256]{1,0:T(8,128)(2,1)}, f32[2,256,896]{2,1,0:T(8,128)}, bf16[2,256,896]{2,1,0:T(8,128)(2,1)}, bf16...) custom-call(s32[1]{0:T(128)} %bitcast.base_ref, bf16[2,256,896]{2,1,0:T(8,128)(2,1)} %queries.1.rq_ref, ...), custom_call_target="tpu_custom_call" | custom-call | flops 1 | bytes 1 | tf_op jit(solution)/shard_map/attend_back/pallas_call | solution.py:228
  232.2 1.1 fusion.12
  234.1 1.3 collective-permute-start.38
  235.4 1.3 collective-permute-start.39
  236.7 13.5 %attend_back.3 = (bf16[256,256]{1,0:T(8,128)(2,1)}, bf16[256,256]{1,0:T(8,128)(2,1)}, f32[2,256,896]{2,1,0:T(8,128)}, bf16[2,256,896]{2,1,0:T(8,128)(2,1)}, bf16...) custom-call(s32[1]{0:T(128)} %bitcast.base_ref, ...), custom_call_target="tpu_custom_call", output_to_operand_aliasing={{2}: (17, {}), {3}: (18, {}), {4}: (19, {}), {5}: (20, {}),... | custom-call | flops 1 | bytes 1 | tf_op jit(solution)/shard_map/attend_back/pallas_call | solution.py:228
  250.2 1.3 collective-permute-start.40
  251.5 1.3 collective-permute-start.41
  252.8 1.9 dynamic-slice_bitcast_fusion.2
  254.7 3.7 %collective-permute-done.40.refs_2_ = bf16[256,256]{1,0:T(8,128)(2,1)S(1)} collective-permute-done((bf16[256,256]{1,0:T(8,128)(2,1)}, bf16[256,256]{1,0:T(8,128)(2,1)S(1)}, u32[]{:S(2)}, u32[]{:S(2)}) %collective-permute-start.40) | collective-permute-done | bytes 131104 | tf_op jit(solution)/shard_map/ppermute | solution.py:649
  258.5 6.2 %collective-permute-done.41.refs_3_ = bf16[256,256]{1,0:T(8,128)(2,1)S(1)} collective-permute-done((bf16[256,256]{1,0:T(8,128)(2,1)}, bf16[256,256]{1,0:T(8,128)(2,1)S(1)}, u32[]{:S(2)}, u32[]{:S(2)}) %collective-permute-start.41) | collective-permute-done | bytes 131104 | tf_op jit(solution)/shard_map/ppermute | solution.py:649
  264.7 1.6 collective-permute-start.42
  266.3 1.9 collective-permute-start.43
  268.2 11.6 %finish.1 = (f32[2,256,896]{2,1,0:T(8,128)}, bf16[448,2176]{1,0:T(8,128)(2,1)}, bf16[448,2176]{1,0:T(8,128)(2,1)}) custom-call(s32[1]{0:T(128)} %bitcast.35.bit_ref, bf16[2,256,896]{2,1,0:T(8,128)(2,1)} %get-tuple-element.334.dq_ref, f32[2,256,256]{2,1,0:T(8,128)} %get-tuple-element.335.own_ref, f32[2,256,128]{2,1,0:T(8,128)} %get-tuple-element.224.cos_ref, ...), custom_call_target="tpu_custom_call" | custom-call | flops 1 | bytes 1 | tf_op jit(solution)/shard_map/finish/pallas_call | solution.py:385
  280.4 3.0 fusion.5
  283.3 1.3 collective-permute-done.44
  284.6 2.0 convert_add_fusion
  287.0 1.2 copy-done.3
  289.1 1.1 collective-permute-start.46
  290.2 1.4 collective-permute-start.45
  291.7 1.1 dynamic-slice_bitcast_fusion.1
  293.5 8.4 %collective-permute-done.46 = bf16[1,2,112,1024]{3,2,1,0:T(8,128)(2,1)} collective-permute-done((bf16[1,2,112,1024]{3,2,1,0:T(8,128)(2,1)}, bf16[1,2,112,1024]{3,2,1,0:T(8,128)(2,1)}, u32[]{:S(2)}, u32[]{:S(2)}) %collective-permute-start.46) | collective-permute-done | bytes 458784 | tf_op jit(solution)/shard_map/ppermute | solution.py:481
  301.9 1.5 fusion.6
  303.9 1.1 fusion.4
  306.1 1.2 collective-permute-start.49
  307.4 6.8 %collective-permute-start.53 = (bf16[112,2560]{1,0:T(8,128)(2,1)S(1)}, bf16[112,2560]{1,0:T(8,128)(2,1)S(1)}, u32[]{:S(2)}, u32[]{:S(2)}) collective-permute-start(bf16[112,2560]{1,0:T(8,128)(2,1)S(1)} %dynamic-slice_bitcast_fusion), channel_id=1, source_target_pairs={{0,4},{2,0},{4,2},{6,6},{1,5},{3,1},{5,3},{7,7},{8,12},{10,8},{12,... | collective-permute-start | bytes 1720328 | tf_op jit(solution)/shard_map/ppermute | solution.py:661
  314.7 3.6 %collective-permute-start.51 = (bf16[28,2176]{1,0:T(8,128)(2,1)S(1)}, bf16[28,2176]{1,0:T(8,128)(2,1)S(1)}, u32[]{:S(2)}, u32[]{:S(2)}) collective-permute-start(bf16[28,2176]{1,0:T(8,128)(2,1)S(1)} %get-tuple-element.448), channel_id=1, source_target_pairs={{0,2},{1,3},{2,0},{3,1},{4,6},{5,7},{6,4},{7,5},{8,10},{9,11},{10,... | collective-permute-start | bytes 365576 | tf_op jit(solution)/shard_map/ppermute | solution.py:490
  318.3 2.8 collective-permute-start.52
  321.2 1.8 add_bitcast_fusion
  323.0 13.3 %collective-permute-done.51 = bf16[28,2176]{1,0:T(8,128)(2,1)S(1)} collective-permute-done((bf16[28,2176]{1,0:T(8,128)(2,1)S(1)}, bf16[28,2176]{1,0:T(8,128)(2,1)S(1)}, u32[]{:S(2)}, u32[]{:S(2)}) %collective-permute-start.51) | collective-permute-done | bytes 121888 | tf_op jit(solution)/shard_map/ppermute | solution.py:490
  (240 shorter events, 29.7 us)
Async XLA Ops:
  7.3 122.1 %all-gather.3.cloned.1.call-start = ((), (), s32[]{:S(2)}) async-start(), calls=%async_computation.2 | async-start | bytes 7741440 | tf_op jit(solution)/shard_map/all_gather | solution.py:516
  9.5 119.8 %all-gather.5.cloned.1.call-start = ((), (), s32[]{:S(2)}) async-start(), calls=%async_computation.3 | async-start | bytes 7741440 | tf_op jit(solution)/shard_map/all_gather | solution.py:565
  9.9 9.7 %collective-permute-start = (bf16[28,2176]{1,0:T(8,128)(2,1)S(1)}, bf16[28,2176]{1,0:T(8,128)(2,1)S(1)}, u32[]{:S(2)}, u32[]{:S(2)}) collective-permute-start(bf16[28,2176]{1,0:T(8,128)(2,1)S(1)} %constant_dynamic-update-slice_fusion), channel_id=1, source_target_pairs={{0,3},{1,0},{2,1},{3,2},{4,7},{5,4},{6,5},{7,6},{8,11},{9,8},{10,9... | collective-permute-start | bytes 365576 | tf_op jit(solution)/shard_map/ppermute | solution.py:490
  15.0 11.8 %collective-permute-start.1 = (bf16[28,2176]{1,0:T(8,128)(2,1)S(1)}, bf16[28,2176]{1,0:T(8,128)(2,1)S(1)}, u32[]{:S(2)}, u32[]{:S(2)}) collective-permute-start(bf16[28,2176]{1,0:T(8,128)(2,1)S(1)} %constant_dynamic-update-slice_fusion), channel_id=1, source_target_pairs={{0,2},{1,3},{2,0},{3,1},{4,6},{5,7},{6,4},{7,5},{8,10},{9,11},{10,... | collective-permute-start | bytes 365576 | tf_op jit(solution)/shard_map/ppermute | solution.py:490
  15.0 11.8 %collective-permute-start.2 = (bf16[28,2176]{1,0:T(8,128)(2,1)S(1)}, bf16[28,2176]{1,0:T(8,128)(2,1)S(1)}, u32[]{:S(2)}, u32[]{:S(2)}) collective-permute-start(bf16[28,2176]{1,0:T(8,128)(2,1)S(1)} %constant_dynamic-update-slice_fusion), channel_id=1, source_target_pairs={{0,1},{1,2},{2,3},{3,0},{4,5},{5,6},{6,7},{7,4},{8,9},{9,10},{10,1... | collective-permute-start | bytes 365576 | tf_op jit(solution)/shard_map/ppermute | solution.py:490
  18.4 107.9 %copy-start.8 = (bf16[256,896]{1,0:T(8,128)(2,1)}, bf16[256,896]{1,0:T(8,128)(2,1)S(1)}, u32[]{:S(2)}) copy-start(bf16[256,896]{1,0:T(8,128)(2,1)S(1)} %get-tuple-element.263.refs_4_) | copy-start | bytes 1376260
  27.2 10.0 %collective-permute-start.3 = (bf16[112,1024]{1,0:T(8,128)(2,1)S(1)}, bf16[112,1024]{1,0:T(8,128)(2,1)S(1)}, u32[]{:S(2)}, u32[]{:S(2)}) collective-permute-start(bf16[112,1024]{1,0:T(8,128)(2,1)S(1)} %slice.75), channel_id=1, source_target_pairs={{0,8},{4,12},{8,0},{12,4},{16,24},{20,28},{24,16},{28,20},{1,9},{5... | collective-permute-start | bytes 688136 | tf_op jit(solution)/shard_map/ppermute | solution.py:481
  29.7 8.6 %collective-permute-start.4 = (bf16[112,1152]{1,0:T(8,128)(2,1)S(1)}, bf16[112,1152]{1,0:T(8,128)(2,1)S(1)}, u32[]{:S(2)}, u32[]{:S(2)}) collective-permute-start(bf16[112,1152]{1,0:T(8,128)(2,1)S(1)} %slice.76), channel_id=1, source_target_pairs={{0,16},{4,20},{8,24},{12,28},{16,0},{20,4},{24,8},{28,12},{1,17},{... | collective-permute-start | bytes 774152 | tf_op jit(solution)/shard_map/ppermute | solution.py:481
  31.3 11.0 %collective-permute-start.5 = (bf16[112,896]{1,0:T(8,128)(2,1)S(1)}, bf16[112,896]{1,0:T(8,128)(2,1)S(1)}, u32[]{:S(2)}, u32[]{:S(2)}) collective-permute-start(bf16[112,896]{1,0:T(8,128)(2,1)S(1)} %slice.77), channel_id=1, source_target_pairs={{0,2},{2,0},{1,3},{3,1},{4,6},{6,4},{5,7},{7,5},{8,10},{10,8},{9,1... | collective-permute-start | bytes 602120 | tf_op jit(solution)/shard_map/ppermute | solution.py:493
  42.3 22.6 %collective-permute-start.6 = (bf16[2,112,1024]{2,1,0:T(8,128)(2,1)S(1)}, bf16[2,112,1024]{2,1,0:T(8,128)(2,1)S(1)}, u32[]{:S(2)}, u32[]{:S(2)}) collective-permute-start(bf16[2,112,1024]{2,1,0:T(8,128)(2,1)S(1)} %pad_maximum_fusion.4), channel_id=1, source_target_pairs={{0,16},{4,20},{8,24},{12,28},{16,0},{20,4},{24,8},{28,12},{1,17},{... | collective-permute-start | bytes 1376264 | tf_op jit(solution)/shard_map/ppermute | solution.py:481
  42.9 25.1 %collective-permute-start.7 = (bf16[2,112,1152]{2,1,0:T(8,128)(2,1)S(1)}, bf16[2,112,1152]{2,1,0:T(8,128)(2,1)S(1)}, u32[]{:S(2)}, u32[]{:S(2)}) collective-permute-start(bf16[2,112,1152]{2,1,0:T(8,128)(2,1)S(1)} %pad_maximum_fusion.3), channel_id=1, source_target_pairs={{0,8},{4,12},{8,0},{12,4},{16,24},{20,28},{24,16},{28,20},{1,9},{5... | collective-permute-start | bytes 1548296 | tf_op jit(solution)/shard_map/ppermute | solution.py:481
  43.4 24.7 %collective-permute-start.8 = (bf16[112,2048]{1,0:T(8,128)(2,1)S(1)}, bf16[112,2048]{1,0:T(8,128)(2,1)S(1)}, u32[]{:S(2)}, u32[]{:S(2)}) collective-permute-start(bf16[112,2048]{1,0:T(8,128)(2,1)S(1)} %slice.80), channel_id=1, source_target_pairs={{0,2},{2,0},{1,3},{3,1},{4,6},{6,4},{5,7},{7,5},{8,10},{10,8},{9,1... | collective-permute-start | bytes 1376264 | tf_op jit(solution)/shard_map/ppermute | solution.py:493
  43.5 24.6 %collective-permute-start.9 = (bf16[256,896]{1,0:T(8,128)(2,1)}, bf16[256,896]{1,0:T(8,128)(2,1)S(1)}, u32[]{:S(2)}, u32[]{:S(2)}) collective-permute-start(bf16[256,896]{1,0:T(8,128)(2,1)} %get-tuple-element.252.refs_4_), channel_id=1, source_target_pairs={{0,1},{1,0},{2,3},{3,2},{4,5},{5,4},{6,7},{7,6},{8,9},{9,8},{10,11... | collective-permute-start | bytes 1376264 | tf_op jit(solution)/shard_map/ppermute | solution.py:493
  68.2 57.6 %copy-start.25 = (bf16[256,896]{1,0:T(8,128)(2,1)}, bf16[256,896]{1,0:T(8,128)(2,1)S(1)}, u32[]{:S(2)}) copy-start(bf16[256,896]{1,0:T(8,128)(2,1)S(1)} %collective-permute-done.9.refs_6_) | copy-start | bytes 1376260
  68.2 10.5 %collective-permute-start.11 = (bf16[2,2,112,1152]{3,2,1,0:T(8,128)(2,1)S(1)}, bf16[2,2,112,1152]{3,2,1,0:T(8,128)(2,1)}, u32[]{:S(2)}, u32[]{:S(2)}) collective-permute-start(bf16[2,2,112,1152]{3,2,1,0:T(8,128)(2,1)S(1)} %pad_maximum_fusion), channel_id=1, source_target_pairs={{0,4},{4,0},{8,12},{12,8},{16,20},{20,16},{24,28},{28,24},{1,5},{5... | collective-permute-start | bytes 3096584 | tf_op jit(solution)/shard_map/ppermute | solution.py:481
  68.3 9.4 %collective-permute-start.10 = (bf16[2,2,112,1024]{3,2,1,0:T(8,128)(2,1)S(1)}, bf16[2,2,112,1024]{3,2,1,0:T(8,128)(2,1)S(1)}, u32[]{:S(2)}, u32[]{:S(2)}) collective-permute-start(bf16[2,2,112,1024]{3,2,1,0:T(8,128)(2,1)S(1)} %pad_maximum_fusion.1), channel_id=1, source_target_pairs={{0,4},{4,0},{8,12},{12,8},{16,20},{20,16},{24,28},{28,24},{1,5},{5... | collective-permute-start | bytes 2752520 | tf_op jit(solution)/shard_map/ppermute | solution.py:481
  68.8 8.9 %collective-permute-start.12 = (bf16[112,896]{1,0:T(8,128)(2,1)S(1)}, bf16[112,896]{1,0:T(8,128)(2,1)S(1)}, u32[]{:S(2)}, u32[]{:S(2)}) collective-permute-start(bf16[112,896]{1,0:T(8,128)(2,1)S(1)} %slice.81), channel_id=1, source_target_pairs={{0,2},{2,0},{1,3},{3,1},{4,6},{6,4},{5,7},{7,5},{8,10},{10,8},{9,1... | collective-permute-start | bytes 602120 | tf_op jit(solution)/shard_map/ppermute | solution.py:493
  79.7 173.1 %reduce-scatter.3.cloned.1.call-start = ((), (), s32[]{:S(2)}) async-start(), calls=%async_computation.4 | async-start | bytes 2867200 | tf_op jit(solution)/shard_map/reduce_scatter | solution.py:633
  88.1 14.0 %collective-permute-start.13 = (bf16[256,256]{1,0:T(8,128)(2,1)}, bf16[256,256]{1,0:T(8,128)(2,1)S(1)}, u32[]{:S(2)}, u32[]{:S(2)}) collective-permute-start(bf16[256,256]{1,0:T(8,128)(2,1)} %get-tuple-element.233.kv0_ref), channel_id=1, source_target_pairs={{0,1},{1,2},{2,3},{4,5},{5,6},{6,7},{8,9},{9,10},{10,11},{12,13},{... | collective-permute-start | bytes 393224 | tf_op jit(solution)/shard_map/ppermute | solution.py:585
  89.4 12.7 %collective-permute-start.14 = (bf16[256,256]{1,0:T(8,128)(2,1)}, bf16[256,256]{1,0:T(8,128)(2,1)S(1)}, u32[]{:S(2)}, u32[]{:S(2)}) collective-permute-start(bf16[256,256]{1,0:T(8,128)(2,1)} %get-tuple-element.233.kv0_ref), channel_id=1, source_target_pairs={{0,2},{1,3},{4,6},{5,7},{8,10},{9,11},{12,14},{13,15},{16,18},{17,... | collective-permute-start | bytes 393224 | tf_op jit(solution)/shard_map/ppermute | solution.py:585
  98.1 14.2 %collective-permute-start.15 = (bf16[256,256]{1,0:T(8,128)(2,1)S(1)}, bf16[256,256]{1,0:T(8,128)(2,1)S(1)}, u32[]{:S(2)}, u32[]{:S(2)}) collective-permute-start(bf16[256,256]{1,0:T(8,128)(2,1)S(1)} %copy-done.15), channel_id=1, source_target_pairs={{0,1},{1,2},{2,3},{4,5},{5,6},{6,7},{8,9},{9,10},{10,11},{12,13},{... | collective-permute-start | bytes 393224 | tf_op jit(solution)/shard_map/ppermute | solution.py:585
  99.4 13.0 %collective-permute-start.16 = (bf16[256,256]{1,0:T(8,128)(2,1)S(1)}, bf16[256,256]{1,0:T(8,128)(2,1)S(1)}, u32[]{:S(2)}, u32[]{:S(2)}) collective-permute-start(bf16[256,256]{1,0:T(8,128)(2,1)S(1)} %copy-done.15), channel_id=1, source_target_pairs={{0,2},{1,3},{4,6},{5,7},{8,10},{9,11},{12,14},{13,15},{16,18},{17,... | collective-permute-start | bytes 393224 | tf_op jit(solution)/shard_map/ppermute | solution.py:585
  112.4 10.0 %collective-permute-start.17 = (bf16[256,896]{1,0:T(8,128)(2,1)}, bf16[256,896]{1,0:T(8,128)(2,1)S(1)}, u32[]{:S(2)}, u32[]{:S(2)}) collective-permute-start(bf16[256,896]{1,0:T(8,128)(2,1)} %get-tuple-element.249.refs_0_), channel_id=1, source_target_pairs={{0,4},{4,0},{1,5},{5,1},{2,6},{6,2},{3,7},{7,3},{8,12},{12,8},{9,1... | collective-permute-start | bytes 1376264 | tf_op jit(solution)/shard_map/ppermute | solution.py:493
  112.5 13.1 %collective-permute-start.18 = (bf16[256,896]{1,0:T(8,128)(2,1)}, bf16[256,896]{1,0:T(8,128)(2,1)S(1)}, u32[]{:S(2)}, u32[]{:S(2)}) collective-permute-start(bf16[256,896]{1,0:T(8,128)(2,1)} %get-tuple-element.249.refs_0_), channel_id=1, source_target_pairs={{0,1},{1,0},{2,3},{3,2},{4,5},{5,4},{6,7},{7,6},{8,9},{9,8},{10,11... | collective-permute-start | bytes 1376264 | tf_op jit(solution)/shard_map/ppermute | solution.py:493
  112.6 13.1 %collective-permute-start.19 = (bf16[256,896]{1,0:T(8,128)(2,1)}, bf16[256,896]{1,0:T(8,128)(2,1)S(1)}, u32[]{:S(2)}, u32[]{:S(2)}) collective-permute-start(bf16[256,896]{1,0:T(8,128)(2,1)} %get-tuple-element.252.refs_4_), channel_id=1, source_target_pairs={{0,4},{4,0},{1,5},{5,1},{2,6},{6,2},{3,7},{7,3},{8,12},{12,8},{9,1... | collective-permute-start | bytes 1376264 | tf_op jit(solution)/shard_map/ppermute | solution.py:493
  125.6 2.0 collective-permute-start.23
  125.7 3.2 collective-permute-start.24
  126.2 27.3 %collective-permute-start.25 = (bf16[256,896]{1,0:T(8,128)(2,1)S(1)}, bf16[256,896]{1,0:T(8,128)(2,1)S(1)}, u32[]{:S(2)}, u32[]{:S(2)}) collective-permute-start(bf16[256,896]{1,0:T(8,128)(2,1)S(1)} %get-tuple-element.263.refs_4_), channel_id=1, source_target_pairs={{0,4},{4,0},{1,5},{5,1},{2,6},{6,2},{3,7},{7,3},{8,12},{12,8},{9,1... | collective-permute-start | bytes 1376264 | tf_op jit(solution)/shard_map/ppermute | solution.py:493
  126.3 27.3 %collective-permute-start.26 = (bf16[256,896]{1,0:T(8,128)(2,1)S(1)}, bf16[256,896]{1,0:T(8,128)(2,1)S(1)}, u32[]{:S(2)}, u32[]{:S(2)}) collective-permute-start(bf16[256,896]{1,0:T(8,128)(2,1)S(1)} %get-tuple-element.263.refs_4_), channel_id=1, source_target_pairs={{0,1},{1,0},{2,3},{3,2},{4,5},{5,4},{6,7},{7,6},{8,9},{9,8},{10,11... | collective-permute-start | bytes 1376264 | tf_op jit(solution)/shard_map/ppermute | solution.py:493
  126.6 28.0 %collective-permute-start.20 = (bf16[256,896]{1,0:T(8,128)(2,1)}, bf16[256,896]{1,0:T(8,128)(2,1)S(1)}, u32[]{:S(2)}, u32[]{:S(2)}) collective-permute-start(bf16[256,896]{1,0:T(8,128)(2,1)} %get-tuple-element.248.refs_0_), channel_id=1, source_target_pairs={{0,4},{4,0},{1,5},{5,1},{2,6},{6,2},{3,7},{7,3},{8,12},{12,8},{9,1... | collective-permute-start | bytes 1376264 | tf_op jit(solution)/shard_map/ppermute | solution.py:493
  127.6 28.3 %collective-permute-start.21 = (bf16[256,896]{1,0:T(8,128)(2,1)}, bf16[256,896]{1,0:T(8,128)(2,1)S(1)}, u32[]{:S(2)}, u32[]{:S(2)}) collective-permute-start(bf16[256,896]{1,0:T(8,128)(2,1)} %get-tuple-element.248.refs_0_), channel_id=1, source_target_pairs={{0,1},{1,0},{2,3},{3,2},{4,5},{5,4},{6,7},{7,6},{8,9},{9,8},{10,11... | collective-permute-start | bytes 1376264 | tf_op jit(solution)/shard_map/ppermute | solution.py:493
  129.0 29.4 %collective-permute-start.22 = (bf16[256,896]{1,0:T(8,128)(2,1)}, bf16[256,896]{1,0:T(8,128)(2,1)S(1)}, u32[]{:S(2)}, u32[]{:S(2)}) collective-permute-start(bf16[256,896]{1,0:T(8,128)(2,1)} %get-tuple-element.248.refs_0_), channel_id=1, source_target_pairs={{0,5},{1,4},{4,1},{5,0},{2,7},{3,6},{6,3},{7,2},{8,13},{9,12},{12,... | collective-permute-start | bytes 1376264 | tf_op jit(solution)/shard_map/ppermute | solution.py:496
  153.6 4.8 %collective-permute-start.27 = (bf16[256,896]{1,0:T(8,128)(2,1)S(1)}, bf16[256,896]{1,0:T(8,128)(2,1)S(1)}, u32[]{:S(2)}, u32[]{:S(2)}) collective-permute-start(bf16[256,896]{1,0:T(8,128)(2,1)S(1)} %collective-permute-done.26.refs_6_), channel_id=1, source_target_pairs={{0,4},{4,0},{1,5},{5,1},{2,6},{6,2},{3,7},{7,3},{8,12},{12,8},{9,1... | collective-permute-start | bytes 1376264 | tf_op jit(solution)/shard_map/ppermute | solution.py:493
  154.5 30.5 %collective-permute-start.28 = (bf16[256,896]{1,0:T(8,128)(2,1)}, bf16[256,896]{1,0:T(8,128)(2,1)S(1)}, u32[]{:S(2)}, u32[]{:S(2)}) collective-permute-start(bf16[256,896]{1,0:T(8,128)(2,1)} %get-tuple-element.275), channel_id=1, source_target_pairs={{0,4},{4,0},{1,5},{5,1},{2,6},{6,2},{3,7},{7,3},{8,12},{12,8},{9,1... | collective-permute-start | bytes 1376264 | tf_op jit(solution)/shard_map/ppermute | solution.py:493
  154.6 30.4 %collective-permute-start.29 = (bf16[256,896]{1,0:T(8,128)(2,1)}, bf16[256,896]{1,0:T(8,128)(2,1)S(1)}, u32[]{:S(2)}, u32[]{:S(2)}) collective-permute-start(bf16[256,896]{1,0:T(8,128)(2,1)} %get-tuple-element.276), channel_id=1, source_target_pairs={{0,1},{1,0},{2,3},{3,2},{4,5},{5,4},{6,7},{7,6},{8,9},{9,8},{10,11... | collective-permute-start | bytes 1376264 | tf_op jit(solution)/shard_map/ppermute | solution.py:493
  155.9 29.2 %collective-permute-start.30 = (bf16[256,896]{1,0:T(8,128)(2,1)}, bf16[256,896]{1,0:T(8,128)(2,1)S(1)}, u32[]{:S(2)}, u32[]{:S(2)}) collective-permute-start(bf16[256,896]{1,0:T(8,128)(2,1)} %get-tuple-element.277), channel_id=1, source_target_pairs={{0,5},{1,4},{4,1},{5,0},{2,7},{3,6},{6,3},{7,2},{8,13},{9,12},{12,... | collective-permute-start | bytes 1376264 | tf_op jit(solution)/shard_map/ppermute | solution.py:496
  183.7 11.8 %collective-permute-start.31 = (bf16[256,896]{1,0:T(8,128)(2,1)}, bf16[256,896]{1,0:T(8,128)(2,1)S(1)}, u32[]{:S(2)}, u32[]{:S(2)}) collective-permute-start(bf16[256,896]{1,0:T(8,128)(2,1)} %get-tuple-element.279), channel_id=1, source_target_pairs={{0,4},{4,0},{1,5},{5,1},{2,6},{6,2},{3,7},{7,3},{8,12},{12,8},{9,1... | collective-permute-start | bytes 1376264 | tf_op jit(solution)/shard_map/ppermute | solution.py:493
  185.0 12.7 %collective-permute-start.32 = (bf16[256,896]{1,0:T(8,128)(2,1)}, bf16[256,896]{1,0:T(8,128)(2,1)S(1)}, u32[]{:S(2)}, u32[]{:S(2)}) collective-permute-start(bf16[256,896]{1,0:T(8,128)(2,1)} %get-tuple-element.280), channel_id=1, source_target_pairs={{0,1},{1,0},{2,3},{3,2},{4,5},{5,4},{6,7},{7,6},{8,9},{9,8},{10,11... | collective-permute-start | bytes 1376264 | tf_op jit(solution)/shard_map/ppermute | solution.py:493
  195.5 19.8 %copy-start.29 = (bf16[256,896]{1,0:T(8,128)(2,1)}, bf16[256,896]{1,0:T(8,128)(2,1)S(1)}, u32[]{:S(2)}) copy-start(bf16[256,896]{1,0:T(8,128)(2,1)S(1)} %collective-permute-done.31.refs_1_) | copy-start | bytes 1376260
  197.8 93.9 %reduce-scatter.5.cloned.1.call-start = ((), (), s32[]{:S(2)}) async-start(), calls=%async_computation.5 | async-start | bytes 5734400 | tf_op jit(solution)/shard_map/reduce_scatter | solution.py:634
  198.5 16.8 %collective-permute-start.34 = (bf16[2,256,896]{2,1,0:T(8,128)(2,1)S(1)}, bf16[2,256,896]{2,1,0:T(8,128)(2,1)S(1)}, u32[]{:S(2)}, u32[]{:S(2)}) collective-permute-start(bf16[2,256,896]{2,1,0:T(8,128)(2,1)S(1)} %copy-done.10), channel_id=1, source_target_pairs={{0,4},{4,0},{1,5},{5,1},{2,6},{6,2},{3,7},{7,3},{8,12},{12,8},{9,1... | collective-permute-start | bytes 2752520 | tf_op jit(solution)/shard_map/ppermute | solution.py:493
  198.5 16.8 %collective-permute-start.35 = (bf16[2,256,896]{2,1,0:T(8,128)(2,1)S(1)}, bf16[2,256,896]{2,1,0:T(8,128)(2,1)}, u32[]{:S(2)}, u32[]{:S(2)}) collective-permute-start(bf16[2,256,896]{2,1,0:T(8,128)(2,1)S(1)} %copy-done.11), channel_id=1, source_target_pairs={{0,4},{4,0},{1,5},{5,1},{2,6},{6,2},{3,7},{7,3},{8,12},{12,8},{9,1... | collective-permute-start | bytes 2752520 | tf_op jit(solution)/shard_map/ppermute | solution.py:493
  199.0 16.2 %collective-permute-start.33 = (bf16[256,896]{1,0:T(8,128)(2,1)}, bf16[256,896]{1,0:T(8,128)(2,1)}, u32[]{:S(2)}, u32[]{:S(2)}) collective-permute-start(bf16[256,896]{1,0:T(8,128)(2,1)} %get-tuple-element.289), channel_id=1, source_target_pairs={{0,5},{1,4},{4,1},{5,0},{2,7},{3,6},{6,3},{7,2},{8,13},{9,12},{12,... | collective-permute-start | bytes 1376264 | tf_op jit(solution)/shard_map/ppermute | solution.py:496
  217.6 14.6 %collective-permute-start.36 = (bf16[256,896]{1,0:T(8,128)(2,1)S(1)}, bf16[256,896]{1,0:T(8,128)(2,1)S(1)}, u32[]{:S(2)}, u32[]{:S(2)}) collective-permute-start(bf16[256,896]{1,0:T(8,128)(2,1)S(1)} %fusion.11), channel_id=1, source_target_pairs={{0,1},{1,0},{2,3},{3,2},{4,5},{5,4},{6,7},{7,6},{8,9},{9,8},{10,11... | collective-permute-start | bytes 1376264 | tf_op jit(solution)/shard_map/ppermute | solution.py:493
  233.3 16.9 %collective-permute-start.37 = (bf16[256,896]{1,0:T(8,128)(2,1)S(1)}, bf16[256,896]{1,0:T(8,128)(2,1)S(1)}, u32[]{:S(2)}, u32[]{:S(2)}) collective-permute-start(bf16[256,896]{1,0:T(8,128)(2,1)S(1)} %fusion.12), channel_id=1, source_target_pairs={{0,1},{1,0},{2,3},{3,2},{4,5},{5,4},{6,7},{7,6},{8,9},{9,8},{10,11... | collective-permute-start | bytes 1376264 | tf_op jit(solution)/shard_map/ppermute | solution.py:493
  234.1 20.6 %collective-permute-start.38 = (bf16[256,256]{1,0:T(8,128)(2,1)}, bf16[256,256]{1,0:T(8,128)(2,1)S(1)}, u32[]{:S(2)}, u32[]{:S(2)}) collective-permute-start(bf16[256,256]{1,0:T(8,128)(2,1)} %get-tuple-element.340), channel_id=1, source_target_pairs={{1,0},{2,1},{3,2},{5,4},{6,5},{7,6},{9,8},{10,9},{11,10},{13,12},{... | collective-permute-start | bytes 393224 | tf_op jit(solution)/shard_map/ppermute | solution.py:649
  235.4 19.3 %collective-permute-start.39 = (bf16[256,256]{1,0:T(8,128)(2,1)}, bf16[256,256]{1,0:T(8,128)(2,1)S(1)}, u32[]{:S(2)}, u32[]{:S(2)}) collective-permute-start(bf16[256,256]{1,0:T(8,128)(2,1)} %get-tuple-element.341), channel_id=1, source_target_pairs={{2,0},{3,1},{6,4},{7,5},{10,8},{11,9},{14,12},{15,13},{18,16},{19,... | collective-permute-start | bytes 393224 | tf_op jit(solution)/shard_map/ppermute | solution.py:649
  250.2 18.0 %copy-start.24 = (bf16[256,896]{1,0:T(8,128)(2,1)}, bf16[256,896]{1,0:T(8,128)(2,1)S(1)}, u32[]{:S(2)}) copy-start(bf16[256,896]{1,0:T(8,128)(2,1)S(1)} %collective-permute-done.37) | copy-start | bytes 1376260
  250.2 8.3 %collective-permute-start.40 = (bf16[256,256]{1,0:T(8,128)(2,1)}, bf16[256,256]{1,0:T(8,128)(2,1)S(1)}, u32[]{:S(2)}, u32[]{:S(2)}) collective-permute-start(bf16[256,256]{1,0:T(8,128)(2,1)} %get-tuple-element.342), channel_id=1, source_target_pairs={{1,0},{2,1},{3,2},{5,4},{6,5},{7,6},{9,8},{10,9},{11,10},{13,12},{... | collective-permute-start | bytes 393224 | tf_op jit(solution)/shard_map/ppermute | solution.py:649
  251.5 13.2 %collective-permute-start.41 = (bf16[256,256]{1,0:T(8,128)(2,1)}, bf16[256,256]{1,0:T(8,128)(2,1)S(1)}, u32[]{:S(2)}, u32[]{:S(2)}) collective-permute-start(bf16[256,256]{1,0:T(8,128)(2,1)} %get-tuple-element.343), channel_id=1, source_target_pairs={{2,0},{3,1},{6,4},{7,5},{10,8},{11,9},{14,12},{15,13},{18,16},{19,... | collective-permute-start | bytes 393224 | tf_op jit(solution)/shard_map/ppermute | solution.py:649
  254.7 13.5 %copy-start.34 = (bf16[256,256]{1,0:T(8,128)(2,1)}, bf16[256,256]{1,0:T(8,128)(2,1)S(1)}, u32[]{:S(2)}) copy-start(bf16[256,256]{1,0:T(8,128)(2,1)S(1)} %collective-permute-done.38.refs_0_) | copy-start | bytes 393220
  254.7 13.5 %copy-start.35 = (bf16[256,256]{1,0:T(8,128)(2,1)}, bf16[256,256]{1,0:T(8,128)(2,1)S(1)}, u32[]{:S(2)}) copy-start(bf16[256,256]{1,0:T(8,128)(2,1)S(1)} %collective-permute-done.39.refs_1_) | copy-start | bytes 393220
  264.7 15.2 %collective-permute-start.42 = (bf16[112,1280]{1,0:T(8,128)(2,1)}, bf16[112,1280]{1,0:T(8,128)(2,1)S(1)}, u32[]{:S(2)}, u32[]{:S(2)}) collective-permute-start(bf16[112,1280]{1,0:T(8,128)(2,1)} %get-tuple-element.352), channel_id=1, source_target_pairs={{0,0},{2,4},{4,6},{6,2},{1,1},{3,5},{5,7},{7,3},{8,8},{10,12},{12,... | collective-permute-start | bytes 860168 | tf_op jit(solution)/shard_map/ppermute | solution.py:661
  266.3 14.1 %collective-permute-start.43 = (bf16[112,1280]{1,0:T(8,128)(2,1)}, bf16[112,1280]{1,0:T(8,128)(2,1)}, u32[]{:S(2)}, u32[]{:S(2)}) collective-permute-start(bf16[112,1280]{1,0:T(8,128)(2,1)} %get-tuple-element.353), channel_id=1, source_target_pairs={{0,4},{2,0},{4,2},{6,6},{1,5},{3,1},{5,3},{7,7},{8,12},{10,8},{12,... | collective-permute-start | bytes 860168 | tf_op jit(solution)/shard_map/ppermute | solution.py:661
  280.3 4.3 %collective-permute-start.44 = (bf16[448,2176]{1,0:T(8,128)(2,1)}, bf16[448,2176]{1,0:T(8,128)(2,1)}, u32[]{:S(2)}, u32[]{:S(2)}) collective-permute-start(bf16[448,2176]{1,0:T(8,128)(2,1)} %get-tuple-element.355), channel_id=1, source_target_pairs={{0,4},{4,0},{8,12},{12,8},{16,20},{20,16},{24,28},{28,24},{1,5},{5... | collective-permute-start | bytes 5849096 | tf_op jit(solution)/shard_map/ppermute | solution.py:481
  289.1 12.8 %collective-permute-start.46 = (bf16[1,2,112,1024]{3,2,1,0:T(8,128)(2,1)}, bf16[1,2,112,1024]{3,2,1,0:T(8,128)(2,1)}, u32[]{:S(2)}, u32[]{:S(2)}) collective-permute-start(bf16[1,2,112,1024]{3,2,1,0:T(8,128)(2,1)} %fusion.13), channel_id=1, source_target_pairs={{0,16},{4,20},{8,24},{12,28},{16,0},{20,4},{24,8},{28,12},{1,17},{... | collective-permute-start | bytes 1376264 | tf_op jit(solution)/shard_map/ppermute | solution.py:481
  290.2 13.7 %collective-permute-start.45 = (bf16[2,1,112,1152]{3,2,0,1:T(8,128)(2,1)S(1)}, bf16[2,1,112,1152]{3,2,0,1:T(8,128)(2,1)}, u32[]{:S(2)}, u32[]{:S(2)}) collective-permute-start(bf16[2,1,112,1152]{3,2,0,1:T(8,128)(2,1)S(1)} %fusion.9), channel_id=1, source_target_pairs={{0,8},{4,12},{8,0},{12,4},{16,24},{20,28},{24,16},{28,20},{1,9},{5... | collective-permute-start | bytes 1548296 | tf_op jit(solution)/shard_map/ppermute | solution.py:481
  292.8 12.3 %collective-permute-start.47 = (bf16[112,2560]{1,0:T(8,128)(2,1)S(1)}, bf16[112,2560]{1,0:T(8,128)(2,1)S(1)}, u32[]{:S(2)}, u32[]{:S(2)}) collective-permute-start(bf16[112,2560]{1,0:T(8,128)(2,1)S(1)} %dynamic-slice_bitcast_fusion.1), channel_id=1, source_target_pairs={{0,0},{2,4},{4,6},{6,2},{1,1},{3,5},{5,7},{7,3},{8,8},{10,12},{12,... | collective-permute-start | bytes 1720328 | tf_op jit(solution)/shard_map/ppermute | solution.py:661
  305.1 9.1 %collective-permute-start.48 = (bf16[1,1,112,1152]{3,2,1,0:T(8,128)(2,1)S(1)}, bf16[1,1,112,1152]{3,2,1,0:T(8,128)(2,1)S(1)}, u32[]{:S(2)}, u32[]{:S(2)}) collective-permute-start(bf16[1,1,112,1152]{3,2,1,0:T(8,128)(2,1)S(1)} %fusion.19), channel_id=1, source_target_pairs={{0,16},{4,20},{8,24},{12,28},{16,0},{20,4},{24,8},{28,12},{1,17},{... | collective-permute-start | bytes 774152 | tf_op jit(solution)/shard_map/ppermute | solution.py:481
  306.1 8.0 %collective-permute-start.49 = (bf16[1,1,112,1024]{3,2,1,0:T(8,128)(2,1)S(1)}, bf16[1,1,112,1024]{3,2,1,0:T(8,128)(2,1)S(1)}, u32[]{:S(2)}, u32[]{:S(2)}) collective-permute-start(bf16[1,1,112,1024]{3,2,1,0:T(8,128)(2,1)S(1)} %fusion.20), channel_id=1, source_target_pairs={{0,8},{4,12},{8,0},{12,4},{16,24},{20,28},{24,16},{28,20},{1,9},{5... | collective-permute-start | bytes 688136 | tf_op jit(solution)/shard_map/ppermute | solution.py:481
  307.4 28.9 %collective-permute-start.53 = (bf16[112,2560]{1,0:T(8,128)(2,1)S(1)}, bf16[112,2560]{1,0:T(8,128)(2,1)S(1)}, u32[]{:S(2)}, u32[]{:S(2)}) collective-permute-start(bf16[112,2560]{1,0:T(8,128)(2,1)S(1)} %dynamic-slice_bitcast_fusion), channel_id=1, source_target_pairs={{0,4},{2,0},{4,2},{6,6},{1,5},{3,1},{5,3},{7,7},{8,12},{10,8},{12,... | collective-permute-start | bytes 1720328 | tf_op jit(solution)/shard_map/ppermute | solution.py:661
  314.5 8.5 %collective-permute-start.50 = (bf16[28,2176]{1,0:T(8,128)(2,1)S(1)}, bf16[28,2176]{1,0:T(8,128)(2,1)S(1)}, u32[]{:S(2)}, u32[]{:S(2)}) collective-permute-start(bf16[28,2176]{1,0:T(8,128)(2,1)S(1)} %get-tuple-element.449), channel_id=1, source_target_pairs={{0,1},{1,2},{2,3},{3,0},{4,5},{5,6},{6,7},{7,4},{8,9},{9,10},{10,1... | collective-permute-start | bytes 365576 | tf_op jit(solution)/shard_map/ppermute | solution.py:490
  314.7 21.5 %collective-permute-start.51 = (bf16[28,2176]{1,0:T(8,128)(2,1)S(1)}, bf16[28,2176]{1,0:T(8,128)(2,1)S(1)}, u32[]{:S(2)}, u32[]{:S(2)}) collective-permute-start(bf16[28,2176]{1,0:T(8,128)(2,1)S(1)} %get-tuple-element.448), channel_id=1, source_target_pairs={{0,2},{1,3},{2,0},{3,1},{4,6},{5,7},{6,4},{7,5},{8,10},{9,11},{10,... | collective-permute-start | bytes 365576 | tf_op jit(solution)/shard_map/ppermute | solution.py:490
  318.3 17.9 %collective-permute-start.52 = (bf16[28,2176]{1,0:T(8,128)(2,1)S(1)}, bf16[28,2176]{1,0:T(8,128)(2,1)S(1)}, u32[]{:S(2)}, u32[]{:S(2)}) collective-permute-start(bf16[28,2176]{1,0:T(8,128)(2,1)S(1)} %get-tuple-element.447), channel_id=1, source_target_pairs={{0,3},{1,0},{2,1},{3,2},{4,7},{5,4},{6,5},{7,6},{8,11},{9,8},{10,9... | collective-permute-start | bytes 365576 | tf_op jit(solution)/shard_map/ppermute | solution.py:490
  (42 other events, 139.5 us)
Sparse Core Ops, SparseCore 0:
  10.0 65.8 all-gather.2
  79.8 46.7 all-gather.4
  197.9 34.5 reduce-scatter.2
  235.5 55.9 reduce-scatter.4
